TPU v7x, 256 devices: a whole 4x4x8 slice. The times are simulated.
256 devices in a mesh: dp: 2 (over y_lo), vocab: 128 (over z, x, y_hi, core).
Axes of the slice: x: 4, y: 4 (y_hi: 2, y_lo: 2; y = y_hi * 2 + y_lo), z: 8, core: 2. Of those that a mesh axis runs over, the one named last changes fastest.
Arguments:
- token_ids: int32 [1024], P(('dp', 'vocab')), may hold values from 0 to 131071
- hidden: bfloat16 [1024, 2304], P(('dp', 'vocab')), may hold values from -6 to 6
- logit_grad: bfloat16 [1024, 131072], P('dp', 'vocab'), may hold values from -0.1875 to 0.1875
- embed_grad: bfloat16 [1024, 2304], P(('dp', 'vocab')), may hold values from -6 to 6
Outputs:
- weight_grad: float32 [131072, 2304], P('vocab', 'dp')
All inputs are finite; a program needn't handle non-finite values.
Results may differ from a plain program's by a relative error of at most 0.0003.
Values may be sent and summed in bfloat16 or wider, within the bound.
No kernel may reach another device: no remote copies, remote signals or barrier semaphores. Data moves between devices by JAX's collectives and lax.ppermute only.
A program may use at most 64 MiB of HBM per device.

v0:
```python
import jax
import jax.numpy as jnp
from jax import lax
from jax.sharding import PartitionSpec as P


def side_by_side(arrays, axis, dim, along):
    widths = [a.shape[along] for a in arrays]
    both = jnp.concatenate(arrays, axis=along)
    result = lax.all_gather(both, axis, axis=dim, tiled=True)
    return tuple(jnp.split(result, [sum(widths[:k]) for k in range(1, len(widths))], axis=along))


def laid_out(tiles, dim):
    tiles = jnp.moveaxis(tiles, 0, dim)
    lengths = tiles.shape
    return tiles.reshape(*lengths[:dim], lengths[dim] * lengths[dim + 1], *lengths[dim + 2 :])


def from_everyone(shard, axis):
    length = lax.axis_size(axis)
    return lax.all_to_all(
        jnp.broadcast_to(shard[None], (length, *shard.shape)), axis, 0, 0, tiled=True
    )


def collect(shard, axis, dim):
    return laid_out(from_everyone(shard, axis), dim)


def contract(logits, features, input_grads, token_list, offset):
    vocab_rows = logits.shape[1]
    columns = offset + lax.broadcasted_iota(jnp.int32, (1, vocab_rows), 1)
    onehot = (token_list[:, None] == columns).astype(jnp.bfloat16)
    dims = (((0,), (0,)), ((), ()))
    output_side = lax.dot_general(logits, features, dims, preferred_element_type=jnp.float32)
    input_side = lax.dot_general(onehot, input_grads, dims, preferred_element_type=jnp.float32)
    return output_side + input_side


def reorder(values, groups, shards):
    stride = values.shape[0] // (groups * shards)
    shaped = values.reshape((groups, shards, stride) + values.shape[1:])
    return jnp.swapaxes(shaped, 0, 1).reshape(values.shape)


def body(token_ids, hidden, logit_grad, embed_grad):
    offset = lax.axis_index("vocab") * logit_grad.shape[1]
    groups = lax.axis_size("dp")
    shards = lax.axis_size("vocab")
    widened = jnp.broadcast_to(token_ids[:, None], (token_ids.shape[0], groups))
    halves = (
        lax.all_to_all(hidden, "dp", split_axis=1, concat_axis=0, tiled=True),
        lax.all_to_all(embed_grad, "dp", split_axis=1, concat_axis=0, tiled=True),
        lax.all_to_all(widened, "dp", split_axis=1, concat_axis=0, tiled=True),
    )
    features, input_grads, id_column = (
        *side_by_side((halves[0], halves[1]), "vocab", 0, 1),
        lax.all_gather(halves[2], "vocab", axis=0, tiled=True),
    )
    logits = collect(logit_grad, "dp", 0)
    logits = reorder(logits, groups, shards)
    token_list = id_column.reshape(-1)
    return contract(logits, features, input_grads, token_list, offset)


def solution(mesh):
    placed = (
        P(("dp", "vocab")),
        P(("dp", "vocab"), None),
        P("dp", "vocab"),
        P(("dp", "vocab"), None),
    )
    return jax.shard_map(
        body, mesh=mesh, in_specs=placed, out_specs=P("vocab", "dp"), check_vma=False
    )
```

profile of v0, /device:TPU:1, one launch (start us, length us, event | category | flops | bytes accessed | tf_op | source)
XLA Modules:
  0.0 170.1 jit_solution(8613822747679268472)
XLA Ops:
  6.5 0.0 copy-start.1
  6.5 6.7 %all_to_all.59 = bf16[4,2,1152]{2,0,1:T(4,128)(2,1)S(1)} all-to-all(bf16[4,2,1152]{2,0,1:T(4,128)(2,1)} %bitcast.16), channel_id=1, replica_groups=mesh['dp'=2,'vocab'=128] {'dp'}, dimensions={1} | all-to-all | bytes 36864 | tf_op jit(solution)/shard_map/all_to_all | solution.py:53
  13.3 3.2 %all-to-all-start.1 = ((bf16[4,2,1152]{2,0,1:T(4,128)(2,1)}), bf16[4,2,1152]{2,0,1:T(4,128)(2,1)S(1)}, u32[]{:S(2)}, u32[]{:S(2)}) async-start(bf16[4,2,1152]{2,0,1:T(4,128)(2,1)} %bitcast.17), calls=%async_computation.1 | async-start | bytes 36864 | tf_op jit(solution)/shard_map/all_to_all | solution.py:54
  16.5 0.0 all-gather.2.cloned.1.call-start
  16.6 2.6 %all-to-all-done.1 = bf16[4,2,1152]{2,0,1:T(4,128)(2,1)S(1)} async-done(((bf16[4,2,1152]{2,0,1:T(4,128)(2,1)}), bf16[4,2,1152]{2,0,1:T(4,128)(2,1)S(1)}, u32[]{:S(2)}, u32[]{:S(2)}) %all-to-all-start.1) | async-done | bytes 18464 | tf_op jit(solution)/shard_map/all_to_all | solution.py:54
  19.2 0.6 pad_maximum_fusion
  19.9 0.0 all-gather.2.cloned.1.call-update
  19.9 0.7 broadcast_in_dim.5
  20.5 4.9 %all_to_all.60 = s32[4,2,1]{0,2,1:T(1,128)S(1)} all-to-all(s32[4,2,1]{0,2,1:T(1,128)S(1)} %broadcast_in_dim.5), channel_id=1, replica_groups=mesh['dp'=2,'vocab'=128] {'dp'}, dimensions={1} | all-to-all | bytes 64 | tf_op jit(solution)/shard_map/all_to_all | solution.py:55
  25.4 2.8 %broadcast_in_dim.4 = bf16[2,512,1024]{2,1,0:T(8,128)(2,1)} broadcast(bf16[512,1024]{1,0:T(8,128)(2,1)} %param.6), dimensions={1,2} | broadcast | bytes 3145728 | tf_op jit(solution)/shard_map/broadcast_in_dim | solution.py:23
  28.3 3.8 %all-to-all-start.2 = ((bf16[2,512,1024]{2,1,0:T(8,128)(2,1)}), bf16[2,512,1024]{2,1,0:T(8,128)(2,1)S(1)}, u32[]{:S(2)}, u32[]{:S(2)}) async-start(bf16[2,512,1024]{2,1,0:T(8,128)(2,1)} %broadcast_in_dim.4), calls=%async_computation.2 | async-start | bytes 4194304 | tf_op jit(solution)/shard_map/all_to_all | solution.py:22
  32.1 0.0 copy-done.1
  32.1 0.6 dynamic-slice
  33.4 0.1 reshape.24
  33.5 0.2 dynamic-update-slice
  33.7 39.2 %all-reduce = s32[1024]{0:T(1024)S(1)} all-reduce(s32[1024]{0:T(1024)S(1)} %dynamic-update-slice), channel_id=1, replica_groups=mesh['dp'=2,'vocab'=128] {'vocab'}, use_global_device_ids=true, to_apply=%add | all-reduce | flops 1024 | bytes 8192
  72.9 0.0 all-to-all-done.2
  72.9 2.2 %copy.18 = bf16[2,512,1024]{2,0,1:T(2,128)(2,1)S(1)} copy(bf16[2,512,1024]{2,1,0:T(8,128)(2,1)S(1)} %all-to-all-done.2) | data formatting | bytes 4194304 | tf_op jit(solution)/shard_map/all_to_all | solution.py:22
  75.0 1.2 copy.19
  76.2 2.0 %reshape.23 = bf16[1024,1024]{1,0:T(8,128)(2,1)} reshape(bf16[128,2,4,1024]{3,2,1,0:T(4,128)(2,1)S(1)} %copy.19) | data formatting | bytes 4194304 | tf_op jit(solution)/shard_map/reshape | solution.py:44
  78.2 68.8 %all-gather.2.cloned.1.call-done = bf16[1024,2304]{1,0:T(8,128)(2,1)} async-done(((bf16[8,2304]{1,0:T(8,128)(2,1)}), bf16[1024,2304]{1,0:T(8,128)(2,1)}) %all-gather.2.cloned.1.call-update) | async-done | bytes 4718608 | tf_op jit(solution)/shard_map/all_gather | solution.py:10
  147.0 0.0 copy-start
  147.0 5.1 %fusion.2 = f32[1152,1024]{1,0:T(8,128)S(1)} fusion(bf16[1024,1024]{1,0:T(8,128)(2,1)} %reshape.23, bf16[1024,2304]{1,0:T(8,128)(2,1)} %all-gather.2.cloned.1.call-done), kind=kOutput, calls=%fused_computation.3 | convolution fusion | flops 2415919104 | bytes 9175040 | tf_op jit(solution)/shard_map/dot_general | solution.py:36
  152.1 0.0 copy-done
  152.1 5.1 %bitcast_add_fusion = f32[1024,1152]{0,1:T(8,128)} fusion(f32[1152,1024]{1,0:T(8,128)S(1)} %fusion.2, bf16[1024,2304]{1,0:T(8,128)(2,1)S(1)} %copy-done, s32[1024]{0:T(1024)S(1)} %iota_add_fusion, s32[1024]{0:T(1024)S(1)} %all-reduce), kind=kOutput, calls=%fused_computation | convolution fusion | flops 2418147328 | bytes 11804672 | tf_op jit(solution)/shard_map/dot_general | solution.py:37
  157.2 6.0 %copy.21 = f32[1024,1152]{1,0:T(8,128)} copy(f32[1024,1152]{0,1:T(8,128)} %bitcast_add_fusion) | data formatting | bytes 9437184 | tf_op jit(solution)/shard_map/add | solution.py:38
  (5 shorter events, 0.1 us)
Async XLA Ops:
  6.5 25.5 %copy-start.1 = (u32[256]{0:T(256)S(1)}, u32[256]{0:T(256)}, u32[]{:S(2)}) copy-start(u32[256]{0:T(256)} %constant.11) | copy-start | bytes 3076
  13.3 6.0 %all-to-all-start.1 = ((bf16[4,2,1152]{2,0,1:T(4,128)(2,1)}), bf16[4,2,1152]{2,0,1:T(4,128)(2,1)S(1)}, u32[]{:S(2)}, u32[]{:S(2)}) async-start(bf16[4,2,1152]{2,0,1:T(4,128)(2,1)} %bitcast.17), calls=%async_computation.1 | async-start | bytes 36864 | tf_op jit(solution)/shard_map/all_to_all | solution.py:54
  16.5 130.5 %all-gather.2.cloned.1.call-start = ((), (), s32[]{:S(2)}) async-start(), calls=%async_computation.4 | async-start | bytes 4755456 | tf_op jit(solution)/shard_map/all_gather | solution.py:10
  28.3 44.6 %all-to-all-start.2 = ((bf16[2,512,1024]{2,1,0:T(8,128)(2,1)}), bf16[2,512,1024]{2,1,0:T(8,128)(2,1)S(1)}, u32[]{:S(2)}, u32[]{:S(2)}) async-start(bf16[2,512,1024]{2,1,0:T(8,128)(2,1)} %broadcast_in_dim.4), calls=%async_computation.2 | async-start | bytes 4194304 | tf_op jit(solution)/shard_map/all_to_all | solution.py:22
  147.0 5.1 %copy-start = (bf16[1024,2304]{1,0:T(8,128)(2,1)S(1)}, bf16[1024,2304]{1,0:T(8,128)(2,1)}, u32[]{:S(2)}) copy-start(bf16[1024,2304]{1,0:T(8,128)(2,1)} %all-gather.2.cloned.1.call-done) | copy-start | bytes 14155780
Sparse Core Ops, SparseCore 0:
  21.2 125.7 all-gather.1
where the time goes:
time: 171 us; the launch traced here: 170 us
  waiting for transfers between devices  71.4 us (42%)
  blocking collectives  50.8 us (30%)
  local copies, waits for them, and re-layouts  15.9 us (9%)
  between operations  14.1 us (8%)
  matrix products  10.2 us (6%)
  starting transfers between devices  7.04 us (4%)
    all_gather x1, waiting for transfers between devices, side_by_side(): result = lax.all_gather(both, axis, axis=dim, tiled=True)  68.8 us
    unnamed x1, blocking collectives  39.2 us
    all_to_all x1, blocking collectives, body(): lax.all_to_all(hidden, 'dp', split_axis=1, concat_axis=0, tiled=True)  6.74 us
    add x1, local copies, waits for them, and re-layouts, contract(): return output_side + input_side  6.04 us
    dot_general x1, matrix products, contract(): lax.dot_general(logits, features, dims, preferred_element_type=jnp.float32)  5.14 us
    dot_general x1, matrix products, contract(): lax.dot_general(onehot, input_grads, dims, preferred_element_type=jnp.flo...  5.06 us
    all_to_all x1, blocking collectives, body(): lax.all_to_all(widened, 'dp', split_axis=1, concat_axis=0, tiled=True)  4.91 us
    all_to_all x1, starting transfers between devices, from_everyone(): lax.all_to_all(jnp.broadcast_to(shard[None], (length, *shard.shape)), axi...  3.76 us
  transfers between devices with their start and end apart: 3, of which 2 were waited for; matrix products, arithmetic and copies ran while one was open for 6% of the time, Pallas kernels for 0%

commit v1 on v0

v1 whole, which is shorter than its diff:
```python
import functools

import jax
import jax.numpy as jnp
import numpy as np
from jax import lax
from jax.experimental import pallas as pl
from jax.experimental.pallas import tpu as pltpu
from jax.sharding import PartitionSpec as P

Z, X, YH, CORE, DP = 8, 4, 2, 2, 2
ROWS = 4
LANES = 128


def coords(vocab):
    return vocab // (X * 4), (vocab // 4) % X, (vocab // 2) % 2, vocab % 2


def flat(dp, z, x, yh, core):
    return dp * (Z * X * 4) + ((z % Z) * X + (x % X)) * 4 + yh * 2 + core


def move(value, dz=0, dx=0, fy=0, fd=0, fc=0):
    pairs = []
    for dp in range(DP):
        for vocab in range(Z * X * 4):
            z, x, yh, core = coords(vocab)
            pairs.append((flat(dp, z, x, yh, core), flat(dp ^ fd, z + dz, x + dx, yh ^ fy, core ^ fc)))
    return lax.ppermute(value, ("dp", "vocab"), pairs)


def gather_tokens(own, other):
    from_dp = move(other, fd=1)
    from_dy = move(other, fd=1, fy=1)
    from_yh = move(own, fy=1)
    chunk = jnp.concatenate([own, from_dp, from_yh, from_dy], axis=0)
    right, left, ups, downs = chunk, chunk, [], []
    for step in range(Z // 2):
        right = move(right, dz=1)
        downs.append(right)
        if step < Z // 2 - 1:
            left = move(left, dz=-1)
            ups.append(left)
    column = jnp.concatenate([chunk] + ups + downs[::-1], axis=0)
    down = move(column, dx=1)
    up = move(column, dx=-1)
    half = column.shape[0] // 2
    across = jnp.concatenate([move(down[:half], dx=1), move(up[half:], dx=-1)], axis=0)
    mine = [column, up, across, down]
    return mine + [move(part, fc=1) for part in mine], from_yh


def arrangement(dp, vocab):
    z, x, yh, core = coords(vocab)
    place = lax.broadcasted_iota(jnp.int32, (1, 2 * Z * X * YH * CORE * ROWS), 1)
    j, r, zi = place % 4, (place // 4) % 4, (place // 16) % Z
    xi, ci = (place // (16 * Z)) % X, place // (16 * Z * X)
    token = ((((z + zi) % Z) * X + (x + xi) % X) * 2 + (yh ^ (r // 2))) * 2 + (core ^ ci)
    token = token * ROWS + j
    spot = lax.broadcasted_iota(jnp.int32, (Z * X * YH * CORE * ROWS, 1), 0)
    hit = spot == token
    near = r % 2 == 0
    return (hit & near).astype(jnp.bfloat16), (hit & ~near).astype(jnp.bfloat16)


def contract_kernel(parts, offset_ref, logit_ref, *refs):
    features = refs[:parts]
    grads = refs[parts : 2 * parts]
    codes = refs[2 * parts : 3 * parts]
    out_ref, onehot = refs[3 * parts :]
    rows, length = logit_ref.shape[0], features[0].shape[0]

    @pl.when(pl.program_id(0) == 0)
    def _():
        lane = lax.broadcasted_iota(jnp.int32, (8, LANES), 1)
        weight = jnp.where(lane == 0, 512.0, jnp.where(lane == 1, 2.0, jnp.where(lane == 2, 1.0, 0.0)))
        weight = weight.astype(jnp.bfloat16)
        row = lax.broadcasted_iota(jnp.int32, (rows, length), 0) + offset_ref[0]
        for k in range(parts):
            ids = lax.dot_general(
                weight, codes[k][...], (((1,), (1,)), ((), ())), preferred_element_type=jnp.float32
            )[:1].astype(jnp.int32)
            onehot[:, k * length : (k + 1) * length] = jnp.where(row == ids, 1.0, 0.0).astype(jnp.bfloat16)

    step = 256

    @pl.loop(0, rows // step)
    def _(block):
        span = pl.ds(pl.multiple_of(block * step, step), step)
        right = jnp.concatenate([f[...] for f in features], axis=0)
        total = jnp.dot(logit_ref[span, :], right, preferred_element_type=jnp.float32)
        right = jnp.concatenate([g[...] for g in grads], axis=0)
        total += jnp.dot(onehot[span, :], right, preferred_element_type=jnp.float32)
        out_ref[span, :] = total


def contract(offset, logits, chunks, columns):
    parts = len(chunks)
    length = chunks[0].shape[0]
    rows, tokens = logits.shape
    width = 384
    steps = columns // width
    once = pl.Buffered(1)
    return pl.pallas_call(
        functools.partial(contract_kernel, parts),
        out_shape=jax.ShapeDtypeStruct((rows, columns), jnp.float32),
        grid=(steps,),
        in_specs=[
            pl.BlockSpec(memory_space=pltpu.SMEM),
            pl.BlockSpec((rows, tokens), lambda n: (0, 0), pipeline_mode=once),
        ]
        + [pl.BlockSpec((length, width), lambda n: (0, n))] * parts
        + [pl.BlockSpec((length, width), lambda n: (0, n + steps))] * parts
        + [pl.BlockSpec((length, LANES), lambda n: (0, 2 * columns // LANES), pipeline_mode=once)] * parts,
        out_specs=pl.BlockSpec((rows, width), lambda n: (0, n)),
        scratch_shapes=[pltpu.VMEM((rows, tokens), jnp.bfloat16)],
        compiler_params=pltpu.CompilerParams(vmem_limit_bytes=40 << 20),
        cost_estimate=pl.CostEstimate(
            flops=4 * rows * tokens * columns, bytes_accessed=12 << 20, transcendentals=0
        ),
    )(offset, logits, *chunks, *chunks, *chunks)


def body(token_ids, hidden, logit_grad, embed_grad):
    dp, vocab = lax.axis_index("dp"), lax.axis_index("vocab")
    columns = hidden.shape[1] // 2
    offset = (vocab * logit_grad.shape[1]).astype(jnp.int32).reshape(1)
    ids = token_ids[:, None]
    lane = lax.broadcasted_iota(jnp.int32, (ROWS, LANES), 1)
    code = jnp.where(lane == 0, ids // 512, jnp.where(lane == 1, (ids // 2) % 256, ids % 2))
    code = jnp.where(lane < 3, code, 0).astype(jnp.bfloat16)

    def payload(side):
        pick = [lax.dynamic_slice_in_dim(a, side * columns, columns, 1) for a in (hidden, embed_grad)]
        return jnp.concatenate(pick + [code], axis=1)

    near, far = arrangement(dp, vocab)
    dims = (((0,), (0,)), ((), ()))
    turned = lax.dot_general(logit_grad, near, dims, preferred_element_type=jnp.float32)
    chunks, early = gather_tokens(payload(dp), payload(1 - dp))
    held, _ = lax.optimization_barrier((logit_grad, early))
    partner = move(held, fd=1)
    turned = turned + lax.dot_general(partner, far, dims, preferred_element_type=jnp.float32)
    return contract(offset, turned.astype(jnp.bfloat16), chunks, columns)


def solution(mesh):
    placed = (
        P(("dp", "vocab")),
        P(("dp", "vocab"), None),
        P("dp", "vocab"),
        P(("dp", "vocab"), None),
    )
    return jax.shard_map(
        body, mesh=mesh, in_specs=placed, out_specs=P("vocab", "dp"), check_vma=False
    )
```

time: 171 us -> 85.7 us (0.50)
  blocking collectives: 50.8 us -> 0 us
  waiting for transfers between devices: 71.4 us -> 23.6 us
  starting transfers between devices: 7.04 us -> 37.9 us
  local copies, waits for them, and re-layouts: 15.9 us -> 1.08 us
  between operations: 14.1 us -> 0.18 us
  Pallas kernels: 0 us -> 12.9 us
  matrix products: 10.2 us -> 8.45 us
    all_gather x1 -> x0, waiting for transfers between devices: 68.8 us -> none  [side_by_side(): result = lax.all_gather(both, axis, axis=dim, tiled=True)]
    unnamed x1 -> x0, blocking collectives: 39.2 us -> none
    ppermute x0 -> x19, starting transfers between devices: none -> 37.9 us  [move(): return lax.ppermute(value, ('dp', 'vocab'), pairs)]
    ppermute x0 -> x19, waiting for transfers between devices: none -> 23.6 us  [move(): return lax.ppermute(value, ('dp', 'vocab'), pairs)]
    pallas_call x0 -> x1, Pallas kernels: none -> 12.9 us  [contract(): pl.pallas_call(functools.partial(contract_kernel, parts), out_shape=jax.S...]
    all_to_all x2 -> x0, blocking collectives: 11.7 us -> none  [the longest x1 6.74 us: body(): lax.all_to_all(hidden, 'dp', split_axis=1, concat_axis=0, tiled=True)]
    all_to_all x2 -> x0, starting transfers between devices: 7 us -> none  [the longest x1 3.76 us: from_everyone(): lax.all_to_all(jnp.broadcast_to(shard[None], (length, *shard.shape)), axi...]
    add x1 -> x0, local copies, waits for them, and re-layouts: 6.04 us -> none  [contract(): return output_side + input_side]
  transfers between devices with their start and end apart: 3 -> 19, of which waited for: 2 -> 9; matrix products, arithmetic and copies ran while one was open for 6% -> 10% of each run, Pallas kernels for 0% -> 0%
where the time goes in v1:
time: 85.7 us; the launch traced here: 85 us
  starting transfers between devices  37.9 us (44%)
  waiting for transfers between devices  23.6 us (28%)
  Pallas kernels  12.9 us (15%)
  matrix products  8.45 us (10%)
  local copies, waits for them, and re-layouts  1.08 us (1%)
  other arithmetic  0.88 us (1%)
    ppermute x19, starting transfers between devices, move(): return lax.ppermute(value, ('dp', 'vocab'), pairs)  37.9 us
    ppermute x19, waiting for transfers between devices, move(): return lax.ppermute(value, ('dp', 'vocab'), pairs)  23.6 us
    pallas_call x1, Pallas kernels, contract(): pl.pallas_call(functools.partial(contract_kernel, parts), out_shape=jax.S...  12.9 us
    dot_general x1, matrix products, body(): lax.dot_general(logit_grad, near, dims, preferred_element_type=jnp.float32)  4.59 us
    dot_general x1, matrix products, body(): lax.dot_general(partner, far, dims, preferred_element_type=jnp.float32)  3.86 us
  transfers between devices with their start and end apart: 19, of which 9 were waited for; matrix products, arithmetic and copies ran while one was open for 10% of the time, Pallas kernels for 0%

profile of v1, /device:TPU:1, one launch (start us, length us, event | category | flops | bytes accessed | tf_op | source)
XLA Modules:
  0.0 85.0 jit_solution(11813784608554596568)
XLA Ops:
  0.0 0.7 and_select_fusion.3
  0.7 0.8 constant_dynamic-slice_fusion
  1.5 0.1 select_convert_fusion
  1.6 3.8 %collective-permute-start = (bf16[4,2432]{1,0:T(4,128)(2,1)S(1)}, bf16[4,2432]{1,0:T(4,128)(2,1)S(1)}, u32[]{:S(2)}, u32[]{:S(2)}) collective-permute-start(bf16[4,2432]{1,0:T(4,128)(2,1)S(1)} %get-tuple-element.12), channel_id=1, source_target_pairs={{0,2},{1,3},{2,0},{3,1},{4,6},{5,7},{6,4},{7,5},{8,10},{9,11},{10,... | collective-permute-start | bytes 58376 | tf_op jit(solution)/shard_map/ppermute | solution.py:30
  5.4 0.4 collective-permute-start.2
  5.8 0.4 collective-permute-start.3
  6.2 0.4 collective-permute-done
  6.6 1.6 %collective-permute-done.2 = bf16[4,2432]{1,0:T(4,128)(2,1)S(1)} collective-permute-done((bf16[4,2432]{1,0:T(4,128)(2,1)S(1)}, bf16[4,2432]{1,0:T(4,128)(2,1)S(1)}, u32[]{:S(2)}, u32[]{:S(2)}) %collective-permute-start.2) | collective-permute-done | bytes 19488 | tf_op jit(solution)/shard_map/ppermute | solution.py:30
  8.2 1.6 %collective-permute-done.3 = bf16[4,2432]{1,0:T(4,128)(2,1)S(1)} collective-permute-done((bf16[4,2432]{1,0:T(4,128)(2,1)S(1)}, bf16[4,2432]{1,0:T(4,128)(2,1)S(1)}, u32[]{:S(2)}, u32[]{:S(2)}) %collective-permute-start.3) | collective-permute-done | bytes 19488 | tf_op jit(solution)/shard_map/ppermute | solution.py:30
  9.8 1.6 %collective-permute-start.7 = (bf16[16,2432]{1,0:T(8,128)(2,1)S(1)}, bf16[16,2432]{1,0:T(8,128)(2,1)S(1)}, u32[]{:S(2)}, u32[]{:S(2)}) collective-permute-start(bf16[16,2432]{1,0:T(8,128)(2,1)S(1)} %pad_maximum_fusion), channel_id=1, source_target_pairs={{0,16},{1,17},{2,18},{3,19},{4,20},{5,21},{6,22},{7,23},{8,24},{9,... | collective-permute-start | bytes 233480 | tf_op jit(solution)/shard_map/ppermute | solution.py:30
  11.4 4.0 %collective-permute-start.4 = (bf16[16,2432]{1,0:T(8,128)(2,1)S(1)}, bf16[16,2432]{1,0:T(8,128)(2,1)S(1)}, u32[]{:S(2)}, u32[]{:S(2)}) collective-permute-start(bf16[16,2432]{1,0:T(8,128)(2,1)S(1)} %pad_maximum_fusion), channel_id=1, source_target_pairs={{0,112},{1,113},{2,114},{3,115},{4,116},{5,117},{6,118},{7,119},{8... | collective-permute-start | bytes 233480 | tf_op jit(solution)/shard_map/ppermute | solution.py:30
  15.4 1.7 %collective-permute-done.7 = bf16[16,2432]{1,0:T(8,128)(2,1)S(1)} collective-permute-done((bf16[16,2432]{1,0:T(8,128)(2,1)S(1)}, bf16[16,2432]{1,0:T(8,128)(2,1)S(1)}, u32[]{:S(2)}, u32[]{:S(2)}) %collective-permute-start.7) | collective-permute-done | bytes 77856 | tf_op jit(solution)/shard_map/ppermute | solution.py:30
  17.1 2.8 %collective-permute-start.5 = (bf16[16,2432]{1,0:T(8,128)(2,1)S(1)}, bf16[16,2432]{1,0:T(8,128)(2,1)S(1)}, u32[]{:S(2)}, u32[]{:S(2)}) collective-permute-start(bf16[16,2432]{1,0:T(8,128)(2,1)S(1)} %collective-permute-done.4), channel_id=1, source_target_pairs={{0,112},{1,113},{2,114},{3,115},{4,116},{5,117},{6,118},{7,119},{8... | collective-permute-start | bytes 233480 | tf_op jit(solution)/shard_map/ppermute | solution.py:30
  19.9 1.7 %collective-permute-done.8 = bf16[16,2432]{1,0:T(8,128)(2,1)S(1)} collective-permute-done((bf16[16,2432]{1,0:T(8,128)(2,1)S(1)}, bf16[16,2432]{1,0:T(8,128)(2,1)S(1)}, u32[]{:S(2)}, u32[]{:S(2)}) %collective-permute-start.8) | collective-permute-done | bytes 77856 | tf_op jit(solution)/shard_map/ppermute | solution.py:30
  21.6 2.8 %collective-permute-start.6 = (bf16[16,2432]{1,0:T(8,128)(2,1)S(1)}, bf16[16,2432]{1,0:T(8,128)(2,1)S(1)}, u32[]{:S(2)}, u32[]{:S(2)}) collective-permute-start(bf16[16,2432]{1,0:T(8,128)(2,1)S(1)} %collective-permute-done.5), channel_id=1, source_target_pairs={{0,112},{1,113},{2,114},{3,115},{4,116},{5,117},{6,118},{7,119},{8... | collective-permute-start | bytes 233480 | tf_op jit(solution)/shard_map/ppermute | solution.py:30
  24.4 1.8 %collective-permute-done.9 = bf16[16,2432]{1,0:T(8,128)(2,1)S(1)} collective-permute-done((bf16[16,2432]{1,0:T(8,128)(2,1)S(1)}, bf16[16,2432]{1,0:T(8,128)(2,1)S(1)}, u32[]{:S(2)}, u32[]{:S(2)}) %collective-permute-start.9) | collective-permute-done | bytes 77856 | tf_op jit(solution)/shard_map/ppermute | solution.py:30
  26.1 5.2 %collective-permute-done.10 = bf16[16,2432]{1,0:T(8,128)(2,1)S(1)} collective-permute-done((bf16[16,2432]{1,0:T(8,128)(2,1)S(1)}, bf16[16,2432]{1,0:T(8,128)(2,1)S(1)}, u32[]{:S(2)}, u32[]{:S(2)}) %collective-permute-start.10) | collective-permute-done | bytes 77856 | tf_op jit(solution)/shard_map/ppermute | solution.py:30
  31.4 0.2 concatenate.19.refs_0_.refs_8_.refs_16_
  31.6 1.3 %collective-permute-start.12 = (bf16[128,2432]{1,0:T(8,128)(2,1)S(1)}, bf16[128,2432]{1,0:T(8,128)(2,1)S(1)}, u32[]{:S(2)}, u32[]{:S(2)}) collective-permute-start(bf16[128,2432]{1,0:T(8,128)(2,1)S(1)} %concatenate.19.refs_0_.refs_8_.refs_16_), channel_id=1, source_target_pairs={{0,4},{1,5},{2,6},{3,7},{4,8},{5,9},{6,10},{7,11},{8,12},{9,13},{1... | collective-permute-start | bytes 1867784 | tf_op jit(solution)/shard_map/ppermute | solution.py:30
  32.9 1.5 %collective-permute-start.11 = (bf16[128,2432]{1,0:T(8,128)(2,1)S(1)}, bf16[128,2432]{1,0:T(8,128)(2,1)S(1)}, u32[]{:S(2)}, u32[]{:S(2)}) collective-permute-start(bf16[128,2432]{1,0:T(8,128)(2,1)S(1)} %concatenate.19.refs_0_.refs_8_.refs_16_), channel_id=1, source_target_pairs={{0,12},{1,13},{2,14},{3,15},{4,0},{5,1},{6,2},{7,3},{8,4},{9,5},{1... | collective-permute-start | bytes 1867784 | tf_op jit(solution)/shard_map/ppermute | solution.py:30
  34.3 7.6 %collective-permute-done.12.refs_3_.refs_11_.refs_19_ = bf16[128,2432]{1,0:T(8,128)(2,1)S(1)} collective-permute-done((bf16[128,2432]{1,0:T(8,128)(2,1)S(1)}, bf16[128,2432]{1,0:T(8,128)(2,1)S(1)}, u32[]{:S(2)}, u32[]{:S(2)}) %collective-permute-start.12) | collective-permute-done | bytes 622624 | tf_op jit(solution)/shard_map/ppermute | solution.py:30
  42.0 0.1 collective-permute-start.13
  42.2 0.1 collective-permute-start.1
  42.3 11.2 %collective-permute-start.15 = (bf16[128,2432]{1,0:T(8,128)(2,1)S(1)}, bf16[128,2432]{1,0:T(8,128)(2,1)S(1)}, u32[]{:S(2)}, u32[]{:S(2)}) collective-permute-start(bf16[128,2432]{1,0:T(8,128)(2,1)S(1)} %concatenate.19.refs_0_.refs_8_.refs_16_), channel_id=1, source_target_pairs={{0,1},{1,0},{2,3},{3,2},{4,5},{5,4},{6,7},{7,6},{8,9},{9,8},{10,11... | collective-permute-start | bytes 1867784 | tf_op jit(solution)/shard_map/ppermute | solution.py:30
  53.5 2.4 %collective-permute-start.14 = (bf16[64,2432]{1,0:T(8,128)(2,1)S(1)}, bf16[64,2432]{1,0:T(8,128)(2,1)S(1)}, u32[]{:S(2)}, u32[]{:S(2)}) collective-permute-start(bf16[64,2432]{1,0:T(8,128)(2,1)S(1)} %slice.9), channel_id=1, source_target_pairs={{0,12},{1,13},{2,14},{3,15},{4,0},{5,1},{6,2},{7,3},{8,4},{9,5},{1... | collective-permute-start | bytes 933896 | tf_op jit(solution)/shard_map/ppermute | solution.py:30
  55.9 0.3 collective-permute-start.16
  56.2 4.5 %collective-permute-start.18 = (bf16[128,2432]{1,0:T(8,128)(2,1)S(1)}, bf16[128,2432]{1,0:T(8,128)(2,1)}, u32[]{:S(2)}, u32[]{:S(2)}) collective-permute-start(bf16[128,2432]{1,0:T(8,128)(2,1)S(1)} %collective-permute-done.12.refs_3_.refs_11_.refs_19_), channel_id=1, source_target_pairs={{0,1},{1,0},{2,3},{3,2},{4,5},{5,4},{6,7},{7,6},{8,9},{9,8},{10,11... | collective-permute-start | bytes 1867784 | tf_op jit(solution)/shard_map/ppermute | solution.py:30
  60.7 2.0 %collective-permute-done.14 = bf16[64,2432]{1,0:T(8,128)(2,1)S(1)} collective-permute-done((bf16[64,2432]{1,0:T(8,128)(2,1)S(1)}, bf16[64,2432]{1,0:T(8,128)(2,1)S(1)}, u32[]{:S(2)}, u32[]{:S(2)}) %collective-permute-start.14) | collective-permute-done | bytes 311328 | tf_op jit(solution)/shard_map/ppermute | solution.py:30
  62.7 0.9 %collective-permute-start.17 = (bf16[128,2432]{1,0:T(8,128)(2,1)S(1)}, bf16[128,2432]{1,0:T(8,128)(2,1)}, u32[]{:S(2)}, u32[]{:S(2)}) collective-permute-start(bf16[128,2432]{1,0:T(8,128)(2,1)S(1)} %constant_dynamic-update-slice_fusion.refs_2_.refs_10_.refs_18_), channel_id=1, source_target_pairs={{0,1},{1,0},{2,3},{3,2},{4,5},{5,4},{6,7},{7,6},{8,9},{9,8},{10,11... | collective-permute-start | bytes 1867784 | tf_op jit(solution)/shard_map/ppermute | solution.py:30
  63.6 4.6 %fusion.3 = f32[1024,1024]{0,1:T(8,128)} fusion(bf16[512,1024]{1,0:T(8,128)(2,1)} %param.6, s32[1024]{0:T(1024)S(1)} %fusion.24, pred[1024]{0:T(1024)(128)(4,1)S(1)} %fusion.33), kind=kOutput, calls=%fused_computation.5 | convolution fusion | flops 1074790400 | bytes 5248000 | tf_op jit(solution)/shard_map/dot_general | solution.py:140
  68.2 3.9 %fusion.logit_ref = bf16[1024,1024]{1,0:T(8,128)(2,1)S(1)} fusion(f32[1024,1024]{0,1:T(8,128)} %fusion.3, bf16[512,1024]{1,0:T(8,128)(2,1)} %collective-permute-done.1, s32[1024]{0:T(1024)S(1)} %fusion.24, pred[1024]{0:T(1024)(128)(4,1)S(1)} %fusion.41), kind=kOutput, calls=%fused_computation.1 | convolution fusion | flops 1076887552 | bytes 7345152 | tf_op jit(solution)/shard_map/dot_general | solution.py:144
  72.1 12.9 %shard_map.46 = f32[1024,1152]{1,0:T(8,128)} custom-call(s32[1]{0:T(128)} %bitcast.offset_ref, bf16[1024,1024]{1,0:T(8,128)(2,1)S(1)} %fusion.logit_ref, bf16[128,2432]{1,0:T(8,128)(2,1)S(1)} %concatenate.19.refs_0_.refs_8_.refs_16_, bf16[128,2432]{1,0:T(8,128)(2,1)S(1)} %collective-permute-done.11.refs_1_.refs_9_.refs_17_, ...), custom_call_target="tpu_custom_call" | custom-call | flops 4831838208 | bytes 12582912 | tf_op jit(solution)/shard_map/pallas_call | solution.py:105
  (24 shorter events, 0.3 us)
Async XLA Ops:
  1.6 5.0 %collective-permute-start = (bf16[4,2432]{1,0:T(4,128)(2,1)S(1)}, bf16[4,2432]{1,0:T(4,128)(2,1)S(1)}, u32[]{:S(2)}, u32[]{:S(2)}) collective-permute-start(bf16[4,2432]{1,0:T(4,128)(2,1)S(1)} %get-tuple-element.12), channel_id=1, source_target_pairs={{0,2},{1,3},{2,0},{3,1},{4,6},{5,7},{6,4},{7,5},{8,10},{9,11},{10,... | collective-permute-start | bytes 58376 | tf_op jit(solution)/shard_map/ppermute | solution.py:30
  5.4 2.8 %collective-permute-start.2 = (bf16[4,2432]{1,0:T(4,128)(2,1)S(1)}, bf16[4,2432]{1,0:T(4,128)(2,1)S(1)}, u32[]{:S(2)}, u32[]{:S(2)}) collective-permute-start(bf16[4,2432]{1,0:T(4,128)(2,1)S(1)} %get-tuple-element.11), channel_id=1, source_target_pairs={{0,128},{1,129},{2,130},{3,131},{4,132},{5,133},{6,134},{7,135},{8... | collective-permute-start | bytes 58376 | tf_op jit(solution)/shard_map/ppermute | solution.py:30
  5.8 4.0 %collective-permute-start.3 = (bf16[4,2432]{1,0:T(4,128)(2,1)S(1)}, bf16[4,2432]{1,0:T(4,128)(2,1)S(1)}, u32[]{:S(2)}, u32[]{:S(2)}) collective-permute-start(bf16[4,2432]{1,0:T(4,128)(2,1)S(1)} %get-tuple-element.11), channel_id=1, source_target_pairs={{0,130},{1,131},{2,128},{3,129},{4,134},{5,135},{6,132},{7,133},{8... | collective-permute-start | bytes 58376 | tf_op jit(solution)/shard_map/ppermute | solution.py:30
  9.8 7.3 %collective-permute-start.7 = (bf16[16,2432]{1,0:T(8,128)(2,1)S(1)}, bf16[16,2432]{1,0:T(8,128)(2,1)S(1)}, u32[]{:S(2)}, u32[]{:S(2)}) collective-permute-start(bf16[16,2432]{1,0:T(8,128)(2,1)S(1)} %pad_maximum_fusion), channel_id=1, source_target_pairs={{0,16},{1,17},{2,18},{3,19},{4,20},{5,21},{6,22},{7,23},{8,24},{9,... | collective-permute-start | bytes 233480 | tf_op jit(solution)/shard_map/ppermute | solution.py:30
  11.4 5.7 %collective-permute-start.4 = (bf16[16,2432]{1,0:T(8,128)(2,1)S(1)}, bf16[16,2432]{1,0:T(8,128)(2,1)S(1)}, u32[]{:S(2)}, u32[]{:S(2)}) collective-permute-start(bf16[16,2432]{1,0:T(8,128)(2,1)S(1)} %pad_maximum_fusion), channel_id=1, source_target_pairs={{0,112},{1,113},{2,114},{3,115},{4,116},{5,117},{6,118},{7,119},{8... | collective-permute-start | bytes 233480 | tf_op jit(solution)/shard_map/ppermute | solution.py:30
  17.1 4.5 %collective-permute-start.8 = (bf16[16,2432]{1,0:T(8,128)(2,1)S(1)}, bf16[16,2432]{1,0:T(8,128)(2,1)S(1)}, u32[]{:S(2)}, u32[]{:S(2)}) collective-permute-start(bf16[16,2432]{1,0:T(8,128)(2,1)S(1)} %collective-permute-done.7), channel_id=1, source_target_pairs={{0,16},{1,17},{2,18},{3,19},{4,20},{5,21},{6,22},{7,23},{8,24},{9,... | collective-permute-start | bytes 233480 | tf_op jit(solution)/shard_map/ppermute | solution.py:30
  17.1 4.5 %collective-permute-start.5 = (bf16[16,2432]{1,0:T(8,128)(2,1)S(1)}, bf16[16,2432]{1,0:T(8,128)(2,1)S(1)}, u32[]{:S(2)}, u32[]{:S(2)}) collective-permute-start(bf16[16,2432]{1,0:T(8,128)(2,1)S(1)} %collective-permute-done.4), channel_id=1, source_target_pairs={{0,112},{1,113},{2,114},{3,115},{4,116},{5,117},{6,118},{7,119},{8... | collective-permute-start | bytes 233480 | tf_op jit(solution)/shard_map/ppermute | solution.py:30
  21.6 4.5 %collective-permute-start.9 = (bf16[16,2432]{1,0:T(8,128)(2,1)S(1)}, bf16[16,2432]{1,0:T(8,128)(2,1)S(1)}, u32[]{:S(2)}, u32[]{:S(2)}) collective-permute-start(bf16[16,2432]{1,0:T(8,128)(2,1)S(1)} %collective-permute-done.8), channel_id=1, source_target_pairs={{0,16},{1,17},{2,18},{3,19},{4,20},{5,21},{6,22},{7,23},{8,24},{9,... | collective-permute-start | bytes 233480 | tf_op jit(solution)/shard_map/ppermute | solution.py:30
  21.6 4.5 %collective-permute-start.6 = (bf16[16,2432]{1,0:T(8,128)(2,1)S(1)}, bf16[16,2432]{1,0:T(8,128)(2,1)S(1)}, u32[]{:S(2)}, u32[]{:S(2)}) collective-permute-start(bf16[16,2432]{1,0:T(8,128)(2,1)S(1)} %collective-permute-done.5), channel_id=1, source_target_pairs={{0,112},{1,113},{2,114},{3,115},{4,116},{5,117},{6,118},{7,119},{8... | collective-permute-start | bytes 233480 | tf_op jit(solution)/shard_map/ppermute | solution.py:30
  26.1 5.2 %collective-permute-start.10 = (bf16[16,2432]{1,0:T(8,128)(2,1)S(1)}, bf16[16,2432]{1,0:T(8,128)(2,1)S(1)}, u32[]{:S(2)}, u32[]{:S(2)}) collective-permute-start(bf16[16,2432]{1,0:T(8,128)(2,1)S(1)} %collective-permute-done.9), channel_id=1, source_target_pairs={{0,16},{1,17},{2,18},{3,19},{4,20},{5,21},{6,22},{7,23},{8,24},{9,... | collective-permute-start | bytes 233480 | tf_op jit(solution)/shard_map/ppermute | solution.py:30
  31.6 10.4 %collective-permute-start.12 = (bf16[128,2432]{1,0:T(8,128)(2,1)S(1)}, bf16[128,2432]{1,0:T(8,128)(2,1)S(1)}, u32[]{:S(2)}, u32[]{:S(2)}) collective-permute-start(bf16[128,2432]{1,0:T(8,128)(2,1)S(1)} %concatenate.19.refs_0_.refs_8_.refs_16_), channel_id=1, source_target_pairs={{0,4},{1,5},{2,6},{3,7},{4,8},{5,9},{6,10},{7,11},{8,12},{9,13},{1... | collective-permute-start | bytes 1867784 | tf_op jit(solution)/shard_map/ppermute | solution.py:30
  32.9 20.6 %collective-permute-start.11 = (bf16[128,2432]{1,0:T(8,128)(2,1)S(1)}, bf16[128,2432]{1,0:T(8,128)(2,1)S(1)}, u32[]{:S(2)}, u32[]{:S(2)}) collective-permute-start(bf16[128,2432]{1,0:T(8,128)(2,1)S(1)} %concatenate.19.refs_0_.refs_8_.refs_16_), channel_id=1, source_target_pairs={{0,12},{1,13},{2,14},{3,15},{4,0},{5,1},{6,2},{7,3},{8,4},{9,5},{1... | collective-permute-start | bytes 1867784 | tf_op jit(solution)/shard_map/ppermute | solution.py:30
  42.0 14.2 %collective-permute-start.13 = (bf16[64,2432]{1,0:T(8,128)(2,1)S(1)}, bf16[64,2432]{1,0:T(8,128)(2,1)S(1)}, u32[]{:S(2)}, u32[]{:S(2)}) collective-permute-start(bf16[64,2432]{1,0:T(8,128)(2,1)S(1)} %slice.8), channel_id=1, source_target_pairs={{0,4},{1,5},{2,6},{3,7},{4,8},{5,9},{6,10},{7,11},{8,12},{9,13},{1... | collective-permute-start | bytes 933896 | tf_op jit(solution)/shard_map/ppermute | solution.py:30
  42.2 26.0 %collective-permute-start.1 = (bf16[512,1024]{1,0:T(8,128)(2,1)}, bf16[512,1024]{1,0:T(8,128)(2,1)}, u32[]{:S(2)}, u32[]{:S(2)}) collective-permute-start(bf16[512,1024]{1,0:T(8,128)(2,1)} %param.6), channel_id=1, source_target_pairs={{0,128},{1,129},{2,130},{3,131},{4,132},{5,133},{6,134},{7,135},{8... | collective-permute-start | bytes 3145736 | tf_op jit(solution)/shard_map/ppermute | solution.py:30
  42.3 29.8 %collective-permute-start.15 = (bf16[128,2432]{1,0:T(8,128)(2,1)S(1)}, bf16[128,2432]{1,0:T(8,128)(2,1)S(1)}, u32[]{:S(2)}, u32[]{:S(2)}) collective-permute-start(bf16[128,2432]{1,0:T(8,128)(2,1)S(1)} %concatenate.19.refs_0_.refs_8_.refs_16_), channel_id=1, source_target_pairs={{0,1},{1,0},{2,3},{3,2},{4,5},{5,4},{6,7},{7,6},{8,9},{9,8},{10,11... | collective-permute-start | bytes 1867784 | tf_op jit(solution)/shard_map/ppermute | solution.py:30
  53.5 9.2 %collective-permute-start.14 = (bf16[64,2432]{1,0:T(8,128)(2,1)S(1)}, bf16[64,2432]{1,0:T(8,128)(2,1)S(1)}, u32[]{:S(2)}, u32[]{:S(2)}) collective-permute-start(bf16[64,2432]{1,0:T(8,128)(2,1)S(1)} %slice.9), channel_id=1, source_target_pairs={{0,12},{1,13},{2,14},{3,15},{4,0},{5,1},{6,2},{7,3},{8,4},{9,5},{1... | collective-permute-start | bytes 933896 | tf_op jit(solution)/shard_map/ppermute | solution.py:30
  55.9 16.2 %collective-permute-start.16 = (bf16[128,2432]{1,0:T(8,128)(2,1)S(1)}, bf16[128,2432]{1,0:T(8,128)(2,1)}, u32[]{:S(2)}, u32[]{:S(2)}) collective-permute-start(bf16[128,2432]{1,0:T(8,128)(2,1)S(1)} %collective-permute-done.11.refs_1_.refs_9_.refs_17_), channel_id=1, source_target_pairs={{0,1},{1,0},{2,3},{3,2},{4,5},{5,4},{6,7},{7,6},{8,9},{9,8},{10,11... | collective-permute-start | bytes 1867784 | tf_op jit(solution)/shard_map/ppermute | solution.py:30
  56.2 15.9 %collective-permute-start.18 = (bf16[128,2432]{1,0:T(8,128)(2,1)S(1)}, bf16[128,2432]{1,0:T(8,128)(2,1)}, u32[]{:S(2)}, u32[]{:S(2)}) collective-permute-start(bf16[128,2432]{1,0:T(8,128)(2,1)S(1)} %collective-permute-done.12.refs_3_.refs_11_.refs_19_), channel_id=1, source_target_pairs={{0,1},{1,0},{2,3},{3,2},{4,5},{5,4},{6,7},{7,6},{8,9},{9,8},{10,11... | collective-permute-start | bytes 1867784 | tf_op jit(solution)/shard_map/ppermute | solution.py:30
  62.7 9.4 %collective-permute-start.17 = (bf16[128,2432]{1,0:T(8,128)(2,1)S(1)}, bf16[128,2432]{1,0:T(8,128)(2,1)}, u32[]{:S(2)}, u32[]{:S(2)}) collective-permute-start(bf16[128,2432]{1,0:T(8,128)(2,1)S(1)} %constant_dynamic-update-slice_fusion.refs_2_.refs_10_.refs_18_), channel_id=1, source_target_pairs={{0,1},{1,0},{2,3},{3,2},{4,5},{5,4},{6,7},{7,6},{8,9},{9,8},{10,11... | collective-permute-start | bytes 1867784 | tf_op jit(solution)/shard_map/ppermute | solution.py:30

commit v2 on v1

v2 whole, which is shorter than its diff:
```python
import functools

import jax
import jax.numpy as jnp
import numpy as np
from jax import lax
from jax.experimental import pallas as pl
from jax.experimental.pallas import tpu as pltpu
from jax.sharding import PartitionSpec as P

Z, X, YH, CORE, DP = 8, 4, 2, 2, 2
ROWS = 4
LANES = 128


def coords(vocab):
    return vocab // (X * 4), (vocab // 4) % X, (vocab // 2) % 2, vocab % 2


def flat(dp, z, x, yh, core):
    return dp * (Z * X * 4) + ((z % Z) * X + (x % X)) * 4 + yh * 2 + core


def move(value, dz=0, dx=0, fy=0, fd=0, fc=0):
    pairs = []
    for dp in range(DP):
        for vocab in range(Z * X * 4):
            z, x, yh, core = coords(vocab)
            pairs.append((flat(dp, z, x, yh, core), flat(dp ^ fd, z + dz, x + dx, yh ^ fy, core ^ fc)))
    return lax.ppermute(value, ("dp", "vocab"), pairs)


def gather_column(own, other):
    from_dp = move(other, fd=1)
    from_dy = move(other, fd=1, fy=1)
    from_yh = move(own, fy=1)
    chunk = jnp.concatenate([own, from_dp, from_yh, from_dy], axis=0)
    right, left, ups, downs = chunk, chunk, [], []
    for step in range(Z // 2):
        right = move(right, dz=1)
        downs.append(right)
        if step < Z // 2 - 1:
            left = move(left, dz=-1)
            ups.append(left)
    return jnp.concatenate([chunk] + ups + downs[::-1], axis=0), from_yh


def arrangement(dp, vocab):
    z, x, yh, core = coords(vocab)
    place = lax.broadcasted_iota(jnp.int32, (1, 2 * Z * X * YH * CORE * ROWS), 1)
    j, r, zi = place % 4, (place // 4) % 4, (place // 16) % Z
    xi, ci = (place // (16 * Z)) % X, place // (16 * Z * X)
    token = ((((z + zi) % Z) * X + (x + xi) % X) * 2 + (yh ^ (r // 2))) * 2 + (core ^ ci)
    token = token * ROWS + j
    spot = lax.broadcasted_iota(jnp.int32, (Z * X * YH * CORE * ROWS, 1), 0)
    hit = spot == token
    near = r % 2 == 0
    return (hit & near).astype(jnp.bfloat16), (hit & ~near).astype(jnp.bfloat16)


def contract_kernel(spots, added, offset_ref, logit_ref, *refs):
    parts = len(spots)
    chunks = refs[:parts]
    out_ref, onehot = refs[parts + added :]
    rows, columns = out_ref.shape
    length = chunks[0].shape[0]
    lane = lax.broadcasted_iota(jnp.int32, (8, LANES), 1)
    weight = jnp.where(lane == 0, 512.0, jnp.where(lane == 1, 2.0, jnp.where(lane == 2, 1.0, 0.0)))
    weight = weight.astype(jnp.bfloat16)
    row = lax.broadcasted_iota(jnp.int32, (rows, length), 0) + (offset_ref[0] + pl.program_id(0) * rows)
    for k, chunk in enumerate(chunks):
        ids = lax.dot_general(
            weight, chunk[:, 2 * columns :], (((1,), (1,)), ((), ())), preferred_element_type=jnp.float32
        )[:1].astype(jnp.int32)
        onehot[:, k * length : (k + 1) * length] = jnp.where(row == ids, 1.0, 0.0).astype(jnp.bfloat16)
    left = jnp.concatenate([logit_ref[:, s * length : (s + 1) * length] for s in spots], axis=1)
    right = jnp.concatenate([c[:, :columns] for c in chunks], axis=0)
    total = jnp.dot(left, right, preferred_element_type=jnp.float32)
    right = jnp.concatenate([c[:, columns : 2 * columns] for c in chunks], axis=0)
    total += jnp.dot(onehot[...], right, preferred_element_type=jnp.float32)
    if added:
        total += refs[parts][...]
    out_ref[...] = total


def contract(offset, logits, chunks, spots, columns, partial=None):
    parts = len(chunks)
    length, width = chunks[0].shape
    rows, tokens = logits.shape
    block = 256
    added = [] if partial is None else [partial]
    return pl.pallas_call(
        functools.partial(contract_kernel, tuple(spots), len(added)),
        out_shape=jax.ShapeDtypeStruct((rows, columns), jnp.float32),
        grid=(rows // block,),
        in_specs=[
            pl.BlockSpec(memory_space=pltpu.SMEM),
            pl.BlockSpec((block, tokens), lambda m: (m, 0)),
        ]
        + [pl.BlockSpec((length, width), lambda m: (0, 0), pipeline_mode=pl.Buffered(1))] * parts
        + [pl.BlockSpec((block, columns), lambda m: (m, 0))] * len(added),
        out_specs=pl.BlockSpec((block, columns), lambda m: (m, 0)),
        scratch_shapes=[pltpu.VMEM((block, parts * length), jnp.bfloat16)],
        compiler_params=pltpu.CompilerParams(vmem_limit_bytes=28 << 20),
        cost_estimate=pl.CostEstimate(
            flops=4 * rows * parts * length * columns, bytes_accessed=12 << 20, transcendentals=0
        ),
    )(offset, logits, *chunks, *added)


def body(token_ids, hidden, logit_grad, embed_grad):
    dp, vocab = lax.axis_index("dp"), lax.axis_index("vocab")
    columns = hidden.shape[1] // 2
    offset = (vocab * logit_grad.shape[1]).astype(jnp.int32).reshape(1)
    ids = token_ids[:, None]
    lane = lax.broadcasted_iota(jnp.int32, (ROWS, LANES), 1)
    code = jnp.where(lane == 0, ids // 512, jnp.where(lane == 1, (ids // 2) % 256, ids % 2))
    code = jnp.where(lane < 3, code, 0).astype(jnp.bfloat16)

    def payload(side):
        pick = [lax.dynamic_slice_in_dim(a, side * columns, columns, 1) for a in (hidden, embed_grad)]
        return jnp.concatenate(pick + [code], axis=1)

    near, far = arrangement(dp, vocab)
    dims = (((0,), (0,)), ((), ()))
    column, early = gather_column(payload(dp), payload(1 - dp))
    held, _ = lax.optimization_barrier((logit_grad, early))
    partner = move(held, fd=1)
    down = move(column, dx=1)
    up = move(column, dx=-1)
    turned = lax.dot_general(logit_grad, near, dims, preferred_element_type=jnp.float32)
    turned = turned + lax.dot_general(partner, far, dims, preferred_element_type=jnp.float32)
    turned = turned.astype(jnp.bfloat16)
    down, up, turned = lax.optimization_barrier((down, up, turned))
    half = column.shape[0] // 2
    across = jnp.concatenate([move(down[:half], dx=1), move(up[half:], dx=-1)], axis=0)
    partial = contract(offset, turned, [column, up, down, move(column, fc=1)], (0, 1, 3, 4), columns)
    across, partial = lax.optimization_barrier((across, partial))
    rest = [across, move(up, fc=1), move(across, fc=1), move(down, fc=1)]
    return contract(offset, turned, rest, (2, 5, 6, 7), columns, partial)


def solution(mesh):
    placed = (
        P(("dp", "vocab")),
        P(("dp", "vocab"), None),
        P("dp", "vocab"),
        P(("dp", "vocab"), None),
    )
    return jax.shard_map(
        body, mesh=mesh, in_specs=placed, out_specs=P("vocab", "dp"), check_vma=False
    )
```

time: 85.7 us -> 70.9 us (0.83)
  waiting for transfers between devices: 23.6 us -> 14.2 us
  local copies, waits for them, and re-layouts: 1.08 us -> 4.39 us
  matrix products: 8.45 us -> 5.24 us
  starting transfers between devices: 37.9 us -> 34.7 us
  Pallas kernels: 12.9 us -> 10 us
  other arithmetic: 0.88 us -> 1.98 us
    ppermute x19, waiting for transfers between devices: 23.6 us -> 14.2 us  [move(): return lax.ppermute(value, ('dp', 'vocab'), pairs)]
    ppermute x19, starting transfers between devices: 37.9 us -> 34.7 us  [move(): return lax.ppermute(value, ('dp', 'vocab'), pairs)]
    pallas_call x1 -> x2, Pallas kernels: 12.9 us -> 10 us  [contract(): pl.pallas_call(functools.partial(contract_kernel, tuple(spots), len(added...]
    dot_general x1, matrix products: 4.59 us -> 2.6 us  [body(): lax.dot_general(logit_grad, near, dims, preferred_element_type=jnp.float32)]
    unnamed x1 -> x4, local copies, waits for them, and re-layouts: 0.02 us -> 1.89 us
    slice x2, local copies, waits for them, and re-layouts: 0.05 us -> 1.51 us  [the longest x1 0.76 us: body(): down[:half]]
    dot_general x1, matrix products: 3.86 us -> 2.65 us  [body(): lax.dot_general(partner, far, dims, preferred_element_type=jnp.float32)]
    concatenate x1 -> x2, other arithmetic: 0.05 us -> 1.16 us  [the longest x1 1.11 us: body(): jnp.concatenate([move(down[:half], dx=1), move(up[half:], dx=-1)], axis=0)]
  transfers between devices with their start and end apart: 19 -> 19, of which waited for: 9 -> 7; matrix products, arithmetic and copies ran while one was open for 10% -> 12% of each run, Pallas kernels for 0% -> 7%
where the time goes in v2:
time: 70.9 us; the launch traced here: 70.6 us
  starting transfers between devices  34.7 us (49%)
  waiting for transfers between devices  14.2 us (20%)
  Pallas kernels  10 us (14%)
  matrix products  5.24 us (7%)
  local copies, waits for them, and re-layouts  4.39 us (6%)
  other arithmetic  1.98 us (3%)
    ppermute x19, starting transfers between devices, move(): return lax.ppermute(value, ('dp', 'vocab'), pairs)  34.7 us
    ppermute x19, waiting for transfers between devices, move(): return lax.ppermute(value, ('dp', 'vocab'), pairs)  14.2 us
    pallas_call x2, Pallas kernels, contract(): pl.pallas_call(functools.partial(contract_kernel, tuple(spots), len(added...  10 us
    dot_general x1, matrix products, body(): lax.dot_general(partner, far, dims, preferred_element_type=jnp.float32)  2.65 us
    dot_general x1, matrix products, body(): lax.dot_general(logit_grad, near, dims, preferred_element_type=jnp.float32)  2.6 us
    unnamed x4, local copies, waits for them, and re-layouts  1.89 us
  transfers between devices with their start and end apart: 19, of which 7 were waited for; matrix products, arithmetic and copies ran while one was open for 12% of the time, Pallas kernels for 7%

profile of v2, /device:TPU:1, one launch (start us, length us, event | category | flops | bytes accessed | tf_op | source)
XLA Modules:
  0.0 70.6 jit_solution(996675657329438127)
XLA Ops:
  0.0 0.7 and_select_fusion.3
  0.7 0.8 %constant_dynamic-slice_fusion = (bf16[4,1152]{1,0:T(4,128)(2,1)S(1)}, bf16[4,1152]{1,0:T(4,128)(2,1)S(1)}, bf16[4,1152]{1,0:T(4,128)(2,1)S(1)}, bf16[4,1152]{1,0:T(4,128)(2,1)S(1)}) fusion(bf16[4,2304]{1,0:T(4,128)(2,1)} %param.7, s32[]{:T(128)S(6)} %select_n.207, s32[]{:T(128)S(6)} %select_n.199, bf16[4,2304]{1,0:T(4,128)(2,1)} %param.5), kind=kLoop, calls=%fused_computation.88 | loop fusion | bytes 73736 | tf_op jit(solution)/shard_map/dynamic_slice | solution.py:121
  1.5 0.1 select_convert_fusion
  1.6 3.8 %collective-permute-start.1 = (bf16[4,2432]{1,0:T(4,128)(2,1)S(1)}, bf16[4,2432]{1,0:T(4,128)(2,1)S(1)}, u32[]{:S(2)}, u32[]{:S(2)}) collective-permute-start(bf16[4,2432]{1,0:T(4,128)(2,1)S(1)} %get-tuple-element.22), channel_id=1, source_target_pairs={{0,2},{1,3},{2,0},{3,1},{4,6},{5,7},{6,4},{7,5},{8,10},{9,11},{10,... | collective-permute-start | bytes 58376 | tf_op jit(solution)/shard_map/ppermute | solution.py:30
  5.4 0.8 %collective-permute-start.2 = (bf16[4,2432]{1,0:T(4,128)(2,1)S(1)}, bf16[4,2432]{1,0:T(4,128)(2,1)S(1)}, u32[]{:S(2)}, u32[]{:S(2)}) collective-permute-start(bf16[4,2432]{1,0:T(4,128)(2,1)S(1)} %get-tuple-element.21), channel_id=1, source_target_pairs={{0,130},{1,131},{2,128},{3,129},{4,134},{5,135},{6,132},{7,133},{8... | collective-permute-start | bytes 58376 | tf_op jit(solution)/shard_map/ppermute | solution.py:30
  6.2 0.4 collective-permute-done.1
  6.6 1.3 %collective-permute-start.12 = (bf16[512,1024]{1,0:T(8,128)(2,1)}, bf16[512,1024]{1,0:T(8,128)(2,1)}, u32[]{:S(2)}, u32[]{:S(2)}) collective-permute-start(bf16[512,1024]{1,0:T(8,128)(2,1)} %param.6), channel_id=1, source_target_pairs={{0,128},{1,129},{2,130},{3,131},{4,132},{5,133},{6,134},{7,135},{8... | collective-permute-start | bytes 3145736 | tf_op jit(solution)/shard_map/ppermute | solution.py:30
  7.9 1.6 %collective-permute-done.2 = bf16[4,2432]{1,0:T(4,128)(2,1)S(1)} collective-permute-done((bf16[4,2432]{1,0:T(4,128)(2,1)S(1)}, bf16[4,2432]{1,0:T(4,128)(2,1)S(1)}, u32[]{:S(2)}, u32[]{:S(2)}) %collective-permute-start.2) | collective-permute-done | bytes 19488 | tf_op jit(solution)/shard_map/ppermute | solution.py:30
  9.6 1.4 %collective-permute-start.6 = (bf16[16,2432]{1,0:T(8,128)(2,1)S(1)}, bf16[16,2432]{1,0:T(8,128)(2,1)S(1)}, u32[]{:S(2)}, u32[]{:S(2)}) collective-permute-start(bf16[16,2432]{1,0:T(8,128)(2,1)S(1)} %pad_maximum_fusion.1), channel_id=1, source_target_pairs={{0,16},{1,17},{2,18},{3,19},{4,20},{5,21},{6,22},{7,23},{8,24},{9,... | collective-permute-start | bytes 233480 | tf_op jit(solution)/shard_map/ppermute | solution.py:30
  11.0 4.0 %collective-permute-start.3 = (bf16[16,2432]{1,0:T(8,128)(2,1)S(1)}, bf16[16,2432]{1,0:T(8,128)(2,1)S(1)}, u32[]{:S(2)}, u32[]{:S(2)}) collective-permute-start(bf16[16,2432]{1,0:T(8,128)(2,1)S(1)} %pad_maximum_fusion.1), channel_id=1, source_target_pairs={{0,112},{1,113},{2,114},{3,115},{4,116},{5,117},{6,118},{7,119},{8... | collective-permute-start | bytes 233480 | tf_op jit(solution)/shard_map/ppermute | solution.py:30
  15.0 1.7 %collective-permute-done.6 = bf16[16,2432]{1,0:T(8,128)(2,1)S(1)} collective-permute-done((bf16[16,2432]{1,0:T(8,128)(2,1)S(1)}, bf16[16,2432]{1,0:T(8,128)(2,1)S(1)}, u32[]{:S(2)}, u32[]{:S(2)}) %collective-permute-start.6) | collective-permute-done | bytes 77856 | tf_op jit(solution)/shard_map/ppermute | solution.py:30
  16.7 2.8 %collective-permute-start.4 = (bf16[16,2432]{1,0:T(8,128)(2,1)S(1)}, bf16[16,2432]{1,0:T(8,128)(2,1)S(1)}, u32[]{:S(2)}, u32[]{:S(2)}) collective-permute-start(bf16[16,2432]{1,0:T(8,128)(2,1)S(1)} %collective-permute-done.3), channel_id=1, source_target_pairs={{0,112},{1,113},{2,114},{3,115},{4,116},{5,117},{6,118},{7,119},{8... | collective-permute-start | bytes 233480 | tf_op jit(solution)/shard_map/ppermute | solution.py:30
  19.5 1.7 %collective-permute-done.7 = bf16[16,2432]{1,0:T(8,128)(2,1)S(1)} collective-permute-done((bf16[16,2432]{1,0:T(8,128)(2,1)S(1)}, bf16[16,2432]{1,0:T(8,128)(2,1)S(1)}, u32[]{:S(2)}, u32[]{:S(2)}) %collective-permute-start.7) | collective-permute-done | bytes 77856 | tf_op jit(solution)/shard_map/ppermute | solution.py:30
  21.2 2.7 %collective-permute-start.5 = (bf16[16,2432]{1,0:T(8,128)(2,1)S(1)}, bf16[16,2432]{1,0:T(8,128)(2,1)S(1)}, u32[]{:S(2)}, u32[]{:S(2)}) collective-permute-start(bf16[16,2432]{1,0:T(8,128)(2,1)S(1)} %collective-permute-done.4), channel_id=1, source_target_pairs={{0,112},{1,113},{2,114},{3,115},{4,116},{5,117},{6,118},{7,119},{8... | collective-permute-start | bytes 233480 | tf_op jit(solution)/shard_map/ppermute | solution.py:30
  24.0 1.7 %collective-permute-done.8 = bf16[16,2432]{1,0:T(8,128)(2,1)S(1)} collective-permute-done((bf16[16,2432]{1,0:T(8,128)(2,1)S(1)}, bf16[16,2432]{1,0:T(8,128)(2,1)S(1)}, u32[]{:S(2)}, u32[]{:S(2)}) %collective-permute-start.8) | collective-permute-done | bytes 77856 | tf_op jit(solution)/shard_map/ppermute | solution.py:30
  25.7 5.4 %collective-permute-done.9 = bf16[16,2432]{1,0:T(8,128)(2,1)S(1)} collective-permute-done((bf16[16,2432]{1,0:T(8,128)(2,1)S(1)}, bf16[16,2432]{1,0:T(8,128)(2,1)S(1)}, u32[]{:S(2)}, u32[]{:S(2)}) %collective-permute-start.9) | collective-permute-done | bytes 77856 | tf_op jit(solution)/shard_map/ppermute | solution.py:30
  31.1 0.2 concatenate.19.refs_0_
  31.3 2.6 %collective-permute-start.11 = (bf16[128,2432]{1,0:T(8,128)(2,1)S(1)}, bf16[128,2432]{1,0:T(8,128)(2,1)S(1)}, u32[]{:S(2)}, u32[]{:S(2)}) collective-permute-start(bf16[128,2432]{1,0:T(8,128)(2,1)S(1)} %concatenate.19.refs_0_), channel_id=1, source_target_pairs={{0,12},{1,13},{2,14},{3,15},{4,0},{5,1},{6,2},{7,3},{8,4},{9,5},{1... | collective-permute-start | bytes 1867784 | tf_op jit(solution)/shard_map/ppermute | solution.py:30
  33.8 2.6 %fusion.3 = f32[1024,1024]{0,1:T(8,128)S(1)} fusion(bf16[512,1024]{1,0:T(8,128)(2,1)} %param.6, s32[1024]{0:T(1024)S(1)} %fusion.24, pred[1024]{0:T(1024)(128)(4,1)S(1)} %fusion.33), kind=kOutput, calls=%fused_computation.5 | convolution fusion | flops 1074790400 | bytes 5248000 | tf_op jit(solution)/shard_map/dot_general | solution.py:131
  36.4 6.7 %collective-permute-start.15 = (bf16[128,2432]{1,0:T(8,128)(2,1)S(1)}, bf16[128,2432]{1,0:T(8,128)(2,1)}, u32[]{:S(2)}, u32[]{:S(2)}) collective-permute-start(bf16[128,2432]{1,0:T(8,128)(2,1)S(1)} %concatenate.19.refs_0_), channel_id=1, source_target_pairs={{0,1},{1,0},{2,3},{3,2},{4,5},{5,4},{6,7},{7,6},{8,9},{9,8},{10,11... | collective-permute-start | bytes 1867784 | tf_op jit(solution)/shard_map/ppermute | solution.py:30
  43.2 2.6 %fusion.logit_ref = bf16[1024,1024]{1,0:T(8,128)(2,1)S(1)} fusion(f32[1024,1024]{0,1:T(8,128)S(1)} %fusion.3, bf16[512,1024]{1,0:T(8,128)(2,1)} %collective-permute-done.12, s32[1024]{0:T(1024)S(1)} %fusion.24, pred[1024]{0:T(1024)(128)(4,1)S(1)} %fusion.41), kind=kOutput, calls=%fused_computation.1 | convolution fusion | flops 1076887552 | bytes 7345152 | tf_op jit(solution)/shard_map/dot_general | solution.py:132
  45.9 0.8 %copy-done = bf16[128,2432]{1,0:T(8,128)(2,1)} copy-done((bf16[128,2432]{1,0:T(8,128)(2,1)}, bf16[128,2432]{1,0:T(8,128)(2,1)S(1)}, u32[]{:S(2)}) %copy-start) | copy-done | bytes 622616
  46.7 0.8 %slice.6 = bf16[64,2432]{1,0:T(8,128)(2,1)} slice(bf16[128,2432]{1,0:T(8,128)(2,1)S(1)} %collective-permute-done.10.refs_2_), slice={[0:64], [0:2432]} | slice | bytes 622592 | tf_op jit(solution)/shard_map/slice | solution.py:136
  47.4 0.8 %slice.7 = bf16[64,2432]{1,0:T(8,128)(2,1)} slice(bf16[128,2432]{1,0:T(8,128)(2,1)S(1)} %collective-permute-done.11.refs_1_), slice={[64:128], [0:2432]} | slice | bytes 622592 | tf_op jit(solution)/shard_map/slice | solution.py:136
  48.2 2.9 %collective-permute-start.14 = (bf16[64,2432]{1,0:T(8,128)(2,1)}, bf16[64,2432]{1,0:T(8,128)(2,1)}, u32[]{:S(2)}, u32[]{:S(2)}) collective-permute-start(bf16[64,2432]{1,0:T(8,128)(2,1)} %slice.7), channel_id=1, source_target_pairs={{0,12},{1,13},{2,14},{3,15},{4,0},{5,1},{6,2},{7,3},{8,4},{9,5},{1... | collective-permute-start | bytes 933896 | tf_op jit(solution)/shard_map/ppermute | solution.py:30
  51.1 5.0 %collective-permute-start.18 = (bf16[128,2432]{1,0:T(8,128)(2,1)}, bf16[128,2432]{1,0:T(8,128)(2,1)S(1)}, u32[]{:S(2)}, u32[]{:S(2)}) collective-permute-start(bf16[128,2432]{1,0:T(8,128)(2,1)} %copy-done), channel_id=1, source_target_pairs={{0,1},{1,0},{2,3},{3,2},{4,5},{5,4},{6,7},{7,6},{8,9},{9,8},{10,11... | collective-permute-start | bytes 1867784 | tf_op jit(solution)/shard_map/ppermute | solution.py:30
  56.1 1.1 %copy-done.1 = bf16[128,2432]{1,0:T(8,128)(2,1)S(1)} copy-done((bf16[128,2432]{1,0:T(8,128)(2,1)S(1)}, bf16[128,2432]{1,0:T(8,128)(2,1)}, u32[]{:S(2)}) %copy-start.1) | copy-done | bytes 622616
  57.2 5.0 %shard_map.46.refs_4_ = f32[1024,1152]{1,0:T(8,128)S(1)} custom-call(s32[1]{0:T(128)} %bitcast.offset_ref, bf16[1024,1024]{1,0:T(8,128)(2,1)S(1)} %fusion.logit_ref, bf16[128,2432]{1,0:T(8,128)(2,1)S(1)} %concatenate.19.refs_0_, bf16[128,2432]{1,0:T(8,128)(2,1)S(1)} %collective-permute-done.11.refs_1_, bf16[128,2432]{1,0:T(8,128)(2,1)S(1)} %copy-done.1, ...), custom_call_target="tpu_custom_call" | custom-call | flops 2415919104 | bytes 12582912 | tf_op jit(solution)/shard_map/pallas_call | solution.py:92
  62.2 1.1 %pad_maximum_fusion.refs_0_ = bf16[128,2432]{1,0:T(8,128)(2,1)S(1)} fusion(bf16[64,2432]{1,0:T(8,128)(2,1)} %collective-permute-done.14, bf16[64,2432]{1,0:T(8,128)(2,1)} %collective-permute-done.13), kind=kLoop, calls=%fused_computation.10 | loop fusion | flops 1245184 | bytes 1245184 | tf_op jit(solution)/shard_map/concatenate | solution.py:136
  63.3 0.6 collective-permute-start.17
  63.9 1.7 %collective-permute-done.17.refs_2_ = bf16[128,2432]{1,0:T(8,128)(2,1)S(1)} collective-permute-done((bf16[128,2432]{1,0:T(8,128)(2,1)S(1)}, bf16[128,2432]{1,0:T(8,128)(2,1)S(1)}, u32[]{:S(2)}, u32[]{:S(2)}) %collective-permute-start.17) | collective-permute-done | bytes 622624 | tf_op jit(solution)/shard_map/ppermute | solution.py:30
  65.6 5.0 %shard_map.47 = f32[1024,1152]{1,0:T(8,128)} custom-call(s32[1]{0:T(128)} %bitcast.offset_ref, bf16[1024,1024]{1,0:T(8,128)(2,1)S(1)} %fusion.logit_ref, bf16[128,2432]{1,0:T(8,128)(2,1)S(1)} %pad_maximum_fusion.refs_0_, bf16[128,2432]{1,0:T(8,128)(2,1)S(1)} %collective-permute-done.16.refs_1_, bf16[128,2432]{1,0:T(8,128)(2,1)S(1)} %collective-permute-done.17.refs_2_, ...), custom_call_target="tpu_custom_call" | custom-call | flops 2415919104 | bytes 12582912 | tf_op jit(solution)/shard_map/pallas_call | solution.py:92
  (28 shorter events, 0.2 us)
Async XLA Ops:
  1.6 5.0 %collective-permute-start.1 = (bf16[4,2432]{1,0:T(4,128)(2,1)S(1)}, bf16[4,2432]{1,0:T(4,128)(2,1)S(1)}, u32[]{:S(2)}, u32[]{:S(2)}) collective-permute-start(bf16[4,2432]{1,0:T(4,128)(2,1)S(1)} %get-tuple-element.22), channel_id=1, source_target_pairs={{0,2},{1,3},{2,0},{3,1},{4,6},{5,7},{6,4},{7,5},{8,10},{9,11},{10,... | collective-permute-start | bytes 58376 | tf_op jit(solution)/shard_map/ppermute | solution.py:30
  5.4 4.1 %collective-permute-start.2 = (bf16[4,2432]{1,0:T(4,128)(2,1)S(1)}, bf16[4,2432]{1,0:T(4,128)(2,1)S(1)}, u32[]{:S(2)}, u32[]{:S(2)}) collective-permute-start(bf16[4,2432]{1,0:T(4,128)(2,1)S(1)} %get-tuple-element.21), channel_id=1, source_target_pairs={{0,130},{1,131},{2,128},{3,129},{4,134},{5,135},{6,132},{7,133},{8... | collective-permute-start | bytes 58376 | tf_op jit(solution)/shard_map/ppermute | solution.py:30
  6.2 3.4 %collective-permute-start = (bf16[4,2432]{1,0:T(4,128)(2,1)S(1)}, bf16[4,2432]{1,0:T(4,128)(2,1)S(1)}, u32[]{:S(2)}, u32[]{:S(2)}) collective-permute-start(bf16[4,2432]{1,0:T(4,128)(2,1)S(1)} %get-tuple-element.21), channel_id=1, source_target_pairs={{0,128},{1,129},{2,130},{3,131},{4,132},{5,133},{6,134},{7,135},{8... | collective-permute-start | bytes 58376 | tf_op jit(solution)/shard_map/ppermute | solution.py:30
  6.6 36.6 %collective-permute-start.12 = (bf16[512,1024]{1,0:T(8,128)(2,1)}, bf16[512,1024]{1,0:T(8,128)(2,1)}, u32[]{:S(2)}, u32[]{:S(2)}) collective-permute-start(bf16[512,1024]{1,0:T(8,128)(2,1)} %param.6), channel_id=1, source_target_pairs={{0,128},{1,129},{2,130},{3,131},{4,132},{5,133},{6,134},{7,135},{8... | collective-permute-start | bytes 3145736 | tf_op jit(solution)/shard_map/ppermute | solution.py:30
  9.6 7.1 %collective-permute-start.6 = (bf16[16,2432]{1,0:T(8,128)(2,1)S(1)}, bf16[16,2432]{1,0:T(8,128)(2,1)S(1)}, u32[]{:S(2)}, u32[]{:S(2)}) collective-permute-start(bf16[16,2432]{1,0:T(8,128)(2,1)S(1)} %pad_maximum_fusion.1), channel_id=1, source_target_pairs={{0,16},{1,17},{2,18},{3,19},{4,20},{5,21},{6,22},{7,23},{8,24},{9,... | collective-permute-start | bytes 233480 | tf_op jit(solution)/shard_map/ppermute | solution.py:30
  11.0 5.7 %collective-permute-start.3 = (bf16[16,2432]{1,0:T(8,128)(2,1)S(1)}, bf16[16,2432]{1,0:T(8,128)(2,1)S(1)}, u32[]{:S(2)}, u32[]{:S(2)}) collective-permute-start(bf16[16,2432]{1,0:T(8,128)(2,1)S(1)} %pad_maximum_fusion.1), channel_id=1, source_target_pairs={{0,112},{1,113},{2,114},{3,115},{4,116},{5,117},{6,118},{7,119},{8... | collective-permute-start | bytes 233480 | tf_op jit(solution)/shard_map/ppermute | solution.py:30
  16.7 4.5 %collective-permute-start.7 = (bf16[16,2432]{1,0:T(8,128)(2,1)S(1)}, bf16[16,2432]{1,0:T(8,128)(2,1)S(1)}, u32[]{:S(2)}, u32[]{:S(2)}) collective-permute-start(bf16[16,2432]{1,0:T(8,128)(2,1)S(1)} %collective-permute-done.6), channel_id=1, source_target_pairs={{0,16},{1,17},{2,18},{3,19},{4,20},{5,21},{6,22},{7,23},{8,24},{9,... | collective-permute-start | bytes 233480 | tf_op jit(solution)/shard_map/ppermute | solution.py:30
  16.7 4.5 %collective-permute-start.4 = (bf16[16,2432]{1,0:T(8,128)(2,1)S(1)}, bf16[16,2432]{1,0:T(8,128)(2,1)S(1)}, u32[]{:S(2)}, u32[]{:S(2)}) collective-permute-start(bf16[16,2432]{1,0:T(8,128)(2,1)S(1)} %collective-permute-done.3), channel_id=1, source_target_pairs={{0,112},{1,113},{2,114},{3,115},{4,116},{5,117},{6,118},{7,119},{8... | collective-permute-start | bytes 233480 | tf_op jit(solution)/shard_map/ppermute | solution.py:30
  21.2 4.5 %collective-permute-start.8 = (bf16[16,2432]{1,0:T(8,128)(2,1)S(1)}, bf16[16,2432]{1,0:T(8,128)(2,1)S(1)}, u32[]{:S(2)}, u32[]{:S(2)}) collective-permute-start(bf16[16,2432]{1,0:T(8,128)(2,1)S(1)} %collective-permute-done.7), channel_id=1, source_target_pairs={{0,16},{1,17},{2,18},{3,19},{4,20},{5,21},{6,22},{7,23},{8,24},{9,... | collective-permute-start | bytes 233480 | tf_op jit(solution)/shard_map/ppermute | solution.py:30
  21.2 4.4 %collective-permute-start.5 = (bf16[16,2432]{1,0:T(8,128)(2,1)S(1)}, bf16[16,2432]{1,0:T(8,128)(2,1)S(1)}, u32[]{:S(2)}, u32[]{:S(2)}) collective-permute-start(bf16[16,2432]{1,0:T(8,128)(2,1)S(1)} %collective-permute-done.4), channel_id=1, source_target_pairs={{0,112},{1,113},{2,114},{3,115},{4,116},{5,117},{6,118},{7,119},{8... | collective-permute-start | bytes 233480 | tf_op jit(solution)/shard_map/ppermute | solution.py:30
  25.6 5.4 %collective-permute-start.9 = (bf16[16,2432]{1,0:T(8,128)(2,1)S(1)}, bf16[16,2432]{1,0:T(8,128)(2,1)S(1)}, u32[]{:S(2)}, u32[]{:S(2)}) collective-permute-start(bf16[16,2432]{1,0:T(8,128)(2,1)S(1)} %collective-permute-done.8), channel_id=1, source_target_pairs={{0,16},{1,17},{2,18},{3,19},{4,20},{5,21},{6,22},{7,23},{8,24},{9,... | collective-permute-start | bytes 233480 | tf_op jit(solution)/shard_map/ppermute | solution.py:30
  31.3 14.6 %collective-permute-start.11 = (bf16[128,2432]{1,0:T(8,128)(2,1)S(1)}, bf16[128,2432]{1,0:T(8,128)(2,1)S(1)}, u32[]{:S(2)}, u32[]{:S(2)}) collective-permute-start(bf16[128,2432]{1,0:T(8,128)(2,1)S(1)} %concatenate.19.refs_0_), channel_id=1, source_target_pairs={{0,12},{1,13},{2,14},{3,15},{4,0},{5,1},{6,2},{7,3},{8,4},{9,5},{1... | collective-permute-start | bytes 1867784 | tf_op jit(solution)/shard_map/ppermute | solution.py:30
  33.8 12.0 %collective-permute-start.10 = (bf16[128,2432]{1,0:T(8,128)(2,1)S(1)}, bf16[128,2432]{1,0:T(8,128)(2,1)S(1)}, u32[]{:S(2)}, u32[]{:S(2)}) collective-permute-start(bf16[128,2432]{1,0:T(8,128)(2,1)S(1)} %concatenate.19.refs_0_), channel_id=1, source_target_pairs={{0,4},{1,5},{2,6},{3,7},{4,8},{5,9},{6,10},{7,11},{8,12},{9,13},{1... | collective-permute-start | bytes 1867784 | tf_op jit(solution)/shard_map/ppermute | solution.py:30
  36.4 19.7 %collective-permute-start.15 = (bf16[128,2432]{1,0:T(8,128)(2,1)S(1)}, bf16[128,2432]{1,0:T(8,128)(2,1)}, u32[]{:S(2)}, u32[]{:S(2)}) collective-permute-start(bf16[128,2432]{1,0:T(8,128)(2,1)S(1)} %concatenate.19.refs_0_), channel_id=1, source_target_pairs={{0,1},{1,0},{2,3},{3,2},{4,5},{5,4},{6,7},{7,6},{8,9},{9,8},{10,11... | collective-permute-start | bytes 1867784 | tf_op jit(solution)/shard_map/ppermute | solution.py:30
  45.9 0.8 %copy-start = (bf16[128,2432]{1,0:T(8,128)(2,1)}, bf16[128,2432]{1,0:T(8,128)(2,1)S(1)}, u32[]{:S(2)}) copy-start(bf16[128,2432]{1,0:T(8,128)(2,1)S(1)} %collective-permute-done.10.refs_2_) | copy-start | bytes 1867780
  48.2 14.0 %collective-permute-start.14 = (bf16[64,2432]{1,0:T(8,128)(2,1)}, bf16[64,2432]{1,0:T(8,128)(2,1)}, u32[]{:S(2)}, u32[]{:S(2)}) collective-permute-start(bf16[64,2432]{1,0:T(8,128)(2,1)} %slice.7), channel_id=1, source_target_pairs={{0,12},{1,13},{2,14},{3,15},{4,0},{5,1},{6,2},{7,3},{8,4},{9,5},{1... | collective-permute-start | bytes 933896 | tf_op jit(solution)/shard_map/ppermute | solution.py:30
  51.1 11.1 %collective-permute-start.13 = (bf16[64,2432]{1,0:T(8,128)(2,1)}, bf16[64,2432]{1,0:T(8,128)(2,1)}, u32[]{:S(2)}, u32[]{:S(2)}) collective-permute-start(bf16[64,2432]{1,0:T(8,128)(2,1)} %slice.6), channel_id=1, source_target_pairs={{0,4},{1,5},{2,6},{3,7},{4,8},{5,9},{6,10},{7,11},{8,12},{9,13},{1... | collective-permute-start | bytes 933896 | tf_op jit(solution)/shard_map/ppermute | solution.py:30
  51.1 12.8 %collective-permute-start.18 = (bf16[128,2432]{1,0:T(8,128)(2,1)}, bf16[128,2432]{1,0:T(8,128)(2,1)S(1)}, u32[]{:S(2)}, u32[]{:S(2)}) collective-permute-start(bf16[128,2432]{1,0:T(8,128)(2,1)} %copy-done), channel_id=1, source_target_pairs={{0,1},{1,0},{2,3},{3,2},{4,5},{5,4},{6,7},{7,6},{8,9},{9,8},{10,11... | collective-permute-start | bytes 1867784 | tf_op jit(solution)/shard_map/ppermute | solution.py:30
  56.1 7.8 %collective-permute-start.16 = (bf16[128,2432]{1,0:T(8,128)(2,1)S(1)}, bf16[128,2432]{1,0:T(8,128)(2,1)S(1)}, u32[]{:S(2)}, u32[]{:S(2)}) collective-permute-start(bf16[128,2432]{1,0:T(8,128)(2,1)S(1)} %collective-permute-done.11.refs_1_), channel_id=1, source_target_pairs={{0,1},{1,0},{2,3},{3,2},{4,5},{5,4},{6,7},{7,6},{8,9},{9,8},{10,11... | collective-permute-start | bytes 1867784 | tf_op jit(solution)/shard_map/ppermute | solution.py:30
  56.1 1.1 %copy-start.1 = (bf16[128,2432]{1,0:T(8,128)(2,1)S(1)}, bf16[128,2432]{1,0:T(8,128)(2,1)}, u32[]{:S(2)}) copy-start(bf16[128,2432]{1,0:T(8,128)(2,1)} %copy-done) | copy-start | bytes 1867780
  63.3 2.3 %collective-permute-start.17 = (bf16[128,2432]{1,0:T(8,128)(2,1)S(1)}, bf16[128,2432]{1,0:T(8,128)(2,1)S(1)}, u32[]{:S(2)}, u32[]{:S(2)}) collective-permute-start(bf16[128,2432]{1,0:T(8,128)(2,1)S(1)} %pad_maximum_fusion.refs_0_), channel_id=1, source_target_pairs={{0,1},{1,0},{2,3},{3,2},{4,5},{5,4},{6,7},{7,6},{8,9},{9,8},{10,11... | collective-permute-start | bytes 1867784 | tf_op jit(solution)/shard_map/ppermute | solution.py:30

commit v3 on v2

v3 whole, which is shorter than its diff:
```python
import functools

import jax
import jax.numpy as jnp
import numpy as np
from jax import lax
from jax.experimental import pallas as pl
from jax.experimental.pallas import tpu as pltpu
from jax.sharding import PartitionSpec as P

Z, X, YH, CORE, DP = 8, 4, 2, 2, 2
ROWS = 4
LANES = 128


def coords(vocab):
    return vocab // (X * 4), (vocab // 4) % X, (vocab // 2) % 2, vocab % 2


def flat(dp, z, x, yh, core):
    return dp * (Z * X * 4) + ((z % Z) * X + (x % X)) * 4 + yh * 2 + core


def move(value, dz=0, dx=0, fy=0, fd=0, fc=0):
    pairs = []
    for dp in range(DP):
        for vocab in range(Z * X * 4):
            z, x, yh, core = coords(vocab)
            pairs.append((flat(dp, z, x, yh, core), flat(dp ^ fd, z + dz, x + dx, yh ^ fy, core ^ fc)))
    return lax.ppermute(value, ("dp", "vocab"), pairs)


def gather_column(own, other):
    from_dp = move(other, fd=1)
    from_dy = move(other, fd=1, fy=1)
    from_yh = move(own, fy=1)
    chunk = jnp.concatenate([own, from_dp, from_yh, from_dy], axis=0)
    p2, m2 = move(chunk, dz=2), move(chunk, dz=-2)
    p1, m1 = move(chunk, dz=1), move(chunk, dz=-1)
    p3, m3, m4 = move(p2, dz=1), move(m2, dz=-1), move(m2, dz=-2)
    return [chunk, m1, m2, m3], [m4, p3, p2, p1], from_yh


def arrangement(dp, vocab):
    z, x, yh, core = coords(vocab)
    place = lax.broadcasted_iota(jnp.int32, (1, 2 * Z * X * YH * CORE * ROWS), 1)
    j, r, zi = place % 4, (place // 4) % 4, (place // 16) % Z
    xi, ci = (place // (16 * Z)) % X, place // (16 * Z * X)
    token = ((((z + zi) % Z) * X + (x + xi) % X) * 2 + (yh ^ (r // 2))) * 2 + (core ^ ci)
    token = token * ROWS + j
    spot = lax.broadcasted_iota(jnp.int32, (Z * X * YH * CORE * ROWS, 1), 0)
    hit = spot == token
    near = r % 2 == 0
    return (hit & near).astype(jnp.bfloat16), (hit & ~near).astype(jnp.bfloat16)


def contract_kernel(spots, pieces, columns, added, last, offset_ref, logit_ref, *refs):
    chunks = refs[:pieces]
    out_ref = refs[pieces + added]
    rows = logit_ref.shape[0]
    step = rows // 2
    lane = lax.broadcasted_iota(jnp.int32, (8, LANES), 1)
    weight = jnp.where(lane == 0, 512.0, jnp.where(lane == 1, 2.0, jnp.where(lane == 2, 1.0, 0.0)))
    code = jnp.concatenate([c[:, 2 * columns :] for c in chunks], axis=0)
    ids = lax.dot_general(
        weight.astype(jnp.bfloat16), code, (((1,), (1,)), ((), ())), preferred_element_type=jnp.float32
    )
    ids = ids[:1].astype(jnp.int32) - offset_ref[0]
    copies = []
    for block in range(2):
        span = slice(block * step, (block + 1) * step)
        row = lax.broadcasted_iota(jnp.int32, (step, ids.shape[1]), 0) + block * step
        onehot = jnp.where(row == ids, 1.0, 0.0).astype(jnp.bfloat16)
        left = jnp.concatenate([logit_ref[span, s * LANES : (s + 1) * LANES] for s in spots], axis=1)
        right = jnp.concatenate([c[:, :columns] for c in chunks], axis=0)
        total = jnp.dot(left, right, preferred_element_type=jnp.float32)
        right = jnp.concatenate([c[:, columns : 2 * columns] for c in chunks], axis=0)
        total += jnp.dot(onehot, right, preferred_element_type=jnp.float32)
        if added:
            total += refs[pieces][span, :]
        if last:
            stage, sems = refs[pieces + added + 1 :]
            stage[span, :] = total
            copies.append(pltpu.make_async_copy(stage.at[span, :], out_ref.at[span, :], sems.at[block]))
            copies[-1].start()
        else:
            out_ref[span, :] = total
    for copy in copies:
        copy.wait()


def contract(offset, logits, chunks, spots, columns, partial=None, last=False):
    rows = logits.shape[0]
    added = [] if partial is None else [partial]
    here = pl.BlockSpec(memory_space=pltpu.VMEM)
    scratch = [pltpu.VMEM((rows, columns), jnp.float32), pltpu.SemaphoreType.DMA((2,))]
    return pl.pallas_call(
        functools.partial(contract_kernel, tuple(spots), len(chunks), columns, len(added), last),
        out_shape=jax.ShapeDtypeStruct((rows, columns), jnp.float32),
        in_specs=[pl.BlockSpec(memory_space=pltpu.SMEM)] + [here] * (1 + len(chunks) + len(added)),
        out_specs=pl.BlockSpec(memory_space=pl.ANY) if last else here,
        scratch_shapes=scratch if last else [],
        compiler_params=pltpu.CompilerParams(vmem_limit_bytes=16 << 20),
        cost_estimate=pl.CostEstimate(
            flops=4 * rows * len(spots) * LANES * columns, bytes_accessed=8 << 20, transcendentals=0
        ),
    )(offset, logits, *chunks, *added)


def body(token_ids, hidden, logit_grad, embed_grad):
    dp, vocab = lax.axis_index("dp"), lax.axis_index("vocab")
    columns = hidden.shape[1] // 2
    offset = (vocab * logit_grad.shape[1]).astype(jnp.int32).reshape(1)
    ids = token_ids[:, None]
    lane = lax.broadcasted_iota(jnp.int32, (ROWS, LANES), 1)
    code = jnp.where(lane == 0, ids // 512, jnp.where(lane == 1, (ids // 2) % 256, ids % 2))
    code = jnp.where(lane < 3, code, 0).astype(jnp.bfloat16)

    def payload(side):
        pick = [lax.dynamic_slice_in_dim(a, side * columns, columns, 1) for a in (hidden, embed_grad)]
        return jnp.concatenate(pick + [code], axis=1)

    near, far = arrangement(dp, vocab)
    dims = (((0,), (0,)), ((), ()))
    low, high, early = gather_column(payload(dp), payload(1 - dp))
    held, _ = lax.optimization_barrier((logit_grad, early))
    partner = move(held, fd=1)
    low, high, column = (jnp.concatenate(part, axis=0) for part in (low, high, low + high))
    down_low, up_high = move(low, dx=1), move(high, dx=-1)
    down_high, up_low = move(high, dx=1), move(low, dx=-1)
    across = [move(down_low, dx=1), move(up_high, dx=-1)]
    turned = lax.dot_general(logit_grad, near, dims, preferred_element_type=jnp.float32)
    turned = turned + lax.dot_general(partner, far, dims, preferred_element_type=jnp.float32)
    turned = turned.astype(jnp.bfloat16)
    around = [up_low, up_high, down_low, down_high]
    *around, turned = lax.optimization_barrier((*around, turned))
    first = [column, move(column, fc=1)] + around
    partial = contract(offset, turned, first, (0, 4, 1, 3), columns)
    *across, partial = lax.optimization_barrier((*across, partial))
    second = [move(part, fc=1) for part in around]
    partial = contract(offset, turned, second, (5, 7), columns, partial)
    third = across + [move(part, fc=1) for part in across]
    return contract(offset, turned, third, (2, 6), columns, partial, last=True)


def solution(mesh):
    placed = (
        P(("dp", "vocab")),
        P(("dp", "vocab"), None),
        P("dp", "vocab"),
        P(("dp", "vocab"), None),
    )
    return jax.shard_map(
        body, mesh=mesh, in_specs=placed, out_specs=P("vocab", "dp"), check_vma=False
    )
```

time: 70.9 us -> 79 us (1.11)
  local copies, waits for them, and re-layouts: 4.39 us -> 7.74 us
  matrix products: 5.24 us -> 8.45 us
  starting transfers between devices: 34.7 us -> 36.1 us
  Pallas kernels: 10 us -> 11.2 us
  other arithmetic: 1.98 us -> 0.87 us
    concatenate x1 -> x3, local copies, waits for them, and re-layouts: 0.21 us -> 4.06 us  [body(): jnp.concatenate(part, axis=0)]
    dot_general x1, matrix products: 2.6 us -> 4.59 us  [body(): lax.dot_general(logit_grad, near, dims, preferred_element_type=jnp.float32)]
    slice x2 -> x0, local copies, waits for them, and re-layouts: 1.51 us -> none  [the longest x1 0.76 us: body(): down[:half]]
    ppermute x19 -> x24, starting transfers between devices: 34.7 us -> 36.1 us  [move(): return lax.ppermute(value, ('dp', 'vocab'), pairs)]
    dot_general x1, matrix products: 2.65 us -> 3.86 us  [body(): lax.dot_general(partner, far, dims, preferred_element_type=jnp.float32)]
    pallas_call x2 -> x3, Pallas kernels: 10 us -> 11.2 us  [contract(): pl.pallas_call(functools.partial(contract_kernel, tuple(spots), len(chunk...]
    concatenate x1 -> x0, other arithmetic: 1.11 us -> none  [body(): jnp.concatenate([move(down[:half], dx=1), move(up[half:], dx=-1)], axis=0)]
    unnamed x4 -> x5, local copies, waits for them, and re-layouts: 1.89 us -> 2.91 us
  transfers between devices with their start and end apart: 19 -> 24, of which waited for: 7 -> 6; matrix products, arithmetic and copies ran while one was open for 12% -> 18% of each run, Pallas kernels for 7% -> 9%
where the time goes in v3:
time: 79 us; the launch traced here: 78.7 us
  starting transfers between devices  36.1 us (46%)
  waiting for transfers between devices  14.1 us (18%)
  Pallas kernels  11.2 us (14%)
  matrix products  8.45 us (11%)
  local copies, waits for them, and re-layouts  7.74 us (10%)
  other arithmetic  0.87 us (1%)
    ppermute x24, starting transfers between devices, move(): return lax.ppermute(value, ('dp', 'vocab'), pairs)  36.1 us
    ppermute x24, waiting for transfers between devices, move(): return lax.ppermute(value, ('dp', 'vocab'), pairs)  14.1 us
    pallas_call x3, Pallas kernels, contract(): pl.pallas_call(functools.partial(contract_kernel, tuple(spots), len(chunk...  11.2 us
    dot_general x1, matrix products, body(): lax.dot_general(logit_grad, near, dims, preferred_element_type=jnp.float32)  4.59 us
    concatenate x3, local copies, waits for them, and re-layouts, body(): jnp.concatenate(part, axis=0)  4.06 us
    dot_general x1, matrix products, body(): lax.dot_general(partner, far, dims, preferred_element_type=jnp.float32)  3.86 us
    unnamed x5, local copies, waits for them, and re-layouts  2.91 us
  transfers between devices with their start and end apart: 24, of which 6 were waited for; matrix products, arithmetic and copies ran while one was open for 18% of the time, Pallas kernels for 9%

profile of v3, /device:TPU:1, one launch (start us, length us, event | category | flops | bytes accessed | tf_op | source)
XLA Modules:
  0.0 78.7 jit_solution(9954890282863229593)
XLA Ops:
  0.0 0.7 and_select_fusion.3
  0.7 0.8 constant_dynamic-slice_fusion
  1.6 3.7 %collective-permute-start.2 = (bf16[4,2432]{1,0:T(4,128)(2,1)S(1)}, bf16[4,2432]{1,0:T(4,128)(2,1)S(1)}, u32[]{:S(2)}, u32[]{:S(2)}) collective-permute-start(bf16[4,2432]{1,0:T(4,128)(2,1)S(1)} %get-tuple-element.27), channel_id=1, source_target_pairs={{0,130},{1,131},{2,128},{3,129},{4,134},{5,135},{6,132},{7,133},{8... | collective-permute-start | bytes 58376 | tf_op jit(solution)/shard_map/ppermute | solution.py:30
  5.2 1.3 %collective-permute-start.1 = (bf16[4,2432]{1,0:T(4,128)(2,1)S(1)}, bf16[4,2432]{1,0:T(4,128)(2,1)S(1)}, u32[]{:S(2)}, u32[]{:S(2)}) collective-permute-start(bf16[4,2432]{1,0:T(4,128)(2,1)S(1)} %get-tuple-element.28), channel_id=1, source_target_pairs={{0,2},{1,3},{2,0},{3,1},{4,6},{5,7},{6,4},{7,5},{8,10},{9,11},{10,... | collective-permute-start | bytes 58376 | tf_op jit(solution)/shard_map/ppermute | solution.py:30
  6.5 1.3 %collective-permute-done = bf16[4,2432]{1,0:T(4,128)(2,1)S(1)} collective-permute-done((bf16[4,2432]{1,0:T(4,128)(2,1)S(1)}, bf16[4,2432]{1,0:T(4,128)(2,1)S(1)}, u32[]{:S(2)}, u32[]{:S(2)}) %collective-permute-start) | collective-permute-done | bytes 19488 | tf_op jit(solution)/shard_map/ppermute | solution.py:30
  7.8 1.6 %collective-permute-done.1 = bf16[4,2432]{1,0:T(4,128)(2,1)S(1)} collective-permute-done((bf16[4,2432]{1,0:T(4,128)(2,1)S(1)}, bf16[4,2432]{1,0:T(4,128)(2,1)S(1)}, u32[]{:S(2)}, u32[]{:S(2)}) %collective-permute-start.1) | collective-permute-done | bytes 19488 | tf_op jit(solution)/shard_map/ppermute | solution.py:30
  9.4 6.1 %collective-permute-start.4 = (bf16[16,2432]{1,0:T(8,128)(2,1)S(1)}, bf16[16,2432]{1,0:T(8,128)(2,1)S(1)}, u32[]{:S(2)}, u32[]{:S(2)}) collective-permute-start(bf16[16,2432]{1,0:T(8,128)(2,1)S(1)} %pad_maximum_fusion), channel_id=1, source_target_pairs={{0,96},{1,97},{2,98},{3,99},{4,100},{5,101},{6,102},{7,103},{8,104... | collective-permute-start | bytes 233480 | tf_op jit(solution)/shard_map/ppermute | solution.py:30
  15.6 2.1 %collective-permute-done.4 = bf16[16,2432]{1,0:T(8,128)(2,1)S(1)} collective-permute-done((bf16[16,2432]{1,0:T(8,128)(2,1)S(1)}, bf16[16,2432]{1,0:T(8,128)(2,1)S(1)}, u32[]{:S(2)}, u32[]{:S(2)}) %collective-permute-start.4) | collective-permute-done | bytes 77856 | tf_op jit(solution)/shard_map/ppermute | solution.py:30
  17.7 4.1 %collective-permute-start.7 = (bf16[16,2432]{1,0:T(8,128)(2,1)S(1)}, bf16[16,2432]{1,0:T(8,128)(2,1)S(1)}, u32[]{:S(2)}, u32[]{:S(2)}) collective-permute-start(bf16[16,2432]{1,0:T(8,128)(2,1)S(1)} %collective-permute-done.4), channel_id=1, source_target_pairs={{0,96},{1,97},{2,98},{3,99},{4,100},{5,101},{6,102},{7,103},{8,104... | collective-permute-start | bytes 233480 | tf_op jit(solution)/shard_map/ppermute | solution.py:30
  21.8 2.7 %collective-permute-start.3 = (bf16[16,2432]{1,0:T(8,128)(2,1)S(1)}, bf16[16,2432]{1,0:T(8,128)(2,1)S(1)}, u32[]{:S(2)}, u32[]{:S(2)}) collective-permute-start(bf16[16,2432]{1,0:T(8,128)(2,1)S(1)} %pad_maximum_fusion), channel_id=1, source_target_pairs={{0,112},{1,113},{2,114},{3,115},{4,116},{5,117},{6,118},{7,119},{8... | collective-permute-start | bytes 233480 | tf_op jit(solution)/shard_map/ppermute | solution.py:30
  24.5 1.5 %collective-permute-start.14 = (bf16[512,1024]{1,0:T(8,128)(2,1)}, bf16[512,1024]{1,0:T(8,128)(2,1)S(1)}, u32[]{:S(2)}, u32[]{:S(2)}) collective-permute-start(bf16[512,1024]{1,0:T(8,128)(2,1)} %param.6), channel_id=1, source_target_pairs={{0,128},{1,129},{2,130},{3,131},{4,132},{5,133},{6,134},{7,135},{8... | collective-permute-start | bytes 3145736 | tf_op jit(solution)/shard_map/ppermute | solution.py:30
  26.0 1.5 %collective-permute-start.9 = (bf16[16,2432]{1,0:T(8,128)(2,1)S(1)}, bf16[16,2432]{1,0:T(8,128)(2,1)S(1)}, u32[]{:S(2)}, u32[]{:S(2)}) collective-permute-start(bf16[16,2432]{1,0:T(8,128)(2,1)S(1)} %collective-permute-done.8), channel_id=1, source_target_pairs={{0,16},{1,17},{2,18},{3,19},{4,20},{5,21},{6,22},{7,23},{8,24},{9,... | collective-permute-start | bytes 233480 | tf_op jit(solution)/shard_map/ppermute | solution.py:30
  27.4 0.6 constant_dynamic-update-slice_fusion.3
  28.0 3.2 %collective-permute-done.9 = bf16[16,2432]{1,0:T(8,128)(2,1)S(1)} collective-permute-done((bf16[16,2432]{1,0:T(8,128)(2,1)S(1)}, bf16[16,2432]{1,0:T(8,128)(2,1)S(1)}, u32[]{:S(2)}, u32[]{:S(2)}) %collective-permute-start.9) | collective-permute-done | bytes 77856 | tf_op jit(solution)/shard_map/ppermute | solution.py:30
  31.2 0.6 constant_dynamic-update-slice_fusion.2
  31.8 0.6 constant_dynamic-update-slice_fusion.1
  32.5 0.6 constant_dynamic-update-slice_fusion
  33.1 2.5 %collective-permute-start.11 = (bf16[64,2432]{1,0:T(8,128)(2,1)}, bf16[64,2432]{1,0:T(8,128)(2,1)}, u32[]{:S(2)}, u32[]{:S(2)}) collective-permute-start(bf16[64,2432]{1,0:T(8,128)(2,1)} %constant_dynamic-update-slice_fusion), channel_id=1, source_target_pairs={{0,12},{1,13},{2,14},{3,15},{4,0},{5,1},{6,2},{7,3},{8,4},{9,5},{1... | collective-permute-start | bytes 933896 | tf_op jit(solution)/shard_map/ppermute | solution.py:30
  35.6 3.2 %concatenate.23 = bf16[64,2432]{1,0:T(8,128)(2,1)} concatenate(bf16[4,2432]{1,0:T(4,128)(2,1)S(1)} %get-tuple-element.28, bf16[4,2432]{1,0:T(4,128)(2,1)S(1)} %collective-permute-done, bf16[4,2432]{1,0:T(4,128)(2,1)S(1)} %collective-permute-done.1, bf16[4,2432]{1,0:T(4,128)(2,1)S(1)} %collective-permute-done.2, bf16[16,2432]{1,0:T(8,128)(2,1)S(1)} %collective-permute-done.3, ...), dimensions={0} | concatenate | bytes 622592 | tf_op jit(solution)/shard_map/concatenate | solution.py:128
  38.8 4.6 %fusion.3 = f32[1024,1024]{0,1:T(8,128)} fusion(bf16[512,1024]{1,0:T(8,128)(2,1)} %param.6, s32[1024]{0:T(1024)S(1)} %fusion.24, pred[1024]{0:T(1024)(128)(4,1)S(1)} %fusion.33), kind=kOutput, calls=%fused_computation.5 | convolution fusion | flops 1074790400 | bytes 5248000 | tf_op jit(solution)/shard_map/dot_general | solution.py:132
  43.6 5.4 %collective-permute-start.17 = (bf16[128,2432]{1,0:T(8,128)(2,1)S(1)}, bf16[128,2432]{1,0:T(8,128)(2,1)S(1)}, u32[]{:S(2)}, u32[]{:S(2)}) collective-permute-start(bf16[128,2432]{1,0:T(8,128)(2,1)S(1)} %concatenate.25.refs_0_), channel_id=1, source_target_pairs={{0,1},{1,0},{2,3},{3,2},{4,5},{5,4},{6,7},{7,6},{8,9},{9,8},{10,11... | collective-permute-start | bytes 1867784 | tf_op jit(solution)/shard_map/ppermute | solution.py:30
  49.5 2.6 %collective-permute-start.6 = (bf16[64,2432]{1,0:T(8,128)(2,1)}, bf16[64,2432]{1,0:T(8,128)(2,1)}, u32[]{:S(2)}, u32[]{:S(2)}) collective-permute-start(bf16[64,2432]{1,0:T(8,128)(2,1)} %concatenate.23), channel_id=1, source_target_pairs={{0,12},{1,13},{2,14},{3,15},{4,0},{5,1},{6,2},{7,3},{8,4},{9,5},{1... | collective-permute-start | bytes 933896 | tf_op jit(solution)/shard_map/ppermute | solution.py:30
  52.0 1.4 %collective-permute-start.16 = (bf16[64,2432]{1,0:T(8,128)(2,1)}, bf16[64,2432]{1,0:T(8,128)(2,1)}, u32[]{:S(2)}, u32[]{:S(2)}) collective-permute-start(bf16[64,2432]{1,0:T(8,128)(2,1)} %collective-permute-done.11.refs_3_), channel_id=1, source_target_pairs={{0,12},{1,13},{2,14},{3,15},{4,0},{5,1},{6,2},{7,3},{8,4},{9,5},{1... | collective-permute-start | bytes 933896 | tf_op jit(solution)/shard_map/ppermute | solution.py:30
  53.4 1.0 %copy-done = bf16[512,1024]{1,0:T(8,128)(2,1)} copy-done((bf16[512,1024]{1,0:T(8,128)(2,1)}, bf16[512,1024]{1,0:T(8,128)(2,1)S(1)}, u32[]{:S(2)}) %copy-start) | copy-done | bytes 1048600
  54.5 3.9 %fusion.logit_ref = bf16[1024,1024]{1,0:T(8,128)(2,1)S(1)} fusion(f32[1024,1024]{0,1:T(8,128)} %fusion.3, bf16[512,1024]{1,0:T(8,128)(2,1)} %copy-done, s32[1024]{0:T(1024)S(1)} %fusion.24, pred[1024]{0:T(1024)(128)(4,1)S(1)} %fusion.41), kind=kOutput, calls=%fused_computation.1 | convolution fusion | flops 1076887552 | bytes 7345152 | tf_op jit(solution)/shard_map/dot_general | solution.py:133
  58.4 1.4 %collective-permute-done.13.refs_5_ = bf16[64,2432]{1,0:T(8,128)(2,1)} collective-permute-done((bf16[64,2432]{1,0:T(8,128)(2,1)}, bf16[64,2432]{1,0:T(8,128)(2,1)}, u32[]{:S(2)}, u32[]{:S(2)}) %collective-permute-start.13) | collective-permute-done | bytes 311328 | tf_op jit(solution)/shard_map/ppermute | solution.py:30
  59.8 1.2 %collective-permute-start.20 = (bf16[64,2432]{1,0:T(8,128)(2,1)}, bf16[64,2432]{1,0:T(8,128)(2,1)}, u32[]{:S(2)}, u32[]{:S(2)}) collective-permute-start(bf16[64,2432]{1,0:T(8,128)(2,1)} %collective-permute-done.6.refs_2_), channel_id=1, source_target_pairs={{0,1},{1,0},{2,3},{3,2},{4,5},{5,4},{6,7},{7,6},{8,9},{9,8},{10,11... | collective-permute-start | bytes 933896 | tf_op jit(solution)/shard_map/ppermute | solution.py:30
  60.9 4.5 %collective-permute-done.16.refs_1_ = bf16[64,2432]{1,0:T(8,128)(2,1)} collective-permute-done((bf16[64,2432]{1,0:T(8,128)(2,1)}, bf16[64,2432]{1,0:T(8,128)(2,1)}, u32[]{:S(2)}, u32[]{:S(2)}) %collective-permute-start.16) | collective-permute-done | bytes 311328 | tf_op jit(solution)/shard_map/ppermute | solution.py:30
  65.5 1.1 %collective-permute-start.22 = (bf16[64,2432]{1,0:T(8,128)(2,1)}, bf16[64,2432]{1,0:T(8,128)(2,1)S(1)}, u32[]{:S(2)}, u32[]{:S(2)}) collective-permute-start(bf16[64,2432]{1,0:T(8,128)(2,1)} %collective-permute-done.12.refs_4_), channel_id=1, source_target_pairs={{0,1},{1,0},{2,3},{3,2},{4,5},{5,4},{6,7},{7,6},{8,9},{9,8},{10,11... | collective-permute-start | bytes 933896 | tf_op jit(solution)/shard_map/ppermute | solution.py:30
  66.6 4.3 %shard_map.46.refs_4_ = f32[1024,1152]{1,0:T(8,128)S(1)} custom-call(s32[1]{0:T(128)} %bitcast.offset_ref, bf16[1024,1024]{1,0:T(8,128)(2,1)S(1)} %fusion.logit_ref, bf16[128,2432]{1,0:T(8,128)(2,1)S(1)} %concatenate.25.refs_0_, bf16[128,2432]{1,0:T(8,128)(2,1)S(1)} %collective-permute-done.17.refs_1_, bf16[64,2432]{1,0:T(8,128)(2,1)} %collective-permute-done.6.refs_2_, ...), custom_call_target="tpu_custom_call" | custom-call | flops 2415919104 | bytes 8388608 | tf_op jit(solution)/shard_map/pallas_call | solution.py:97
  71.6 2.7 %shard_map.47.refs_4_ = f32[1024,1152]{1,0:T(8,128)S(1)} custom-call(s32[1]{0:T(128)} %bitcast.offset_ref, bf16[1024,1024]{1,0:T(8,128)(2,1)S(1)} %fusion.logit_ref, bf16[64,2432]{1,0:T(8,128)(2,1)} %collective-permute-done.20.refs_0_, bf16[64,2432]{1,0:T(8,128)(2,1)S(1)} %collective-permute-done.21.refs_1_, ...), custom_call_target="tpu_custom_call" | custom-call | flops 1207959552 | bytes 8388608 | tf_op jit(solution)/shard_map/pallas_call | solution.py:97
  74.3 4.3 %shard_map.48 = f32[1024,1152]{1,0:T(8,128)} custom-call(s32[1]{0:T(128)} %bitcast.offset_ref, bf16[1024,1024]{1,0:T(8,128)(2,1)S(1)} %fusion.logit_ref, bf16[64,2432]{1,0:T(8,128)(2,1)} %collective-permute-done.15.refs_0_, bf16[64,2432]{1,0:T(8,128)(2,1)} %collective-permute-done.16.refs_1_, bf16[64,2432]{1,0:T(8,128)(2,1)S(1)} %collective-permute-done.18.refs_2_, ...), custom_call_target="tpu_custom_call" | custom-call | flops 1207959552 | bytes 8388608 | tf_op jit(solution)/shard_map/pallas_call | solution.py:97
  (39 shorter events, 1.8 us)
Async XLA Ops:
  1.6 4.9 %collective-permute-start.2 = (bf16[4,2432]{1,0:T(4,128)(2,1)S(1)}, bf16[4,2432]{1,0:T(4,128)(2,1)S(1)}, u32[]{:S(2)}, u32[]{:S(2)}) collective-permute-start(bf16[4,2432]{1,0:T(4,128)(2,1)S(1)} %get-tuple-element.27), channel_id=1, source_target_pairs={{0,130},{1,131},{2,128},{3,129},{4,134},{5,135},{6,132},{7,133},{8... | collective-permute-start | bytes 58376 | tf_op jit(solution)/shard_map/ppermute | solution.py:30
  5.2 2.6 %collective-permute-start = (bf16[4,2432]{1,0:T(4,128)(2,1)S(1)}, bf16[4,2432]{1,0:T(4,128)(2,1)S(1)}, u32[]{:S(2)}, u32[]{:S(2)}) collective-permute-start(bf16[4,2432]{1,0:T(4,128)(2,1)S(1)} %get-tuple-element.27), channel_id=1, source_target_pairs={{0,128},{1,129},{2,130},{3,131},{4,132},{5,133},{6,134},{7,135},{8... | collective-permute-start | bytes 58376 | tf_op jit(solution)/shard_map/ppermute | solution.py:30
  5.2 4.2 %collective-permute-start.1 = (bf16[4,2432]{1,0:T(4,128)(2,1)S(1)}, bf16[4,2432]{1,0:T(4,128)(2,1)S(1)}, u32[]{:S(2)}, u32[]{:S(2)}) collective-permute-start(bf16[4,2432]{1,0:T(4,128)(2,1)S(1)} %get-tuple-element.28), channel_id=1, source_target_pairs={{0,2},{1,3},{2,0},{3,1},{4,6},{5,7},{6,4},{7,5},{8,10},{9,11},{10,... | collective-permute-start | bytes 58376 | tf_op jit(solution)/shard_map/ppermute | solution.py:30
  9.4 8.2 %collective-permute-start.4 = (bf16[16,2432]{1,0:T(8,128)(2,1)S(1)}, bf16[16,2432]{1,0:T(8,128)(2,1)S(1)}, u32[]{:S(2)}, u32[]{:S(2)}) collective-permute-start(bf16[16,2432]{1,0:T(8,128)(2,1)S(1)} %pad_maximum_fusion), channel_id=1, source_target_pairs={{0,96},{1,97},{2,98},{3,99},{4,100},{5,101},{6,102},{7,103},{8,104... | collective-permute-start | bytes 233480 | tf_op jit(solution)/shard_map/ppermute | solution.py:30
  15.5 10.4 %collective-permute-start.8 = (bf16[16,2432]{1,0:T(8,128)(2,1)S(1)}, bf16[16,2432]{1,0:T(8,128)(2,1)S(1)}, u32[]{:S(2)}, u32[]{:S(2)}) collective-permute-start(bf16[16,2432]{1,0:T(8,128)(2,1)S(1)} %pad_maximum_fusion), channel_id=1, source_target_pairs={{0,32},{1,33},{2,34},{3,35},{4,36},{5,37},{6,38},{7,39},{8,40},{9,... | collective-permute-start | bytes 233480 | tf_op jit(solution)/shard_map/ppermute | solution.py:30
  17.7 8.3 %collective-permute-start.7 = (bf16[16,2432]{1,0:T(8,128)(2,1)S(1)}, bf16[16,2432]{1,0:T(8,128)(2,1)S(1)}, u32[]{:S(2)}, u32[]{:S(2)}) collective-permute-start(bf16[16,2432]{1,0:T(8,128)(2,1)S(1)} %collective-permute-done.4), channel_id=1, source_target_pairs={{0,96},{1,97},{2,98},{3,99},{4,100},{5,101},{6,102},{7,103},{8,104... | collective-permute-start | bytes 233480 | tf_op jit(solution)/shard_map/ppermute | solution.py:30
  21.8 10.7 %collective-permute-start.10 = (bf16[16,2432]{1,0:T(8,128)(2,1)S(1)}, bf16[16,2432]{1,0:T(8,128)(2,1)S(1)}, u32[]{:S(2)}, u32[]{:S(2)}) collective-permute-start(bf16[16,2432]{1,0:T(8,128)(2,1)S(1)} %pad_maximum_fusion), channel_id=1, source_target_pairs={{0,16},{1,17},{2,18},{3,19},{4,20},{5,21},{6,22},{7,23},{8,24},{9,... | collective-permute-start | bytes 233480 | tf_op jit(solution)/shard_map/ppermute | solution.py:30
  21.8 13.8 %collective-permute-start.3 = (bf16[16,2432]{1,0:T(8,128)(2,1)S(1)}, bf16[16,2432]{1,0:T(8,128)(2,1)S(1)}, u32[]{:S(2)}, u32[]{:S(2)}) collective-permute-start(bf16[16,2432]{1,0:T(8,128)(2,1)S(1)} %pad_maximum_fusion), channel_id=1, source_target_pairs={{0,112},{1,113},{2,114},{3,115},{4,116},{5,117},{6,118},{7,119},{8... | collective-permute-start | bytes 233480 | tf_op jit(solution)/shard_map/ppermute | solution.py:30
  24.5 28.9 %collective-permute-start.14 = (bf16[512,1024]{1,0:T(8,128)(2,1)}, bf16[512,1024]{1,0:T(8,128)(2,1)S(1)}, u32[]{:S(2)}, u32[]{:S(2)}) collective-permute-start(bf16[512,1024]{1,0:T(8,128)(2,1)} %param.6), channel_id=1, source_target_pairs={{0,128},{1,129},{2,130},{3,131},{4,132},{5,133},{6,134},{7,135},{8... | collective-permute-start | bytes 3145736 | tf_op jit(solution)/shard_map/ppermute | solution.py:30
  25.9 9.7 %collective-permute-start.5 = (bf16[16,2432]{1,0:T(8,128)(2,1)S(1)}, bf16[16,2432]{1,0:T(8,128)(2,1)S(1)}, u32[]{:S(2)}, u32[]{:S(2)}) collective-permute-start(bf16[16,2432]{1,0:T(8,128)(2,1)S(1)} %collective-permute-done.4), channel_id=1, source_target_pairs={{0,112},{1,113},{2,114},{3,115},{4,116},{5,117},{6,118},{7,119},{8... | collective-permute-start | bytes 233480 | tf_op jit(solution)/shard_map/ppermute | solution.py:30
  26.0 5.3 %collective-permute-start.9 = (bf16[16,2432]{1,0:T(8,128)(2,1)S(1)}, bf16[16,2432]{1,0:T(8,128)(2,1)S(1)}, u32[]{:S(2)}, u32[]{:S(2)}) collective-permute-start(bf16[16,2432]{1,0:T(8,128)(2,1)S(1)} %collective-permute-done.8), channel_id=1, source_target_pairs={{0,16},{1,17},{2,18},{3,19},{4,20},{5,21},{6,22},{7,23},{8,24},{9,... | collective-permute-start | bytes 233480 | tf_op jit(solution)/shard_map/ppermute | solution.py:30
  33.1 16.3 %collective-permute-start.11 = (bf16[64,2432]{1,0:T(8,128)(2,1)}, bf16[64,2432]{1,0:T(8,128)(2,1)}, u32[]{:S(2)}, u32[]{:S(2)}) collective-permute-start(bf16[64,2432]{1,0:T(8,128)(2,1)} %constant_dynamic-update-slice_fusion), channel_id=1, source_target_pairs={{0,12},{1,13},{2,14},{3,15},{4,0},{5,1},{6,2},{7,3},{8,4},{9,5},{1... | collective-permute-start | bytes 933896 | tf_op jit(solution)/shard_map/ppermute | solution.py:30
  38.8 13.2 %collective-permute-start.12 = (bf16[64,2432]{1,0:T(8,128)(2,1)}, bf16[64,2432]{1,0:T(8,128)(2,1)}, u32[]{:S(2)}, u32[]{:S(2)}) collective-permute-start(bf16[64,2432]{1,0:T(8,128)(2,1)} %concatenate.23), channel_id=1, source_target_pairs={{0,4},{1,5},{2,6},{3,7},{4,8},{5,9},{6,10},{7,11},{8,12},{9,13},{1... | collective-permute-start | bytes 933896 | tf_op jit(solution)/shard_map/ppermute | solution.py:30
  43.6 23.0 %collective-permute-start.17 = (bf16[128,2432]{1,0:T(8,128)(2,1)S(1)}, bf16[128,2432]{1,0:T(8,128)(2,1)S(1)}, u32[]{:S(2)}, u32[]{:S(2)}) collective-permute-start(bf16[128,2432]{1,0:T(8,128)(2,1)S(1)} %concatenate.25.refs_0_), channel_id=1, source_target_pairs={{0,1},{1,0},{2,3},{3,2},{4,5},{5,4},{6,7},{7,6},{8,9},{9,8},{10,11... | collective-permute-start | bytes 1867784 | tf_op jit(solution)/shard_map/ppermute | solution.py:30
  49.0 10.8 %collective-permute-start.13 = (bf16[64,2432]{1,0:T(8,128)(2,1)}, bf16[64,2432]{1,0:T(8,128)(2,1)}, u32[]{:S(2)}, u32[]{:S(2)}) collective-permute-start(bf16[64,2432]{1,0:T(8,128)(2,1)} %constant_dynamic-update-slice_fusion), channel_id=1, source_target_pairs={{0,4},{1,5},{2,6},{3,7},{4,8},{5,9},{6,10},{7,11},{8,12},{9,13},{1... | collective-permute-start | bytes 933896 | tf_op jit(solution)/shard_map/ppermute | solution.py:30
  49.5 10.3 %collective-permute-start.6 = (bf16[64,2432]{1,0:T(8,128)(2,1)}, bf16[64,2432]{1,0:T(8,128)(2,1)}, u32[]{:S(2)}, u32[]{:S(2)}) collective-permute-start(bf16[64,2432]{1,0:T(8,128)(2,1)} %concatenate.23), channel_id=1, source_target_pairs={{0,12},{1,13},{2,14},{3,15},{4,0},{5,1},{6,2},{7,3},{8,4},{9,5},{1... | collective-permute-start | bytes 933896 | tf_op jit(solution)/shard_map/ppermute | solution.py:30
  52.0 13.5 %collective-permute-start.16 = (bf16[64,2432]{1,0:T(8,128)(2,1)}, bf16[64,2432]{1,0:T(8,128)(2,1)}, u32[]{:S(2)}, u32[]{:S(2)}) collective-permute-start(bf16[64,2432]{1,0:T(8,128)(2,1)} %collective-permute-done.11.refs_3_), channel_id=1, source_target_pairs={{0,12},{1,13},{2,14},{3,15},{4,0},{5,1},{6,2},{7,3},{8,4},{9,5},{1... | collective-permute-start | bytes 933896 | tf_op jit(solution)/shard_map/ppermute | solution.py:30
  53.4 1.0 %copy-start = (bf16[512,1024]{1,0:T(8,128)(2,1)}, bf16[512,1024]{1,0:T(8,128)(2,1)S(1)}, u32[]{:S(2)}) copy-start(bf16[512,1024]{1,0:T(8,128)(2,1)S(1)} %collective-permute-done.14) | copy-start | bytes 3145732
  54.4 16.4 %collective-permute-start.15 = (bf16[64,2432]{1,0:T(8,128)(2,1)}, bf16[64,2432]{1,0:T(8,128)(2,1)}, u32[]{:S(2)}, u32[]{:S(2)}) collective-permute-start(bf16[64,2432]{1,0:T(8,128)(2,1)} %collective-permute-done.12.refs_4_), channel_id=1, source_target_pairs={{0,4},{1,5},{2,6},{3,7},{4,8},{5,9},{6,10},{7,11},{8,12},{9,13},{1... | collective-permute-start | bytes 933896 | tf_op jit(solution)/shard_map/ppermute | solution.py:30
  59.8 11.7 %collective-permute-start.20 = (bf16[64,2432]{1,0:T(8,128)(2,1)}, bf16[64,2432]{1,0:T(8,128)(2,1)}, u32[]{:S(2)}, u32[]{:S(2)}) collective-permute-start(bf16[64,2432]{1,0:T(8,128)(2,1)} %collective-permute-done.6.refs_2_), channel_id=1, source_target_pairs={{0,1},{1,0},{2,3},{3,2},{4,5},{5,4},{6,7},{7,6},{8,9},{9,8},{10,11... | collective-permute-start | bytes 933896 | tf_op jit(solution)/shard_map/ppermute | solution.py:30
  60.9 10.6 %collective-permute-start.21 = (bf16[64,2432]{1,0:T(8,128)(2,1)}, bf16[64,2432]{1,0:T(8,128)(2,1)S(1)}, u32[]{:S(2)}, u32[]{:S(2)}) collective-permute-start(bf16[64,2432]{1,0:T(8,128)(2,1)} %collective-permute-done.11.refs_3_), channel_id=1, source_target_pairs={{0,1},{1,0},{2,3},{3,2},{4,5},{5,4},{6,7},{7,6},{8,9},{9,8},{10,11... | collective-permute-start | bytes 933896 | tf_op jit(solution)/shard_map/ppermute | solution.py:30
  65.5 6.1 %collective-permute-start.22 = (bf16[64,2432]{1,0:T(8,128)(2,1)}, bf16[64,2432]{1,0:T(8,128)(2,1)S(1)}, u32[]{:S(2)}, u32[]{:S(2)}) collective-permute-start(bf16[64,2432]{1,0:T(8,128)(2,1)} %collective-permute-done.12.refs_4_), channel_id=1, source_target_pairs={{0,1},{1,0},{2,3},{3,2},{4,5},{5,4},{6,7},{7,6},{8,9},{9,8},{10,11... | collective-permute-start | bytes 933896 | tf_op jit(solution)/shard_map/ppermute | solution.py:30
  66.6 5.0 %collective-permute-start.23 = (bf16[64,2432]{1,0:T(8,128)(2,1)}, bf16[64,2432]{1,0:T(8,128)(2,1)S(1)}, u32[]{:S(2)}, u32[]{:S(2)}) collective-permute-start(bf16[64,2432]{1,0:T(8,128)(2,1)} %collective-permute-done.13.refs_5_), channel_id=1, source_target_pairs={{0,1},{1,0},{2,3},{3,2},{4,5},{5,4},{6,7},{7,6},{8,9},{9,8},{10,11... | collective-permute-start | bytes 933896 | tf_op jit(solution)/shard_map/ppermute | solution.py:30
  70.9 3.4 %collective-permute-start.18 = (bf16[64,2432]{1,0:T(8,128)(2,1)}, bf16[64,2432]{1,0:T(8,128)(2,1)S(1)}, u32[]{:S(2)}, u32[]{:S(2)}) collective-permute-start(bf16[64,2432]{1,0:T(8,128)(2,1)} %collective-permute-done.15.refs_0_), channel_id=1, source_target_pairs={{0,1},{1,0},{2,3},{3,2},{4,5},{5,4},{6,7},{7,6},{8,9},{9,8},{10,11... | collective-permute-start | bytes 933896 | tf_op jit(solution)/shard_map/ppermute | solution.py:30
  71.5 2.8 %collective-permute-start.19 = (bf16[64,2432]{1,0:T(8,128)(2,1)}, bf16[64,2432]{1,0:T(8,128)(2,1)S(1)}, u32[]{:S(2)}, u32[]{:S(2)}) collective-permute-start(bf16[64,2432]{1,0:T(8,128)(2,1)} %collective-permute-done.16.refs_1_), channel_id=1, source_target_pairs={{0,1},{1,0},{2,3},{3,2},{4,5},{5,4},{6,7},{7,6},{8,9},{9,8},{10,11... | collective-permute-start | bytes 933896 | tf_op jit(solution)/shard_map/ppermute | solution.py:30

commit v4 on v3

--- a/solution.py
+++ b/solution.py
@@ -26,32 +26,42 @@
     for dp in range(DP):
         for vocab in range(Z * X * 4):
             z, x, yh, core = coords(vocab)
-            pairs.append((flat(dp, z, x, yh, core), flat(dp ^ fd, z + dz, x + dx, yh ^ fy, core ^ fc)))
+            way = 1 - 2 * core
+            pairs.append((flat(dp, z, x, yh, core), flat(dp ^ fd, z + way * dz, x + way * dx, yh ^ fy, core ^ fc)))
     return lax.ppermute(value, ("dp", "vocab"), pairs)
 
 
 def gather_column(own, other):
+    from_dy = move(other, fd=1, fy=1)
     from_dp = move(other, fd=1)
-    from_dy = move(other, fd=1, fy=1)
     from_yh = move(own, fy=1)
     chunk = jnp.concatenate([own, from_dp, from_yh, from_dy], axis=0)
-    p2, m2 = move(chunk, dz=2), move(chunk, dz=-2)
-    p1, m1 = move(chunk, dz=1), move(chunk, dz=-1)
-    p3, m3, m4 = move(p2, dz=1), move(m2, dz=-1), move(m2, dz=-2)
-    return [chunk, m1, m2, m3], [m4, p3, p2, p1], from_yh
+    both = jnp.concatenate([chunk, move(chunk, fc=1)], axis=0)
+    two, one = move(both, dz=2), move(both, dz=1)
+    three, four = move(two, dz=1), move(two[:16], dz=2)
+    return jnp.concatenate([chunk, one, two, three, four], axis=0), from_yh
+
+
+STEPS = (0, 0, 1, 1, 2, -1, -1, 2)
+SWAPPED = (0, 1, 0, 1, 0, 1, 0, 1)
 
 
 def arrangement(dp, vocab):
     z, x, yh, core = coords(vocab)
     place = lax.broadcasted_iota(jnp.int32, (1, 2 * Z * X * YH * CORE * ROWS), 1)
-    j, r, zi = place % 4, (place // 4) % 4, (place // 16) % Z
-    xi, ci = (place // (16 * Z)) % X, place // (16 * Z * X)
-    token = ((((z + zi) % Z) * X + (x + xi) % X) * 2 + (yh ^ (r // 2))) * 2 + (core ^ ci)
-    token = token * ROWS + j
-    spot = lax.broadcasted_iota(jnp.int32, (Z * X * YH * CORE * ROWS, 1), 0)
-    hit = spot == token
-    near = r % 2 == 0
-    return (hit & near).astype(jnp.bfloat16), (hit & ~near).astype(jnp.bfloat16)
+    j, r, part, column = place % 4, (place // 4) % 4, (place // 16) % Z, place // (16 * Z)
+    steps, swapped = jnp.zeros_like(place), jnp.zeros_like(place)
+    for k in range(len(STEPS)):
+        steps = jnp.where(column == k, STEPS[k], steps)
+        swapped = jnp.where(column == k, SWAPPED[k], swapped)
+    way = 1 - 2 * core
+    from_x = (x - way * steps + 2 * X) % X
+    holder = core ^ swapped
+    back = (part + 1) // 2
+    from_z = (z - (1 - 2 * holder) * back + 2 * Z) % Z
+    from_core = holder ^ jnp.where((part % 2 == 0) & (part > 0), 1, 0)
+    token = ((from_z * X + from_x) * 2 + (yh ^ (r // 2))) * 2 + from_core
+    return token * ROWS + j, r % 2
 
 
 def contract_kernel(spots, pieces, columns, added, last, offset_ref, logit_ref, *refs):
@@ -120,27 +130,25 @@
         pick = [lax.dynamic_slice_in_dim(a, side * columns, columns, 1) for a in (hidden, embed_grad)]
         return jnp.concatenate(pick + [code], axis=1)
 
-    near, far = arrangement(dp, vocab)
     dims = (((0,), (0,)), ((), ()))
-    low, high, early = gather_column(payload(dp), payload(1 - dp))
+    token, away = arrangement(dp, vocab)
+    own, other, offset, token = lax.optimization_barrier((payload(dp), payload(1 - dp), offset, token))
+    spot = lax.broadcasted_iota(jnp.int32, (logit_grad.shape[0], 1), 0)
+    near, far = (((spot == token) & (away == side)).astype(jnp.bfloat16) for side in (0, 1))
+    column, early = gather_column(own, other)
     held, _ = lax.optimization_barrier((logit_grad, early))
     partner = move(held, fd=1)
-    low, high, column = (jnp.concatenate(part, axis=0) for part in (low, high, low + high))
-    down_low, up_high = move(low, dx=1), move(high, dx=-1)
-    down_high, up_low = move(high, dx=1), move(low, dx=-1)
-    across = [move(down_low, dx=1), move(up_high, dx=-1)]
+    swapped = move(column, fc=1)
+    direct = [move(column, dx=1), move(swapped, dx=1)]
     turned = lax.dot_general(logit_grad, near, dims, preferred_element_type=jnp.float32)
     turned = turned + lax.dot_general(partner, far, dims, preferred_element_type=jnp.float32)
     turned = turned.astype(jnp.bfloat16)
-    around = [up_low, up_high, down_low, down_high]
-    *around, turned = lax.optimization_barrier((*around, turned))
-    first = [column, move(column, fc=1)] + around
-    partial = contract(offset, turned, first, (0, 4, 1, 3), columns)
-    *across, partial = lax.optimization_barrier((*across, partial))
-    second = [move(part, fc=1) for part in around]
-    partial = contract(offset, turned, second, (5, 7), columns, partial)
-    third = across + [move(part, fc=1) for part in across]
-    return contract(offset, turned, third, (2, 6), columns, partial, last=True)
+    direct[0], turned = lax.optimization_barrier((direct[0], turned))
+    passed = move(direct[0], dx=1)
+    partial = contract(offset, turned, [column, swapped] + direct, (0, 1, 2, 3), columns)
+    passed, partial = lax.optimization_barrier((passed, partial))
+    partial = contract(offset, turned, [move(part, fc=1) for part in direct], (5, 6), columns, partial)
+    return contract(offset, turned, [passed, move(passed, fc=1)], (4, 7), columns, partial, last=True)
 
 
 def solution(mesh):

time: 79 us -> 63.8 us (0.81)
  local copies, waits for them, and re-layouts: 7.74 us -> 1.24 us
  matrix products: 8.45 us -> 4.02 us
  starting transfers between devices: 36.1 us -> 32.4 us
  Pallas kernels: 11.2 us -> 7.96 us
  waiting for transfers between devices: 14.1 us -> 16.8 us
    ppermute x24 -> x16, starting transfers between devices: 36.1 us -> 32.4 us  [move(): return lax.ppermute(value, ('dp', 'vocab'), pairs)]
    concatenate x3 -> x2, local copies, waits for them, and re-layouts: 4.06 us -> 0.46 us  [the longest x1 0.36 us: gather_column(): return (jnp.concatenate([chunk, one, two, three, four], axis=0), from_yh)]
    pallas_call x3, Pallas kernels: 11.2 us -> 7.96 us  [contract(): pl.pallas_call(functools.partial(contract_kernel, tuple(spots), len(chunk...]
    unnamed x5 -> x0, local copies, waits for them, and re-layouts: 2.91 us -> none
    ppermute x24 -> x16, waiting for transfers between devices: 14.1 us -> 16.8 us  [move(): return lax.ppermute(value, ('dp', 'vocab'), pairs)]
    dot_general x1, matrix products: 3.86 us -> 1.43 us  [body(): lax.dot_general(partner, far, dims, preferred_element_type=jnp.float32)]
    dot_general x1, matrix products: 4.59 us -> 2.59 us  [body(): lax.dot_general(logit_grad, near, dims, preferred_element_type=jnp.float32)]
  transfers between devices with their start and end apart: 24 -> 16, of which waited for: 6 -> 8; matrix products, arithmetic and copies ran while one was open for 18% -> 7% of each run, Pallas kernels for 9% -> 7%
where the time goes in v4:
time: 63.8 us; the launch traced here: 63.6 us
  starting transfers between devices  32.4 us (51%)
  waiting for transfers between devices  16.8 us (26%)
  Pallas kernels  7.96 us (12%)
  matrix products  4.02 us (6%)
  local copies, waits for them, and re-layouts  1.24 us (2%)
  other arithmetic  0.95 us (1%)
    ppermute x16, starting transfers between devices, move(): return lax.ppermute(value, ('dp', 'vocab'), pairs)  32.4 us
    ppermute x16, waiting for transfers between devices, move(): return lax.ppermute(value, ('dp', 'vocab'), pairs)  16.8 us
    pallas_call x3, Pallas kernels, contract(): pl.pallas_call(functools.partial(contract_kernel, tuple(spots), len(chunk...  7.96 us
    dot_general x1, matrix products, body(): lax.dot_general(logit_grad, near, dims, preferred_element_type=jnp.float32)  2.59 us
    dot_general x1, matrix products, body(): lax.dot_general(partner, far, dims, preferred_element_type=jnp.float32)  1.43 us
  transfers between devices with their start and end apart: 16, of which 8 were waited for; matrix products, arithmetic and copies ran while one was open for 7% of the time, Pallas kernels for 7%

profile of v4, /device:TPU:1, one launch (start us, length us, event | category | flops | bytes accessed | tf_op | source)
XLA Modules:
  0.0 63.6 jit_solution(227359121102113084)
XLA Ops:
  0.0 0.7 %and_select_fusion.15 = (s32[4]{0:T(128)S(1)}, s32[4]{0:T(128)S(1)}, s32[4]{0:T(128)S(1)}) fusion(s32[4]{0:T(128)} %param.4), kind=kLoop, calls=%fused_computation.100 | loop fusion | flops 160 | bytes 64 | tf_op jit(solution)/shard_map/jit(floor_divide)/jit(_where)/select_n | solution.py:126
  0.7 0.1 fusion.10
  0.8 0.8 %constant_dynamic-slice_fusion = (bf16[4,1152]{1,0:T(4,128)(2,1)S(1)}, bf16[4,1152]{1,0:T(4,128)(2,1)S(1)}, bf16[4,1152]{1,0:T(4,128)(2,1)S(1)}, bf16[4,1152]{1,0:T(4,128)(2,1)S(1)}) fusion(bf16[4,2304]{1,0:T(4,128)(2,1)} %param.7, s32[]{:T(128)S(6)} %select_n.405, s32[]{:T(128)S(6)} %select_n.397, bf16[4,2304]{1,0:T(4,128)(2,1)} %param.5), kind=kLoop, calls=%fused_computation.101 | loop fusion | bytes 73736 | tf_op jit(solution)/shard_map/dynamic_slice | solution.py:130
  1.7 3.8 %collective-permute-start.1 = (bf16[4,2432]{1,0:T(4,128)(2,1)S(1)}, bf16[4,2432]{1,0:T(4,128)(2,1)S(1)}, u32[]{:S(2)}, u32[]{:S(2)}) collective-permute-start(bf16[4,2432]{1,0:T(4,128)(2,1)S(1)} %get-tuple-element.15), channel_id=1, source_target_pairs={{0,2},{1,3},{2,0},{3,1},{4,6},{5,7},{6,4},{7,5},{8,10},{9,11},{10,... | collective-permute-start | bytes 58376 | tf_op jit(solution)/shard_map/ppermute | solution.py:31
  5.5 0.8 %collective-permute-start.2 = (bf16[4,2432]{1,0:T(4,128)(2,1)S(1)}, bf16[4,2432]{1,0:T(4,128)(2,1)S(1)}, u32[]{:S(2)}, u32[]{:S(2)}) collective-permute-start(bf16[4,2432]{1,0:T(4,128)(2,1)S(1)} %get-tuple-element.16), channel_id=1, source_target_pairs={{0,130},{1,131},{2,128},{3,129},{4,134},{5,135},{6,132},{7,133},{8... | collective-permute-start | bytes 58376 | tf_op jit(solution)/shard_map/ppermute | solution.py:31
  6.3 0.4 collective-permute-done.1
  6.7 1.3 %collective-permute-start.9 = (bf16[512,1024]{1,0:T(8,128)(2,1)}, bf16[512,1024]{1,0:T(8,128)(2,1)S(1)}, u32[]{:S(2)}, u32[]{:S(2)}) collective-permute-start(bf16[512,1024]{1,0:T(8,128)(2,1)} %param.6), channel_id=1, source_target_pairs={{0,128},{1,129},{2,130},{3,131},{4,132},{5,133},{6,134},{7,135},{8... | collective-permute-start | bytes 3145736 | tf_op jit(solution)/shard_map/ppermute | solution.py:31
  8.1 1.6 %collective-permute-done.2 = bf16[4,2432]{1,0:T(4,128)(2,1)S(1)} collective-permute-done((bf16[4,2432]{1,0:T(4,128)(2,1)S(1)}, bf16[4,2432]{1,0:T(4,128)(2,1)S(1)}, u32[]{:S(2)}, u32[]{:S(2)}) %collective-permute-start.2) | collective-permute-done | bytes 19488 | tf_op jit(solution)/shard_map/ppermute | solution.py:31
  9.7 2.0 %collective-permute-start.3 = (bf16[16,2432]{1,0:T(8,128)(2,1)S(1)}, bf16[16,2432]{1,0:T(8,128)(2,1)S(1)}, u32[]{:S(2)}, u32[]{:S(2)}) collective-permute-start(bf16[16,2432]{1,0:T(8,128)(2,1)S(1)} %pad_maximum_fusion), channel_id=1, source_target_pairs={{0,1},{1,0},{2,3},{3,2},{4,5},{5,4},{6,7},{7,6},{8,9},{9,8},{10,11... | collective-permute-start | bytes 233480 | tf_op jit(solution)/shard_map/ppermute | solution.py:31
  11.7 0.9 %collective-permute-done.3 = bf16[16,2432]{1,0:T(8,128)(2,1)S(1)} collective-permute-done((bf16[16,2432]{1,0:T(8,128)(2,1)S(1)}, bf16[16,2432]{1,0:T(8,128)(2,1)S(1)}, u32[]{:S(2)}, u32[]{:S(2)}) %collective-permute-start.3) | collective-permute-done | bytes 77856 | tf_op jit(solution)/shard_map/ppermute | solution.py:31
  12.6 0.1 concatenate.20
  12.7 6.1 %collective-permute-start.5 = (bf16[32,2432]{1,0:T(8,128)(2,1)S(1)}, bf16[32,2432]{1,0:T(8,128)(2,1)S(1)}, u32[]{:S(2)}, u32[]{:S(2)}) collective-permute-start(bf16[32,2432]{1,0:T(8,128)(2,1)S(1)} %concatenate.20), channel_id=1, source_target_pairs={{0,32},{1,97},{2,34},{3,99},{4,36},{5,101},{6,38},{7,103},{8,40},{... | collective-permute-start | bytes 466952 | tf_op jit(solution)/shard_map/ppermute | solution.py:31
  18.8 0.7 %collective-permute-start.4 = (bf16[32,2432]{1,0:T(8,128)(2,1)S(1)}, bf16[32,2432]{1,0:T(8,128)(2,1)S(1)}, u32[]{:S(2)}, u32[]{:S(2)}) collective-permute-start(bf16[32,2432]{1,0:T(8,128)(2,1)S(1)} %concatenate.20), channel_id=1, source_target_pairs={{0,16},{1,113},{2,18},{3,115},{4,20},{5,117},{6,22},{7,119},{8,24}... | collective-permute-start | bytes 466952 | tf_op jit(solution)/shard_map/ppermute | solution.py:31
  19.5 3.1 %collective-permute-done.5 = bf16[32,2432]{1,0:T(8,128)(2,1)S(1)} collective-permute-done((bf16[32,2432]{1,0:T(8,128)(2,1)S(1)}, bf16[32,2432]{1,0:T(8,128)(2,1)S(1)}, u32[]{:S(2)}, u32[]{:S(2)}) %collective-permute-start.5) | collective-permute-done | bytes 155680 | tf_op jit(solution)/shard_map/ppermute | solution.py:31
  22.6 2.0 %collective-permute-start.6 = (bf16[32,2432]{1,0:T(8,128)(2,1)S(1)}, bf16[32,2432]{1,0:T(8,128)(2,1)S(1)}, u32[]{:S(2)}, u32[]{:S(2)}) collective-permute-start(bf16[32,2432]{1,0:T(8,128)(2,1)S(1)} %collective-permute-done.5), channel_id=1, source_target_pairs={{0,16},{1,113},{2,18},{3,115},{4,20},{5,117},{6,22},{7,119},{8,24}... | collective-permute-start | bytes 466952 | tf_op jit(solution)/shard_map/ppermute | solution.py:31
  24.7 2.1 %collective-permute-start.7 = (bf16[16,2432]{1,0:T(8,128)(2,1)S(1)}, bf16[16,2432]{1,0:T(8,128)(2,1)S(1)}, u32[]{:S(2)}, u32[]{:S(2)}) collective-permute-start(bf16[16,2432]{1,0:T(8,128)(2,1)S(1)} %slice.4), channel_id=1, source_target_pairs={{0,32},{1,97},{2,34},{3,99},{4,36},{5,101},{6,38},{7,103},{8,40},{... | collective-permute-start | bytes 233480 | tf_op jit(solution)/shard_map/ppermute | solution.py:31
  26.8 2.9 %collective-permute-done.7 = bf16[16,2432]{1,0:T(8,128)(2,1)S(1)} collective-permute-done((bf16[16,2432]{1,0:T(8,128)(2,1)S(1)}, bf16[16,2432]{1,0:T(8,128)(2,1)S(1)}, u32[]{:S(2)}, u32[]{:S(2)}) %collective-permute-start.7) | collective-permute-done | bytes 77856 | tf_op jit(solution)/shard_map/ppermute | solution.py:31
  29.7 0.4 concatenate.21.refs_0_
  30.1 3.5 %collective-permute-start.11 = (bf16[128,2432]{1,0:T(8,128)(2,1)S(1)}, bf16[128,2432]{1,0:T(8,128)(2,1)S(1)}, u32[]{:S(2)}, u32[]{:S(2)}) collective-permute-start(bf16[128,2432]{1,0:T(8,128)(2,1)S(1)} %concatenate.21.refs_0_), channel_id=1, source_target_pairs={{0,1},{1,0},{2,3},{3,2},{4,5},{5,4},{6,7},{7,6},{8,9},{9,8},{10,11... | collective-permute-start | bytes 1867784 | tf_op jit(solution)/shard_map/ppermute | solution.py:31
  33.6 2.5 %collective-permute-start.8 = (bf16[128,2432]{1,0:T(8,128)(2,1)S(1)}, bf16[128,2432]{1,0:T(8,128)(2,1)S(1)}, u32[]{:S(2)}, u32[]{:S(2)}) collective-permute-start(bf16[128,2432]{1,0:T(8,128)(2,1)S(1)} %concatenate.21.refs_0_), channel_id=1, source_target_pairs={{0,4},{1,13},{2,6},{3,15},{4,8},{5,1},{6,10},{7,3},{8,12},{9,5},{1... | collective-permute-start | bytes 1867784 | tf_op jit(solution)/shard_map/ppermute | solution.py:31
  36.1 2.6 %fusion.3 = f32[1024,1024]{0,1:T(8,128)S(1)} fusion(bf16[512,1024]{1,0:T(8,128)(2,1)} %param.6, s32[1024]{0:T(1024)S(1)} %bitcast.8, pred[1024]{0:T(1024)(128)(4,1)S(1)} %broadcast_compare_fusion), kind=kOutput, calls=%fused_computation.5 | convolution fusion | flops 1074790400 | bytes 5248000 | tf_op jit(solution)/shard_map/dot_general | solution.py:143
  38.7 0.6 collective-permute-start.12
  39.3 1.4 %fusion.logit_ref = bf16[1024,1024]{1,0:T(8,128)(2,1)S(1)} fusion(f32[1024,1024]{0,1:T(8,128)S(1)} %fusion.3, bf16[512,1024]{1,0:T(8,128)(2,1)S(1)} %collective-permute-done.9, s32[1024]{0:T(1024)S(1)} %bitcast.9, pred[1024]{0:T(1024)(128)(4,1)S(1)} %broadcast_compare_fusion.1), kind=kOutput, calls=%fused_computation.1 | convolution fusion | flops 1076887552 | bytes 7345152 | tf_op jit(solution)/shard_map/dot_general | solution.py:144
  40.7 2.5 %collective-permute-done.8.refs_2_ = bf16[128,2432]{1,0:T(8,128)(2,1)S(1)} collective-permute-done((bf16[128,2432]{1,0:T(8,128)(2,1)S(1)}, bf16[128,2432]{1,0:T(8,128)(2,1)S(1)}, u32[]{:S(2)}, u32[]{:S(2)}) %collective-permute-start.8) | collective-permute-done | bytes 622624 | tf_op jit(solution)/shard_map/ppermute | solution.py:31
  43.2 3.1 %collective-permute-start.10 = (bf16[128,2432]{1,0:T(8,128)(2,1)S(1)}, bf16[128,2432]{1,0:T(8,128)(2,1)S(1)}, u32[]{:S(2)}, u32[]{:S(2)}) collective-permute-start(bf16[128,2432]{1,0:T(8,128)(2,1)S(1)} %collective-permute-done.8.refs_2_), channel_id=1, source_target_pairs={{0,4},{1,13},{2,6},{3,15},{4,8},{5,1},{6,10},{7,3},{8,12},{9,5},{1... | collective-permute-start | bytes 1867784 | tf_op jit(solution)/shard_map/ppermute | solution.py:31
  46.4 3.6 %collective-permute-done.12.refs_3_ = bf16[128,2432]{1,0:T(8,128)(2,1)S(1)} collective-permute-done((bf16[128,2432]{1,0:T(8,128)(2,1)S(1)}, bf16[128,2432]{1,0:T(8,128)(2,1)S(1)}, u32[]{:S(2)}, u32[]{:S(2)}) %collective-permute-start.12) | collective-permute-done | bytes 622624 | tf_op jit(solution)/shard_map/ppermute | solution.py:31
  49.9 1.9 %collective-permute-start.15 = (bf16[128,2432]{1,0:T(8,128)(2,1)S(1)}, bf16[128,2432]{1,0:T(8,128)(2,1)S(1)}, u32[]{:S(2)}, u32[]{:S(2)}) collective-permute-start(bf16[128,2432]{1,0:T(8,128)(2,1)S(1)} %collective-permute-done.12.refs_3_), channel_id=1, source_target_pairs={{0,1},{1,0},{2,3},{3,2},{4,5},{5,4},{6,7},{7,6},{8,9},{9,8},{10,11... | collective-permute-start | bytes 1867784 | tf_op jit(solution)/shard_map/ppermute | solution.py:31
  51.8 3.0 %shard_map.46.refs_2_ = f32[1024,1152]{1,0:T(8,128)S(1)} custom-call(s32[1]{0:T(128)} %bitcast.offset_ref, bf16[1024,1024]{1,0:T(8,128)(2,1)S(1)} %fusion.logit_ref, bf16[128,2432]{1,0:T(8,128)(2,1)S(1)} %concatenate.21.refs_0_, bf16[128,2432]{1,0:T(8,128)(2,1)S(1)} %collective-permute-done.11.refs_1_, bf16[128,2432]{1,0:T(8,128)(2,1)S(1)} %collective-permute-done.8.refs_2_, ...), custom_call_target="tpu_custom_call" | custom-call | flops 2415919104 | bytes 8388608 | tf_op jit(solution)/shard_map/pallas_call | solution.py:107
  54.8 1.8 %collective-permute-done.10.refs_0_ = bf16[128,2432]{1,0:T(8,128)(2,1)S(1)} collective-permute-done((bf16[128,2432]{1,0:T(8,128)(2,1)S(1)}, bf16[128,2432]{1,0:T(8,128)(2,1)S(1)}, u32[]{:S(2)}, u32[]{:S(2)}) %collective-permute-start.10) | collective-permute-done | bytes 622624 | tf_op jit(solution)/shard_map/ppermute | solution.py:31
  56.6 1.9 %collective-permute-start.13 = (bf16[128,2432]{1,0:T(8,128)(2,1)S(1)}, bf16[128,2432]{1,0:T(8,128)(2,1)S(1)}, u32[]{:S(2)}, u32[]{:S(2)}) collective-permute-start(bf16[128,2432]{1,0:T(8,128)(2,1)S(1)} %collective-permute-done.10.refs_0_), channel_id=1, source_target_pairs={{0,1},{1,0},{2,3},{3,2},{4,5},{5,4},{6,7},{7,6},{8,9},{9,8},{10,11... | collective-permute-start | bytes 1867784 | tf_op jit(solution)/shard_map/ppermute | solution.py:31
  58.5 1.7 %shard_map.47.refs_2_ = f32[1024,1152]{1,0:T(8,128)S(1)} custom-call(s32[1]{0:T(128)} %bitcast.offset_ref, bf16[1024,1024]{1,0:T(8,128)(2,1)S(1)} %fusion.logit_ref, bf16[128,2432]{1,0:T(8,128)(2,1)S(1)} %collective-permute-done.14.refs_0_, bf16[128,2432]{1,0:T(8,128)(2,1)S(1)} %collective-permute-done.15.refs_1_, f32[1024,1152]{1,0:T(8,128)S(1)} %shard_map.46.refs_2_), custom_call_target="tpu_custom_call" | custom-call | flops 1207959552 | bytes 8388608 | tf_op jit(solution)/shard_map/pallas_call | solution.py:107
  60.2 3.2 %shard_map.48 = f32[1024,1152]{1,0:T(8,128)} custom-call(s32[1]{0:T(128)} %bitcast.offset_ref, bf16[1024,1024]{1,0:T(8,128)(2,1)S(1)} %fusion.logit_ref, bf16[128,2432]{1,0:T(8,128)(2,1)S(1)} %collective-permute-done.10.refs_0_, bf16[128,2432]{1,0:T(8,128)(2,1)S(1)} %collective-permute-done.13.refs_1_, f32[1024,1152]{1,0:T(8,128)S(1)} %shard_map.47.refs_2_), custom_call_target="tpu_custom_call" | custom-call | flops 1207959552 | bytes 8388608 | tf_op jit(solution)/shard_map/pallas_call | solution.py:107
  (18 shorter events, 0.2 us)
Async XLA Ops:
  1.7 5.0 %collective-permute-start.1 = (bf16[4,2432]{1,0:T(4,128)(2,1)S(1)}, bf16[4,2432]{1,0:T(4,128)(2,1)S(1)}, u32[]{:S(2)}, u32[]{:S(2)}) collective-permute-start(bf16[4,2432]{1,0:T(4,128)(2,1)S(1)} %get-tuple-element.15), channel_id=1, source_target_pairs={{0,2},{1,3},{2,0},{3,1},{4,6},{5,7},{6,4},{7,5},{8,10},{9,11},{10,... | collective-permute-start | bytes 58376 | tf_op jit(solution)/shard_map/ppermute | solution.py:31
  5.5 4.1 %collective-permute-start.2 = (bf16[4,2432]{1,0:T(4,128)(2,1)S(1)}, bf16[4,2432]{1,0:T(4,128)(2,1)S(1)}, u32[]{:S(2)}, u32[]{:S(2)}) collective-permute-start(bf16[4,2432]{1,0:T(4,128)(2,1)S(1)} %get-tuple-element.16), channel_id=1, source_target_pairs={{0,130},{1,131},{2,128},{3,129},{4,134},{5,135},{6,132},{7,133},{8... | collective-permute-start | bytes 58376 | tf_op jit(solution)/shard_map/ppermute | solution.py:31
  6.3 3.4 %collective-permute-start = (bf16[4,2432]{1,0:T(4,128)(2,1)S(1)}, bf16[4,2432]{1,0:T(4,128)(2,1)S(1)}, u32[]{:S(2)}, u32[]{:S(2)}) collective-permute-start(bf16[4,2432]{1,0:T(4,128)(2,1)S(1)} %get-tuple-element.16), channel_id=1, source_target_pairs={{0,128},{1,129},{2,130},{3,131},{4,132},{5,133},{6,134},{7,135},{8... | collective-permute-start | bytes 58376 | tf_op jit(solution)/shard_map/ppermute | solution.py:31
  6.7 32.6 %collective-permute-start.9 = (bf16[512,1024]{1,0:T(8,128)(2,1)}, bf16[512,1024]{1,0:T(8,128)(2,1)S(1)}, u32[]{:S(2)}, u32[]{:S(2)}) collective-permute-start(bf16[512,1024]{1,0:T(8,128)(2,1)} %param.6), channel_id=1, source_target_pairs={{0,128},{1,129},{2,130},{3,131},{4,132},{5,133},{6,134},{7,135},{8... | collective-permute-start | bytes 3145736 | tf_op jit(solution)/shard_map/ppermute | solution.py:31
  9.7 2.9 %collective-permute-start.3 = (bf16[16,2432]{1,0:T(8,128)(2,1)S(1)}, bf16[16,2432]{1,0:T(8,128)(2,1)S(1)}, u32[]{:S(2)}, u32[]{:S(2)}) collective-permute-start(bf16[16,2432]{1,0:T(8,128)(2,1)S(1)} %pad_maximum_fusion), channel_id=1, source_target_pairs={{0,1},{1,0},{2,3},{3,2},{4,5},{5,4},{6,7},{7,6},{8,9},{9,8},{10,11... | collective-permute-start | bytes 233480 | tf_op jit(solution)/shard_map/ppermute | solution.py:31
  12.7 9.9 %collective-permute-start.5 = (bf16[32,2432]{1,0:T(8,128)(2,1)S(1)}, bf16[32,2432]{1,0:T(8,128)(2,1)S(1)}, u32[]{:S(2)}, u32[]{:S(2)}) collective-permute-start(bf16[32,2432]{1,0:T(8,128)(2,1)S(1)} %concatenate.20), channel_id=1, source_target_pairs={{0,32},{1,97},{2,34},{3,99},{4,36},{5,101},{6,38},{7,103},{8,40},{... | collective-permute-start | bytes 466952 | tf_op jit(solution)/shard_map/ppermute | solution.py:31
  18.8 8.0 %collective-permute-start.4 = (bf16[32,2432]{1,0:T(8,128)(2,1)S(1)}, bf16[32,2432]{1,0:T(8,128)(2,1)S(1)}, u32[]{:S(2)}, u32[]{:S(2)}) collective-permute-start(bf16[32,2432]{1,0:T(8,128)(2,1)S(1)} %concatenate.20), channel_id=1, source_target_pairs={{0,16},{1,113},{2,18},{3,115},{4,20},{5,117},{6,22},{7,119},{8,24}... | collective-permute-start | bytes 466952 | tf_op jit(solution)/shard_map/ppermute | solution.py:31
  22.6 7.0 %collective-permute-start.6 = (bf16[32,2432]{1,0:T(8,128)(2,1)S(1)}, bf16[32,2432]{1,0:T(8,128)(2,1)S(1)}, u32[]{:S(2)}, u32[]{:S(2)}) collective-permute-start(bf16[32,2432]{1,0:T(8,128)(2,1)S(1)} %collective-permute-done.5), channel_id=1, source_target_pairs={{0,16},{1,113},{2,18},{3,115},{4,20},{5,117},{6,22},{7,119},{8,24}... | collective-permute-start | bytes 466952 | tf_op jit(solution)/shard_map/ppermute | solution.py:31
  24.7 5.0 %collective-permute-start.7 = (bf16[16,2432]{1,0:T(8,128)(2,1)S(1)}, bf16[16,2432]{1,0:T(8,128)(2,1)S(1)}, u32[]{:S(2)}, u32[]{:S(2)}) collective-permute-start(bf16[16,2432]{1,0:T(8,128)(2,1)S(1)} %slice.4), channel_id=1, source_target_pairs={{0,32},{1,97},{2,34},{3,99},{4,36},{5,101},{6,38},{7,103},{8,40},{... | collective-permute-start | bytes 233480 | tf_op jit(solution)/shard_map/ppermute | solution.py:31
  30.1 8.6 %collective-permute-start.11 = (bf16[128,2432]{1,0:T(8,128)(2,1)S(1)}, bf16[128,2432]{1,0:T(8,128)(2,1)S(1)}, u32[]{:S(2)}, u32[]{:S(2)}) collective-permute-start(bf16[128,2432]{1,0:T(8,128)(2,1)S(1)} %concatenate.21.refs_0_), channel_id=1, source_target_pairs={{0,1},{1,0},{2,3},{3,2},{4,5},{5,4},{6,7},{7,6},{8,9},{9,8},{10,11... | collective-permute-start | bytes 1867784 | tf_op jit(solution)/shard_map/ppermute | solution.py:31
  33.6 9.7 %collective-permute-start.8 = (bf16[128,2432]{1,0:T(8,128)(2,1)S(1)}, bf16[128,2432]{1,0:T(8,128)(2,1)S(1)}, u32[]{:S(2)}, u32[]{:S(2)}) collective-permute-start(bf16[128,2432]{1,0:T(8,128)(2,1)S(1)} %concatenate.21.refs_0_), channel_id=1, source_target_pairs={{0,4},{1,13},{2,6},{3,15},{4,8},{5,1},{6,10},{7,3},{8,12},{9,5},{1... | collective-permute-start | bytes 1867784 | tf_op jit(solution)/shard_map/ppermute | solution.py:31
  38.7 11.2 %collective-permute-start.12 = (bf16[128,2432]{1,0:T(8,128)(2,1)S(1)}, bf16[128,2432]{1,0:T(8,128)(2,1)S(1)}, u32[]{:S(2)}, u32[]{:S(2)}) collective-permute-start(bf16[128,2432]{1,0:T(8,128)(2,1)S(1)} %collective-permute-done.11.refs_1_), channel_id=1, source_target_pairs={{0,4},{1,13},{2,6},{3,15},{4,8},{5,1},{6,10},{7,3},{8,12},{9,5},{1... | collective-permute-start | bytes 1867784 | tf_op jit(solution)/shard_map/ppermute | solution.py:31
  43.2 13.3 %collective-permute-start.10 = (bf16[128,2432]{1,0:T(8,128)(2,1)S(1)}, bf16[128,2432]{1,0:T(8,128)(2,1)S(1)}, u32[]{:S(2)}, u32[]{:S(2)}) collective-permute-start(bf16[128,2432]{1,0:T(8,128)(2,1)S(1)} %collective-permute-done.8.refs_2_), channel_id=1, source_target_pairs={{0,4},{1,13},{2,6},{3,15},{4,8},{5,1},{6,10},{7,3},{8,12},{9,5},{1... | collective-permute-start | bytes 1867784 | tf_op jit(solution)/shard_map/ppermute | solution.py:31
  46.4 12.1 %collective-permute-start.14 = (bf16[128,2432]{1,0:T(8,128)(2,1)S(1)}, bf16[128,2432]{1,0:T(8,128)(2,1)S(1)}, u32[]{:S(2)}, u32[]{:S(2)}) collective-permute-start(bf16[128,2432]{1,0:T(8,128)(2,1)S(1)} %collective-permute-done.8.refs_2_), channel_id=1, source_target_pairs={{0,1},{1,0},{2,3},{3,2},{4,5},{5,4},{6,7},{7,6},{8,9},{9,8},{10,11... | collective-permute-start | bytes 1867784 | tf_op jit(solution)/shard_map/ppermute | solution.py:31
  49.9 8.6 %collective-permute-start.15 = (bf16[128,2432]{1,0:T(8,128)(2,1)S(1)}, bf16[128,2432]{1,0:T(8,128)(2,1)S(1)}, u32[]{:S(2)}, u32[]{:S(2)}) collective-permute-start(bf16[128,2432]{1,0:T(8,128)(2,1)S(1)} %collective-permute-done.12.refs_3_), channel_id=1, source_target_pairs={{0,1},{1,0},{2,3},{3,2},{4,5},{5,4},{6,7},{7,6},{8,9},{9,8},{10,11... | collective-permute-start | bytes 1867784 | tf_op jit(solution)/shard_map/ppermute | solution.py:31
  56.6 3.6 %collective-permute-start.13 = (bf16[128,2432]{1,0:T(8,128)(2,1)S(1)}, bf16[128,2432]{1,0:T(8,128)(2,1)S(1)}, u32[]{:S(2)}, u32[]{:S(2)}) collective-permute-start(bf16[128,2432]{1,0:T(8,128)(2,1)S(1)} %collective-permute-done.10.refs_0_), channel_id=1, source_target_pairs={{0,1},{1,0},{2,3},{3,2},{4,5},{5,4},{6,7},{7,6},{8,9},{9,8},{10,11... | collective-permute-start | bytes 1867784 | tf_op jit(solution)/shard_map/ppermute | solution.py:31

commit v5 on v4

--- a/solution.py
+++ b/solution.py
@@ -11,6 +11,9 @@
 Z, X, YH, CORE, DP = 8, 4, 2, 2, 2
 ROWS = 4
 LANES = 128
+TOKENS = 128
+SLOTS = 32
+CODES = 16
 
 
 def coords(vocab):
@@ -39,7 +42,7 @@
     both = jnp.concatenate([chunk, move(chunk, fc=1)], axis=0)
     two, one = move(both, dz=2), move(both, dz=1)
     three, four = move(two, dz=1), move(two[:16], dz=2)
-    return jnp.concatenate([chunk, one, two, three, four], axis=0), from_yh
+    return [chunk, one, two, three, four], from_yh
 
 
 STEPS = (0, 0, 1, 1, 2, -1, -1, 2)
@@ -64,57 +67,136 @@
     return token * ROWS + j, r % 2
 
 
-def contract_kernel(spots, pieces, columns, added, last, offset_ref, logit_ref, *refs):
+def pack_kernel(columns, plane_ref, *refs):
+    parts, (out_ref, rest_ref) = refs[:-2], refs[-2:]
+    side = (((1,), (1,)), ((), ()))
+    out_ref[:TOKENS, :] = jnp.concatenate([p[:, :columns] for p in parts], axis=0)
+    grads = jnp.concatenate([p[:, columns : 2 * columns] for p in parts], axis=0)
+    codes = jnp.concatenate([p[:, 2 * columns :] for p in parts], axis=0)
+    line = lax.broadcasted_iota(jnp.int32, (CODES, LANES), 0)
+    lane = lax.broadcasted_iota(jnp.int32, (CODES, LANES), 1)
+    pick = jnp.where(line == lane, 1.0, 0.0).astype(jnp.bfloat16)
+    turned = lax.dot_general(pick, codes, side, preferred_element_type=jnp.float32)
+    top = turned[:1].astype(jnp.int32)
+    match = ((top >> 5) == plane_ref[0]) & (((top >> 2) & 1) == plane_ref[1])
+    found = jnp.where(match, 1.0, 0.0)
+    row = lax.broadcasted_iota(jnp.int32, (TOKENS, TOKENS), 0)
+    col = lax.broadcasted_iota(jnp.int32, (TOKENS, TOKENS), 1)
+    before = jnp.where(row < col, 1.0, 0.0).astype(jnp.bfloat16)
+    many = jnp.broadcast_to(found, (CODES, TOKENS)).astype(jnp.bfloat16)
+    rank = jnp.dot(many, before, preferred_element_type=jnp.float32)[:1].astype(jnp.int32)
+    rank = jnp.where(match, rank, -1)
+    over = jnp.max(jnp.where(rank >= SLOTS, 1.0, 0.0), axis=1, keepdims=True)
+    turned = jnp.where(line == 3, 1.0, turned).astype(jnp.bfloat16)
+    for ref, start, first, slots in ((out_ref, TOKENS, 0, SLOTS), (rest_ref, 0, SLOTS, TOKENS - SLOTS)):
+        chosen = jnp.where(rank == row[:slots] + first, 1.0, 0.0).astype(jnp.bfloat16)
+        ref[start : start + slots, :] = jnp.dot(chosen, grads, preferred_element_type=jnp.float32).astype(jnp.bfloat16)
+        chosen = jnp.where(rank == row + first, 1.0, 0.0).astype(jnp.bfloat16)
+        code = lax.dot_general(turned, chosen, side, preferred_element_type=jnp.float32)
+        code = jnp.where(line == 4, over, code).astype(jnp.bfloat16)
+        ref[start + slots : start + slots + CODES, :LANES] = code
+        ref[start + slots : start + slots + CODES, LANES:] = jnp.zeros((CODES, columns - LANES), jnp.bfloat16)
+
+
+def pack(plane, parts, columns):
+    here = pl.BlockSpec(memory_space=pltpu.VMEM)
+    shapes = (TOKENS + SLOTS + CODES, TOKENS - SLOTS + CODES)
+    return pl.pallas_call(
+        functools.partial(pack_kernel, columns),
+        out_shape=[jax.ShapeDtypeStruct((rows, columns), jnp.bfloat16) for rows in shapes],
+        in_specs=[pl.BlockSpec(memory_space=pltpu.SMEM)] + [here] * len(parts),
+        out_specs=[here, here],
+        compiler_params=pltpu.CompilerParams(vmem_limit_bytes=8 << 20),
+        cost_estimate=pl.CostEstimate(flops=1 << 26, bytes_accessed=2 << 20, transcendentals=0),
+    )(plane, *parts)
+
+
+def slot_ids(chunks, first, slots, offset):
+    ids = []
+    for c in chunks:
+        code = c[first + slots : first + slots + CODES, :LANES].astype(jnp.float32)
+        row = (code[:1] * 512.0 + code[1:2] * 2.0 + code[2:3]).astype(jnp.int32) - offset
+        ids.append(jnp.where(code[3:4] > 0.5, row, -1)[:, :slots])
+    return jnp.concatenate(ids, axis=1)
+
+
+def contract_kernel(spots, added, others, offset_ref, logit_ref, *refs):
+    pieces = len(spots)
     chunks = refs[:pieces]
-    out_ref = refs[pieces + added]
+    out_ref = refs[pieces + added + others]
     rows = logit_ref.shape[0]
     step = rows // 2
-    lane = lax.broadcasted_iota(jnp.int32, (8, LANES), 1)
-    weight = jnp.where(lane == 0, 512.0, jnp.where(lane == 1, 2.0, jnp.where(lane == 2, 1.0, 0.0)))
-    code = jnp.concatenate([c[:, 2 * columns :] for c in chunks], axis=0)
-    ids = lax.dot_general(
-        weight.astype(jnp.bfloat16), code, (((1,), (1,)), ((), ())), preferred_element_type=jnp.float32
-    )
-    ids = ids[:1].astype(jnp.int32) - offset_ref[0]
+    ids = slot_ids(chunks, TOKENS, SLOTS, offset_ref[0])
     copies = []
     for block in range(2):
         span = slice(block * step, (block + 1) * step)
         row = lax.broadcasted_iota(jnp.int32, (step, ids.shape[1]), 0) + block * step
         onehot = jnp.where(row == ids, 1.0, 0.0).astype(jnp.bfloat16)
         left = jnp.concatenate([logit_ref[span, s * LANES : (s + 1) * LANES] for s in spots], axis=1)
-        right = jnp.concatenate([c[:, :columns] for c in chunks], axis=0)
+        right = jnp.concatenate([c[:TOKENS, :] for c in chunks], axis=0)
         total = jnp.dot(left, right, preferred_element_type=jnp.float32)
-        right = jnp.concatenate([c[:, columns : 2 * columns] for c in chunks], axis=0)
+        right = jnp.concatenate([c[TOKENS : TOKENS + SLOTS, :] for c in chunks], axis=0)
         total += jnp.dot(onehot, right, preferred_element_type=jnp.float32)
         if added:
             total += refs[pieces][span, :]
-        if last:
-            stage, sems = refs[pieces + added + 1 :]
+        if others:
+            over_ref, stage, sems = refs[pieces + added + others + 1 :]
             stage[span, :] = total
             copies.append(pltpu.make_async_copy(stage.at[span, :], out_ref.at[span, :], sems.at[block]))
             copies[-1].start()
         else:
             out_ref[span, :] = total
+    if others:
+        over = [c[TOKENS + SLOTS : TOKENS + SLOTS + CODES, :LANES] for c in chunks + refs[pieces + added :][:others]]
+        over = functools.reduce(jnp.maximum, [c.astype(jnp.float32)[4:5] for c in over])
+        over_ref[...] = jnp.broadcast_to(over, over_ref.shape).astype(jnp.int32)
     for copy in copies:
         copy.wait()
 
 
-def contract(offset, logits, chunks, spots, columns, partial=None, last=False):
-    rows = logits.shape[0]
+def contract(offset, logits, chunks, spots, partial=None, others=()):
+    rows, columns = logits.shape[0], chunks[0].shape[1]
     added = [] if partial is None else [partial]
     here = pl.BlockSpec(memory_space=pltpu.VMEM)
+    out = jax.ShapeDtypeStruct((rows, columns), jnp.float32)
     scratch = [pltpu.VMEM((rows, columns), jnp.float32), pltpu.SemaphoreType.DMA((2,))]
     return pl.pallas_call(
-        functools.partial(contract_kernel, tuple(spots), len(chunks), columns, len(added), last),
-        out_shape=jax.ShapeDtypeStruct((rows, columns), jnp.float32),
-        in_specs=[pl.BlockSpec(memory_space=pltpu.SMEM)] + [here] * (1 + len(chunks) + len(added)),
-        out_specs=pl.BlockSpec(memory_space=pl.ANY) if last else here,
-        scratch_shapes=scratch if last else [],
+        functools.partial(contract_kernel, tuple(spots), len(added), len(others)),
+        out_shape=[out, jax.ShapeDtypeStruct((8, LANES), jnp.int32)] if others else out,
+        in_specs=[pl.BlockSpec(memory_space=pltpu.SMEM)] + [here] * (1 + len(chunks) + len(added) + len(others)),
+        out_specs=[pl.BlockSpec(memory_space=pl.ANY), here] if others else here,
+        scratch_shapes=scratch if others else [],
         compiler_params=pltpu.CompilerParams(vmem_limit_bytes=16 << 20),
         cost_estimate=pl.CostEstimate(
-            flops=4 * rows * len(spots) * LANES * columns, bytes_accessed=8 << 20, transcendentals=0
+            flops=3 * rows * len(spots) * LANES * columns, bytes_accessed=8 << 20, transcendentals=0
         ),
-    )(offset, logits, *chunks, *added)
+    )(offset, logits, *chunks, *added, *others)
+
+
+def append_kernel(pieces, slots, offset_ref, *refs):
+    chunks, base_ref, out_ref = refs[:pieces], refs[pieces], refs[pieces + 1]
+    rows = out_ref.shape[0]
+    ids = slot_ids(chunks, 0, slots, offset_ref[0] + pl.program_id(0) * rows)
+    row = lax.broadcasted_iota(jnp.int32, (rows, ids.shape[1]), 0)
+    onehot = jnp.where(row == ids, 1.0, 0.0).astype(jnp.bfloat16)
+    right = jnp.concatenate([c[:slots, :] for c in chunks], axis=0)
+    out_ref[...] = base_ref[...] + jnp.dot(onehot, right, preferred_element_type=jnp.float32)
+
+
+def append(offset, chunks, base):
+    rows, columns = base.shape
+    block = rows // 4
+    whole = pl.BlockSpec(chunks[0].shape, lambda m: (0, 0), pipeline_mode=pl.Buffered(1))
+    tile = pl.BlockSpec((block, columns), lambda m: (m, 0))
+    return pl.pallas_call(
+        functools.partial(append_kernel, len(chunks), chunks[0].shape[0] - CODES),
+        out_shape=jax.ShapeDtypeStruct(base.shape, base.dtype),
+        grid=(rows // block,),
+        in_specs=[pl.BlockSpec(memory_space=pltpu.SMEM)] + [whole] * len(chunks) + [tile],
+        out_specs=tile,
+        input_output_aliases={1 + len(chunks): 0},
+        compiler_params=pltpu.CompilerParams(vmem_limit_bytes=16 << 20),
+    )(offset, *chunks, base)
 
 
 def body(token_ids, hidden, logit_grad, embed_grad):
@@ -132,23 +214,40 @@
 
     dims = (((0,), (0,)), ((), ()))
     token, away = arrangement(dp, vocab)
-    own, other, offset, token = lax.optimization_barrier((payload(dp), payload(1 - dp), offset, token))
+    z, _, yh, _ = coords(vocab)
+    plane = jnp.stack([z, yh]).astype(jnp.int32)
+    own, other, offset, token, plane = lax.optimization_barrier(
+        (payload(dp), payload(1 - dp), offset, token, plane)
+    )
     spot = lax.broadcasted_iota(jnp.int32, (logit_grad.shape[0], 1), 0)
     near, far = (((spot == token) & (away == side)).astype(jnp.bfloat16) for side in (0, 1))
-    column, early = gather_column(own, other)
+    parts, early = gather_column(own, other)
     held, _ = lax.optimization_barrier((logit_grad, early))
     partner = move(held, fd=1)
+    column, rest = pack(plane, parts, columns)
     swapped = move(column, fc=1)
     direct = [move(column, dx=1), move(swapped, dx=1)]
-    turned = lax.dot_general(logit_grad, near, dims, preferred_element_type=jnp.float32)
+    local, _ = lax.optimization_barrier((logit_grad, swapped))
+    turned = lax.dot_general(local, near, dims, preferred_element_type=jnp.float32)
     turned = turned + lax.dot_general(partner, far, dims, preferred_element_type=jnp.float32)
     turned = turned.astype(jnp.bfloat16)
     direct[0], turned = lax.optimization_barrier((direct[0], turned))
     passed = move(direct[0], dx=1)
-    partial = contract(offset, turned, [column, swapped] + direct, (0, 1, 2, 3), columns)
+    first = [column, swapped] + direct
+    partial = contract(offset, turned, first, (0, 1, 2, 3))
     passed, partial = lax.optimization_barrier((passed, partial))
-    partial = contract(offset, turned, [move(part, fc=1) for part in direct], (5, 6), columns, partial)
-    return contract(offset, turned, [passed, move(passed, fc=1)], (4, 7), columns, partial, last=True)
+    second = [move(part, fc=1) for part in direct]
+    partial = contract(offset, turned, second, (5, 6), partial)
+    result, over = contract(offset, turned, [passed, move(passed, fc=1)], (4, 7), partial, first + second)
+
+    def again(state):
+        total, _ = state
+        pair = [rest, move(rest, fc=1)]
+        came = [move(part, dx=1) for part in pair]
+        came.append(move(came[0], dx=1))
+        return append(offset, pair + came + [move(part, fc=1) for part in came], total), jnp.int32(0)
+
+    return lax.while_loop(lambda state: state[1] > 0, again, (result, over[0, 0]))[0]
 
 
 def solution(mesh):

time: 63.8 us -> 59 us (0.925)
  waiting for transfers between devices: 16.8 us -> 11.3 us
  matrix products: 4.02 us -> 2.78 us
  starting transfers between devices: 32.4 us -> 33.4 us
    ppermute x16, waiting for transfers between devices: 16.8 us -> 11.3 us  [move(): return lax.ppermute(value, ('dp', 'vocab'), pairs)]
    dot_general x1, matrix products: 2.59 us -> 1.43 us  [body(): lax.dot_general(local, near, dims, preferred_element_type=jnp.float32)]
    ppermute x16, starting transfers between devices: 32.4 us -> 33.4 us  [move(): return lax.ppermute(value, ('dp', 'vocab'), pairs)]
    pallas_call x3 -> x4, Pallas kernels: 7.96 us -> 8.07 us  [the longest x3 6.95 us: contract(): pl.pallas_call(functools.partial(contract_kernel, tuple(spots), len(added...]
  transfers between devices with their start and end apart: 16 -> 16, of which waited for: 8 -> 8; matrix products, arithmetic and copies ran while one was open for 7% -> 5% of each run, Pallas kernels for 7% -> 8%
where the time goes in v5:
time: 59 us; the launch traced here: 58.8 us
  starting transfers between devices  33.4 us (57%)
  waiting for transfers between devices  11.3 us (19%)
  Pallas kernels  8.07 us (14%)
  matrix products  2.78 us (5%)
  local copies, waits for them, and re-layouts  1.39 us (2%)
  other arithmetic  1.02 us (2%)
    ppermute x16, starting transfers between devices, move(): return lax.ppermute(value, ('dp', 'vocab'), pairs)  33.4 us
    ppermute x16, waiting for transfers between devices, move(): return lax.ppermute(value, ('dp', 'vocab'), pairs)  11.3 us
    pallas_call x3, Pallas kernels, contract(): pl.pallas_call(functools.partial(contract_kernel, tuple(spots), len(added...  6.95 us
    dot_general x1, matrix products, body(): lax.dot_general(local, near, dims, preferred_element_type=jnp.float32)  1.43 us
    dot_general x1, matrix products, body(): lax.dot_general(partner, far, dims, preferred_element_type=jnp.float32)  1.36 us
  transfers between devices with their start and end apart: 16, of which 8 were waited for; matrix products, arithmetic and copies ran while one was open for 5% of the time, Pallas kernels for 8%

profile of v5, /device:TPU:1, one launch (start us, length us, event | category | flops | bytes accessed | tf_op | source)
XLA Modules:
  0.0 58.8 jit_solution(14072900427927257965)
XLA Ops:
  0.0 0.7 %and_select_fusion.15 = (s32[4]{0:T(128)S(1)}, s32[4]{0:T(128)S(1)}, s32[4]{0:T(128)S(1)}) fusion(s32[4]{0:T(128)} %param.6), kind=kLoop, calls=%fused_computation.99 | loop fusion | flops 160 | bytes 64 | tf_op jit(solution)/shard_map/jit(floor_divide)/jit(_where)/select_n | solution.py:208
  0.9 0.8 %constant_dynamic-slice_fusion = (bf16[4,1152]{1,0:T(4,128)(2,1)S(1)}, bf16[4,1152]{1,0:T(4,128)(2,1)S(1)}, bf16[4,1152]{1,0:T(4,128)(2,1)S(1)}, bf16[4,1152]{1,0:T(4,128)(2,1)S(1)}) fusion(bf16[4,2304]{1,0:T(4,128)(2,1)} %param.9, s32[]{:T(128)S(6)} %select_n.409, s32[]{:T(128)S(6)} %select_n.401, bf16[4,2304]{1,0:T(4,128)(2,1)} %param.7), kind=kLoop, calls=%fused_computation.100 | loop fusion | bytes 73736 | tf_op jit(solution)/shard_map/dynamic_slice | solution.py:212
  1.8 3.8 %collective-permute-start.8 = (bf16[4,2432]{1,0:T(4,128)(2,1)S(1)}, bf16[4,2432]{1,0:T(4,128)(2,1)S(1)}, u32[]{:S(2)}, u32[]{:S(2)}) collective-permute-start(bf16[4,2432]{1,0:T(4,128)(2,1)S(1)} %get-tuple-element.43), channel_id=1, source_target_pairs={{0,2},{1,3},{2,0},{3,1},{4,6},{5,7},{6,4},{7,5},{8,10},{9,11},{10,... | collective-permute-start | bytes 58376 | tf_op jit(solution)/shard_map/ppermute | solution.py:34
  5.6 0.8 %collective-permute-start.9 = (bf16[4,2432]{1,0:T(4,128)(2,1)S(1)}, bf16[4,2432]{1,0:T(4,128)(2,1)S(1)}, u32[]{:S(2)}, u32[]{:S(2)}) collective-permute-start(bf16[4,2432]{1,0:T(4,128)(2,1)S(1)} %get-tuple-element.44), channel_id=1, source_target_pairs={{0,130},{1,131},{2,128},{3,129},{4,134},{5,135},{6,132},{7,133},{8... | collective-permute-start | bytes 58376 | tf_op jit(solution)/shard_map/ppermute | solution.py:34
  6.4 0.4 collective-permute-done.8
  6.8 1.3 %collective-permute-start.17 = (bf16[512,1024]{1,0:T(8,128)(2,1)}, bf16[512,1024]{1,0:T(8,128)(2,1)S(1)}, u32[]{:S(2)}, u32[]{:S(2)}) collective-permute-start(bf16[512,1024]{1,0:T(8,128)(2,1)} %param.8), channel_id=1, source_target_pairs={{0,128},{1,129},{2,130},{3,131},{4,132},{5,133},{6,134},{7,135},{8... | collective-permute-start | bytes 3145736 | tf_op jit(solution)/shard_map/ppermute | solution.py:34
  8.1 1.6 %collective-permute-done.9 = bf16[4,2432]{1,0:T(4,128)(2,1)S(1)} collective-permute-done((bf16[4,2432]{1,0:T(4,128)(2,1)S(1)}, bf16[4,2432]{1,0:T(4,128)(2,1)S(1)}, u32[]{:S(2)}, u32[]{:S(2)}) %collective-permute-start.9) | collective-permute-done | bytes 19488 | tf_op jit(solution)/shard_map/ppermute | solution.py:34
  9.8 2.0 %collective-permute-start.10 = (bf16[16,2432]{1,0:T(8,128)(2,1)S(1)}, bf16[16,2432]{1,0:T(8,128)(2,1)S(1)}, u32[]{:S(2)}, u32[]{:S(2)}) collective-permute-start(bf16[16,2432]{1,0:T(8,128)(2,1)S(1)} %pad_maximum_fusion.refs_0_), channel_id=1, source_target_pairs={{0,1},{1,0},{2,3},{3,2},{4,5},{5,4},{6,7},{7,6},{8,9},{9,8},{10,11... | collective-permute-start | bytes 233480 | tf_op jit(solution)/shard_map/ppermute | solution.py:34
  11.8 0.9 %collective-permute-done.10 = bf16[16,2432]{1,0:T(8,128)(2,1)S(1)} collective-permute-done((bf16[16,2432]{1,0:T(8,128)(2,1)S(1)}, bf16[16,2432]{1,0:T(8,128)(2,1)S(1)}, u32[]{:S(2)}, u32[]{:S(2)}) %collective-permute-start.10) | collective-permute-done | bytes 77856 | tf_op jit(solution)/shard_map/ppermute | solution.py:34
  12.8 6.1 %collective-permute-start.12 = (bf16[32,2432]{1,0:T(8,128)(2,1)S(1)}, bf16[32,2432]{1,0:T(8,128)(2,1)S(1)}, u32[]{:S(2)}, u32[]{:S(2)}) collective-permute-start(bf16[32,2432]{1,0:T(8,128)(2,1)S(1)} %concatenate.16), channel_id=1, source_target_pairs={{0,32},{1,97},{2,34},{3,99},{4,36},{5,101},{6,38},{7,103},{8,40},{... | collective-permute-start | bytes 466952 | tf_op jit(solution)/shard_map/ppermute | solution.py:34
  18.9 0.7 %collective-permute-start.11 = (bf16[32,2432]{1,0:T(8,128)(2,1)S(1)}, bf16[32,2432]{1,0:T(8,128)(2,1)S(1)}, u32[]{:S(2)}, u32[]{:S(2)}) collective-permute-start(bf16[32,2432]{1,0:T(8,128)(2,1)S(1)} %concatenate.16), channel_id=1, source_target_pairs={{0,16},{1,113},{2,18},{3,115},{4,20},{5,117},{6,22},{7,119},{8,24}... | collective-permute-start | bytes 466952 | tf_op jit(solution)/shard_map/ppermute | solution.py:34
  19.6 3.1 %collective-permute-done.12.refs_2_ = bf16[32,2432]{1,0:T(8,128)(2,1)S(1)} collective-permute-done((bf16[32,2432]{1,0:T(8,128)(2,1)S(1)}, bf16[32,2432]{1,0:T(8,128)(2,1)S(1)}, u32[]{:S(2)}, u32[]{:S(2)}) %collective-permute-start.12) | collective-permute-done | bytes 155680 | tf_op jit(solution)/shard_map/ppermute | solution.py:34
  22.7 2.0 %collective-permute-start.13 = (bf16[32,2432]{1,0:T(8,128)(2,1)S(1)}, bf16[32,2432]{1,0:T(8,128)(2,1)S(1)}, u32[]{:S(2)}, u32[]{:S(2)}) collective-permute-start(bf16[32,2432]{1,0:T(8,128)(2,1)S(1)} %collective-permute-done.12.refs_2_), channel_id=1, source_target_pairs={{0,16},{1,113},{2,18},{3,115},{4,20},{5,117},{6,22},{7,119},{8,24}... | collective-permute-start | bytes 466952 | tf_op jit(solution)/shard_map/ppermute | solution.py:34
  24.7 2.1 %collective-permute-start.14 = (bf16[16,2432]{1,0:T(8,128)(2,1)S(1)}, bf16[16,2432]{1,0:T(8,128)(2,1)S(1)}, u32[]{:S(2)}, u32[]{:S(2)}) collective-permute-start(bf16[16,2432]{1,0:T(8,128)(2,1)S(1)} %slice.8), channel_id=1, source_target_pairs={{0,32},{1,97},{2,34},{3,99},{4,36},{5,101},{6,38},{7,103},{8,40},{... | collective-permute-start | bytes 233480 | tf_op jit(solution)/shard_map/ppermute | solution.py:34
  26.9 2.9 %collective-permute-done.14.refs_4_ = bf16[16,2432]{1,0:T(8,128)(2,1)S(1)} collective-permute-done((bf16[16,2432]{1,0:T(8,128)(2,1)S(1)}, bf16[16,2432]{1,0:T(8,128)(2,1)S(1)}, u32[]{:S(2)}, u32[]{:S(2)}) %collective-permute-start.14) | collective-permute-done | bytes 77856 | tf_op jit(solution)/shard_map/ppermute | solution.py:34
  29.8 1.1 %shard_map.46 = (bf16[176,1152]{1,0:T(8,128)(2,1)S(1)}, bf16[112,1152]{1,0:T(8,128)(2,1)S(1)}) custom-call(s32[2]{0:T(128)S(1)} %pad_add_fusion.plane_ref, bf16[16,2432]{1,0:T(8,128)(2,1)S(1)} %pad_maximum_fusion.refs_0_, bf16[32,2432]{1,0:T(8,128)(2,1)S(1)} %collective-permute-done.11.refs_1_, bf16[32,2432]{1,0:T(8,128)(2,1)S(1)} %collective-permute-done.12.refs_2_, ...), custom_call_target="tpu_custom_call" | custom-call | flops 67108864 | bytes 2097152 | tf_op jit(solution)/shard_map/pallas_call | solution.py:104
  30.9 3.5 %collective-permute-start.16 = (bf16[176,1152]{1,0:T(8,128)(2,1)S(1)}, bf16[176,1152]{1,0:T(8,128)(2,1)S(1)}, u32[]{:S(2)}, u32[]{:S(2)}) collective-permute-start(bf16[176,1152]{1,0:T(8,128)(2,1)S(1)} %get-tuple-element.45.refs_0_.refs_3_), channel_id=1, source_target_pairs={{0,1},{1,0},{2,3},{3,2},{4,5},{5,4},{6,7},{7,6},{8,9},{9,8},{10,11... | collective-permute-start | bytes 1216520 | tf_op jit(solution)/shard_map/ppermute | solution.py:34
  34.4 2.6 %collective-permute-start.15 = (bf16[176,1152]{1,0:T(8,128)(2,1)S(1)}, bf16[176,1152]{1,0:T(8,128)(2,1)S(1)}, u32[]{:S(2)}, u32[]{:S(2)}) collective-permute-start(bf16[176,1152]{1,0:T(8,128)(2,1)S(1)} %get-tuple-element.45.refs_0_.refs_3_), channel_id=1, source_target_pairs={{0,4},{1,13},{2,6},{3,15},{4,8},{5,1},{6,10},{7,3},{8,12},{9,5},{1... | collective-permute-start | bytes 1216520 | tf_op jit(solution)/shard_map/ppermute | solution.py:34
  37.0 1.3 %collective-permute-start.19 = (bf16[176,1152]{1,0:T(8,128)(2,1)S(1)}, bf16[176,1152]{1,0:T(8,128)(2,1)S(1)}, u32[]{:S(2)}, u32[]{:S(2)}) collective-permute-start(bf16[176,1152]{1,0:T(8,128)(2,1)S(1)} %collective-permute-done.16.refs_1_.refs_4_), channel_id=1, source_target_pairs={{0,4},{1,13},{2,6},{3,15},{4,8},{5,1},{6,10},{7,3},{8,12},{9,5},{1... | collective-permute-start | bytes 1216520 | tf_op jit(solution)/shard_map/ppermute | solution.py:34
  38.2 1.4 %fusion.3 = f32[1024,1024]{1,0:T(8,128)S(1)} fusion(bf16[512,1024]{1,0:T(8,128)(2,1)S(1)} %collective-permute-done.17, s32[1024]{0:T(1024)S(1)} %bitcast.7, pred[1024]{0:T(1024)(128)(4,1)S(1)} %broadcast_compare_fusion.1), kind=kOutput, calls=%fused_computation.4 | convolution fusion | flops 1074790400 | bytes 5248000 | tf_op jit(solution)/shard_map/dot_general | solution.py:232
  39.6 1.4 %add_convert_fusion.logit_ref = bf16[1024,1024]{1,0:T(8,128)(2,1)S(1)} fusion(f32[1024,1024]{1,0:T(8,128)S(1)} %fusion.3, bf16[512,1024]{1,0:T(8,128)(2,1)S(1)} %copy-done, s32[1024]{0:T(1024)S(1)} %bitcast.8, pred[1024]{0:T(1024)(128)(4,1)S(1)} %broadcast_compare_fusion), kind=kOutput, calls=%fused_computation | convolution fusion | flops 1076887552 | bytes 7345152 | tf_op jit(solution)/shard_map/dot_general | solution.py:231
  41.1 0.8 %collective-permute-done.15.refs_2_.refs_5_ = bf16[176,1152]{1,0:T(8,128)(2,1)S(1)} collective-permute-done((bf16[176,1152]{1,0:T(8,128)(2,1)S(1)}, bf16[176,1152]{1,0:T(8,128)(2,1)S(1)}, u32[]{:S(2)}, u32[]{:S(2)}) %collective-permute-start.15) | collective-permute-done | bytes 405536 | tf_op jit(solution)/shard_map/ppermute | solution.py:34
  41.8 3.1 %collective-permute-start.18 = (bf16[176,1152]{1,0:T(8,128)(2,1)S(1)}, bf16[176,1152]{1,0:T(8,128)(2,1)S(1)}, u32[]{:S(2)}, u32[]{:S(2)}) collective-permute-start(bf16[176,1152]{1,0:T(8,128)(2,1)S(1)} %collective-permute-done.15.refs_2_.refs_5_), channel_id=1, source_target_pairs={{0,4},{1,13},{2,6},{3,15},{4,8},{5,1},{6,10},{7,3},{8,12},{9,5},{1... | collective-permute-start | bytes 1216520 | tf_op jit(solution)/shard_map/ppermute | solution.py:34
  44.9 1.2 %collective-permute-done.19.refs_3_.refs_6_ = bf16[176,1152]{1,0:T(8,128)(2,1)S(1)} collective-permute-done((bf16[176,1152]{1,0:T(8,128)(2,1)S(1)}, bf16[176,1152]{1,0:T(8,128)(2,1)S(1)}, u32[]{:S(2)}, u32[]{:S(2)}) %collective-permute-start.19) | collective-permute-done | bytes 405536 | tf_op jit(solution)/shard_map/ppermute | solution.py:34
  46.2 1.8 %collective-permute-start.22 = (bf16[176,1152]{1,0:T(8,128)(2,1)S(1)}, bf16[176,1152]{1,0:T(8,128)(2,1)S(1)}, u32[]{:S(2)}, u32[]{:S(2)}) collective-permute-start(bf16[176,1152]{1,0:T(8,128)(2,1)S(1)} %collective-permute-done.19.refs_3_.refs_6_), channel_id=1, source_target_pairs={{0,1},{1,0},{2,3},{3,2},{4,5},{5,4},{6,7},{7,6},{8,9},{9,8},{10,11... | collective-permute-start | bytes 1216520 | tf_op jit(solution)/shard_map/ppermute | solution.py:34
  48.0 2.2 %shard_map.47.refs_2_ = f32[1024,1152]{1,0:T(8,128)S(1)} custom-call(s32[1]{0:T(128)} %bitcast.offset_ref, bf16[1024,1024]{1,0:T(8,128)(2,1)S(1)} %add_convert_fusion.logit_ref, bf16[176,1152]{1,0:T(8,128)(2,1)S(1)} %get-tuple-element.45.refs_0_.refs_3_, bf16[176,1152]{1,0:T(8,128)(2,1)S(1)} %collective-permute-done.16.refs_1_.refs_4_, ...), custom_call_target="tpu_custom_call" | custom-call | flops 1811939328 | bytes 8388608 | tf_op jit(solution)/shard_map/pallas_call | solution.py:163
  50.2 0.3 collective-permute-done.18.refs_0_
  50.5 2.2 %collective-permute-start.20 = (bf16[176,1152]{1,0:T(8,128)(2,1)S(1)}, bf16[176,1152]{1,0:T(8,128)(2,1)S(1)}, u32[]{:S(2)}, u32[]{:S(2)}) collective-permute-start(bf16[176,1152]{1,0:T(8,128)(2,1)S(1)} %collective-permute-done.18.refs_0_), channel_id=1, source_target_pairs={{0,1},{1,0},{2,3},{3,2},{4,5},{5,4},{6,7},{7,6},{8,9},{9,8},{10,11... | collective-permute-start | bytes 1216520 | tf_op jit(solution)/shard_map/ppermute | solution.py:34
  52.8 1.6 %shard_map.48.refs_2_ = f32[1024,1152]{1,0:T(8,128)S(1)} custom-call(s32[1]{0:T(128)} %bitcast.offset_ref, bf16[1024,1024]{1,0:T(8,128)(2,1)S(1)} %add_convert_fusion.logit_ref, bf16[176,1152]{1,0:T(8,128)(2,1)S(1)} %collective-permute-done.21.refs_0_.refs_7_, bf16[176,1152]{1,0:T(8,128)(2,1)S(1)} %collective-permute-done.22.refs_1_.refs_8_, ...), custom_call_target="tpu_custom_call" | custom-call | flops 905969664 | bytes 8388608 | tf_op jit(solution)/shard_map/pallas_call | solution.py:163
  54.3 3.2 %shard_map.49 = (f32[1024,1152]{1,0:T(8,128)}, s32[8,128]{1,0:T(8,128)S(1)}) custom-call(s32[1]{0:T(128)} %bitcast.offset_ref, bf16[1024,1024]{1,0:T(8,128)(2,1)S(1)} %add_convert_fusion.logit_ref, bf16[176,1152]{1,0:T(8,128)(2,1)S(1)} %collective-permute-done.18.refs_0_, bf16[176,1152]{1,0:T(8,128)(2,1)S(1)} %collective-permute-done.20.refs_1_, ...), custom_call_target="tpu_custom_call" | custom-call | flops 905969664 | bytes 8388608 | tf_op jit(solution)/shard_map/pallas_call | solution.py:163
  57.5 0.5 slice.7
  58.0 0.6 while.9
  (23 shorter events, 0.5 us)
Async XLA Ops:
  1.8 5.0 %collective-permute-start.8 = (bf16[4,2432]{1,0:T(4,128)(2,1)S(1)}, bf16[4,2432]{1,0:T(4,128)(2,1)S(1)}, u32[]{:S(2)}, u32[]{:S(2)}) collective-permute-start(bf16[4,2432]{1,0:T(4,128)(2,1)S(1)} %get-tuple-element.43), channel_id=1, source_target_pairs={{0,2},{1,3},{2,0},{3,1},{4,6},{5,7},{6,4},{7,5},{8,10},{9,11},{10,... | collective-permute-start | bytes 58376 | tf_op jit(solution)/shard_map/ppermute | solution.py:34
  5.6 4.1 %collective-permute-start.9 = (bf16[4,2432]{1,0:T(4,128)(2,1)S(1)}, bf16[4,2432]{1,0:T(4,128)(2,1)S(1)}, u32[]{:S(2)}, u32[]{:S(2)}) collective-permute-start(bf16[4,2432]{1,0:T(4,128)(2,1)S(1)} %get-tuple-element.44), channel_id=1, source_target_pairs={{0,130},{1,131},{2,128},{3,129},{4,134},{5,135},{6,132},{7,133},{8... | collective-permute-start | bytes 58376 | tf_op jit(solution)/shard_map/ppermute | solution.py:34
  6.4 3.4 %collective-permute-start.7 = (bf16[4,2432]{1,0:T(4,128)(2,1)S(1)}, bf16[4,2432]{1,0:T(4,128)(2,1)S(1)}, u32[]{:S(2)}, u32[]{:S(2)}) collective-permute-start(bf16[4,2432]{1,0:T(4,128)(2,1)S(1)} %get-tuple-element.44), channel_id=1, source_target_pairs={{0,128},{1,129},{2,130},{3,131},{4,132},{5,133},{6,134},{7,135},{8... | collective-permute-start | bytes 58376 | tf_op jit(solution)/shard_map/ppermute | solution.py:34
  6.8 31.5 %collective-permute-start.17 = (bf16[512,1024]{1,0:T(8,128)(2,1)}, bf16[512,1024]{1,0:T(8,128)(2,1)S(1)}, u32[]{:S(2)}, u32[]{:S(2)}) collective-permute-start(bf16[512,1024]{1,0:T(8,128)(2,1)} %param.8), channel_id=1, source_target_pairs={{0,128},{1,129},{2,130},{3,131},{4,132},{5,133},{6,134},{7,135},{8... | collective-permute-start | bytes 3145736 | tf_op jit(solution)/shard_map/ppermute | solution.py:34
  9.8 2.9 %collective-permute-start.10 = (bf16[16,2432]{1,0:T(8,128)(2,1)S(1)}, bf16[16,2432]{1,0:T(8,128)(2,1)S(1)}, u32[]{:S(2)}, u32[]{:S(2)}) collective-permute-start(bf16[16,2432]{1,0:T(8,128)(2,1)S(1)} %pad_maximum_fusion.refs_0_), channel_id=1, source_target_pairs={{0,1},{1,0},{2,3},{3,2},{4,5},{5,4},{6,7},{7,6},{8,9},{9,8},{10,11... | collective-permute-start | bytes 233480 | tf_op jit(solution)/shard_map/ppermute | solution.py:34
  12.8 9.9 %collective-permute-start.12 = (bf16[32,2432]{1,0:T(8,128)(2,1)S(1)}, bf16[32,2432]{1,0:T(8,128)(2,1)S(1)}, u32[]{:S(2)}, u32[]{:S(2)}) collective-permute-start(bf16[32,2432]{1,0:T(8,128)(2,1)S(1)} %concatenate.16), channel_id=1, source_target_pairs={{0,32},{1,97},{2,34},{3,99},{4,36},{5,101},{6,38},{7,103},{8,40},{... | collective-permute-start | bytes 466952 | tf_op jit(solution)/shard_map/ppermute | solution.py:34
  18.9 8.0 %collective-permute-start.11 = (bf16[32,2432]{1,0:T(8,128)(2,1)S(1)}, bf16[32,2432]{1,0:T(8,128)(2,1)S(1)}, u32[]{:S(2)}, u32[]{:S(2)}) collective-permute-start(bf16[32,2432]{1,0:T(8,128)(2,1)S(1)} %concatenate.16), channel_id=1, source_target_pairs={{0,16},{1,113},{2,18},{3,115},{4,20},{5,117},{6,22},{7,119},{8,24}... | collective-permute-start | bytes 466952 | tf_op jit(solution)/shard_map/ppermute | solution.py:34
  22.7 7.0 %collective-permute-start.13 = (bf16[32,2432]{1,0:T(8,128)(2,1)S(1)}, bf16[32,2432]{1,0:T(8,128)(2,1)S(1)}, u32[]{:S(2)}, u32[]{:S(2)}) collective-permute-start(bf16[32,2432]{1,0:T(8,128)(2,1)S(1)} %collective-permute-done.12.refs_2_), channel_id=1, source_target_pairs={{0,16},{1,113},{2,18},{3,115},{4,20},{5,117},{6,22},{7,119},{8,24}... | collective-permute-start | bytes 466952 | tf_op jit(solution)/shard_map/ppermute | solution.py:34
  24.7 5.0 %collective-permute-start.14 = (bf16[16,2432]{1,0:T(8,128)(2,1)S(1)}, bf16[16,2432]{1,0:T(8,128)(2,1)S(1)}, u32[]{:S(2)}, u32[]{:S(2)}) collective-permute-start(bf16[16,2432]{1,0:T(8,128)(2,1)S(1)} %slice.8), channel_id=1, source_target_pairs={{0,32},{1,97},{2,34},{3,99},{4,36},{5,101},{6,38},{7,103},{8,40},{... | collective-permute-start | bytes 233480 | tf_op jit(solution)/shard_map/ppermute | solution.py:34
  30.9 6.1 %collective-permute-start.16 = (bf16[176,1152]{1,0:T(8,128)(2,1)S(1)}, bf16[176,1152]{1,0:T(8,128)(2,1)S(1)}, u32[]{:S(2)}, u32[]{:S(2)}) collective-permute-start(bf16[176,1152]{1,0:T(8,128)(2,1)S(1)} %get-tuple-element.45.refs_0_.refs_3_), channel_id=1, source_target_pairs={{0,1},{1,0},{2,3},{3,2},{4,5},{5,4},{6,7},{7,6},{8,9},{9,8},{10,11... | collective-permute-start | bytes 1216520 | tf_op jit(solution)/shard_map/ppermute | solution.py:34
  34.4 7.4 %collective-permute-start.15 = (bf16[176,1152]{1,0:T(8,128)(2,1)S(1)}, bf16[176,1152]{1,0:T(8,128)(2,1)S(1)}, u32[]{:S(2)}, u32[]{:S(2)}) collective-permute-start(bf16[176,1152]{1,0:T(8,128)(2,1)S(1)} %get-tuple-element.45.refs_0_.refs_3_), channel_id=1, source_target_pairs={{0,4},{1,13},{2,6},{3,15},{4,8},{5,1},{6,10},{7,3},{8,12},{9,5},{1... | collective-permute-start | bytes 1216520 | tf_op jit(solution)/shard_map/ppermute | solution.py:34
  37.0 9.2 %collective-permute-start.19 = (bf16[176,1152]{1,0:T(8,128)(2,1)S(1)}, bf16[176,1152]{1,0:T(8,128)(2,1)S(1)}, u32[]{:S(2)}, u32[]{:S(2)}) collective-permute-start(bf16[176,1152]{1,0:T(8,128)(2,1)S(1)} %collective-permute-done.16.refs_1_.refs_4_), channel_id=1, source_target_pairs={{0,4},{1,13},{2,6},{3,15},{4,8},{5,1},{6,10},{7,3},{8,12},{9,5},{1... | collective-permute-start | bytes 1216520 | tf_op jit(solution)/shard_map/ppermute | solution.py:34
  38.2 1.4 %copy-start = (bf16[512,1024]{1,0:T(8,128)(2,1)S(1)}, bf16[512,1024]{1,0:T(8,128)(2,1)}, u32[]{:S(2)}) copy-start(bf16[512,1024]{1,0:T(8,128)(2,1)} %param.8) | copy-start | bytes 3145732
  41.8 8.7 %collective-permute-start.18 = (bf16[176,1152]{1,0:T(8,128)(2,1)S(1)}, bf16[176,1152]{1,0:T(8,128)(2,1)S(1)}, u32[]{:S(2)}, u32[]{:S(2)}) collective-permute-start(bf16[176,1152]{1,0:T(8,128)(2,1)S(1)} %collective-permute-done.15.refs_2_.refs_5_), channel_id=1, source_target_pairs={{0,4},{1,13},{2,6},{3,15},{4,8},{5,1},{6,10},{7,3},{8,12},{9,5},{1... | collective-permute-start | bytes 1216520 | tf_op jit(solution)/shard_map/ppermute | solution.py:34
  44.9 7.8 %collective-permute-start.21 = (bf16[176,1152]{1,0:T(8,128)(2,1)S(1)}, bf16[176,1152]{1,0:T(8,128)(2,1)S(1)}, u32[]{:S(2)}, u32[]{:S(2)}) collective-permute-start(bf16[176,1152]{1,0:T(8,128)(2,1)S(1)} %collective-permute-done.15.refs_2_.refs_5_), channel_id=1, source_target_pairs={{0,1},{1,0},{2,3},{3,2},{4,5},{5,4},{6,7},{7,6},{8,9},{9,8},{10,11... | collective-permute-start | bytes 1216520 | tf_op jit(solution)/shard_map/ppermute | solution.py:34
  46.2 6.6 %collective-permute-start.22 = (bf16[176,1152]{1,0:T(8,128)(2,1)S(1)}, bf16[176,1152]{1,0:T(8,128)(2,1)S(1)}, u32[]{:S(2)}, u32[]{:S(2)}) collective-permute-start(bf16[176,1152]{1,0:T(8,128)(2,1)S(1)} %collective-permute-done.19.refs_3_.refs_6_), channel_id=1, source_target_pairs={{0,1},{1,0},{2,3},{3,2},{4,5},{5,4},{6,7},{7,6},{8,9},{9,8},{10,11... | collective-permute-start | bytes 1216520 | tf_op jit(solution)/shard_map/ppermute | solution.py:34
  50.5 3.8 %collective-permute-start.20 = (bf16[176,1152]{1,0:T(8,128)(2,1)S(1)}, bf16[176,1152]{1,0:T(8,128)(2,1)S(1)}, u32[]{:S(2)}, u32[]{:S(2)}) collective-permute-start(bf16[176,1152]{1,0:T(8,128)(2,1)S(1)} %collective-permute-done.18.refs_0_), channel_id=1, source_target_pairs={{0,1},{1,0},{2,3},{3,2},{4,5},{5,4},{6,7},{7,6},{8,9},{9,8},{10,11... | collective-permute-start | bytes 1216520 | tf_op jit(solution)/shard_map/ppermute | solution.py:34

commit v6 on v5

--- a/solution.py
+++ b/solution.py
@@ -65,6 +65,48 @@
     from_core = holder ^ jnp.where((part % 2 == 0) & (part > 0), 1, 0)
     token = ((from_z * X + from_x) * 2 + (yh ^ (r // 2))) * 2 + from_core
     return token * ROWS + j, r % 2
+
+
+def payload_kernel(dp_ref, *refs):
+    own_ref, other_ref, ids_ref, hidden_ref, grad_ref, sems = refs[3:]
+    copies = [pltpu.make_async_copy(a, b, sems.at[k]) for k, (a, b) in enumerate(zip(refs[:3], refs[5:8]))]
+    for copy in copies:
+        copy.start()
+    for copy in copies:
+        copy.wait()
+    columns = hidden_ref.shape[1] // 2
+    row = lax.broadcasted_iota(jnp.int32, (ROWS, LANES), 0)
+    lane = lax.broadcasted_iota(jnp.int32, (ROWS, LANES), 1)
+    ids = jnp.zeros((ROWS, LANES), jnp.int32)
+    for k in range(ROWS):
+        ids = jnp.where(row == k, ids_ref[k], ids)
+    code = jnp.where(lane == 0, ids >> 9, jnp.where(lane == 1, (ids >> 1) & 255, ids & 1))
+    code = jnp.where(lane < 3, code, 0).astype(jnp.float32).astype(jnp.bfloat16)
+    for side, refs in ((0, (own_ref, other_ref)), (1, (other_ref, own_ref))):
+
+        @pl.when(dp_ref[0] == side)
+        def _():
+            for half, ref in enumerate(refs):
+                span = slice(half * columns, (half + 1) * columns)
+                ref[:, :columns] = hidden_ref[:, span]
+                ref[:, columns : 2 * columns] = grad_ref[:, span]
+
+    own_ref[:, 2 * columns :] = code
+    other_ref[:, 2 * columns :] = code
+
+
+def payloads(dp, ids, hidden, grads):
+    here, scalars = pl.BlockSpec(memory_space=pltpu.VMEM), pl.BlockSpec(memory_space=pltpu.SMEM)
+    shape = jax.ShapeDtypeStruct((ROWS, hidden.shape[1] + LANES), jnp.bfloat16)
+    held = [pltpu.SMEM(ids.shape, ids.dtype), pltpu.VMEM(hidden.shape, hidden.dtype), pltpu.VMEM(grads.shape, grads.dtype)]
+    return pl.pallas_call(
+        payload_kernel,
+        out_shape=[shape, shape],
+        in_specs=[scalars] + [pl.BlockSpec(memory_space=pltpu.HBM)] * 3,
+        out_specs=[here, here],
+        scratch_shapes=held + [pltpu.SemaphoreType.DMA((3,))],
+        compiler_params=pltpu.CompilerParams(vmem_limit_bytes=4 << 20),
+    )(dp, ids, hidden, grads)
 
 
 def pack_kernel(columns, plane_ref, *refs):
@@ -132,11 +174,9 @@
         span = slice(block * step, (block + 1) * step)
         row = lax.broadcasted_iota(jnp.int32, (step, ids.shape[1]), 0) + block * step
         onehot = jnp.where(row == ids, 1.0, 0.0).astype(jnp.bfloat16)
-        left = jnp.concatenate([logit_ref[span, s * LANES : (s + 1) * LANES] for s in spots], axis=1)
-        right = jnp.concatenate([c[:TOKENS, :] for c in chunks], axis=0)
-        total = jnp.dot(left, right, preferred_element_type=jnp.float32)
-        right = jnp.concatenate([c[TOKENS : TOKENS + SLOTS, :] for c in chunks], axis=0)
-        total += jnp.dot(onehot, right, preferred_element_type=jnp.float32)
+        left = [logit_ref[span, s * LANES : (s + 1) * LANES] for s in spots]
+        right = jnp.concatenate([c[:TOKENS, :] for c in chunks] + [c[TOKENS : TOKENS + SLOTS, :] for c in chunks], axis=0)
+        total = jnp.dot(jnp.concatenate(left + [onehot], axis=1), right, preferred_element_type=jnp.float32)
         if added:
             total += refs[pieces][span, :]
         if others:
@@ -149,7 +189,7 @@
     if others:
         over = [c[TOKENS + SLOTS : TOKENS + SLOTS + CODES, :LANES] for c in chunks + refs[pieces + added :][:others]]
         over = functools.reduce(jnp.maximum, [c.astype(jnp.float32)[4:5] for c in over])
-        over_ref[...] = jnp.broadcast_to(over, over_ref.shape).astype(jnp.int32)
+        over_ref[0] = jnp.max(over).astype(jnp.int32)
     for copy in copies:
         copy.wait()
 
@@ -162,9 +202,9 @@
     scratch = [pltpu.VMEM((rows, columns), jnp.float32), pltpu.SemaphoreType.DMA((2,))]
     return pl.pallas_call(
         functools.partial(contract_kernel, tuple(spots), len(added), len(others)),
-        out_shape=[out, jax.ShapeDtypeStruct((8, LANES), jnp.int32)] if others else out,
+        out_shape=[out, jax.ShapeDtypeStruct((1,), jnp.int32)] if others else out,
         in_specs=[pl.BlockSpec(memory_space=pltpu.SMEM)] + [here] * (1 + len(chunks) + len(added) + len(others)),
-        out_specs=[pl.BlockSpec(memory_space=pl.ANY), here] if others else here,
+        out_specs=[pl.BlockSpec(memory_space=pl.ANY), pl.BlockSpec(memory_space=pltpu.SMEM)] if others else here,
         scratch_shapes=scratch if others else [],
         compiler_params=pltpu.CompilerParams(vmem_limit_bytes=16 << 20),
         cost_estimate=pl.CostEstimate(
@@ -203,22 +243,12 @@
     dp, vocab = lax.axis_index("dp"), lax.axis_index("vocab")
     columns = hidden.shape[1] // 2
     offset = (vocab * logit_grad.shape[1]).astype(jnp.int32).reshape(1)
-    ids = token_ids[:, None]
-    lane = lax.broadcasted_iota(jnp.int32, (ROWS, LANES), 1)
-    code = jnp.where(lane == 0, ids // 512, jnp.where(lane == 1, (ids // 2) % 256, ids % 2))
-    code = jnp.where(lane < 3, code, 0).astype(jnp.bfloat16)
-
-    def payload(side):
-        pick = [lax.dynamic_slice_in_dim(a, side * columns, columns, 1) for a in (hidden, embed_grad)]
-        return jnp.concatenate(pick + [code], axis=1)
-
     dims = (((0,), (0,)), ((), ()))
     token, away = arrangement(dp, vocab)
     z, _, yh, _ = coords(vocab)
     plane = jnp.stack([z, yh]).astype(jnp.int32)
-    own, other, offset, token, plane = lax.optimization_barrier(
-        (payload(dp), payload(1 - dp), offset, token, plane)
-    )
+    own, other = payloads(dp.astype(jnp.int32).reshape(1), token_ids, hidden, embed_grad)
+    own, other, offset, token, plane = lax.optimization_barrier((own, other, offset, token, plane))
     spot = lax.broadcasted_iota(jnp.int32, (logit_grad.shape[0], 1), 0)
     near, far = (((spot == token) & (away == side)).astype(jnp.bfloat16) for side in (0, 1))
     parts, early = gather_column(own, other)
@@ -226,19 +256,19 @@
     partner = move(held, fd=1)
     column, rest = pack(plane, parts, columns)
     swapped = move(column, fc=1)
-    direct = [move(column, dx=1), move(swapped, dx=1)]
+    direct = move(column, dx=1)
     local, _ = lax.optimization_barrier((logit_grad, swapped))
     turned = lax.dot_general(local, near, dims, preferred_element_type=jnp.float32)
     turned = turned + lax.dot_general(partner, far, dims, preferred_element_type=jnp.float32)
-    turned = turned.astype(jnp.bfloat16)
-    direct[0], turned = lax.optimization_barrier((direct[0], turned))
-    passed = move(direct[0], dx=1)
+    late, turned = lax.optimization_barrier((swapped, turned.astype(jnp.bfloat16)))
+    passed = move(direct, dx=1)
+    direct = [direct, move(late, dx=1)]
     first = [column, swapped] + direct
     partial = contract(offset, turned, first, (0, 1, 2, 3))
     passed, partial = lax.optimization_barrier((passed, partial))
-    second = [move(part, fc=1) for part in direct]
-    partial = contract(offset, turned, second, (5, 6), partial)
-    result, over = contract(offset, turned, [passed, move(passed, fc=1)], (4, 7), partial, first + second)
+    second = [passed] + [move(part, fc=1) for part in direct]
+    partial = contract(offset, turned, second, (4, 5, 6), partial)
+    result, over = contract(offset, turned, [move(passed, fc=1)], (7,), partial, first + second)
 
     def again(state):
         total, _ = state
@@ -247,7 +277,7 @@
         came.append(move(came[0], dx=1))
         return append(offset, pair + came + [move(part, fc=1) for part in came], total), jnp.int32(0)
 
-    return lax.while_loop(lambda state: state[1] > 0, again, (result, over[0, 0]))[0]
+    return lax.while_loop(lambda state: state[1] > 0, again, (result, over[0]))[0]
 
 
 def solution(mesh):

time: 59 us -> 59.7 us (1.012)
  waiting for transfers between devices: 11.3 us -> 12.6 us
  starting transfers between devices: 33.4 us -> 32.1 us
  local copies, waits for them, and re-layouts: 1.39 us -> 2.2 us
  other arithmetic: 1.02 us -> 0.24 us
  Pallas kernels: 8.07 us -> 8.77 us
    unnamed x2 -> x8, local copies, waits for them, and re-layouts: 0.01 us -> 2.1 us
    ppermute x16, waiting for transfers between devices: 11.3 us -> 12.6 us  [move(): return lax.ppermute(value, ('dp', 'vocab'), pairs)]
    ppermute x16, starting transfers between devices: 33.4 us -> 32.1 us  [move(): return lax.ppermute(value, ('dp', 'vocab'), pairs)]
    dynamic_slice x1 -> x0, local copies, waits for them, and re-layouts: 0.77 us -> none  [payload(): lax.dynamic_slice_in_dim(a, side * columns, columns, 1)]
    select_n x1 -> x0, other arithmetic: 0.67 us -> none  [body(): ids // 512]
where the time goes in v6:
time: 59.7 us; the launch traced here: 59.5 us
  starting transfers between devices  32.1 us (54%)
  waiting for transfers between devices  12.6 us (21%)
  Pallas kernels  8.77 us (15%)
  matrix products  2.79 us (5%)
  local copies, waits for them, and re-layouts  2.2 us (4%)
    ppermute x16, starting transfers between devices, move(): return lax.ppermute(value, ('dp', 'vocab'), pairs)  32.1 us
    ppermute x16, waiting for transfers between devices, move(): return lax.ppermute(value, ('dp', 'vocab'), pairs)  12.6 us
    pallas_call x3, Pallas kernels, contract(): pl.pallas_call(functools.partial(contract_kernel, tuple(spots), len(added...  7.07 us
    unnamed x8, local copies, waits for them, and re-layouts  2.1 us
    dot_general x1, matrix products, body(): lax.dot_general(local, near, dims, preferred_element_type=jnp.float32)  1.43 us
    dot_general x1, matrix products, body(): lax.dot_general(partner, far, dims, preferred_element_type=jnp.float32)  1.35 us
  transfers between devices with their start and end apart: 16, of which 8 were waited for; matrix products, arithmetic and copies ran while one was open for 5% of the time, Pallas kernels for 8%

profile of v6, /device:TPU:1, one launch (start us, length us, event | category | flops | bytes accessed | tf_op | source)
XLA Modules:
  0.0 59.5 jit_solution(6145698229723785067)
XLA Ops:
  0.2 0.7 %copy-done = bf16[4,2304]{1,0:T(4,128)(2,1)S(1)} copy-done((bf16[4,2304]{1,0:T(4,128)(2,1)S(1)}, bf16[4,2304]{1,0:T(4,128)(2,1)}, u32[]{:S(2)}) %copy-start) | copy-done | bytes 18456
  0.9 0.7 %copy-done.1 = bf16[4,2304]{1,0:T(4,128)(2,1)S(1)} copy-done((bf16[4,2304]{1,0:T(4,128)(2,1)S(1)}, bf16[4,2304]{1,0:T(4,128)(2,1)}, u32[]{:S(2)}) %copy-start.1) | copy-done | bytes 18456
  1.6 0.7 %copy-done.2 = s32[4]{0:T(128)S(1)} copy-done((s32[4]{0:T(128)S(1)}, s32[4]{0:T(128)}, u32[]{:S(2)}) %copy-start.2) | copy-done | bytes 40
  2.3 0.6 shard_map.46
  2.9 3.8 %collective-permute-start.8 = (bf16[4,2432]{1,0:T(4,128)(2,1)S(1)}, bf16[4,2432]{1,0:T(4,128)(2,1)S(1)}, u32[]{:S(2)}, u32[]{:S(2)}) collective-permute-start(bf16[4,2432]{1,0:T(4,128)(2,1)S(1)} %get-tuple-element.47), channel_id=1, source_target_pairs={{0,2},{1,3},{2,0},{3,1},{4,6},{5,7},{6,4},{7,5},{8,10},{9,11},{10,... | collective-permute-start | bytes 58376 | tf_op jit(solution)/shard_map/ppermute | solution.py:34
  6.7 0.8 %collective-permute-start.9 = (bf16[4,2432]{1,0:T(4,128)(2,1)S(1)}, bf16[4,2432]{1,0:T(4,128)(2,1)S(1)}, u32[]{:S(2)}, u32[]{:S(2)}) collective-permute-start(bf16[4,2432]{1,0:T(4,128)(2,1)S(1)} %get-tuple-element.48), channel_id=1, source_target_pairs={{0,130},{1,131},{2,128},{3,129},{4,134},{5,135},{6,132},{7,133},{8... | collective-permute-start | bytes 58376 | tf_op jit(solution)/shard_map/ppermute | solution.py:34
  7.9 1.3 %collective-permute-start.16 = (bf16[512,1024]{1,0:T(8,128)(2,1)}, bf16[512,1024]{1,0:T(8,128)(2,1)S(1)}, u32[]{:S(2)}, u32[]{:S(2)}) collective-permute-start(bf16[512,1024]{1,0:T(8,128)(2,1)} %param.8), channel_id=1, source_target_pairs={{0,128},{1,129},{2,130},{3,131},{4,132},{5,133},{6,134},{7,135},{8... | collective-permute-start | bytes 3145736 | tf_op jit(solution)/shard_map/ppermute | solution.py:34
  9.2 1.6 %collective-permute-done.9 = bf16[4,2432]{1,0:T(4,128)(2,1)S(1)} collective-permute-done((bf16[4,2432]{1,0:T(4,128)(2,1)S(1)}, bf16[4,2432]{1,0:T(4,128)(2,1)S(1)}, u32[]{:S(2)}, u32[]{:S(2)}) %collective-permute-start.9) | collective-permute-done | bytes 19488 | tf_op jit(solution)/shard_map/ppermute | solution.py:34
  10.9 2.0 %collective-permute-start.10 = (bf16[16,2432]{1,0:T(8,128)(2,1)S(1)}, bf16[16,2432]{1,0:T(8,128)(2,1)S(1)}, u32[]{:S(2)}, u32[]{:S(2)}) collective-permute-start(bf16[16,2432]{1,0:T(8,128)(2,1)S(1)} %pad_maximum_fusion.refs_0_), channel_id=1, source_target_pairs={{0,1},{1,0},{2,3},{3,2},{4,5},{5,4},{6,7},{7,6},{8,9},{9,8},{10,11... | collective-permute-start | bytes 233480 | tf_op jit(solution)/shard_map/ppermute | solution.py:34
  12.8 0.9 %collective-permute-done.10 = bf16[16,2432]{1,0:T(8,128)(2,1)S(1)} collective-permute-done((bf16[16,2432]{1,0:T(8,128)(2,1)S(1)}, bf16[16,2432]{1,0:T(8,128)(2,1)S(1)}, u32[]{:S(2)}, u32[]{:S(2)}) %collective-permute-start.10) | collective-permute-done | bytes 77856 | tf_op jit(solution)/shard_map/ppermute | solution.py:34
  13.9 6.1 %collective-permute-start.12 = (bf16[32,2432]{1,0:T(8,128)(2,1)S(1)}, bf16[32,2432]{1,0:T(8,128)(2,1)S(1)}, u32[]{:S(2)}, u32[]{:S(2)}) collective-permute-start(bf16[32,2432]{1,0:T(8,128)(2,1)S(1)} %concatenate.8), channel_id=1, source_target_pairs={{0,32},{1,97},{2,34},{3,99},{4,36},{5,101},{6,38},{7,103},{8,40},{... | collective-permute-start | bytes 466952 | tf_op jit(solution)/shard_map/ppermute | solution.py:34
  20.0 0.7 %collective-permute-start.11 = (bf16[32,2432]{1,0:T(8,128)(2,1)S(1)}, bf16[32,2432]{1,0:T(8,128)(2,1)S(1)}, u32[]{:S(2)}, u32[]{:S(2)}) collective-permute-start(bf16[32,2432]{1,0:T(8,128)(2,1)S(1)} %concatenate.8), channel_id=1, source_target_pairs={{0,16},{1,113},{2,18},{3,115},{4,20},{5,117},{6,22},{7,119},{8,24}... | collective-permute-start | bytes 466952 | tf_op jit(solution)/shard_map/ppermute | solution.py:34
  20.7 3.1 %collective-permute-done.12.refs_2_ = bf16[32,2432]{1,0:T(8,128)(2,1)S(1)} collective-permute-done((bf16[32,2432]{1,0:T(8,128)(2,1)S(1)}, bf16[32,2432]{1,0:T(8,128)(2,1)S(1)}, u32[]{:S(2)}, u32[]{:S(2)}) %collective-permute-start.12) | collective-permute-done | bytes 155680 | tf_op jit(solution)/shard_map/ppermute | solution.py:34
  23.8 2.0 %collective-permute-start.13 = (bf16[32,2432]{1,0:T(8,128)(2,1)S(1)}, bf16[32,2432]{1,0:T(8,128)(2,1)S(1)}, u32[]{:S(2)}, u32[]{:S(2)}) collective-permute-start(bf16[32,2432]{1,0:T(8,128)(2,1)S(1)} %collective-permute-done.12.refs_2_), channel_id=1, source_target_pairs={{0,16},{1,113},{2,18},{3,115},{4,20},{5,117},{6,22},{7,119},{8,24}... | collective-permute-start | bytes 466952 | tf_op jit(solution)/shard_map/ppermute | solution.py:34
  25.8 2.1 %collective-permute-start.14 = (bf16[16,2432]{1,0:T(8,128)(2,1)S(1)}, bf16[16,2432]{1,0:T(8,128)(2,1)S(1)}, u32[]{:S(2)}, u32[]{:S(2)}) collective-permute-start(bf16[16,2432]{1,0:T(8,128)(2,1)S(1)} %slice.4), channel_id=1, source_target_pairs={{0,32},{1,97},{2,34},{3,99},{4,36},{5,101},{6,38},{7,103},{8,40},{... | collective-permute-start | bytes 233480 | tf_op jit(solution)/shard_map/ppermute | solution.py:34
  28.0 2.9 %collective-permute-done.14.refs_4_ = bf16[16,2432]{1,0:T(8,128)(2,1)S(1)} collective-permute-done((bf16[16,2432]{1,0:T(8,128)(2,1)S(1)}, bf16[16,2432]{1,0:T(8,128)(2,1)S(1)}, u32[]{:S(2)}, u32[]{:S(2)}) %collective-permute-start.14) | collective-permute-done | bytes 77856 | tf_op jit(solution)/shard_map/ppermute | solution.py:34
  30.8 1.1 %shard_map.47 = (bf16[176,1152]{1,0:T(8,128)(2,1)S(1)}, bf16[112,1152]{1,0:T(8,128)(2,1)S(1)}) custom-call(s32[2]{0:T(128)S(1)} %pad_add_fusion.plane_ref, bf16[16,2432]{1,0:T(8,128)(2,1)S(1)} %pad_maximum_fusion.refs_0_, bf16[32,2432]{1,0:T(8,128)(2,1)S(1)} %collective-permute-done.11.refs_1_, bf16[32,2432]{1,0:T(8,128)(2,1)S(1)} %collective-permute-done.12.refs_2_, ...), custom_call_target="tpu_custom_call" | custom-call | flops 67108864 | bytes 2097152 | tf_op jit(solution)/shard_map/pallas_call | solution.py:146
  32.0 3.5 %collective-permute-start.15 = (bf16[176,1152]{1,0:T(8,128)(2,1)S(1)}, bf16[176,1152]{1,0:T(8,128)(2,1)S(1)}, u32[]{:S(2)}, u32[]{:S(2)}) collective-permute-start(bf16[176,1152]{1,0:T(8,128)(2,1)S(1)} %get-tuple-element.49.refs_0_.refs_2_), channel_id=1, source_target_pairs={{0,1},{1,0},{2,3},{3,2},{4,5},{5,4},{6,7},{7,6},{8,9},{9,8},{10,11... | collective-permute-start | bytes 1216520 | tf_op jit(solution)/shard_map/ppermute | solution.py:34
  35.5 2.6 %collective-permute-start.17 = (bf16[176,1152]{1,0:T(8,128)(2,1)S(1)}, bf16[176,1152]{1,0:T(8,128)(2,1)S(1)}, u32[]{:S(2)}, u32[]{:S(2)}) collective-permute-start(bf16[176,1152]{1,0:T(8,128)(2,1)S(1)} %get-tuple-element.49.refs_0_.refs_2_), channel_id=1, source_target_pairs={{0,4},{1,13},{2,6},{3,15},{4,8},{5,1},{6,10},{7,3},{8,12},{9,5},{1... | collective-permute-start | bytes 1216520 | tf_op jit(solution)/shard_map/ppermute | solution.py:34
  38.1 1.4 %fusion.3 = f32[1024,1024]{1,0:T(8,128)S(1)} fusion(bf16[512,1024]{1,0:T(8,128)(2,1)S(1)} %collective-permute-done.16, s32[1024]{0:T(1024)S(1)} %bitcast.8, pred[1024]{0:T(1024)(128)(4,1)S(1)} %broadcast_compare_fusion.1), kind=kOutput, calls=%fused_computation.4 | convolution fusion | flops 1074790400 | bytes 5248000 | tf_op jit(solution)/shard_map/dot_general | solution.py:262
  39.4 1.4 %add_convert_fusion.logit_ref = bf16[1024,1024]{1,0:T(8,128)(2,1)S(1)} fusion(f32[1024,1024]{1,0:T(8,128)S(1)} %fusion.3, bf16[512,1024]{1,0:T(8,128)(2,1)S(1)} %copy-done.3, s32[1024]{0:T(1024)S(1)} %bitcast.9, pred[1024]{0:T(1024)(128)(4,1)S(1)} %broadcast_compare_fusion), kind=kOutput, calls=%fused_computation | convolution fusion | flops 1076887552 | bytes 7345152 | tf_op jit(solution)/shard_map/dot_general | solution.py:261
  40.9 1.3 %collective-permute-start.19 = (bf16[176,1152]{1,0:T(8,128)(2,1)S(1)}, bf16[176,1152]{1,0:T(8,128)(2,1)S(1)}, u32[]{:S(2)}, u32[]{:S(2)}) collective-permute-start(bf16[176,1152]{1,0:T(8,128)(2,1)S(1)} %collective-permute-done.15.refs_1_.refs_3_), channel_id=1, source_target_pairs={{0,4},{1,13},{2,6},{3,15},{4,8},{5,1},{6,10},{7,3},{8,12},{9,5},{1... | collective-permute-start | bytes 1216520 | tf_op jit(solution)/shard_map/ppermute | solution.py:34
  42.2 0.7 %collective-permute-done.17.refs_2_.refs_4_ = bf16[176,1152]{1,0:T(8,128)(2,1)S(1)} collective-permute-done((bf16[176,1152]{1,0:T(8,128)(2,1)S(1)}, bf16[176,1152]{1,0:T(8,128)(2,1)S(1)}, u32[]{:S(2)}, u32[]{:S(2)}) %collective-permute-start.17) | collective-permute-done | bytes 405536 | tf_op jit(solution)/shard_map/ppermute | solution.py:34
  42.9 3.1 %collective-permute-start.18 = (bf16[176,1152]{1,0:T(8,128)(2,1)S(1)}, bf16[176,1152]{1,0:T(8,128)(2,1)S(1)}, u32[]{:S(2)}, u32[]{:S(2)}) collective-permute-start(bf16[176,1152]{1,0:T(8,128)(2,1)S(1)} %collective-permute-done.17.refs_2_.refs_4_), channel_id=1, source_target_pairs={{0,4},{1,13},{2,6},{3,15},{4,8},{5,1},{6,10},{7,3},{8,12},{9,5},{1... | collective-permute-start | bytes 1216520 | tf_op jit(solution)/shard_map/ppermute | solution.py:34
  46.0 2.0 %collective-permute-done.19.refs_3_.refs_5_ = bf16[176,1152]{1,0:T(8,128)(2,1)S(1)} collective-permute-done((bf16[176,1152]{1,0:T(8,128)(2,1)S(1)}, bf16[176,1152]{1,0:T(8,128)(2,1)S(1)}, u32[]{:S(2)}, u32[]{:S(2)}) %collective-permute-start.19) | collective-permute-done | bytes 405536 | tf_op jit(solution)/shard_map/ppermute | solution.py:34
  48.0 1.2 %collective-permute-start.22 = (bf16[176,1152]{1,0:T(8,128)(2,1)S(1)}, bf16[176,1152]{1,0:T(8,128)(2,1)S(1)}, u32[]{:S(2)}, u32[]{:S(2)}) collective-permute-start(bf16[176,1152]{1,0:T(8,128)(2,1)S(1)} %collective-permute-done.19.refs_3_.refs_5_), channel_id=1, source_target_pairs={{0,1},{1,0},{2,3},{3,2},{4,5},{5,4},{6,7},{7,6},{8,9},{9,8},{10,11... | collective-permute-start | bytes 1216520 | tf_op jit(solution)/shard_map/ppermute | solution.py:34
  49.2 2.2 %shard_map.48.refs_3_ = f32[1024,1152]{1,0:T(8,128)S(1)} custom-call(s32[1]{0:T(128)} %bitcast.1.offset_ref, bf16[1024,1024]{1,0:T(8,128)(2,1)S(1)} %add_convert_fusion.logit_ref, bf16[176,1152]{1,0:T(8,128)(2,1)S(1)} %get-tuple-element.49.refs_0_.refs_2_, bf16[176,1152]{1,0:T(8,128)(2,1)S(1)} %collective-permute-done.15.refs_1_.refs_3_, ...), custom_call_target="tpu_custom_call" | custom-call | flops 1811939328 | bytes 8388608 | tf_op jit(solution)/shard_map/pallas_call | solution.py:203
  51.4 1.0 %collective-permute-done.18.refs_0_.refs_6_ = bf16[176,1152]{1,0:T(8,128)(2,1)S(1)} collective-permute-done((bf16[176,1152]{1,0:T(8,128)(2,1)S(1)}, bf16[176,1152]{1,0:T(8,128)(2,1)S(1)}, u32[]{:S(2)}, u32[]{:S(2)}) %collective-permute-start.18) | collective-permute-done | bytes 405536 | tf_op jit(solution)/shard_map/ppermute | solution.py:34
  52.4 1.5 %collective-permute-start.20 = (bf16[176,1152]{1,0:T(8,128)(2,1)S(1)}, bf16[176,1152]{1,0:T(8,128)(2,1)S(1)}, u32[]{:S(2)}, u32[]{:S(2)}) collective-permute-start(bf16[176,1152]{1,0:T(8,128)(2,1)S(1)} %collective-permute-done.18.refs_0_.refs_6_), channel_id=1, source_target_pairs={{0,1},{1,0},{2,3},{3,2},{4,5},{5,4},{6,7},{7,6},{8,9},{9,8},{10,11... | collective-permute-start | bytes 1216520 | tf_op jit(solution)/shard_map/ppermute | solution.py:34
  53.8 1.6 %shard_map.49.refs_1_ = f32[1024,1152]{1,0:T(8,128)S(1)} custom-call(s32[1]{0:T(128)} %bitcast.1.offset_ref, bf16[1024,1024]{1,0:T(8,128)(2,1)S(1)} %add_convert_fusion.logit_ref, bf16[176,1152]{1,0:T(8,128)(2,1)S(1)} %collective-permute-done.18.refs_0_.refs_6_, bf16[176,1152]{1,0:T(8,128)(2,1)S(1)} %collective-permute-done.21.refs_1_.refs_7_, ...), custom_call_target="tpu_custom_call" | custom-call | flops 1358954496 | bytes 8388608 | tf_op jit(solution)/shard_map/pallas_call | solution.py:203
  55.4 3.3 %shard_map.50 = (f32[1024,1152]{1,0:T(8,128)}, s32[1]{0:T(128)}) custom-call(s32[1]{0:T(128)} %bitcast.1.offset_ref, bf16[1024,1024]{1,0:T(8,128)(2,1)S(1)} %add_convert_fusion.logit_ref, bf16[176,1152]{1,0:T(8,128)(2,1)S(1)} %collective-permute-done.20.refs_0_, f32[1024,1152]{1,0:T(8,128)S(1)} %shard_map.49.refs_1_, ...), custom_call_target="tpu_custom_call" | custom-call | flops 452984832 | bytes 8388608 | tf_op jit(solution)/shard_map/pallas_call | solution.py:203
  58.8 0.6 while.9
  (23 shorter events, 0.8 us)
Async XLA Ops:
  0.2 0.7 %copy-start = (bf16[4,2304]{1,0:T(4,128)(2,1)S(1)}, bf16[4,2304]{1,0:T(4,128)(2,1)}, u32[]{:S(2)}) copy-start(bf16[4,2304]{1,0:T(4,128)(2,1)} %refs_1_.1) | copy-start | bytes 55300
  0.9 0.7 %copy-start.1 = (bf16[4,2304]{1,0:T(4,128)(2,1)S(1)}, bf16[4,2304]{1,0:T(4,128)(2,1)}, u32[]{:S(2)}) copy-start(bf16[4,2304]{1,0:T(4,128)(2,1)} %refs_2_.1) | copy-start | bytes 55300
  1.6 0.7 %copy-start.2 = (s32[4]{0:T(128)S(1)}, s32[4]{0:T(128)}, u32[]{:S(2)}) copy-start(s32[4]{0:T(128)} %refs_0_.1) | copy-start | bytes 52
  2.9 5.0 %collective-permute-start.8 = (bf16[4,2432]{1,0:T(4,128)(2,1)S(1)}, bf16[4,2432]{1,0:T(4,128)(2,1)S(1)}, u32[]{:S(2)}, u32[]{:S(2)}) collective-permute-start(bf16[4,2432]{1,0:T(4,128)(2,1)S(1)} %get-tuple-element.47), channel_id=1, source_target_pairs={{0,2},{1,3},{2,0},{3,1},{4,6},{5,7},{6,4},{7,5},{8,10},{9,11},{10,... | collective-permute-start | bytes 58376 | tf_op jit(solution)/shard_map/ppermute | solution.py:34
  6.7 4.1 %collective-permute-start.9 = (bf16[4,2432]{1,0:T(4,128)(2,1)S(1)}, bf16[4,2432]{1,0:T(4,128)(2,1)S(1)}, u32[]{:S(2)}, u32[]{:S(2)}) collective-permute-start(bf16[4,2432]{1,0:T(4,128)(2,1)S(1)} %get-tuple-element.48), channel_id=1, source_target_pairs={{0,130},{1,131},{2,128},{3,129},{4,134},{5,135},{6,132},{7,133},{8... | collective-permute-start | bytes 58376 | tf_op jit(solution)/shard_map/ppermute | solution.py:34
  7.5 3.4 %collective-permute-start.7 = (bf16[4,2432]{1,0:T(4,128)(2,1)S(1)}, bf16[4,2432]{1,0:T(4,128)(2,1)S(1)}, u32[]{:S(2)}, u32[]{:S(2)}) collective-permute-start(bf16[4,2432]{1,0:T(4,128)(2,1)S(1)} %get-tuple-element.48), channel_id=1, source_target_pairs={{0,128},{1,129},{2,130},{3,131},{4,132},{5,133},{6,134},{7,135},{8... | collective-permute-start | bytes 58376 | tf_op jit(solution)/shard_map/ppermute | solution.py:34
  7.9 30.2 %collective-permute-start.16 = (bf16[512,1024]{1,0:T(8,128)(2,1)}, bf16[512,1024]{1,0:T(8,128)(2,1)S(1)}, u32[]{:S(2)}, u32[]{:S(2)}) collective-permute-start(bf16[512,1024]{1,0:T(8,128)(2,1)} %param.8), channel_id=1, source_target_pairs={{0,128},{1,129},{2,130},{3,131},{4,132},{5,133},{6,134},{7,135},{8... | collective-permute-start | bytes 3145736 | tf_op jit(solution)/shard_map/ppermute | solution.py:34
  10.9 2.9 %collective-permute-start.10 = (bf16[16,2432]{1,0:T(8,128)(2,1)S(1)}, bf16[16,2432]{1,0:T(8,128)(2,1)S(1)}, u32[]{:S(2)}, u32[]{:S(2)}) collective-permute-start(bf16[16,2432]{1,0:T(8,128)(2,1)S(1)} %pad_maximum_fusion.refs_0_), channel_id=1, source_target_pairs={{0,1},{1,0},{2,3},{3,2},{4,5},{5,4},{6,7},{7,6},{8,9},{9,8},{10,11... | collective-permute-start | bytes 233480 | tf_op jit(solution)/shard_map/ppermute | solution.py:34
  13.9 9.9 %collective-permute-start.12 = (bf16[32,2432]{1,0:T(8,128)(2,1)S(1)}, bf16[32,2432]{1,0:T(8,128)(2,1)S(1)}, u32[]{:S(2)}, u32[]{:S(2)}) collective-permute-start(bf16[32,2432]{1,0:T(8,128)(2,1)S(1)} %concatenate.8), channel_id=1, source_target_pairs={{0,32},{1,97},{2,34},{3,99},{4,36},{5,101},{6,38},{7,103},{8,40},{... | collective-permute-start | bytes 466952 | tf_op jit(solution)/shard_map/ppermute | solution.py:34
  20.0 8.0 %collective-permute-start.11 = (bf16[32,2432]{1,0:T(8,128)(2,1)S(1)}, bf16[32,2432]{1,0:T(8,128)(2,1)S(1)}, u32[]{:S(2)}, u32[]{:S(2)}) collective-permute-start(bf16[32,2432]{1,0:T(8,128)(2,1)S(1)} %concatenate.8), channel_id=1, source_target_pairs={{0,16},{1,113},{2,18},{3,115},{4,20},{5,117},{6,22},{7,119},{8,24}... | collective-permute-start | bytes 466952 | tf_op jit(solution)/shard_map/ppermute | solution.py:34
  23.8 7.0 %collective-permute-start.13 = (bf16[32,2432]{1,0:T(8,128)(2,1)S(1)}, bf16[32,2432]{1,0:T(8,128)(2,1)S(1)}, u32[]{:S(2)}, u32[]{:S(2)}) collective-permute-start(bf16[32,2432]{1,0:T(8,128)(2,1)S(1)} %collective-permute-done.12.refs_2_), channel_id=1, source_target_pairs={{0,16},{1,113},{2,18},{3,115},{4,20},{5,117},{6,22},{7,119},{8,24}... | collective-permute-start | bytes 466952 | tf_op jit(solution)/shard_map/ppermute | solution.py:34
  25.8 5.0 %collective-permute-start.14 = (bf16[16,2432]{1,0:T(8,128)(2,1)S(1)}, bf16[16,2432]{1,0:T(8,128)(2,1)S(1)}, u32[]{:S(2)}, u32[]{:S(2)}) collective-permute-start(bf16[16,2432]{1,0:T(8,128)(2,1)S(1)} %slice.4), channel_id=1, source_target_pairs={{0,32},{1,97},{2,34},{3,99},{4,36},{5,101},{6,38},{7,103},{8,40},{... | collective-permute-start | bytes 233480 | tf_op jit(solution)/shard_map/ppermute | solution.py:34
  32.0 6.1 %collective-permute-start.15 = (bf16[176,1152]{1,0:T(8,128)(2,1)S(1)}, bf16[176,1152]{1,0:T(8,128)(2,1)S(1)}, u32[]{:S(2)}, u32[]{:S(2)}) collective-permute-start(bf16[176,1152]{1,0:T(8,128)(2,1)S(1)} %get-tuple-element.49.refs_0_.refs_2_), channel_id=1, source_target_pairs={{0,1},{1,0},{2,3},{3,2},{4,5},{5,4},{6,7},{7,6},{8,9},{9,8},{10,11... | collective-permute-start | bytes 1216520 | tf_op jit(solution)/shard_map/ppermute | solution.py:34
  35.5 7.4 %collective-permute-start.17 = (bf16[176,1152]{1,0:T(8,128)(2,1)S(1)}, bf16[176,1152]{1,0:T(8,128)(2,1)S(1)}, u32[]{:S(2)}, u32[]{:S(2)}) collective-permute-start(bf16[176,1152]{1,0:T(8,128)(2,1)S(1)} %get-tuple-element.49.refs_0_.refs_2_), channel_id=1, source_target_pairs={{0,4},{1,13},{2,6},{3,15},{4,8},{5,1},{6,10},{7,3},{8,12},{9,5},{1... | collective-permute-start | bytes 1216520 | tf_op jit(solution)/shard_map/ppermute | solution.py:34
  38.1 1.4 %copy-start.3 = (bf16[512,1024]{1,0:T(8,128)(2,1)S(1)}, bf16[512,1024]{1,0:T(8,128)(2,1)}, u32[]{:S(2)}) copy-start(bf16[512,1024]{1,0:T(8,128)(2,1)} %param.8) | copy-start | bytes 3145732
  40.9 7.1 %collective-permute-start.19 = (bf16[176,1152]{1,0:T(8,128)(2,1)S(1)}, bf16[176,1152]{1,0:T(8,128)(2,1)S(1)}, u32[]{:S(2)}, u32[]{:S(2)}) collective-permute-start(bf16[176,1152]{1,0:T(8,128)(2,1)S(1)} %collective-permute-done.15.refs_1_.refs_3_), channel_id=1, source_target_pairs={{0,4},{1,13},{2,6},{3,15},{4,8},{5,1},{6,10},{7,3},{8,12},{9,5},{1... | collective-permute-start | bytes 1216520 | tf_op jit(solution)/shard_map/ppermute | solution.py:34
  42.9 9.4 %collective-permute-start.18 = (bf16[176,1152]{1,0:T(8,128)(2,1)S(1)}, bf16[176,1152]{1,0:T(8,128)(2,1)S(1)}, u32[]{:S(2)}, u32[]{:S(2)}) collective-permute-start(bf16[176,1152]{1,0:T(8,128)(2,1)S(1)} %collective-permute-done.17.refs_2_.refs_4_), channel_id=1, source_target_pairs={{0,4},{1,13},{2,6},{3,15},{4,8},{5,1},{6,10},{7,3},{8,12},{9,5},{1... | collective-permute-start | bytes 1216520 | tf_op jit(solution)/shard_map/ppermute | solution.py:34
  46.0 7.8 %collective-permute-start.21 = (bf16[176,1152]{1,0:T(8,128)(2,1)S(1)}, bf16[176,1152]{1,0:T(8,128)(2,1)S(1)}, u32[]{:S(2)}, u32[]{:S(2)}) collective-permute-start(bf16[176,1152]{1,0:T(8,128)(2,1)S(1)} %collective-permute-done.17.refs_2_.refs_4_), channel_id=1, source_target_pairs={{0,1},{1,0},{2,3},{3,2},{4,5},{5,4},{6,7},{7,6},{8,9},{9,8},{10,11... | collective-permute-start | bytes 1216520 | tf_op jit(solution)/shard_map/ppermute | solution.py:34
  48.0 5.8 %collective-permute-start.22 = (bf16[176,1152]{1,0:T(8,128)(2,1)S(1)}, bf16[176,1152]{1,0:T(8,128)(2,1)S(1)}, u32[]{:S(2)}, u32[]{:S(2)}) collective-permute-start(bf16[176,1152]{1,0:T(8,128)(2,1)S(1)} %collective-permute-done.19.refs_3_.refs_5_), channel_id=1, source_target_pairs={{0,1},{1,0},{2,3},{3,2},{4,5},{5,4},{6,7},{7,6},{8,9},{9,8},{10,11... | collective-permute-start | bytes 1216520 | tf_op jit(solution)/shard_map/ppermute | solution.py:34
  52.4 3.1 %collective-permute-start.20 = (bf16[176,1152]{1,0:T(8,128)(2,1)S(1)}, bf16[176,1152]{1,0:T(8,128)(2,1)S(1)}, u32[]{:S(2)}, u32[]{:S(2)}) collective-permute-start(bf16[176,1152]{1,0:T(8,128)(2,1)S(1)} %collective-permute-done.18.refs_0_.refs_6_), channel_id=1, source_target_pairs={{0,1},{1,0},{2,3},{3,2},{4,5},{5,4},{6,7},{7,6},{8,9},{9,8},{10,11... | collective-permute-start | bytes 1216520 | tf_op jit(solution)/shard_map/ppermute | solution.py:34

commit v7 on v5

--- a/solution.py
+++ b/solution.py
@@ -13,7 +13,7 @@
 LANES = 128
 TOKENS = 128
 SLOTS = 32
-CODES = 16
+CODES = 8
 
 
 def coords(vocab):
@@ -125,18 +125,17 @@
     chunks = refs[:pieces]
     out_ref = refs[pieces + added + others]
     rows = logit_ref.shape[0]
-    step = rows // 2
+    blocks = 8 if others else 2
+    step = rows // blocks
     ids = slot_ids(chunks, TOKENS, SLOTS, offset_ref[0])
     copies = []
-    for block in range(2):
+    for block in range(blocks):
         span = slice(block * step, (block + 1) * step)
         row = lax.broadcasted_iota(jnp.int32, (step, ids.shape[1]), 0) + block * step
         onehot = jnp.where(row == ids, 1.0, 0.0).astype(jnp.bfloat16)
-        left = jnp.concatenate([logit_ref[span, s * LANES : (s + 1) * LANES] for s in spots], axis=1)
-        right = jnp.concatenate([c[:TOKENS, :] for c in chunks], axis=0)
-        total = jnp.dot(left, right, preferred_element_type=jnp.float32)
-        right = jnp.concatenate([c[TOKENS : TOKENS + SLOTS, :] for c in chunks], axis=0)
-        total += jnp.dot(onehot, right, preferred_element_type=jnp.float32)
+        left = [logit_ref[span, s * LANES : (s + 1) * LANES] for s in spots]
+        right = jnp.concatenate([c[:TOKENS, :] for c in chunks] + [c[TOKENS : TOKENS + SLOTS, :] for c in chunks], axis=0)
+        total = jnp.dot(jnp.concatenate(left + [onehot], axis=1), right, preferred_element_type=jnp.float32)
         if added:
             total += refs[pieces][span, :]
         if others:
@@ -149,7 +148,7 @@
     if others:
         over = [c[TOKENS + SLOTS : TOKENS + SLOTS + CODES, :LANES] for c in chunks + refs[pieces + added :][:others]]
         over = functools.reduce(jnp.maximum, [c.astype(jnp.float32)[4:5] for c in over])
-        over_ref[...] = jnp.broadcast_to(over, over_ref.shape).astype(jnp.int32)
+        over_ref[0] = jnp.max(over).astype(jnp.int32)
     for copy in copies:
         copy.wait()
 
@@ -159,12 +158,12 @@
     added = [] if partial is None else [partial]
     here = pl.BlockSpec(memory_space=pltpu.VMEM)
     out = jax.ShapeDtypeStruct((rows, columns), jnp.float32)
-    scratch = [pltpu.VMEM((rows, columns), jnp.float32), pltpu.SemaphoreType.DMA((2,))]
+    scratch = [pltpu.VMEM((rows, columns), jnp.float32), pltpu.SemaphoreType.DMA((8,))]
     return pl.pallas_call(
         functools.partial(contract_kernel, tuple(spots), len(added), len(others)),
-        out_shape=[out, jax.ShapeDtypeStruct((8, LANES), jnp.int32)] if others else out,
+        out_shape=[out, jax.ShapeDtypeStruct((1,), jnp.int32)] if others else out,
         in_specs=[pl.BlockSpec(memory_space=pltpu.SMEM)] + [here] * (1 + len(chunks) + len(added) + len(others)),
-        out_specs=[pl.BlockSpec(memory_space=pl.ANY), here] if others else here,
+        out_specs=[pl.BlockSpec(memory_space=pl.ANY), pl.BlockSpec(memory_space=pltpu.SMEM)] if others else here,
         scratch_shapes=scratch if others else [],
         compiler_params=pltpu.CompilerParams(vmem_limit_bytes=16 << 20),
         cost_estimate=pl.CostEstimate(
@@ -205,7 +204,7 @@
     offset = (vocab * logit_grad.shape[1]).astype(jnp.int32).reshape(1)
     ids = token_ids[:, None]
     lane = lax.broadcasted_iota(jnp.int32, (ROWS, LANES), 1)
-    code = jnp.where(lane == 0, ids // 512, jnp.where(lane == 1, (ids // 2) % 256, ids % 2))
+    code = jnp.where(lane == 0, ids >> 9, jnp.where(lane == 1, (ids >> 1) & 255, ids & 1))
     code = jnp.where(lane < 3, code, 0).astype(jnp.bfloat16)
 
     def payload(side):
@@ -226,19 +225,19 @@
     partner = move(held, fd=1)
     column, rest = pack(plane, parts, columns)
     swapped = move(column, fc=1)
-    direct = [move(column, dx=1), move(swapped, dx=1)]
+    direct = move(column, dx=1)
     local, _ = lax.optimization_barrier((logit_grad, swapped))
     turned = lax.dot_general(local, near, dims, preferred_element_type=jnp.float32)
     turned = turned + lax.dot_general(partner, far, dims, preferred_element_type=jnp.float32)
-    turned = turned.astype(jnp.bfloat16)
-    direct[0], turned = lax.optimization_barrier((direct[0], turned))
-    passed = move(direct[0], dx=1)
+    late, turned = lax.optimization_barrier((swapped, turned.astype(jnp.bfloat16)))
+    passed = move(direct, dx=1)
+    direct = [direct, move(late, dx=1)]
     first = [column, swapped] + direct
     partial = contract(offset, turned, first, (0, 1, 2, 3))
     passed, partial = lax.optimization_barrier((passed, partial))
-    second = [move(part, fc=1) for part in direct]
-    partial = contract(offset, turned, second, (5, 6), partial)
-    result, over = contract(offset, turned, [passed, move(passed, fc=1)], (4, 7), partial, first + second)
+    second = [passed] + [move(part, fc=1) for part in direct]
+    partial = contract(offset, turned, second, (4, 5, 6), partial)
+    result, over = contract(offset, turned, [move(passed, fc=1)], (7,), partial, first + second)
 
     def again(state):
         total, _ = state
@@ -247,7 +246,7 @@
         came.append(move(came[0], dx=1))
         return append(offset, pair + came + [move(part, fc=1) for part in came], total), jnp.int32(0)
 
-    return lax.while_loop(lambda state: state[1] > 0, again, (result, over[0, 0]))[0]
+    return lax.while_loop(lambda state: state[1] > 0, again, (result, over[0]))[0]
 
 
 def solution(mesh):

time: 59 us -> 57.9 us (0.981)
  starting transfers between devices: 33.4 us -> 32.1 us
  waiting for transfers between devices: 11.3 us -> 12.2 us
    ppermute x16, starting transfers between devices: 33.4 us -> 32.1 us  [move(): return lax.ppermute(value, ('dp', 'vocab'), pairs)]
    ppermute x16, waiting for transfers between devices: 11.3 us -> 12.2 us  [move(): return lax.ppermute(value, ('dp', 'vocab'), pairs)]
    select_n x1 -> x0, other arithmetic: 0.67 us -> none  [body(): ids // 512]
    shift_right_arithmetic x0 -> x1, other arithmetic: none -> 0.66 us  [body(): ids >> 9]
where the time goes in v7:
time: 57.9 us; the launch traced here: 57.7 us
  starting transfers between devices  32.1 us (55%)
  waiting for transfers between devices  12.2 us (21%)
  Pallas kernels  7.89 us (14%)
  matrix products  2.79 us (5%)
  other arithmetic  1.01 us (2%)
  local copies, waits for them, and re-layouts  0.88 us (2%)
    ppermute x16, starting transfers between devices, move(): return lax.ppermute(value, ('dp', 'vocab'), pairs)  32.1 us
    ppermute x16, waiting for transfers between devices, move(): return lax.ppermute(value, ('dp', 'vocab'), pairs)  12.2 us
    pallas_call x3, Pallas kernels, contract(): pl.pallas_call(functools.partial(contract_kernel, tuple(spots), len(added...  6.77 us
    dot_general x1, matrix products, body(): lax.dot_general(local, near, dims, preferred_element_type=jnp.float32)  1.43 us
    dot_general x1, matrix products, body(): lax.dot_general(partner, far, dims, preferred_element_type=jnp.float32)  1.35 us
  transfers between devices with their start and end apart: 16, of which 8 were waited for; matrix products, arithmetic and copies ran while one was open for 5% of the time, Pallas kernels for 8%

profile of v7, /device:TPU:1, one launch (start us, length us, event | category | flops | bytes accessed | tf_op | source)
XLA Modules:
  0.0 57.7 jit_solution(5202981438373664945)
XLA Ops:
  0.0 0.7 %broadcast_shift-right-arithmetic_fusion = (s32[4]{0:T(128)S(1)}, s32[4]{0:T(128)S(1)}, s32[4]{0:T(128)S(1)}) fusion(s32[4]{0:T(128)} %param.6), kind=kLoop, calls=%fused_computation.104 | loop fusion | flops 16 | bytes 64 | tf_op jit(solution)/shard_map/shift_right_arithmetic | solution.py:207
  0.9 0.8 %constant_dynamic-slice_fusion = (bf16[4,1152]{1,0:T(4,128)(2,1)S(1)}, bf16[4,1152]{1,0:T(4,128)(2,1)S(1)}, bf16[4,1152]{1,0:T(4,128)(2,1)S(1)}, bf16[4,1152]{1,0:T(4,128)(2,1)S(1)}) fusion(bf16[4,2304]{1,0:T(4,128)(2,1)} %param.9, s32[]{:T(128)S(6)} %select_n.383, s32[]{:T(128)S(6)} %select_n.379, bf16[4,2304]{1,0:T(4,128)(2,1)} %param.7), kind=kLoop, calls=%fused_computation.94 | loop fusion | bytes 73736 | tf_op jit(solution)/shard_map/dynamic_slice | solution.py:211
  1.8 3.8 %collective-permute-start.8 = (bf16[4,2432]{1,0:T(4,128)(2,1)S(1)}, bf16[4,2432]{1,0:T(4,128)(2,1)S(1)}, u32[]{:S(2)}, u32[]{:S(2)}) collective-permute-start(bf16[4,2432]{1,0:T(4,128)(2,1)S(1)} %get-tuple-element.43), channel_id=1, source_target_pairs={{0,2},{1,3},{2,0},{3,1},{4,6},{5,7},{6,4},{7,5},{8,10},{9,11},{10,... | collective-permute-start | bytes 58376 | tf_op jit(solution)/shard_map/ppermute | solution.py:34
  5.6 0.8 %collective-permute-start.9 = (bf16[4,2432]{1,0:T(4,128)(2,1)S(1)}, bf16[4,2432]{1,0:T(4,128)(2,1)S(1)}, u32[]{:S(2)}, u32[]{:S(2)}) collective-permute-start(bf16[4,2432]{1,0:T(4,128)(2,1)S(1)} %get-tuple-element.44), channel_id=1, source_target_pairs={{0,130},{1,131},{2,128},{3,129},{4,134},{5,135},{6,132},{7,133},{8... | collective-permute-start | bytes 58376 | tf_op jit(solution)/shard_map/ppermute | solution.py:34
  6.4 0.4 collective-permute-done.8
  6.7 1.3 %collective-permute-start.16 = (bf16[512,1024]{1,0:T(8,128)(2,1)}, bf16[512,1024]{1,0:T(8,128)(2,1)S(1)}, u32[]{:S(2)}, u32[]{:S(2)}) collective-permute-start(bf16[512,1024]{1,0:T(8,128)(2,1)} %param.8), channel_id=1, source_target_pairs={{0,128},{1,129},{2,130},{3,131},{4,132},{5,133},{6,134},{7,135},{8... | collective-permute-start | bytes 3145736 | tf_op jit(solution)/shard_map/ppermute | solution.py:34
  8.1 1.6 %collective-permute-done.9 = bf16[4,2432]{1,0:T(4,128)(2,1)S(1)} collective-permute-done((bf16[4,2432]{1,0:T(4,128)(2,1)S(1)}, bf16[4,2432]{1,0:T(4,128)(2,1)S(1)}, u32[]{:S(2)}, u32[]{:S(2)}) %collective-permute-start.9) | collective-permute-done | bytes 19488 | tf_op jit(solution)/shard_map/ppermute | solution.py:34
  9.8 2.0 %collective-permute-start.10 = (bf16[16,2432]{1,0:T(8,128)(2,1)S(1)}, bf16[16,2432]{1,0:T(8,128)(2,1)S(1)}, u32[]{:S(2)}, u32[]{:S(2)}) collective-permute-start(bf16[16,2432]{1,0:T(8,128)(2,1)S(1)} %pad_maximum_fusion.refs_0_), channel_id=1, source_target_pairs={{0,1},{1,0},{2,3},{3,2},{4,5},{5,4},{6,7},{7,6},{8,9},{9,8},{10,11... | collective-permute-start | bytes 233480 | tf_op jit(solution)/shard_map/ppermute | solution.py:34
  11.7 0.9 %collective-permute-done.10 = bf16[16,2432]{1,0:T(8,128)(2,1)S(1)} collective-permute-done((bf16[16,2432]{1,0:T(8,128)(2,1)S(1)}, bf16[16,2432]{1,0:T(8,128)(2,1)S(1)}, u32[]{:S(2)}, u32[]{:S(2)}) %collective-permute-start.10) | collective-permute-done | bytes 77856 | tf_op jit(solution)/shard_map/ppermute | solution.py:34
  12.6 0.1 concatenate.16
  12.7 6.1 %collective-permute-start.12 = (bf16[32,2432]{1,0:T(8,128)(2,1)S(1)}, bf16[32,2432]{1,0:T(8,128)(2,1)S(1)}, u32[]{:S(2)}, u32[]{:S(2)}) collective-permute-start(bf16[32,2432]{1,0:T(8,128)(2,1)S(1)} %concatenate.16), channel_id=1, source_target_pairs={{0,32},{1,97},{2,34},{3,99},{4,36},{5,101},{6,38},{7,103},{8,40},{... | collective-permute-start | bytes 466952 | tf_op jit(solution)/shard_map/ppermute | solution.py:34
  18.8 0.7 %collective-permute-start.11 = (bf16[32,2432]{1,0:T(8,128)(2,1)S(1)}, bf16[32,2432]{1,0:T(8,128)(2,1)S(1)}, u32[]{:S(2)}, u32[]{:S(2)}) collective-permute-start(bf16[32,2432]{1,0:T(8,128)(2,1)S(1)} %concatenate.16), channel_id=1, source_target_pairs={{0,16},{1,113},{2,18},{3,115},{4,20},{5,117},{6,22},{7,119},{8,24}... | collective-permute-start | bytes 466952 | tf_op jit(solution)/shard_map/ppermute | solution.py:34
  19.6 3.1 %collective-permute-done.12.refs_2_ = bf16[32,2432]{1,0:T(8,128)(2,1)S(1)} collective-permute-done((bf16[32,2432]{1,0:T(8,128)(2,1)S(1)}, bf16[32,2432]{1,0:T(8,128)(2,1)S(1)}, u32[]{:S(2)}, u32[]{:S(2)}) %collective-permute-start.12) | collective-permute-done | bytes 155680 | tf_op jit(solution)/shard_map/ppermute | solution.py:34
  22.7 2.0 %collective-permute-start.13 = (bf16[32,2432]{1,0:T(8,128)(2,1)S(1)}, bf16[32,2432]{1,0:T(8,128)(2,1)S(1)}, u32[]{:S(2)}, u32[]{:S(2)}) collective-permute-start(bf16[32,2432]{1,0:T(8,128)(2,1)S(1)} %collective-permute-done.12.refs_2_), channel_id=1, source_target_pairs={{0,16},{1,113},{2,18},{3,115},{4,20},{5,117},{6,22},{7,119},{8,24}... | collective-permute-start | bytes 466952 | tf_op jit(solution)/shard_map/ppermute | solution.py:34
  24.7 2.1 %collective-permute-start.14 = (bf16[16,2432]{1,0:T(8,128)(2,1)S(1)}, bf16[16,2432]{1,0:T(8,128)(2,1)S(1)}, u32[]{:S(2)}, u32[]{:S(2)}) collective-permute-start(bf16[16,2432]{1,0:T(8,128)(2,1)S(1)} %slice.4), channel_id=1, source_target_pairs={{0,32},{1,97},{2,34},{3,99},{4,36},{5,101},{6,38},{7,103},{8,40},{... | collective-permute-start | bytes 233480 | tf_op jit(solution)/shard_map/ppermute | solution.py:34
  26.8 2.9 %collective-permute-done.14.refs_4_ = bf16[16,2432]{1,0:T(8,128)(2,1)S(1)} collective-permute-done((bf16[16,2432]{1,0:T(8,128)(2,1)S(1)}, bf16[16,2432]{1,0:T(8,128)(2,1)S(1)}, u32[]{:S(2)}, u32[]{:S(2)}) %collective-permute-start.14) | collective-permute-done | bytes 77856 | tf_op jit(solution)/shard_map/ppermute | solution.py:34
  29.7 1.1 %shard_map.46 = (bf16[168,1152]{1,0:T(8,128)(2,1)S(1)}, bf16[104,1152]{1,0:T(8,128)(2,1)S(1)}) custom-call(s32[2]{0:T(128)S(1)} %pad_add_fusion.plane_ref, bf16[16,2432]{1,0:T(8,128)(2,1)S(1)} %pad_maximum_fusion.refs_0_, bf16[32,2432]{1,0:T(8,128)(2,1)S(1)} %collective-permute-done.11.refs_1_, bf16[32,2432]{1,0:T(8,128)(2,1)S(1)} %collective-permute-done.12.refs_2_, ...), custom_call_target="tpu_custom_call" | custom-call | flops 67108864 | bytes 2097152 | tf_op jit(solution)/shard_map/pallas_call | solution.py:104
  30.8 3.5 %collective-permute-start.15 = (bf16[168,1152]{1,0:T(8,128)(2,1)S(1)}, bf16[168,1152]{1,0:T(8,128)(2,1)S(1)}, u32[]{:S(2)}, u32[]{:S(2)}) collective-permute-start(bf16[168,1152]{1,0:T(8,128)(2,1)S(1)} %get-tuple-element.45.refs_0_.refs_2_), channel_id=1, source_target_pairs={{0,1},{1,0},{2,3},{3,2},{4,5},{5,4},{6,7},{7,6},{8,9},{9,8},{10,11... | collective-permute-start | bytes 1161224 | tf_op jit(solution)/shard_map/ppermute | solution.py:34
  34.4 2.6 %collective-permute-start.17 = (bf16[168,1152]{1,0:T(8,128)(2,1)S(1)}, bf16[168,1152]{1,0:T(8,128)(2,1)S(1)}, u32[]{:S(2)}, u32[]{:S(2)}) collective-permute-start(bf16[168,1152]{1,0:T(8,128)(2,1)S(1)} %get-tuple-element.45.refs_0_.refs_2_), channel_id=1, source_target_pairs={{0,4},{1,13},{2,6},{3,15},{4,8},{5,1},{6,10},{7,3},{8,12},{9,5},{1... | collective-permute-start | bytes 1161224 | tf_op jit(solution)/shard_map/ppermute | solution.py:34
  36.9 1.4 %fusion.3 = f32[1024,1024]{1,0:T(8,128)S(1)} fusion(bf16[512,1024]{1,0:T(8,128)(2,1)S(1)} %collective-permute-done.16, s32[1024]{0:T(1024)S(1)} %bitcast.7, pred[1024]{0:T(1024)(128)(4,1)S(1)} %broadcast_compare_fusion.1), kind=kOutput, calls=%fused_computation.4 | convolution fusion | flops 1074790400 | bytes 5248000 | tf_op jit(solution)/shard_map/dot_general | solution.py:231
  38.3 1.4 %add_convert_fusion.logit_ref = bf16[1024,1024]{1,0:T(8,128)(2,1)S(1)} fusion(f32[1024,1024]{1,0:T(8,128)S(1)} %fusion.3, bf16[512,1024]{1,0:T(8,128)(2,1)S(1)} %copy-done, s32[1024]{0:T(1024)S(1)} %bitcast.8, pred[1024]{0:T(1024)(128)(4,1)S(1)} %broadcast_compare_fusion), kind=kOutput, calls=%fused_computation | convolution fusion | flops 1076887552 | bytes 7345152 | tf_op jit(solution)/shard_map/dot_general | solution.py:230
  39.8 1.3 %collective-permute-start.19 = (bf16[168,1152]{1,0:T(8,128)(2,1)S(1)}, bf16[168,1152]{1,0:T(8,128)(2,1)S(1)}, u32[]{:S(2)}, u32[]{:S(2)}) collective-permute-start(bf16[168,1152]{1,0:T(8,128)(2,1)S(1)} %collective-permute-done.15.refs_1_.refs_3_), channel_id=1, source_target_pairs={{0,4},{1,13},{2,6},{3,15},{4,8},{5,1},{6,10},{7,3},{8,12},{9,5},{1... | collective-permute-start | bytes 1161224 | tf_op jit(solution)/shard_map/ppermute | solution.py:34
  41.1 0.5 collective-permute-done.17.refs_2_.refs_4_
  41.6 3.1 %collective-permute-start.18 = (bf16[168,1152]{1,0:T(8,128)(2,1)S(1)}, bf16[168,1152]{1,0:T(8,128)(2,1)S(1)}, u32[]{:S(2)}, u32[]{:S(2)}) collective-permute-start(bf16[168,1152]{1,0:T(8,128)(2,1)S(1)} %collective-permute-done.17.refs_2_.refs_4_), channel_id=1, source_target_pairs={{0,4},{1,13},{2,6},{3,15},{4,8},{5,1},{6,10},{7,3},{8,12},{9,5},{1... | collective-permute-start | bytes 1161224 | tf_op jit(solution)/shard_map/ppermute | solution.py:34
  44.7 2.0 %collective-permute-done.19.refs_3_.refs_5_ = bf16[168,1152]{1,0:T(8,128)(2,1)S(1)} collective-permute-done((bf16[168,1152]{1,0:T(8,128)(2,1)S(1)}, bf16[168,1152]{1,0:T(8,128)(2,1)S(1)}, u32[]{:S(2)}, u32[]{:S(2)}) %collective-permute-start.19) | collective-permute-done | bytes 387104 | tf_op jit(solution)/shard_map/ppermute | solution.py:34
  46.7 1.2 %collective-permute-start.22 = (bf16[168,1152]{1,0:T(8,128)(2,1)S(1)}, bf16[168,1152]{1,0:T(8,128)(2,1)S(1)}, u32[]{:S(2)}, u32[]{:S(2)}) collective-permute-start(bf16[168,1152]{1,0:T(8,128)(2,1)S(1)} %collective-permute-done.19.refs_3_.refs_5_), channel_id=1, source_target_pairs={{0,1},{1,0},{2,3},{3,2},{4,5},{5,4},{6,7},{7,6},{8,9},{9,8},{10,11... | collective-permute-start | bytes 1161224 | tf_op jit(solution)/shard_map/ppermute | solution.py:34
  47.9 2.2 %shard_map.47.refs_3_ = f32[1024,1152]{1,0:T(8,128)S(1)} custom-call(s32[1]{0:T(128)} %bitcast.offset_ref, bf16[1024,1024]{1,0:T(8,128)(2,1)S(1)} %add_convert_fusion.logit_ref, bf16[168,1152]{1,0:T(8,128)(2,1)S(1)} %get-tuple-element.45.refs_0_.refs_2_, bf16[168,1152]{1,0:T(8,128)(2,1)S(1)} %collective-permute-done.15.refs_1_.refs_3_, ...), custom_call_target="tpu_custom_call" | custom-call | flops 1811939328 | bytes 8388608 | tf_op jit(solution)/shard_map/pallas_call | solution.py:162
  50.0 0.8 %collective-permute-done.18.refs_0_.refs_6_ = bf16[168,1152]{1,0:T(8,128)(2,1)S(1)} collective-permute-done((bf16[168,1152]{1,0:T(8,128)(2,1)S(1)}, bf16[168,1152]{1,0:T(8,128)(2,1)S(1)}, u32[]{:S(2)}, u32[]{:S(2)}) %collective-permute-start.18) | collective-permute-done | bytes 387104 | tf_op jit(solution)/shard_map/ppermute | solution.py:34
  50.8 1.5 %collective-permute-start.20 = (bf16[168,1152]{1,0:T(8,128)(2,1)S(1)}, bf16[168,1152]{1,0:T(8,128)(2,1)S(1)}, u32[]{:S(2)}, u32[]{:S(2)}) collective-permute-start(bf16[168,1152]{1,0:T(8,128)(2,1)S(1)} %collective-permute-done.18.refs_0_.refs_6_), channel_id=1, source_target_pairs={{0,1},{1,0},{2,3},{3,2},{4,5},{5,4},{6,7},{7,6},{8,9},{9,8},{10,11... | collective-permute-start | bytes 1161224 | tf_op jit(solution)/shard_map/ppermute | solution.py:34
  52.3 1.6 %shard_map.48.refs_1_ = f32[1024,1152]{1,0:T(8,128)S(1)} custom-call(s32[1]{0:T(128)} %bitcast.offset_ref, bf16[1024,1024]{1,0:T(8,128)(2,1)S(1)} %add_convert_fusion.logit_ref, bf16[168,1152]{1,0:T(8,128)(2,1)S(1)} %collective-permute-done.18.refs_0_.refs_6_, bf16[168,1152]{1,0:T(8,128)(2,1)S(1)} %collective-permute-done.21.refs_1_.refs_7_, ...), custom_call_target="tpu_custom_call" | custom-call | flops 1358954496 | bytes 8388608 | tf_op jit(solution)/shard_map/pallas_call | solution.py:162
  53.9 3.0 %shard_map.49 = (f32[1024,1152]{1,0:T(8,128)}, s32[1]{0:T(128)}) custom-call(s32[1]{0:T(128)} %bitcast.offset_ref, bf16[1024,1024]{1,0:T(8,128)(2,1)S(1)} %add_convert_fusion.logit_ref, bf16[168,1152]{1,0:T(8,128)(2,1)S(1)} %collective-permute-done.20.refs_0_, f32[1024,1152]{1,0:T(8,128)S(1)} %shard_map.48.refs_1_, ...), custom_call_target="tpu_custom_call" | custom-call | flops 452984832 | bytes 8388608 | tf_op jit(solution)/shard_map/pallas_call | solution.py:162
  57.0 0.6 while.9
  (22 shorter events, 0.4 us)
Async XLA Ops:
  1.8 5.0 %collective-permute-start.8 = (bf16[4,2432]{1,0:T(4,128)(2,1)S(1)}, bf16[4,2432]{1,0:T(4,128)(2,1)S(1)}, u32[]{:S(2)}, u32[]{:S(2)}) collective-permute-start(bf16[4,2432]{1,0:T(4,128)(2,1)S(1)} %get-tuple-element.43), channel_id=1, source_target_pairs={{0,2},{1,3},{2,0},{3,1},{4,6},{5,7},{6,4},{7,5},{8,10},{9,11},{10,... | collective-permute-start | bytes 58376 | tf_op jit(solution)/shard_map/ppermute | solution.py:34
  5.6 4.1 %collective-permute-start.9 = (bf16[4,2432]{1,0:T(4,128)(2,1)S(1)}, bf16[4,2432]{1,0:T(4,128)(2,1)S(1)}, u32[]{:S(2)}, u32[]{:S(2)}) collective-permute-start(bf16[4,2432]{1,0:T(4,128)(2,1)S(1)} %get-tuple-element.44), channel_id=1, source_target_pairs={{0,130},{1,131},{2,128},{3,129},{4,134},{5,135},{6,132},{7,133},{8... | collective-permute-start | bytes 58376 | tf_op jit(solution)/shard_map/ppermute | solution.py:34
  6.4 3.4 %collective-permute-start.7 = (bf16[4,2432]{1,0:T(4,128)(2,1)S(1)}, bf16[4,2432]{1,0:T(4,128)(2,1)S(1)}, u32[]{:S(2)}, u32[]{:S(2)}) collective-permute-start(bf16[4,2432]{1,0:T(4,128)(2,1)S(1)} %get-tuple-element.44), channel_id=1, source_target_pairs={{0,128},{1,129},{2,130},{3,131},{4,132},{5,133},{6,134},{7,135},{8... | collective-permute-start | bytes 58376 | tf_op jit(solution)/shard_map/ppermute | solution.py:34
  6.7 30.2 %collective-permute-start.16 = (bf16[512,1024]{1,0:T(8,128)(2,1)}, bf16[512,1024]{1,0:T(8,128)(2,1)S(1)}, u32[]{:S(2)}, u32[]{:S(2)}) collective-permute-start(bf16[512,1024]{1,0:T(8,128)(2,1)} %param.8), channel_id=1, source_target_pairs={{0,128},{1,129},{2,130},{3,131},{4,132},{5,133},{6,134},{7,135},{8... | collective-permute-start | bytes 3145736 | tf_op jit(solution)/shard_map/ppermute | solution.py:34
  9.8 2.9 %collective-permute-start.10 = (bf16[16,2432]{1,0:T(8,128)(2,1)S(1)}, bf16[16,2432]{1,0:T(8,128)(2,1)S(1)}, u32[]{:S(2)}, u32[]{:S(2)}) collective-permute-start(bf16[16,2432]{1,0:T(8,128)(2,1)S(1)} %pad_maximum_fusion.refs_0_), channel_id=1, source_target_pairs={{0,1},{1,0},{2,3},{3,2},{4,5},{5,4},{6,7},{7,6},{8,9},{9,8},{10,11... | collective-permute-start | bytes 233480 | tf_op jit(solution)/shard_map/ppermute | solution.py:34
  12.7 9.9 %collective-permute-start.12 = (bf16[32,2432]{1,0:T(8,128)(2,1)S(1)}, bf16[32,2432]{1,0:T(8,128)(2,1)S(1)}, u32[]{:S(2)}, u32[]{:S(2)}) collective-permute-start(bf16[32,2432]{1,0:T(8,128)(2,1)S(1)} %concatenate.16), channel_id=1, source_target_pairs={{0,32},{1,97},{2,34},{3,99},{4,36},{5,101},{6,38},{7,103},{8,40},{... | collective-permute-start | bytes 466952 | tf_op jit(solution)/shard_map/ppermute | solution.py:34
  18.8 8.0 %collective-permute-start.11 = (bf16[32,2432]{1,0:T(8,128)(2,1)S(1)}, bf16[32,2432]{1,0:T(8,128)(2,1)S(1)}, u32[]{:S(2)}, u32[]{:S(2)}) collective-permute-start(bf16[32,2432]{1,0:T(8,128)(2,1)S(1)} %concatenate.16), channel_id=1, source_target_pairs={{0,16},{1,113},{2,18},{3,115},{4,20},{5,117},{6,22},{7,119},{8,24}... | collective-permute-start | bytes 466952 | tf_op jit(solution)/shard_map/ppermute | solution.py:34
  22.7 7.0 %collective-permute-start.13 = (bf16[32,2432]{1,0:T(8,128)(2,1)S(1)}, bf16[32,2432]{1,0:T(8,128)(2,1)S(1)}, u32[]{:S(2)}, u32[]{:S(2)}) collective-permute-start(bf16[32,2432]{1,0:T(8,128)(2,1)S(1)} %collective-permute-done.12.refs_2_), channel_id=1, source_target_pairs={{0,16},{1,113},{2,18},{3,115},{4,20},{5,117},{6,22},{7,119},{8,24}... | collective-permute-start | bytes 466952 | tf_op jit(solution)/shard_map/ppermute | solution.py:34
  24.7 5.0 %collective-permute-start.14 = (bf16[16,2432]{1,0:T(8,128)(2,1)S(1)}, bf16[16,2432]{1,0:T(8,128)(2,1)S(1)}, u32[]{:S(2)}, u32[]{:S(2)}) collective-permute-start(bf16[16,2432]{1,0:T(8,128)(2,1)S(1)} %slice.4), channel_id=1, source_target_pairs={{0,32},{1,97},{2,34},{3,99},{4,36},{5,101},{6,38},{7,103},{8,40},{... | collective-permute-start | bytes 233480 | tf_op jit(solution)/shard_map/ppermute | solution.py:34
  30.8 6.1 %collective-permute-start.15 = (bf16[168,1152]{1,0:T(8,128)(2,1)S(1)}, bf16[168,1152]{1,0:T(8,128)(2,1)S(1)}, u32[]{:S(2)}, u32[]{:S(2)}) collective-permute-start(bf16[168,1152]{1,0:T(8,128)(2,1)S(1)} %get-tuple-element.45.refs_0_.refs_2_), channel_id=1, source_target_pairs={{0,1},{1,0},{2,3},{3,2},{4,5},{5,4},{6,7},{7,6},{8,9},{9,8},{10,11... | collective-permute-start | bytes 1161224 | tf_op jit(solution)/shard_map/ppermute | solution.py:34
  34.4 7.2 %collective-permute-start.17 = (bf16[168,1152]{1,0:T(8,128)(2,1)S(1)}, bf16[168,1152]{1,0:T(8,128)(2,1)S(1)}, u32[]{:S(2)}, u32[]{:S(2)}) collective-permute-start(bf16[168,1152]{1,0:T(8,128)(2,1)S(1)} %get-tuple-element.45.refs_0_.refs_2_), channel_id=1, source_target_pairs={{0,4},{1,13},{2,6},{3,15},{4,8},{5,1},{6,10},{7,3},{8,12},{9,5},{1... | collective-permute-start | bytes 1161224 | tf_op jit(solution)/shard_map/ppermute | solution.py:34
  36.9 1.4 %copy-start = (bf16[512,1024]{1,0:T(8,128)(2,1)S(1)}, bf16[512,1024]{1,0:T(8,128)(2,1)}, u32[]{:S(2)}) copy-start(bf16[512,1024]{1,0:T(8,128)(2,1)} %param.8) | copy-start | bytes 3145732
  39.8 6.9 %collective-permute-start.19 = (bf16[168,1152]{1,0:T(8,128)(2,1)S(1)}, bf16[168,1152]{1,0:T(8,128)(2,1)S(1)}, u32[]{:S(2)}, u32[]{:S(2)}) collective-permute-start(bf16[168,1152]{1,0:T(8,128)(2,1)S(1)} %collective-permute-done.15.refs_1_.refs_3_), channel_id=1, source_target_pairs={{0,4},{1,13},{2,6},{3,15},{4,8},{5,1},{6,10},{7,3},{8,12},{9,5},{1... | collective-permute-start | bytes 1161224 | tf_op jit(solution)/shard_map/ppermute | solution.py:34
  41.6 9.2 %collective-permute-start.18 = (bf16[168,1152]{1,0:T(8,128)(2,1)S(1)}, bf16[168,1152]{1,0:T(8,128)(2,1)S(1)}, u32[]{:S(2)}, u32[]{:S(2)}) collective-permute-start(bf16[168,1152]{1,0:T(8,128)(2,1)S(1)} %collective-permute-done.17.refs_2_.refs_4_), channel_id=1, source_target_pairs={{0,4},{1,13},{2,6},{3,15},{4,8},{5,1},{6,10},{7,3},{8,12},{9,5},{1... | collective-permute-start | bytes 1161224 | tf_op jit(solution)/shard_map/ppermute | solution.py:34
  44.7 7.6 %collective-permute-start.21 = (bf16[168,1152]{1,0:T(8,128)(2,1)S(1)}, bf16[168,1152]{1,0:T(8,128)(2,1)S(1)}, u32[]{:S(2)}, u32[]{:S(2)}) collective-permute-start(bf16[168,1152]{1,0:T(8,128)(2,1)S(1)} %collective-permute-done.17.refs_2_.refs_4_), channel_id=1, source_target_pairs={{0,1},{1,0},{2,3},{3,2},{4,5},{5,4},{6,7},{7,6},{8,9},{9,8},{10,11... | collective-permute-start | bytes 1161224 | tf_op jit(solution)/shard_map/ppermute | solution.py:34
  46.7 5.6 %collective-permute-start.22 = (bf16[168,1152]{1,0:T(8,128)(2,1)S(1)}, bf16[168,1152]{1,0:T(8,128)(2,1)S(1)}, u32[]{:S(2)}, u32[]{:S(2)}) collective-permute-start(bf16[168,1152]{1,0:T(8,128)(2,1)S(1)} %collective-permute-done.19.refs_3_.refs_5_), channel_id=1, source_target_pairs={{0,1},{1,0},{2,3},{3,2},{4,5},{5,4},{6,7},{7,6},{8,9},{9,8},{10,11... | collective-permute-start | bytes 1161224 | tf_op jit(solution)/shard_map/ppermute | solution.py:34
  50.8 3.1 %collective-permute-start.20 = (bf16[168,1152]{1,0:T(8,128)(2,1)S(1)}, bf16[168,1152]{1,0:T(8,128)(2,1)S(1)}, u32[]{:S(2)}, u32[]{:S(2)}) collective-permute-start(bf16[168,1152]{1,0:T(8,128)(2,1)S(1)} %collective-permute-done.18.refs_0_.refs_6_), channel_id=1, source_target_pairs={{0,1},{1,0},{2,3},{3,2},{4,5},{5,4},{6,7},{7,6},{8,9},{9,8},{10,11... | collective-permute-start | bytes 1161224 | tf_op jit(solution)/shard_map/ppermute | solution.py:34

commit v8 on v7

--- a/solution.py
+++ b/solution.py
@@ -39,10 +39,13 @@
     from_dp = move(other, fd=1)
     from_yh = move(own, fy=1)
     chunk = jnp.concatenate([own, from_dp, from_yh, from_dy], axis=0)
-    both = jnp.concatenate([chunk, move(chunk, fc=1)], axis=0)
+    return chunk, move(chunk, fc=1), from_yh
+
+
+def along_z(mine, both):
     two, one = move(both, dz=2), move(both, dz=1)
     three, four = move(two, dz=1), move(two[:16], dz=2)
-    return [chunk, one, two, three, four], from_yh
+    return [mine, one, two, three, four]
 
 
 STEPS = (0, 0, 1, 1, 2, -1, -1, 2)
@@ -70,11 +73,10 @@
 def pack_kernel(columns, plane_ref, *refs):
     parts, (out_ref, rest_ref) = refs[:-2], refs[-2:]
     side = (((1,), (1,)), ((), ()))
-    out_ref[:TOKENS, :] = jnp.concatenate([p[:, :columns] for p in parts], axis=0)
-    grads = jnp.concatenate([p[:, columns : 2 * columns] for p in parts], axis=0)
-    codes = jnp.concatenate([p[:, 2 * columns :] for p in parts], axis=0)
-    line = lax.broadcasted_iota(jnp.int32, (CODES, LANES), 0)
-    lane = lax.broadcasted_iota(jnp.int32, (CODES, LANES), 1)
+    grads = jnp.concatenate([p[:, :columns] for p in parts], axis=0)
+    codes = jnp.concatenate([p[:, columns:] for p in parts], axis=0)
+    line = lax.broadcasted_iota(jnp.int32, (2 * CODES, LANES), 0)
+    lane = lax.broadcasted_iota(jnp.int32, (2 * CODES, LANES), 1)
     pick = jnp.where(line == lane, 1.0, 0.0).astype(jnp.bfloat16)
     turned = lax.dot_general(pick, codes, side, preferred_element_type=jnp.float32)
     top = turned[:1].astype(jnp.int32)
@@ -83,24 +85,24 @@
     row = lax.broadcasted_iota(jnp.int32, (TOKENS, TOKENS), 0)
     col = lax.broadcasted_iota(jnp.int32, (TOKENS, TOKENS), 1)
     before = jnp.where(row < col, 1.0, 0.0).astype(jnp.bfloat16)
-    many = jnp.broadcast_to(found, (CODES, TOKENS)).astype(jnp.bfloat16)
+    many = jnp.broadcast_to(found, (2 * CODES, TOKENS)).astype(jnp.bfloat16)
     rank = jnp.dot(many, before, preferred_element_type=jnp.float32)[:1].astype(jnp.int32)
     rank = jnp.where(match, rank, -1)
     over = jnp.max(jnp.where(rank >= SLOTS, 1.0, 0.0), axis=1, keepdims=True)
     turned = jnp.where(line == 3, 1.0, turned).astype(jnp.bfloat16)
-    for ref, start, first, slots in ((out_ref, TOKENS, 0, SLOTS), (rest_ref, 0, SLOTS, TOKENS - SLOTS)):
+    for ref, first, slots in ((out_ref, 0, SLOTS), (rest_ref, SLOTS, TOKENS - SLOTS)):
         chosen = jnp.where(rank == row[:slots] + first, 1.0, 0.0).astype(jnp.bfloat16)
-        ref[start : start + slots, :] = jnp.dot(chosen, grads, preferred_element_type=jnp.float32).astype(jnp.bfloat16)
+        ref[:slots, :] = jnp.dot(chosen, grads, preferred_element_type=jnp.float32).astype(jnp.bfloat16)
         chosen = jnp.where(rank == row + first, 1.0, 0.0).astype(jnp.bfloat16)
         code = lax.dot_general(turned, chosen, side, preferred_element_type=jnp.float32)
-        code = jnp.where(line == 4, over, code).astype(jnp.bfloat16)
-        ref[start + slots : start + slots + CODES, :LANES] = code
-        ref[start + slots : start + slots + CODES, LANES:] = jnp.zeros((CODES, columns - LANES), jnp.bfloat16)
+        code = jnp.where(line == 4, over, code)[:CODES].astype(jnp.bfloat16)
+        ref[slots : slots + CODES, :LANES] = code
+        ref[slots : slots + CODES, LANES:] = jnp.zeros((CODES, columns - LANES), jnp.bfloat16)
 
 
 def pack(plane, parts, columns):
     here = pl.BlockSpec(memory_space=pltpu.VMEM)
-    shapes = (TOKENS + SLOTS + CODES, TOKENS - SLOTS + CODES)
+    shapes = (SLOTS + CODES, TOKENS - SLOTS + CODES)
     return pl.pallas_call(
         functools.partial(pack_kernel, columns),
         out_shape=[jax.ShapeDtypeStruct((rows, columns), jnp.bfloat16) for rows in shapes],
@@ -111,71 +113,77 @@
     )(plane, *parts)
 
 
-def slot_ids(chunks, first, slots, offset):
+def blocks_of(packed, slots):
+    size = slots + CODES
+    return [p.at[k * size : (k + 1) * size, :] for p in packed for k in range(p.shape[0] // size)]
+
+
+def slot_ids(packs, slots, offset):
     ids = []
-    for c in chunks:
-        code = c[first + slots : first + slots + CODES, :LANES].astype(jnp.float32)
+    for c in packs:
+        code = c[slots : slots + CODES, :LANES].astype(jnp.float32)
         row = (code[:1] * 512.0 + code[1:2] * 2.0 + code[2:3]).astype(jnp.int32) - offset
         ids.append(jnp.where(code[3:4] > 0.5, row, -1)[:, :slots])
     return jnp.concatenate(ids, axis=1)
 
 
-def contract_kernel(spots, added, others, offset_ref, logit_ref, *refs):
+def contract_kernel(spots, grads, added, others, offset_ref, logit_ref, *refs):
     pieces = len(spots)
-    chunks = refs[:pieces]
-    out_ref = refs[pieces + added + others]
+    chunks, packs = refs[:pieces], blocks_of(refs[pieces : pieces + grads], SLOTS)
+    rest = refs[pieces + grads :]
+    out_ref = rest[added + others]
     rows = logit_ref.shape[0]
     blocks = 8 if others else 2
     step = rows // blocks
-    ids = slot_ids(chunks, TOKENS, SLOTS, offset_ref[0])
+    ids = slot_ids(packs, SLOTS, offset_ref[0])
     copies = []
     for block in range(blocks):
         span = slice(block * step, (block + 1) * step)
         row = lax.broadcasted_iota(jnp.int32, (step, ids.shape[1]), 0) + block * step
         onehot = jnp.where(row == ids, 1.0, 0.0).astype(jnp.bfloat16)
         left = [logit_ref[span, s * LANES : (s + 1) * LANES] for s in spots]
-        right = jnp.concatenate([c[:TOKENS, :] for c in chunks] + [c[TOKENS : TOKENS + SLOTS, :] for c in chunks], axis=0)
+        right = jnp.concatenate([c[...] for c in chunks] + [p[:SLOTS, :] for p in packs], axis=0)
         total = jnp.dot(jnp.concatenate(left + [onehot], axis=1), right, preferred_element_type=jnp.float32)
         if added:
-            total += refs[pieces][span, :]
+            total += rest[0][span, :]
         if others:
-            over_ref, stage, sems = refs[pieces + added + others + 1 :]
+            over_ref, stage, sems = rest[added + others + 1 :]
             stage[span, :] = total
             copies.append(pltpu.make_async_copy(stage.at[span, :], out_ref.at[span, :], sems.at[block]))
             copies[-1].start()
         else:
             out_ref[span, :] = total
     if others:
-        over = [c[TOKENS + SLOTS : TOKENS + SLOTS + CODES, :LANES] for c in chunks + refs[pieces + added :][:others]]
+        over = [c[SLOTS : SLOTS + CODES, :LANES] for c in packs + blocks_of(rest[added : added + others], SLOTS)]
         over = functools.reduce(jnp.maximum, [c.astype(jnp.float32)[4:5] for c in over])
         over_ref[0] = jnp.max(over).astype(jnp.int32)
     for copy in copies:
         copy.wait()
 
 
-def contract(offset, logits, chunks, spots, partial=None, others=()):
+def contract(offset, logits, chunks, spots, grads, partial=None, others=()):
     rows, columns = logits.shape[0], chunks[0].shape[1]
     added = [] if partial is None else [partial]
     here = pl.BlockSpec(memory_space=pltpu.VMEM)
     out = jax.ShapeDtypeStruct((rows, columns), jnp.float32)
-    scratch = [pltpu.VMEM((rows, columns), jnp.float32), pltpu.SemaphoreType.DMA((8,))]
+    operands = [logits, *chunks, *grads, *added, *others]
     return pl.pallas_call(
-        functools.partial(contract_kernel, tuple(spots), len(added), len(others)),
+        functools.partial(contract_kernel, tuple(spots), len(grads), len(added), len(others)),
         out_shape=[out, jax.ShapeDtypeStruct((1,), jnp.int32)] if others else out,
-        in_specs=[pl.BlockSpec(memory_space=pltpu.SMEM)] + [here] * (1 + len(chunks) + len(added) + len(others)),
+        in_specs=[pl.BlockSpec(memory_space=pltpu.SMEM)] + [here] * len(operands),
         out_specs=[pl.BlockSpec(memory_space=pl.ANY), pl.BlockSpec(memory_space=pltpu.SMEM)] if others else here,
-        scratch_shapes=scratch if others else [],
+        scratch_shapes=[pltpu.VMEM((rows, columns), jnp.float32), pltpu.SemaphoreType.DMA((8,))] if others else [],
         compiler_params=pltpu.CompilerParams(vmem_limit_bytes=16 << 20),
         cost_estimate=pl.CostEstimate(
             flops=3 * rows * len(spots) * LANES * columns, bytes_accessed=8 << 20, transcendentals=0
         ),
-    )(offset, logits, *chunks, *added, *others)
+    )(offset, *operands)
 
 
 def append_kernel(pieces, slots, offset_ref, *refs):
     chunks, base_ref, out_ref = refs[:pieces], refs[pieces], refs[pieces + 1]
     rows = out_ref.shape[0]
-    ids = slot_ids(chunks, 0, slots, offset_ref[0] + pl.program_id(0) * rows)
+    ids = slot_ids(chunks, slots, offset_ref[0] + pl.program_id(0) * rows)
     row = lax.broadcasted_iota(jnp.int32, (rows, ids.shape[1]), 0)
     onehot = jnp.where(row == ids, 1.0, 0.0).astype(jnp.bfloat16)
     right = jnp.concatenate([c[:slots, :] for c in chunks], axis=0)
@@ -220,24 +228,37 @@
     )
     spot = lax.broadcasted_iota(jnp.int32, (logit_grad.shape[0], 1), 0)
     near, far = (((spot == token) & (away == side)).astype(jnp.bfloat16) for side in (0, 1))
-    parts, early = gather_column(own, other)
-    held, _ = lax.optimization_barrier((logit_grad, early))
-    partner = move(held, fd=1)
-    column, rest = pack(plane, parts, columns)
+    chunk, traded, early = gather_column(own, other)
+    half = logit_grad.shape[0] // 2
+    *held, _ = lax.optimization_barrier((logit_grad[:half], logit_grad[half:], early))
+    partner = [move(held[0], fd=1)]
+    mine = chunk[:, :columns], chunk[:, columns:]
+    both = [jnp.concatenate(pair, axis=0) for pair in zip(mine, (traded[:, :columns], traded[:, columns:]))]
+    hid, grads = along_z(mine[0], both[0]), along_z(mine[1], both[1])
+    hid[4], grads[1], grads[2], partner[0] = lax.optimization_barrier((hid[4], grads[1], grads[2], partner[0]))
+    column = jnp.concatenate(hid, axis=0)
+    held[1], partner[0] = lax.optimization_barrier((held[1], partner[0]))
+    partner.append(move(held[1], fd=1))
     swapped = move(column, fc=1)
-    direct = move(column, dx=1)
-    local, _ = lax.optimization_barrier((logit_grad, swapped))
+    grads[0], swapped = lax.optimization_barrier((grads[0], swapped))
+    packed, rest = pack(plane, grads, columns)
+    direct = [move(column, dx=1), move(swapped, dx=1)]
+    passed = move(direct[0], dx=1)
+    pairs = [jnp.concatenate([packed, move(packed, fc=1)], axis=0)]
+    pairs.append(move(pairs[0], dx=1))
+    lone = move(pairs[1][: SLOTS + CODES], dx=1)
+    local, partner[0], _ = lax.optimization_barrier((logit_grad, partner[0], swapped))
     turned = lax.dot_general(local, near, dims, preferred_element_type=jnp.float32)
-    turned = turned + lax.dot_general(partner, far, dims, preferred_element_type=jnp.float32)
-    late, turned = lax.optimization_barrier((swapped, turned.astype(jnp.bfloat16)))
-    passed = move(direct, dx=1)
-    direct = [direct, move(late, dx=1)]
-    first = [column, swapped] + direct
-    partial = contract(offset, turned, first, (0, 1, 2, 3))
-    passed, partial = lax.optimization_barrier((passed, partial))
-    second = [passed] + [move(part, fc=1) for part in direct]
-    partial = contract(offset, turned, second, (4, 5, 6), partial)
-    result, over = contract(offset, turned, [move(passed, fc=1)], (7,), partial, first + second)
+    for part, spots in zip(partner, (far[:half], far[half:])):
+        turned = turned + lax.dot_general(part, spots, dims, preferred_element_type=jnp.float32)
+    *came, turned = lax.optimization_barrier((*direct, pairs[1], turned.astype(jnp.bfloat16)))
+    partial = contract(offset, turned, [column, swapped] + direct, (0, 1, 2, 3), pairs[:1])
+    passed, lone, partial = lax.optimization_barrier((passed, lone, partial))
+    came = [move(part, fc=1) for part in came]
+    pairs.append(came.pop())
+    partial = contract(offset, turned, [passed] + came, (4, 5, 6), pairs[1:], partial)
+    lone = [lone, move(lone, fc=1)]
+    result, over = contract(offset, turned, [move(passed, fc=1)], (7,), lone, partial, pairs)
 
     def again(state):
         total, _ = state

time: 57.9 us -> 64.3 us (1.11)
  starting transfers between devices: 32.1 us -> 37.3 us
  waiting for transfers between devices: 12.2 us -> 10.9 us
  local copies, waits for them, and re-layouts: 0.88 us -> 2.15 us
    ppermute x16 -> x26, starting transfers between devices: 32.1 us -> 37.3 us  [move(): return lax.ppermute(value, ('dp', 'vocab'), pairs)]
    ppermute x16 -> x26, waiting for transfers between devices: 12.2 us -> 10.9 us  [move(): return lax.ppermute(value, ('dp', 'vocab'), pairs)]
    slice x1 -> x8, local copies, waits for them, and re-layouts: 0.01 us -> 1.3 us  [the longest x1 1.27 us: body(): logit_grad[half:]]
    dot_general x1 -> x2, matrix products: 1.35 us -> 1.61 us  [body(): lax.dot_general(part, spots, dims, preferred_element_type=jnp.float32)]
  transfers between devices with their start and end apart: 16 -> 26, of which waited for: 8 -> 6; matrix products, arithmetic and copies ran while one was open for 5% -> 7% of each run, Pallas kernels for 8% -> 8%
where the time goes in v8:
time: 64.3 us; the launch traced here: 63.8 us
  starting transfers between devices  37.3 us (58%)
  waiting for transfers between devices  10.9 us (17%)
  Pallas kernels  7.99 us (12%)
  matrix products  2.96 us (5%)
  local copies, waits for them, and re-layouts  2.15 us (3%)
  other arithmetic  1.48 us (2%)
    ppermute x26, starting transfers between devices, move(): return lax.ppermute(value, ('dp', 'vocab'), pairs)  37.3 us
    ppermute x26, waiting for transfers between devices, move(): return lax.ppermute(value, ('dp', 'vocab'), pairs)  10.9 us
    pallas_call x3, Pallas kernels, contract(): pl.pallas_call(functools.partial(contract_kernel, tuple(spots), len(grads...  6.89 us
    dot_general x2, matrix products, body(): lax.dot_general(part, spots, dims, preferred_element_type=jnp.float32)  1.61 us
    dot_general x1, matrix products, body(): lax.dot_general(local, near, dims, preferred_element_type=jnp.float32)  1.35 us
  transfers between devices with their start and end apart: 26, of which 6 were waited for; matrix products, arithmetic and copies ran while one was open for 7% of the time, Pallas kernels for 8%

profile of v8, /device:TPU:1, one launch (start us, length us, event | category | flops | bytes accessed | tf_op | source)
XLA Modules:
  0.0 63.8 jit_solution(1638326998299786265)
XLA Ops:
  0.0 0.7 %broadcast_shift-right-arithmetic_fusion = (s32[4]{0:T(128)S(1)}, s32[4]{0:T(128)S(1)}, s32[4]{0:T(128)S(1)}) fusion(s32[4]{0:T(128)} %param.6), kind=kLoop, calls=%fused_computation.114 | loop fusion | flops 16 | bytes 64 | tf_op jit(solution)/shard_map/shift_right_arithmetic | solution.py:215
  1.0 0.8 %constant_dynamic-slice_fusion = (bf16[4,1152]{1,0:T(4,128)(2,1)S(1)}, bf16[4,1152]{1,0:T(4,128)(2,1)S(1)}, bf16[4,1152]{1,0:T(4,128)(2,1)S(1)}, bf16[4,1152]{1,0:T(4,128)(2,1)S(1)}) fusion(bf16[4,2304]{1,0:T(4,128)(2,1)} %param.9, s32[]{:T(128)S(6)} %select_n.383, s32[]{:T(128)S(6)} %select_n.379, bf16[4,2304]{1,0:T(4,128)(2,1)} %param.7), kind=kLoop, calls=%fused_computation.104 | loop fusion | bytes 73736 | tf_op jit(solution)/shard_map/dynamic_slice | solution.py:219
  1.8 2.2 %collective-permute-start.7 = (bf16[4,2432]{1,0:T(4,128)(2,1)S(1)}, bf16[4,2432]{1,0:T(4,128)(2,1)S(1)}, u32[]{:S(2)}, u32[]{:S(2)}) collective-permute-start(bf16[4,2432]{1,0:T(4,128)(2,1)S(1)} %get-tuple-element.56), channel_id=1, source_target_pairs={{0,128},{1,129},{2,130},{3,131},{4,132},{5,133},{6,134},{7,135},{8... | collective-permute-start | bytes 58376 | tf_op jit(solution)/shard_map/ppermute | solution.py:34
  4.1 1.9 %collective-permute-start.9 = (bf16[4,2432]{1,0:T(4,128)(2,1)S(1)}, bf16[4,2432]{1,0:T(4,128)(2,1)S(1)}, u32[]{:S(2)}, u32[]{:S(2)}) collective-permute-start(bf16[4,2432]{1,0:T(4,128)(2,1)S(1)} %get-tuple-element.56), channel_id=1, source_target_pairs={{0,130},{1,131},{2,128},{3,129},{4,134},{5,135},{6,132},{7,133},{8... | collective-permute-start | bytes 58376 | tf_op jit(solution)/shard_map/ppermute | solution.py:34
  6.0 0.7 %collective-permute-start.8 = (bf16[4,2432]{1,0:T(4,128)(2,1)S(1)}, bf16[4,2432]{1,0:T(4,128)(2,1)S(1)}, u32[]{:S(2)}, u32[]{:S(2)}) collective-permute-start(bf16[4,2432]{1,0:T(4,128)(2,1)S(1)} %get-tuple-element.55), channel_id=1, source_target_pairs={{0,2},{1,3},{2,0},{3,1},{4,6},{5,7},{6,4},{7,5},{8,10},{9,11},{10,... | collective-permute-start | bytes 58376 | tf_op jit(solution)/shard_map/ppermute | solution.py:34
  6.7 1.3 %fusion.29 = (bf16[256,1024]{1,0:T(8,128)(2,1)S(1)}, bf16[256,1024]{1,0:T(8,128)(2,1)S(1)}) fusion(bf16[512,1024]{1,0:T(8,128)(2,1)} %param.8), kind=kLoop, calls=%fused_computation.115 | loop fusion | bytes 2097152 | tf_op jit(solution)/shard_map/slice | solution.py:233
  8.0 2.1 %collective-permute-done.8 = bf16[4,2432]{1,0:T(4,128)(2,1)S(1)} collective-permute-done((bf16[4,2432]{1,0:T(4,128)(2,1)S(1)}, bf16[4,2432]{1,0:T(4,128)(2,1)S(1)}, u32[]{:S(2)}, u32[]{:S(2)}) %collective-permute-start.8) | collective-permute-done | bytes 19488 | tf_op jit(solution)/shard_map/ppermute | solution.py:34
  10.1 2.5 %collective-permute-start.10 = (bf16[16,2432]{1,0:T(8,128)(2,1)S(1)}, bf16[16,2432]{1,0:T(8,128)(2,1)S(1)}, u32[]{:S(2)}, u32[]{:S(2)}) collective-permute-start(bf16[16,2432]{1,0:T(8,128)(2,1)S(1)} %pad_maximum_fusion.1), channel_id=1, source_target_pairs={{0,1},{1,0},{2,3},{3,2},{4,5},{5,4},{6,7},{7,6},{8,9},{9,8},{10,11... | collective-permute-start | bytes 233480 | tf_op jit(solution)/shard_map/ppermute | solution.py:34
  13.5 6.1 %collective-permute-start.12 = (bf16[32,1152]{1,0:T(8,128)(2,1)S(1)}, bf16[32,1152]{1,0:T(8,128)(2,1)S(1)}, u32[]{:S(2)}, u32[]{:S(2)}) collective-permute-start(bf16[32,1152]{1,0:T(8,128)(2,1)S(1)} %pad_maximum_fusion.2), channel_id=1, source_target_pairs={{0,32},{1,97},{2,34},{3,99},{4,36},{5,101},{6,38},{7,103},{8,40},{... | collective-permute-start | bytes 221192 | tf_op jit(solution)/shard_map/ppermute | solution.py:34
  19.6 0.7 %collective-permute-start.11 = (bf16[32,1152]{1,0:T(8,128)(2,1)S(1)}, bf16[32,1152]{1,0:T(8,128)(2,1)S(1)}, u32[]{:S(2)}, u32[]{:S(2)}) collective-permute-start(bf16[32,1152]{1,0:T(8,128)(2,1)S(1)} %pad_maximum_fusion.2), channel_id=1, source_target_pairs={{0,16},{1,113},{2,18},{3,115},{4,20},{5,117},{6,22},{7,119},{8,24}... | collective-permute-start | bytes 221192 | tf_op jit(solution)/shard_map/ppermute | solution.py:34
  20.4 0.8 %collective-permute-start.15 = (bf16[32,1280]{1,0:T(8,128)(2,1)S(1)}, bf16[32,1280]{1,0:T(8,128)(2,1)S(1)}, u32[]{:S(2)}, u32[]{:S(2)}) collective-permute-start(bf16[32,1280]{1,0:T(8,128)(2,1)S(1)} %pad_maximum_fusion), channel_id=1, source_target_pairs={{0,16},{1,113},{2,18},{3,115},{4,20},{5,117},{6,22},{7,119},{8,24}... | collective-permute-start | bytes 245768 | tf_op jit(solution)/shard_map/ppermute | solution.py:34
  21.7 2.9 %collective-permute-start.13 = (bf16[32,1152]{1,0:T(8,128)(2,1)S(1)}, bf16[32,1152]{1,0:T(8,128)(2,1)S(1)}, u32[]{:S(2)}, u32[]{:S(2)}) collective-permute-start(bf16[32,1152]{1,0:T(8,128)(2,1)S(1)} %collective-permute-done.12), channel_id=1, source_target_pairs={{0,16},{1,113},{2,18},{3,115},{4,20},{5,117},{6,22},{7,119},{8,24}... | collective-permute-start | bytes 221192 | tf_op jit(solution)/shard_map/ppermute | solution.py:34
  24.7 1.3 %collective-permute-start.14 = (bf16[16,1152]{1,0:T(8,128)(2,1)S(1)}, bf16[16,1152]{1,0:T(8,128)(2,1)S(1)}, u32[]{:S(2)}, u32[]{:S(2)}) collective-permute-start(bf16[16,1152]{1,0:T(8,128)(2,1)S(1)} %slice.46), channel_id=1, source_target_pairs={{0,32},{1,97},{2,34},{3,99},{4,36},{5,101},{6,38},{7,103},{8,40},{... | collective-permute-start | bytes 110600 | tf_op jit(solution)/shard_map/ppermute | solution.py:34
  26.4 2.3 %collective-permute-done.14 = bf16[16,1152]{1,0:T(8,128)(2,1)S(1)} collective-permute-done((bf16[16,1152]{1,0:T(8,128)(2,1)S(1)}, bf16[16,1152]{1,0:T(8,128)(2,1)S(1)}, u32[]{:S(2)}, u32[]{:S(2)}) %collective-permute-start.14) | collective-permute-done | bytes 36896 | tf_op jit(solution)/shard_map/ppermute | solution.py:34
  28.7 2.5 %collective-permute-start.19 = (bf16[128,1152]{1,0:T(8,128)(2,1)S(1)}, bf16[128,1152]{1,0:T(8,128)(2,1)S(1)}, u32[]{:S(2)}, u32[]{:S(2)}) collective-permute-start(bf16[128,1152]{1,0:T(8,128)(2,1)S(1)} %constant_dynamic-update-slice_fusion.refs_0_), channel_id=1, source_target_pairs={{0,1},{1,0},{2,3},{3,2},{4,5},{5,4},{6,7},{7,6},{8,9},{9,8},{10,11... | collective-permute-start | bytes 884744 | tf_op jit(solution)/shard_map/ppermute | solution.py:34
  31.6 2.0 %collective-permute-start.22 = (bf16[16,1280]{1,0:T(8,128)(2,1)S(1)}, bf16[16,1280]{1,0:T(8,128)(2,1)S(1)}, u32[]{:S(2)}, u32[]{:S(2)}) collective-permute-start(bf16[16,1280]{1,0:T(8,128)(2,1)S(1)} %slice.49), channel_id=1, source_target_pairs={{0,32},{1,97},{2,34},{3,99},{4,36},{5,101},{6,38},{7,103},{8,40},{... | collective-permute-start | bytes 122888 | tf_op jit(solution)/shard_map/ppermute | solution.py:34
  33.6 1.3 %collective-permute-start.21 = (bf16[32,1280]{1,0:T(8,128)(2,1)S(1)}, bf16[32,1280]{1,0:T(8,128)(2,1)S(1)}, u32[]{:S(2)}, u32[]{:S(2)}) collective-permute-start(bf16[32,1280]{1,0:T(8,128)(2,1)S(1)} %collective-permute-done.16.refs_2_), channel_id=1, source_target_pairs={{0,16},{1,113},{2,18},{3,115},{4,20},{5,117},{6,22},{7,119},{8,24}... | collective-permute-start | bytes 245768 | tf_op jit(solution)/shard_map/ppermute | solution.py:34
  34.9 2.5 %collective-permute-start.18 = (bf16[128,1152]{1,0:T(8,128)(2,1)S(1)}, bf16[128,1152]{1,0:T(8,128)(2,1)S(1)}, u32[]{:S(2)}, u32[]{:S(2)}) collective-permute-start(bf16[128,1152]{1,0:T(8,128)(2,1)S(1)} %constant_dynamic-update-slice_fusion.refs_0_), channel_id=1, source_target_pairs={{0,4},{1,13},{2,6},{3,15},{4,8},{5,1},{6,10},{7,3},{8,12},{9,5},{1... | collective-permute-start | bytes 884744 | tf_op jit(solution)/shard_map/ppermute | solution.py:34
  37.3 0.6 collective-permute-start.25
  38.5 1.1 %shard_map.46 = (bf16[40,1152]{1,0:T(8,128)(2,1)S(1)}, bf16[104,1152]{1,0:T(8,128)(2,1)S(1)}) custom-call(s32[2]{0:T(128)S(1)} %pad_add_fusion.plane_ref, bf16[16,1280]{1,0:T(8,128)(2,1)S(1)} %slice.47.refs_0_, bf16[32,1280]{1,0:T(8,128)(2,1)S(1)} %collective-permute-done.15.refs_1_, bf16[32,1280]{1,0:T(8,128)(2,1)S(1)} %collective-permute-done.16.refs_2_, ...), custom_call_target="tpu_custom_call" | custom-call | flops 67108864 | bytes 2097152 | tf_op jit(solution)/shard_map/pallas_call | solution.py:106
  39.8 1.4 %fusion.2 = f32[1024,1024]{1,0:T(8,128)S(1)} fusion(bf16[512,1024]{1,0:T(8,128)(2,1)S(1)} %copy-done, s32[1024]{0:T(1024)S(1)} %bitcast.9, pred[1024]{0:T(1024)(128)(4,1)S(1)} %broadcast_compare_fusion), kind=kOutput, calls=%fused_computation.4 | convolution fusion | flops 1074790400 | bytes 5248000 | tf_op jit(solution)/shard_map/dot_general | solution.py:251
  41.1 0.8 %fusion.6 = f32[1024,1024]{1,0:T(8,128)S(1)} fusion(bf16[256,1024]{1,0:T(8,128)(2,1)S(1)} %collective-permute-done.17, pred[512,1024]{1,0:T(32,128)(4,1)S(1)} %fusion), kind=kOutput, calls=%fused_computation.7 | convolution fusion | flops 536870912 | bytes 4980736 | tf_op jit(solution)/shard_map/dot_general | solution.py:253
  41.9 2.6 %collective-permute-start.26 = (bf16[128,1152]{1,0:T(8,128)(2,1)S(1)}, bf16[128,1152]{1,0:T(8,128)(2,1)S(1)}, u32[]{:S(2)}, u32[]{:S(2)}) collective-permute-start(bf16[128,1152]{1,0:T(8,128)(2,1)S(1)} %collective-permute-done.18.refs_2_), channel_id=1, source_target_pairs={{0,4},{1,13},{2,6},{3,15},{4,8},{5,1},{6,10},{7,3},{8,12},{9,5},{1... | collective-permute-start | bytes 884744 | tf_op jit(solution)/shard_map/ppermute | solution.py:34
  44.5 0.6 collective-permute-start.24
  45.1 5.2 %collective-permute-done.25 = bf16[256,1024]{1,0:T(8,128)(2,1)S(1)} collective-permute-done((bf16[256,1024]{1,0:T(8,128)(2,1)S(1)}, bf16[256,1024]{1,0:T(8,128)(2,1)S(1)}, u32[]{:S(2)}, u32[]{:S(2)}) %collective-permute-start.25) | collective-permute-done | bytes 524320 | tf_op jit(solution)/shard_map/ppermute | solution.py:34
  50.3 0.8 %add_convert_fusion.logit_ref = bf16[1024,1024]{1,0:T(8,128)(2,1)S(1)} fusion(f32[1024,1024]{1,0:T(8,128)S(1)} %fusion.2, f32[1024,1024]{1,0:T(8,128)S(1)} %fusion.6, bf16[256,1024]{1,0:T(8,128)(2,1)S(1)} %collective-permute-done.25, pred[512,1024]{1,0:T(32,128)(4,1)S(1)} %fusion), kind=kOutput, calls=%fused_computation | convolution fusion | flops 540016640 | bytes 11272192 | tf_op jit(solution)/shard_map/dot_general | solution.py:253
  51.2 2.1 %collective-permute-start.27 = (bf16[40,1152]{1,0:T(8,128)(2,1)S(1)}, bf16[40,1152]{1,0:T(8,128)(2,1)S(1)}, u32[]{:S(2)}, u32[]{:S(2)}) collective-permute-start(bf16[40,1152]{1,0:T(8,128)(2,1)S(1)} %slice.52), channel_id=1, source_target_pairs={{0,4},{1,13},{2,6},{3,15},{4,8},{5,1},{6,10},{7,3},{8,12},{9,5},{1... | collective-permute-start | bytes 276488 | tf_op jit(solution)/shard_map/ppermute | solution.py:34
  53.9 2.1 %shard_map.47.refs_5_ = f32[1024,1152]{1,0:T(8,128)S(1)} custom-call(s32[1]{0:T(128)} %bitcast.offset_ref, bf16[1024,1024]{1,0:T(8,128)(2,1)S(1)} %add_convert_fusion.logit_ref, bf16[128,1152]{1,0:T(8,128)(2,1)S(1)} %constant_dynamic-update-slice_fusion.refs_0_, bf16[128,1152]{1,0:T(8,128)(2,1)S(1)} %collective-permute-done.19.refs_1_, ...), custom_call_target="tpu_custom_call" | custom-call | flops 1811939328 | bytes 8388608 | tf_op jit(solution)/shard_map/pallas_call | solution.py:170
  56.0 2.2 %collective-permute-start.28 = (bf16[128,1152]{1,0:T(8,128)(2,1)S(1)}, bf16[128,1152]{1,0:T(8,128)(2,1)S(1)}, u32[]{:S(2)}, u32[]{:S(2)}) collective-permute-start(bf16[128,1152]{1,0:T(8,128)(2,1)S(1)} %collective-permute-done.26.refs_0_), channel_id=1, source_target_pairs={{0,1},{1,0},{2,3},{3,2},{4,5},{5,4},{6,7},{7,6},{8,9},{9,8},{10,11... | collective-permute-start | bytes 884744 | tf_op jit(solution)/shard_map/ppermute | solution.py:34
  58.2 1.6 %shard_map.48.refs_3_ = f32[1024,1152]{1,0:T(8,128)S(1)} custom-call(s32[1]{0:T(128)} %bitcast.offset_ref, bf16[1024,1024]{1,0:T(8,128)(2,1)S(1)} %add_convert_fusion.logit_ref, bf16[128,1152]{1,0:T(8,128)(2,1)S(1)} %collective-permute-done.26.refs_0_, bf16[128,1152]{1,0:T(8,128)(2,1)S(1)} %collective-permute-done.30.refs_1_, ...), custom_call_target="tpu_custom_call" | custom-call | flops 1358954496 | bytes 8388608 | tf_op jit(solution)/shard_map/pallas_call | solution.py:170
  59.9 3.1 %shard_map.49 = (f32[1024,1152]{1,0:T(8,128)}, s32[1]{0:T(128)}) custom-call(s32[1]{0:T(128)} %bitcast.offset_ref, bf16[1024,1024]{1,0:T(8,128)(2,1)S(1)} %add_convert_fusion.logit_ref, bf16[128,1152]{1,0:T(8,128)(2,1)S(1)} %collective-permute-done.28.refs_0_, bf16[40,1152]{1,0:T(8,128)(2,1)S(1)} %collective-permute-done.27.refs_1_, ...), custom_call_target="tpu_custom_call" | custom-call | flops 452984832 | bytes 8388608 | tf_op jit(solution)/shard_map/pallas_call | solution.py:170
  63.0 0.6 while.9
  (58 shorter events, 3.9 us)
Async XLA Ops:
  0.0 39.8 %copy-start = (bf16[512,1024]{1,0:T(8,128)(2,1)S(1)}, bf16[512,1024]{1,0:T(8,128)(2,1)}, u32[]{:S(2)}) copy-start(bf16[512,1024]{1,0:T(8,128)(2,1)} %param.8) | copy-start | bytes 3145732
  1.8 8.2 %collective-permute-start.7 = (bf16[4,2432]{1,0:T(4,128)(2,1)S(1)}, bf16[4,2432]{1,0:T(4,128)(2,1)S(1)}, u32[]{:S(2)}, u32[]{:S(2)}) collective-permute-start(bf16[4,2432]{1,0:T(4,128)(2,1)S(1)} %get-tuple-element.56), channel_id=1, source_target_pairs={{0,128},{1,129},{2,130},{3,131},{4,132},{5,133},{6,134},{7,135},{8... | collective-permute-start | bytes 58376 | tf_op jit(solution)/shard_map/ppermute | solution.py:34
  4.1 6.0 %collective-permute-start.9 = (bf16[4,2432]{1,0:T(4,128)(2,1)S(1)}, bf16[4,2432]{1,0:T(4,128)(2,1)S(1)}, u32[]{:S(2)}, u32[]{:S(2)}) collective-permute-start(bf16[4,2432]{1,0:T(4,128)(2,1)S(1)} %get-tuple-element.56), channel_id=1, source_target_pairs={{0,130},{1,131},{2,128},{3,129},{4,134},{5,135},{6,132},{7,133},{8... | collective-permute-start | bytes 58376 | tf_op jit(solution)/shard_map/ppermute | solution.py:34
  6.0 4.1 %collective-permute-start.8 = (bf16[4,2432]{1,0:T(4,128)(2,1)S(1)}, bf16[4,2432]{1,0:T(4,128)(2,1)S(1)}, u32[]{:S(2)}, u32[]{:S(2)}) collective-permute-start(bf16[4,2432]{1,0:T(4,128)(2,1)S(1)} %get-tuple-element.55), channel_id=1, source_target_pairs={{0,2},{1,3},{2,0},{3,1},{4,6},{5,7},{6,4},{7,5},{8,10},{9,11},{10,... | collective-permute-start | bytes 58376 | tf_op jit(solution)/shard_map/ppermute | solution.py:34
  10.1 3.4 %collective-permute-start.10 = (bf16[16,2432]{1,0:T(8,128)(2,1)S(1)}, bf16[16,2432]{1,0:T(8,128)(2,1)S(1)}, u32[]{:S(2)}, u32[]{:S(2)}) collective-permute-start(bf16[16,2432]{1,0:T(8,128)(2,1)S(1)} %pad_maximum_fusion.1), channel_id=1, source_target_pairs={{0,1},{1,0},{2,3},{3,2},{4,5},{5,4},{6,7},{7,6},{8,9},{9,8},{10,11... | collective-permute-start | bytes 233480 | tf_op jit(solution)/shard_map/ppermute | solution.py:34
  12.6 16.0 %collective-permute-start.17 = (bf16[256,1024]{1,0:T(8,128)(2,1)S(1)}, bf16[256,1024]{1,0:T(8,128)(2,1)S(1)}, u32[]{:S(2)}, u32[]{:S(2)}) collective-permute-start(bf16[256,1024]{1,0:T(8,128)(2,1)S(1)} %get-tuple-element.57), channel_id=1, source_target_pairs={{0,128},{1,129},{2,130},{3,131},{4,132},{5,133},{6,134},{7,135},{8... | collective-permute-start | bytes 1572872 | tf_op jit(solution)/shard_map/ppermute | solution.py:34
  13.5 8.2 %collective-permute-start.12 = (bf16[32,1152]{1,0:T(8,128)(2,1)S(1)}, bf16[32,1152]{1,0:T(8,128)(2,1)S(1)}, u32[]{:S(2)}, u32[]{:S(2)}) collective-permute-start(bf16[32,1152]{1,0:T(8,128)(2,1)S(1)} %pad_maximum_fusion.2), channel_id=1, source_target_pairs={{0,32},{1,97},{2,34},{3,99},{4,36},{5,101},{6,38},{7,103},{8,40},{... | collective-permute-start | bytes 221192 | tf_op jit(solution)/shard_map/ppermute | solution.py:34
  19.6 5.0 %collective-permute-start.11 = (bf16[32,1152]{1,0:T(8,128)(2,1)S(1)}, bf16[32,1152]{1,0:T(8,128)(2,1)S(1)}, u32[]{:S(2)}, u32[]{:S(2)}) collective-permute-start(bf16[32,1152]{1,0:T(8,128)(2,1)S(1)} %pad_maximum_fusion.2), channel_id=1, source_target_pairs={{0,16},{1,113},{2,18},{3,115},{4,20},{5,117},{6,22},{7,119},{8,24}... | collective-permute-start | bytes 221192 | tf_op jit(solution)/shard_map/ppermute | solution.py:34
  20.4 5.9 %collective-permute-start.15 = (bf16[32,1280]{1,0:T(8,128)(2,1)S(1)}, bf16[32,1280]{1,0:T(8,128)(2,1)S(1)}, u32[]{:S(2)}, u32[]{:S(2)}) collective-permute-start(bf16[32,1280]{1,0:T(8,128)(2,1)S(1)} %pad_maximum_fusion), channel_id=1, source_target_pairs={{0,16},{1,113},{2,18},{3,115},{4,20},{5,117},{6,22},{7,119},{8,24}... | collective-permute-start | bytes 245768 | tf_op jit(solution)/shard_map/ppermute | solution.py:34
  21.2 5.1 %collective-permute-start.16 = (bf16[32,1280]{1,0:T(8,128)(2,1)S(1)}, bf16[32,1280]{1,0:T(8,128)(2,1)S(1)}, u32[]{:S(2)}, u32[]{:S(2)}) collective-permute-start(bf16[32,1280]{1,0:T(8,128)(2,1)S(1)} %pad_maximum_fusion), channel_id=1, source_target_pairs={{0,32},{1,97},{2,34},{3,99},{4,36},{5,101},{6,38},{7,103},{8,40},{... | collective-permute-start | bytes 245768 | tf_op jit(solution)/shard_map/ppermute | solution.py:34
  21.7 4.6 %collective-permute-start.13 = (bf16[32,1152]{1,0:T(8,128)(2,1)S(1)}, bf16[32,1152]{1,0:T(8,128)(2,1)S(1)}, u32[]{:S(2)}, u32[]{:S(2)}) collective-permute-start(bf16[32,1152]{1,0:T(8,128)(2,1)S(1)} %collective-permute-done.12), channel_id=1, source_target_pairs={{0,16},{1,113},{2,18},{3,115},{4,20},{5,117},{6,22},{7,119},{8,24}... | collective-permute-start | bytes 221192 | tf_op jit(solution)/shard_map/ppermute | solution.py:34
  24.7 4.0 %collective-permute-start.14 = (bf16[16,1152]{1,0:T(8,128)(2,1)S(1)}, bf16[16,1152]{1,0:T(8,128)(2,1)S(1)}, u32[]{:S(2)}, u32[]{:S(2)}) collective-permute-start(bf16[16,1152]{1,0:T(8,128)(2,1)S(1)} %slice.46), channel_id=1, source_target_pairs={{0,32},{1,97},{2,34},{3,99},{4,36},{5,101},{6,38},{7,103},{8,40},{... | collective-permute-start | bytes 110600 | tf_op jit(solution)/shard_map/ppermute | solution.py:34
  28.7 9.3 %collective-permute-start.19 = (bf16[128,1152]{1,0:T(8,128)(2,1)S(1)}, bf16[128,1152]{1,0:T(8,128)(2,1)S(1)}, u32[]{:S(2)}, u32[]{:S(2)}) collective-permute-start(bf16[128,1152]{1,0:T(8,128)(2,1)S(1)} %constant_dynamic-update-slice_fusion.refs_0_), channel_id=1, source_target_pairs={{0,1},{1,0},{2,3},{3,2},{4,5},{5,4},{6,7},{7,6},{8,9},{9,8},{10,11... | collective-permute-start | bytes 884744 | tf_op jit(solution)/shard_map/ppermute | solution.py:34
  31.6 6.9 %collective-permute-start.22 = (bf16[16,1280]{1,0:T(8,128)(2,1)S(1)}, bf16[16,1280]{1,0:T(8,128)(2,1)S(1)}, u32[]{:S(2)}, u32[]{:S(2)}) collective-permute-start(bf16[16,1280]{1,0:T(8,128)(2,1)S(1)} %slice.49), channel_id=1, source_target_pairs={{0,32},{1,97},{2,34},{3,99},{4,36},{5,101},{6,38},{7,103},{8,40},{... | collective-permute-start | bytes 122888 | tf_op jit(solution)/shard_map/ppermute | solution.py:34
  33.6 5.0 %collective-permute-start.21 = (bf16[32,1280]{1,0:T(8,128)(2,1)S(1)}, bf16[32,1280]{1,0:T(8,128)(2,1)S(1)}, u32[]{:S(2)}, u32[]{:S(2)}) collective-permute-start(bf16[32,1280]{1,0:T(8,128)(2,1)S(1)} %collective-permute-done.16.refs_2_), channel_id=1, source_target_pairs={{0,16},{1,113},{2,18},{3,115},{4,20},{5,117},{6,22},{7,119},{8,24}... | collective-permute-start | bytes 245768 | tf_op jit(solution)/shard_map/ppermute | solution.py:34
  34.9 7.1 %collective-permute-start.18 = (bf16[128,1152]{1,0:T(8,128)(2,1)S(1)}, bf16[128,1152]{1,0:T(8,128)(2,1)S(1)}, u32[]{:S(2)}, u32[]{:S(2)}) collective-permute-start(bf16[128,1152]{1,0:T(8,128)(2,1)S(1)} %constant_dynamic-update-slice_fusion.refs_0_), channel_id=1, source_target_pairs={{0,4},{1,13},{2,6},{3,15},{4,8},{5,1},{6,10},{7,3},{8,12},{9,5},{1... | collective-permute-start | bytes 884744 | tf_op jit(solution)/shard_map/ppermute | solution.py:34
  37.3 13.0 %collective-permute-start.25 = (bf16[256,1024]{1,0:T(8,128)(2,1)S(1)}, bf16[256,1024]{1,0:T(8,128)(2,1)S(1)}, u32[]{:S(2)}, u32[]{:S(2)}) collective-permute-start(bf16[256,1024]{1,0:T(8,128)(2,1)S(1)} %get-tuple-element.71), channel_id=1, source_target_pairs={{0,128},{1,129},{2,130},{3,131},{4,132},{5,133},{6,134},{7,135},{8... | collective-permute-start | bytes 1572872 | tf_op jit(solution)/shard_map/ppermute | solution.py:34
  38.0 15.4 %collective-permute-start.20 = (bf16[128,1152]{1,0:T(8,128)(2,1)S(1)}, bf16[128,1152]{1,0:T(8,128)(2,1)S(1)}, u32[]{:S(2)}, u32[]{:S(2)}) collective-permute-start(bf16[128,1152]{1,0:T(8,128)(2,1)S(1)} %collective-permute-done.19.refs_1_), channel_id=1, source_target_pairs={{0,4},{1,13},{2,6},{3,15},{4,8},{5,1},{6,10},{7,3},{8,12},{9,5},{1... | collective-permute-start | bytes 884744 | tf_op jit(solution)/shard_map/ppermute | solution.py:34
  39.6 4.9 %collective-permute-start.23 = (bf16[40,1152]{1,0:T(8,128)(2,1)S(1)}, bf16[40,1152]{1,0:T(8,128)(2,1)S(1)}, u32[]{:S(2)}, u32[]{:S(2)}) collective-permute-start(bf16[40,1152]{1,0:T(8,128)(2,1)S(1)} %get-tuple-element.64), channel_id=1, source_target_pairs={{0,1},{1,0},{2,3},{3,2},{4,5},{5,4},{6,7},{7,6},{8,9},{9,8},{10,11... | collective-permute-start | bytes 276488 | tf_op jit(solution)/shard_map/ppermute | solution.py:34
  41.9 14.1 %collective-permute-start.26 = (bf16[128,1152]{1,0:T(8,128)(2,1)S(1)}, bf16[128,1152]{1,0:T(8,128)(2,1)S(1)}, u32[]{:S(2)}, u32[]{:S(2)}) collective-permute-start(bf16[128,1152]{1,0:T(8,128)(2,1)S(1)} %collective-permute-done.18.refs_2_), channel_id=1, source_target_pairs={{0,4},{1,13},{2,6},{3,15},{4,8},{5,1},{6,10},{7,3},{8,12},{9,5},{1... | collective-permute-start | bytes 884744 | tf_op jit(solution)/shard_map/ppermute | solution.py:34
  44.5 6.7 %collective-permute-start.24 = (bf16[80,1152]{1,0:T(8,128)(2,1)S(1)}, bf16[80,1152]{1,0:T(8,128)(2,1)S(1)}, u32[]{:S(2)}, u32[]{:S(2)}) collective-permute-start(bf16[80,1152]{1,0:T(8,128)(2,1)S(1)} %constant_dynamic-update-slice_fusion.5.refs_4_), channel_id=1, source_target_pairs={{0,4},{1,13},{2,6},{3,15},{4,8},{5,1},{6,10},{7,3},{8,12},{9,5},{1... | collective-permute-start | bytes 552968 | tf_op jit(solution)/shard_map/ppermute | solution.py:34
  51.2 4.8 %collective-permute-start.27 = (bf16[40,1152]{1,0:T(8,128)(2,1)S(1)}, bf16[40,1152]{1,0:T(8,128)(2,1)S(1)}, u32[]{:S(2)}, u32[]{:S(2)}) collective-permute-start(bf16[40,1152]{1,0:T(8,128)(2,1)S(1)} %slice.52), channel_id=1, source_target_pairs={{0,4},{1,13},{2,6},{3,15},{4,8},{5,1},{6,10},{7,3},{8,12},{9,5},{1... | collective-permute-start | bytes 276488 | tf_op jit(solution)/shard_map/ppermute | solution.py:34
  53.3 4.9 %collective-permute-start.30 = (bf16[128,1152]{1,0:T(8,128)(2,1)S(1)}, bf16[128,1152]{1,0:T(8,128)(2,1)S(1)}, u32[]{:S(2)}, u32[]{:S(2)}) collective-permute-start(bf16[128,1152]{1,0:T(8,128)(2,1)S(1)} %collective-permute-done.18.refs_2_), channel_id=1, source_target_pairs={{0,1},{1,0},{2,3},{3,2},{4,5},{5,4},{6,7},{7,6},{8,9},{9,8},{10,11... | collective-permute-start | bytes 884744 | tf_op jit(solution)/shard_map/ppermute | solution.py:34
  53.3 4.9 %collective-permute-start.31 = (bf16[128,1152]{1,0:T(8,128)(2,1)S(1)}, bf16[128,1152]{1,0:T(8,128)(2,1)S(1)}, u32[]{:S(2)}, u32[]{:S(2)}) collective-permute-start(bf16[128,1152]{1,0:T(8,128)(2,1)S(1)} %collective-permute-done.20.refs_3_), channel_id=1, source_target_pairs={{0,1},{1,0},{2,3},{3,2},{4,5},{5,4},{6,7},{7,6},{8,9},{9,8},{10,11... | collective-permute-start | bytes 884744 | tf_op jit(solution)/shard_map/ppermute | solution.py:34
  53.8 4.4 %collective-permute-start.32 = (bf16[80,1152]{1,0:T(8,128)(2,1)S(1)}, bf16[80,1152]{1,0:T(8,128)(2,1)S(1)}, u32[]{:S(2)}, u32[]{:S(2)}) collective-permute-start(bf16[80,1152]{1,0:T(8,128)(2,1)S(1)} %collective-permute-done.24.refs_3_.refs_5_), channel_id=1, source_target_pairs={{0,1},{1,0},{2,3},{3,2},{4,5},{5,4},{6,7},{7,6},{8,9},{9,8},{10,11... | collective-permute-start | bytes 552968 | tf_op jit(solution)/shard_map/ppermute | solution.py:34
  56.0 3.9 %collective-permute-start.28 = (bf16[128,1152]{1,0:T(8,128)(2,1)S(1)}, bf16[128,1152]{1,0:T(8,128)(2,1)S(1)}, u32[]{:S(2)}, u32[]{:S(2)}) collective-permute-start(bf16[128,1152]{1,0:T(8,128)(2,1)S(1)} %collective-permute-done.26.refs_0_), channel_id=1, source_target_pairs={{0,1},{1,0},{2,3},{3,2},{4,5},{5,4},{6,7},{7,6},{8,9},{9,8},{10,11... | collective-permute-start | bytes 884744 | tf_op jit(solution)/shard_map/ppermute | solution.py:34
  58.2 1.7 %collective-permute-start.29 = (bf16[40,1152]{1,0:T(8,128)(2,1)S(1)}, bf16[40,1152]{1,0:T(8,128)(2,1)S(1)}, u32[]{:S(2)}, u32[]{:S(2)}) collective-permute-start(bf16[40,1152]{1,0:T(8,128)(2,1)S(1)} %collective-permute-done.27.refs_1_), channel_id=1, source_target_pairs={{0,1},{1,0},{2,3},{3,2},{4,5},{5,4},{6,7},{7,6},{8,9},{9,8},{10,11... | collective-permute-start | bytes 276488 | tf_op jit(solution)/shard_map/ppermute | solution.py:34

commit v9 on v7

--- a/solution.py
+++ b/solution.py
@@ -67,10 +67,11 @@
     return token * ROWS + j, r % 2
 
 
-def pack_kernel(columns, plane_ref, *refs):
-    parts, (out_ref, rest_ref) = refs[:-2], refs[-2:]
+def pack_kernel(columns, start, first, slots, plane_ref, *refs):
+    parts, ref = refs[:-1], refs[-1]
     side = (((1,), (1,)), ((), ()))
-    out_ref[:TOKENS, :] = jnp.concatenate([p[:, :columns] for p in parts], axis=0)
+    if start:
+        ref[:start, :] = jnp.concatenate([p[:, :columns] for p in parts], axis=0)
     grads = jnp.concatenate([p[:, columns : 2 * columns] for p in parts], axis=0)
     codes = jnp.concatenate([p[:, 2 * columns :] for p in parts], axis=0)
     line = lax.broadcasted_iota(jnp.int32, (CODES, LANES), 0)
@@ -88,24 +89,22 @@
     rank = jnp.where(match, rank, -1)
     over = jnp.max(jnp.where(rank >= SLOTS, 1.0, 0.0), axis=1, keepdims=True)
     turned = jnp.where(line == 3, 1.0, turned).astype(jnp.bfloat16)
-    for ref, start, first, slots in ((out_ref, TOKENS, 0, SLOTS), (rest_ref, 0, SLOTS, TOKENS - SLOTS)):
-        chosen = jnp.where(rank == row[:slots] + first, 1.0, 0.0).astype(jnp.bfloat16)
-        ref[start : start + slots, :] = jnp.dot(chosen, grads, preferred_element_type=jnp.float32).astype(jnp.bfloat16)
-        chosen = jnp.where(rank == row + first, 1.0, 0.0).astype(jnp.bfloat16)
-        code = lax.dot_general(turned, chosen, side, preferred_element_type=jnp.float32)
-        code = jnp.where(line == 4, over, code).astype(jnp.bfloat16)
-        ref[start + slots : start + slots + CODES, :LANES] = code
-        ref[start + slots : start + slots + CODES, LANES:] = jnp.zeros((CODES, columns - LANES), jnp.bfloat16)
-
-
-def pack(plane, parts, columns):
+    chosen = jnp.where(rank == row[:slots] + first, 1.0, 0.0).astype(jnp.bfloat16)
+    ref[start : start + slots, :] = jnp.dot(chosen, grads, preferred_element_type=jnp.float32).astype(jnp.bfloat16)
+    chosen = jnp.where(rank == row + first, 1.0, 0.0).astype(jnp.bfloat16)
+    code = lax.dot_general(turned, chosen, side, preferred_element_type=jnp.float32)
+    code = jnp.where(line == 4, over, code).astype(jnp.bfloat16)
+    ref[start + slots : start + slots + CODES, :LANES] = code
+    ref[start + slots : start + slots + CODES, LANES:] = jnp.zeros((CODES, columns - LANES), jnp.bfloat16)
+
+
+def pack(plane, parts, columns, start, first, slots):
     here = pl.BlockSpec(memory_space=pltpu.VMEM)
-    shapes = (TOKENS + SLOTS + CODES, TOKENS - SLOTS + CODES)
     return pl.pallas_call(
-        functools.partial(pack_kernel, columns),
-        out_shape=[jax.ShapeDtypeStruct((rows, columns), jnp.bfloat16) for rows in shapes],
+        functools.partial(pack_kernel, columns, start, first, slots),
+        out_shape=jax.ShapeDtypeStruct((start + slots + CODES, columns), jnp.bfloat16),
         in_specs=[pl.BlockSpec(memory_space=pltpu.SMEM)] + [here] * len(parts),
-        out_specs=[here, here],
+        out_specs=here,
         compiler_params=pltpu.CompilerParams(vmem_limit_bytes=8 << 20),
         cost_estimate=pl.CostEstimate(flops=1 << 26, bytes_accessed=2 << 20, transcendentals=0),
     )(plane, *parts)
@@ -223,19 +222,20 @@
     parts, early = gather_column(own, other)
     held, _ = lax.optimization_barrier((logit_grad, early))
     partner = move(held, fd=1)
-    column, rest = pack(plane, parts, columns)
+    column = pack(plane, parts, columns, TOKENS, 0, SLOTS)
     swapped = move(column, fc=1)
-    direct = move(column, dx=1)
+    direct = [move(column, dx=1), move(swapped, dx=1)]
     local, _ = lax.optimization_barrier((logit_grad, swapped))
     turned = lax.dot_general(local, near, dims, preferred_element_type=jnp.float32)
     turned = turned + lax.dot_general(partner, far, dims, preferred_element_type=jnp.float32)
-    late, turned = lax.optimization_barrier((swapped, turned.astype(jnp.bfloat16)))
-    passed = move(direct, dx=1)
-    direct = [direct, move(late, dx=1)]
+    passed = move(direct[0], dx=1)
+    came, turned = lax.optimization_barrier((direct[0], turned.astype(jnp.bfloat16)))
     first = [column, swapped] + direct
     partial = contract(offset, turned, first, (0, 1, 2, 3))
-    passed, partial = lax.optimization_barrier((passed, partial))
-    second = [passed] + [move(part, fc=1) for part in direct]
+    *parts, partial = lax.optimization_barrier((*parts, partial))
+    rest = pack(plane, parts, columns, 0, SLOTS, TOKENS - SLOTS)
+    passed, partial, rest = lax.optimization_barrier((passed, partial, rest))
+    second = [passed] + [move(part, fc=1) for part in (came, direct[1])]
     partial = contract(offset, turned, second, (4, 5, 6), partial)
     result, over = contract(offset, turned, [move(passed, fc=1)], (7,), partial, first + second)
 

time: 57.9 us -> 57.9 us (level)
  starting transfers between devices: 32.1 us -> 31 us
  Pallas kernels: 7.89 us -> 8.78 us
    ppermute x16, starting transfers between devices: 32.1 us -> 31 us  [move(): return lax.ppermute(value, ('dp', 'vocab'), pairs)]
    pallas_call x1 -> x2, Pallas kernels: 1.11 us -> 2.01 us  [pack(): pl.pallas_call(functools.partial(pack_kernel, columns, start, first, slot...]
  transfers between devices with their start and end apart: 16 -> 16, of which waited for: 8 -> 6; matrix products, arithmetic and copies ran while one was open for 5% -> 5% of each run, Pallas kernels for 8% -> 10%
where the time goes in v9:
time: 57.9 us; the launch traced here: 57.7 us
  starting transfers between devices  31 us (54%)
  waiting for transfers between devices  12.3 us (21%)
  Pallas kernels  8.78 us (15%)
  matrix products  2.77 us (5%)
  other arithmetic  1.01 us (2%)
  local copies, waits for them, and re-layouts  0.88 us (2%)
  loops' own time  0.7 us (1%)
    ppermute x16, starting transfers between devices, move(): return lax.ppermute(value, ('dp', 'vocab'), pairs)  31 us
    ppermute x16, waiting for transfers between devices, move(): return lax.ppermute(value, ('dp', 'vocab'), pairs)  12.3 us
    pallas_call x3, Pallas kernels, contract(): pl.pallas_call(functools.partial(contract_kernel, tuple(spots), len(added...  6.77 us
    pallas_call x2, Pallas kernels, pack(): pl.pallas_call(functools.partial(pack_kernel, columns, start, first, slot...  2.01 us
    dot_general x1, matrix products, body(): lax.dot_general(local, near, dims, preferred_element_type=jnp.float32)  1.42 us
    dot_general x1, matrix products, body(): lax.dot_general(partner, far, dims, preferred_element_type=jnp.float32)  1.36 us
  transfers between devices with their start and end apart: 16, of which 6 were waited for; matrix products, arithmetic and copies ran while one was open for 5% of the time, Pallas kernels for 10%

profile of v9, /device:TPU:1, one launch (start us, length us, event | category | flops | bytes accessed | tf_op | source)
XLA Modules:
  0.0 57.7 jit_solution(6369805375696573408)
XLA Ops:
  0.0 0.7 %broadcast_shift-right-arithmetic_fusion = (s32[4]{0:T(128)S(1)}, s32[4]{0:T(128)S(1)}, s32[4]{0:T(128)S(1)}) fusion(s32[4]{0:T(128)} %param.6), kind=kLoop, calls=%fused_computation.104 | loop fusion | flops 16 | bytes 64 | tf_op jit(solution)/shard_map/shift_right_arithmetic | solution.py:206
  0.9 0.8 %constant_dynamic-slice_fusion = (bf16[4,1152]{1,0:T(4,128)(2,1)S(1)}, bf16[4,1152]{1,0:T(4,128)(2,1)S(1)}, bf16[4,1152]{1,0:T(4,128)(2,1)S(1)}, bf16[4,1152]{1,0:T(4,128)(2,1)S(1)}) fusion(bf16[4,2304]{1,0:T(4,128)(2,1)} %param.9, s32[]{:T(128)S(6)} %select_n.383, s32[]{:T(128)S(6)} %select_n.379, bf16[4,2304]{1,0:T(4,128)(2,1)} %param.7), kind=kLoop, calls=%fused_computation.94 | loop fusion | bytes 73736 | tf_op jit(solution)/shard_map/dynamic_slice | solution.py:210
  1.8 3.8 %collective-permute-start.8 = (bf16[4,2432]{1,0:T(4,128)(2,1)S(1)}, bf16[4,2432]{1,0:T(4,128)(2,1)S(1)}, u32[]{:S(2)}, u32[]{:S(2)}) collective-permute-start(bf16[4,2432]{1,0:T(4,128)(2,1)S(1)} %get-tuple-element.48), channel_id=1, source_target_pairs={{0,2},{1,3},{2,0},{3,1},{4,6},{5,7},{6,4},{7,5},{8,10},{9,11},{10,... | collective-permute-start | bytes 58376 | tf_op jit(solution)/shard_map/ppermute | solution.py:34
  5.6 0.8 %collective-permute-start.9 = (bf16[4,2432]{1,0:T(4,128)(2,1)S(1)}, bf16[4,2432]{1,0:T(4,128)(2,1)S(1)}, u32[]{:S(2)}, u32[]{:S(2)}) collective-permute-start(bf16[4,2432]{1,0:T(4,128)(2,1)S(1)} %get-tuple-element.49), channel_id=1, source_target_pairs={{0,130},{1,131},{2,128},{3,129},{4,134},{5,135},{6,132},{7,133},{8... | collective-permute-start | bytes 58376 | tf_op jit(solution)/shard_map/ppermute | solution.py:34
  6.4 0.4 collective-permute-done.8
  6.7 1.3 %collective-permute-start.17 = (bf16[512,1024]{1,0:T(8,128)(2,1)}, bf16[512,1024]{1,0:T(8,128)(2,1)S(1)}, u32[]{:S(2)}, u32[]{:S(2)}) collective-permute-start(bf16[512,1024]{1,0:T(8,128)(2,1)} %param.8), channel_id=1, source_target_pairs={{0,128},{1,129},{2,130},{3,131},{4,132},{5,133},{6,134},{7,135},{8... | collective-permute-start | bytes 3145736 | tf_op jit(solution)/shard_map/ppermute | solution.py:34
  8.1 1.6 %collective-permute-done.9 = bf16[4,2432]{1,0:T(4,128)(2,1)S(1)} collective-permute-done((bf16[4,2432]{1,0:T(4,128)(2,1)S(1)}, bf16[4,2432]{1,0:T(4,128)(2,1)S(1)}, u32[]{:S(2)}, u32[]{:S(2)}) %collective-permute-start.9) | collective-permute-done | bytes 19488 | tf_op jit(solution)/shard_map/ppermute | solution.py:34
  9.8 2.0 %collective-permute-start.10 = (bf16[16,2432]{1,0:T(8,128)(2,1)S(1)}, bf16[16,2432]{1,0:T(8,128)(2,1)S(1)}, u32[]{:S(2)}, u32[]{:S(2)}) collective-permute-start(bf16[16,2432]{1,0:T(8,128)(2,1)S(1)} %pad_maximum_fusion.refs_0_), channel_id=1, source_target_pairs={{0,1},{1,0},{2,3},{3,2},{4,5},{5,4},{6,7},{7,6},{8,9},{9,8},{10,11... | collective-permute-start | bytes 233480 | tf_op jit(solution)/shard_map/ppermute | solution.py:34
  11.7 0.9 %collective-permute-done.10 = bf16[16,2432]{1,0:T(8,128)(2,1)S(1)} collective-permute-done((bf16[16,2432]{1,0:T(8,128)(2,1)S(1)}, bf16[16,2432]{1,0:T(8,128)(2,1)S(1)}, u32[]{:S(2)}, u32[]{:S(2)}) %collective-permute-start.10) | collective-permute-done | bytes 77856 | tf_op jit(solution)/shard_map/ppermute | solution.py:34
  12.6 0.1 concatenate.16
  12.7 6.1 %collective-permute-start.12 = (bf16[32,2432]{1,0:T(8,128)(2,1)S(1)}, bf16[32,2432]{1,0:T(8,128)(2,1)S(1)}, u32[]{:S(2)}, u32[]{:S(2)}) collective-permute-start(bf16[32,2432]{1,0:T(8,128)(2,1)S(1)} %concatenate.16), channel_id=1, source_target_pairs={{0,32},{1,97},{2,34},{3,99},{4,36},{5,101},{6,38},{7,103},{8,40},{... | collective-permute-start | bytes 466952 | tf_op jit(solution)/shard_map/ppermute | solution.py:34
  18.8 0.7 %collective-permute-start.11 = (bf16[32,2432]{1,0:T(8,128)(2,1)S(1)}, bf16[32,2432]{1,0:T(8,128)(2,1)S(1)}, u32[]{:S(2)}, u32[]{:S(2)}) collective-permute-start(bf16[32,2432]{1,0:T(8,128)(2,1)S(1)} %concatenate.16), channel_id=1, source_target_pairs={{0,16},{1,113},{2,18},{3,115},{4,20},{5,117},{6,22},{7,119},{8,24}... | collective-permute-start | bytes 466952 | tf_op jit(solution)/shard_map/ppermute | solution.py:34
  19.6 3.1 %collective-permute-done.12.refs_2_ = bf16[32,2432]{1,0:T(8,128)(2,1)S(1)} collective-permute-done((bf16[32,2432]{1,0:T(8,128)(2,1)S(1)}, bf16[32,2432]{1,0:T(8,128)(2,1)S(1)}, u32[]{:S(2)}, u32[]{:S(2)}) %collective-permute-start.12) | collective-permute-done | bytes 155680 | tf_op jit(solution)/shard_map/ppermute | solution.py:34
  22.7 2.0 %collective-permute-start.13 = (bf16[32,2432]{1,0:T(8,128)(2,1)S(1)}, bf16[32,2432]{1,0:T(8,128)(2,1)S(1)}, u32[]{:S(2)}, u32[]{:S(2)}) collective-permute-start(bf16[32,2432]{1,0:T(8,128)(2,1)S(1)} %collective-permute-done.12.refs_2_), channel_id=1, source_target_pairs={{0,16},{1,113},{2,18},{3,115},{4,20},{5,117},{6,22},{7,119},{8,24}... | collective-permute-start | bytes 466952 | tf_op jit(solution)/shard_map/ppermute | solution.py:34
  24.7 2.1 %collective-permute-start.14 = (bf16[16,2432]{1,0:T(8,128)(2,1)S(1)}, bf16[16,2432]{1,0:T(8,128)(2,1)S(1)}, u32[]{:S(2)}, u32[]{:S(2)}) collective-permute-start(bf16[16,2432]{1,0:T(8,128)(2,1)S(1)} %slice.4), channel_id=1, source_target_pairs={{0,32},{1,97},{2,34},{3,99},{4,36},{5,101},{6,38},{7,103},{8,40},{... | collective-permute-start | bytes 233480 | tf_op jit(solution)/shard_map/ppermute | solution.py:34
  26.8 2.9 %collective-permute-done.14.refs_4_ = bf16[16,2432]{1,0:T(8,128)(2,1)S(1)} collective-permute-done((bf16[16,2432]{1,0:T(8,128)(2,1)S(1)}, bf16[16,2432]{1,0:T(8,128)(2,1)S(1)}, u32[]{:S(2)}, u32[]{:S(2)}) %collective-permute-start.14) | collective-permute-done | bytes 77856 | tf_op jit(solution)/shard_map/ppermute | solution.py:34
  29.7 1.0 %shard_map.46.refs_0_.refs_2_ = bf16[168,1152]{1,0:T(8,128)(2,1)S(1)} custom-call(s32[2]{0:T(128)S(1)} %pad_add_fusion.plane_ref, bf16[16,2432]{1,0:T(8,128)(2,1)S(1)} %pad_maximum_fusion.refs_0_, bf16[32,2432]{1,0:T(8,128)(2,1)S(1)} %collective-permute-done.11.refs_1_, bf16[32,2432]{1,0:T(8,128)(2,1)S(1)} %collective-permute-done.12.refs_2_, ...), custom_call_target="tpu_custom_call" | custom-call | flops 67108864 | bytes 2097152 | tf_op jit(solution)/shard_map/pallas_call | solution.py:103
  30.7 3.5 %collective-permute-start.16 = (bf16[168,1152]{1,0:T(8,128)(2,1)S(1)}, bf16[168,1152]{1,0:T(8,128)(2,1)S(1)}, u32[]{:S(2)}, u32[]{:S(2)}) collective-permute-start(bf16[168,1152]{1,0:T(8,128)(2,1)S(1)} %shard_map.46.refs_0_.refs_2_), channel_id=1, source_target_pairs={{0,1},{1,0},{2,3},{3,2},{4,5},{5,4},{6,7},{7,6},{8,9},{9,8},{10,11... | collective-permute-start | bytes 1161224 | tf_op jit(solution)/shard_map/ppermute | solution.py:34
  34.3 2.5 %collective-permute-start.15 = (bf16[168,1152]{1,0:T(8,128)(2,1)S(1)}, bf16[168,1152]{1,0:T(8,128)(2,1)S(1)}, u32[]{:S(2)}, u32[]{:S(2)}) collective-permute-start(bf16[168,1152]{1,0:T(8,128)(2,1)S(1)} %shard_map.46.refs_0_.refs_2_), channel_id=1, source_target_pairs={{0,4},{1,13},{2,6},{3,15},{4,8},{5,1},{6,10},{7,3},{8,12},{9,5},{1... | collective-permute-start | bytes 1161224 | tf_op jit(solution)/shard_map/ppermute | solution.py:34
  36.8 1.3 %collective-permute-start.19 = (bf16[168,1152]{1,0:T(8,128)(2,1)S(1)}, bf16[168,1152]{1,0:T(8,128)(2,1)S(1)}, u32[]{:S(2)}, u32[]{:S(2)}) collective-permute-start(bf16[168,1152]{1,0:T(8,128)(2,1)S(1)} %collective-permute-done.16.refs_1_.refs_3_), channel_id=1, source_target_pairs={{0,4},{1,13},{2,6},{3,15},{4,8},{5,1},{6,10},{7,3},{8,12},{9,5},{1... | collective-permute-start | bytes 1161224 | tf_op jit(solution)/shard_map/ppermute | solution.py:34
  38.1 3.3 %collective-permute-done.15.refs_2_.refs_4_ = bf16[168,1152]{1,0:T(8,128)(2,1)S(1)} collective-permute-done((bf16[168,1152]{1,0:T(8,128)(2,1)S(1)}, bf16[168,1152]{1,0:T(8,128)(2,1)S(1)}, u32[]{:S(2)}, u32[]{:S(2)}) %collective-permute-start.15) | collective-permute-done | bytes 387104 | tf_op jit(solution)/shard_map/ppermute | solution.py:34
  41.4 3.1 %collective-permute-start.18 = (bf16[168,1152]{1,0:T(8,128)(2,1)S(1)}, bf16[168,1152]{1,0:T(8,128)(2,1)S(1)}, u32[]{:S(2)}, u32[]{:S(2)}) collective-permute-start(bf16[168,1152]{1,0:T(8,128)(2,1)S(1)} %collective-permute-done.15.refs_2_.refs_4_), channel_id=1, source_target_pairs={{0,4},{1,13},{2,6},{3,15},{4,8},{5,1},{6,10},{7,3},{8,12},{9,5},{1... | collective-permute-start | bytes 1161224 | tf_op jit(solution)/shard_map/ppermute | solution.py:34
  44.5 1.4 %fusion.3 = f32[1024,1024]{1,0:T(8,128)S(1)} fusion(bf16[512,1024]{1,0:T(8,128)(2,1)S(1)} %collective-permute-done.17, s32[1024]{0:T(1024)S(1)} %bitcast.7, pred[1024]{0:T(1024)(128)(4,1)S(1)} %broadcast_compare_fusion.1), kind=kOutput, calls=%fused_computation.4 | convolution fusion | flops 1074790400 | bytes 5248000 | tf_op jit(solution)/shard_map/dot_general | solution.py:230
  45.9 1.4 %add_convert_fusion.logit_ref = bf16[1024,1024]{1,0:T(8,128)(2,1)S(1)} fusion(f32[1024,1024]{1,0:T(8,128)S(1)} %fusion.3, bf16[512,1024]{1,0:T(8,128)(2,1)S(1)} %copy-done, s32[1024]{0:T(1024)S(1)} %bitcast.8, pred[1024]{0:T(1024)(128)(4,1)S(1)} %broadcast_compare_fusion), kind=kOutput, calls=%fused_computation | convolution fusion | flops 1076887552 | bytes 7345152 | tf_op jit(solution)/shard_map/dot_general | solution.py:229
  47.3 0.3 collective-permute-start.21
  47.6 0.5 collective-permute-start.22
  48.1 2.2 %shard_map.47.refs_3_ = f32[1024,1152]{1,0:T(8,128)S(1)} custom-call(s32[1]{0:T(128)} %bitcast.offset_ref, bf16[1024,1024]{1,0:T(8,128)(2,1)S(1)} %add_convert_fusion.logit_ref, bf16[168,1152]{1,0:T(8,128)(2,1)S(1)} %shard_map.46.refs_0_.refs_2_, bf16[168,1152]{1,0:T(8,128)(2,1)S(1)} %collective-permute-done.16.refs_1_.refs_3_, ...), custom_call_target="tpu_custom_call" | custom-call | flops 1811939328 | bytes 8388608 | tf_op jit(solution)/shard_map/pallas_call | solution.py:161
  50.2 1.0 %shard_map.48 = bf16[104,1152]{1,0:T(8,128)(2,1)S(1)} custom-call(s32[2]{0:T(128)S(1)} %pad_add_fusion.plane_ref, bf16[16,2432]{1,0:T(8,128)(2,1)S(1)} %pad_maximum_fusion.refs_0_, bf16[32,2432]{1,0:T(8,128)(2,1)S(1)} %collective-permute-done.11.refs_1_, bf16[32,2432]{1,0:T(8,128)(2,1)S(1)} %collective-permute-done.12.refs_2_, ...), custom_call_target="tpu_custom_call" | custom-call | flops 67108864 | bytes 2097152 | tf_op jit(solution)/shard_map/pallas_call | solution.py:103
  51.3 0.9 %collective-permute-start.20 = (bf16[168,1152]{1,0:T(8,128)(2,1)S(1)}, bf16[168,1152]{1,0:T(8,128)(2,1)S(1)}, u32[]{:S(2)}, u32[]{:S(2)}) collective-permute-start(bf16[168,1152]{1,0:T(8,128)(2,1)S(1)} %collective-permute-done.18.refs_0_.refs_6_), channel_id=1, source_target_pairs={{0,1},{1,0},{2,3},{3,2},{4,5},{5,4},{6,7},{7,6},{8,9},{9,8},{10,11... | collective-permute-start | bytes 1161224 | tf_op jit(solution)/shard_map/ppermute | solution.py:34
  52.2 1.6 %shard_map.49.refs_1_ = f32[1024,1152]{1,0:T(8,128)S(1)} custom-call(s32[1]{0:T(128)} %bitcast.offset_ref, bf16[1024,1024]{1,0:T(8,128)(2,1)S(1)} %add_convert_fusion.logit_ref, bf16[168,1152]{1,0:T(8,128)(2,1)S(1)} %collective-permute-done.18.refs_0_.refs_6_, bf16[168,1152]{1,0:T(8,128)(2,1)S(1)} %collective-permute-done.21.refs_1_.refs_7_, ...), custom_call_target="tpu_custom_call" | custom-call | flops 1358954496 | bytes 8388608 | tf_op jit(solution)/shard_map/pallas_call | solution.py:161
  53.8 3.0 %shard_map.50 = (f32[1024,1152]{1,0:T(8,128)}, s32[1]{0:T(128)}) custom-call(s32[1]{0:T(128)} %bitcast.offset_ref, bf16[1024,1024]{1,0:T(8,128)(2,1)S(1)} %add_convert_fusion.logit_ref, bf16[168,1152]{1,0:T(8,128)(2,1)S(1)} %collective-permute-done.20.refs_0_, f32[1024,1152]{1,0:T(8,128)S(1)} %shard_map.49.refs_1_, ...), custom_call_target="tpu_custom_call" | custom-call | flops 452984832 | bytes 8388608 | tf_op jit(solution)/shard_map/pallas_call | solution.py:161
  56.8 0.7 %while.9 = (f32[1024,1152]{1,0:T(8,128)}, s32[]{:T(128)}, bf16[104,1152]{1,0:T(8,128)(2,1)S(1)}, s32[1]{0:T(128)}) while((f32[1024,1152]{1,0:T(8,128)}, s32[]{:T(128)}, bf16[104,1152]{1,0:T(8,128)(2,1)S(1)}, s32[1]{0:T(128)}) %tuple.33), condition=%region_1.2_spmd, body=%region_0.1_spmd | while | flops 1 | bytes 6709577 | solution.py:249
  (23 shorter events, 0.4 us)
Async XLA Ops:
  1.8 5.0 %collective-permute-start.8 = (bf16[4,2432]{1,0:T(4,128)(2,1)S(1)}, bf16[4,2432]{1,0:T(4,128)(2,1)S(1)}, u32[]{:S(2)}, u32[]{:S(2)}) collective-permute-start(bf16[4,2432]{1,0:T(4,128)(2,1)S(1)} %get-tuple-element.48), channel_id=1, source_target_pairs={{0,2},{1,3},{2,0},{3,1},{4,6},{5,7},{6,4},{7,5},{8,10},{9,11},{10,... | collective-permute-start | bytes 58376 | tf_op jit(solution)/shard_map/ppermute | solution.py:34
  5.6 4.1 %collective-permute-start.9 = (bf16[4,2432]{1,0:T(4,128)(2,1)S(1)}, bf16[4,2432]{1,0:T(4,128)(2,1)S(1)}, u32[]{:S(2)}, u32[]{:S(2)}) collective-permute-start(bf16[4,2432]{1,0:T(4,128)(2,1)S(1)} %get-tuple-element.49), channel_id=1, source_target_pairs={{0,130},{1,131},{2,128},{3,129},{4,134},{5,135},{6,132},{7,133},{8... | collective-permute-start | bytes 58376 | tf_op jit(solution)/shard_map/ppermute | solution.py:34
  6.4 3.4 %collective-permute-start.7 = (bf16[4,2432]{1,0:T(4,128)(2,1)S(1)}, bf16[4,2432]{1,0:T(4,128)(2,1)S(1)}, u32[]{:S(2)}, u32[]{:S(2)}) collective-permute-start(bf16[4,2432]{1,0:T(4,128)(2,1)S(1)} %get-tuple-element.49), channel_id=1, source_target_pairs={{0,128},{1,129},{2,130},{3,131},{4,132},{5,133},{6,134},{7,135},{8... | collective-permute-start | bytes 58376 | tf_op jit(solution)/shard_map/ppermute | solution.py:34
  6.7 37.8 %collective-permute-start.17 = (bf16[512,1024]{1,0:T(8,128)(2,1)}, bf16[512,1024]{1,0:T(8,128)(2,1)S(1)}, u32[]{:S(2)}, u32[]{:S(2)}) collective-permute-start(bf16[512,1024]{1,0:T(8,128)(2,1)} %param.8), channel_id=1, source_target_pairs={{0,128},{1,129},{2,130},{3,131},{4,132},{5,133},{6,134},{7,135},{8... | collective-permute-start | bytes 3145736 | tf_op jit(solution)/shard_map/ppermute | solution.py:34
  9.8 2.9 %collective-permute-start.10 = (bf16[16,2432]{1,0:T(8,128)(2,1)S(1)}, bf16[16,2432]{1,0:T(8,128)(2,1)S(1)}, u32[]{:S(2)}, u32[]{:S(2)}) collective-permute-start(bf16[16,2432]{1,0:T(8,128)(2,1)S(1)} %pad_maximum_fusion.refs_0_), channel_id=1, source_target_pairs={{0,1},{1,0},{2,3},{3,2},{4,5},{5,4},{6,7},{7,6},{8,9},{9,8},{10,11... | collective-permute-start | bytes 233480 | tf_op jit(solution)/shard_map/ppermute | solution.py:34
  12.7 9.9 %collective-permute-start.12 = (bf16[32,2432]{1,0:T(8,128)(2,1)S(1)}, bf16[32,2432]{1,0:T(8,128)(2,1)S(1)}, u32[]{:S(2)}, u32[]{:S(2)}) collective-permute-start(bf16[32,2432]{1,0:T(8,128)(2,1)S(1)} %concatenate.16), channel_id=1, source_target_pairs={{0,32},{1,97},{2,34},{3,99},{4,36},{5,101},{6,38},{7,103},{8,40},{... | collective-permute-start | bytes 466952 | tf_op jit(solution)/shard_map/ppermute | solution.py:34
  18.8 8.0 %collective-permute-start.11 = (bf16[32,2432]{1,0:T(8,128)(2,1)S(1)}, bf16[32,2432]{1,0:T(8,128)(2,1)S(1)}, u32[]{:S(2)}, u32[]{:S(2)}) collective-permute-start(bf16[32,2432]{1,0:T(8,128)(2,1)S(1)} %concatenate.16), channel_id=1, source_target_pairs={{0,16},{1,113},{2,18},{3,115},{4,20},{5,117},{6,22},{7,119},{8,24}... | collective-permute-start | bytes 466952 | tf_op jit(solution)/shard_map/ppermute | solution.py:34
  22.7 7.0 %collective-permute-start.13 = (bf16[32,2432]{1,0:T(8,128)(2,1)S(1)}, bf16[32,2432]{1,0:T(8,128)(2,1)S(1)}, u32[]{:S(2)}, u32[]{:S(2)}) collective-permute-start(bf16[32,2432]{1,0:T(8,128)(2,1)S(1)} %collective-permute-done.12.refs_2_), channel_id=1, source_target_pairs={{0,16},{1,113},{2,18},{3,115},{4,20},{5,117},{6,22},{7,119},{8,24}... | collective-permute-start | bytes 466952 | tf_op jit(solution)/shard_map/ppermute | solution.py:34
  24.7 5.0 %collective-permute-start.14 = (bf16[16,2432]{1,0:T(8,128)(2,1)S(1)}, bf16[16,2432]{1,0:T(8,128)(2,1)S(1)}, u32[]{:S(2)}, u32[]{:S(2)}) collective-permute-start(bf16[16,2432]{1,0:T(8,128)(2,1)S(1)} %slice.4), channel_id=1, source_target_pairs={{0,32},{1,97},{2,34},{3,99},{4,36},{5,101},{6,38},{7,103},{8,40},{... | collective-permute-start | bytes 233480 | tf_op jit(solution)/shard_map/ppermute | solution.py:34
  30.7 6.0 %collective-permute-start.16 = (bf16[168,1152]{1,0:T(8,128)(2,1)S(1)}, bf16[168,1152]{1,0:T(8,128)(2,1)S(1)}, u32[]{:S(2)}, u32[]{:S(2)}) collective-permute-start(bf16[168,1152]{1,0:T(8,128)(2,1)S(1)} %shard_map.46.refs_0_.refs_2_), channel_id=1, source_target_pairs={{0,1},{1,0},{2,3},{3,2},{4,5},{5,4},{6,7},{7,6},{8,9},{9,8},{10,11... | collective-permute-start | bytes 1161224 | tf_op jit(solution)/shard_map/ppermute | solution.py:34
  34.3 7.1 %collective-permute-start.15 = (bf16[168,1152]{1,0:T(8,128)(2,1)S(1)}, bf16[168,1152]{1,0:T(8,128)(2,1)S(1)}, u32[]{:S(2)}, u32[]{:S(2)}) collective-permute-start(bf16[168,1152]{1,0:T(8,128)(2,1)S(1)} %shard_map.46.refs_0_.refs_2_), channel_id=1, source_target_pairs={{0,4},{1,13},{2,6},{3,15},{4,8},{5,1},{6,10},{7,3},{8,12},{9,5},{1... | collective-permute-start | bytes 1161224 | tf_op jit(solution)/shard_map/ppermute | solution.py:34
  36.8 10.8 %collective-permute-start.19 = (bf16[168,1152]{1,0:T(8,128)(2,1)S(1)}, bf16[168,1152]{1,0:T(8,128)(2,1)S(1)}, u32[]{:S(2)}, u32[]{:S(2)}) collective-permute-start(bf16[168,1152]{1,0:T(8,128)(2,1)S(1)} %collective-permute-done.16.refs_1_.refs_3_), channel_id=1, source_target_pairs={{0,4},{1,13},{2,6},{3,15},{4,8},{5,1},{6,10},{7,3},{8,12},{9,5},{1... | collective-permute-start | bytes 1161224 | tf_op jit(solution)/shard_map/ppermute | solution.py:34
  41.4 9.9 %collective-permute-start.18 = (bf16[168,1152]{1,0:T(8,128)(2,1)S(1)}, bf16[168,1152]{1,0:T(8,128)(2,1)S(1)}, u32[]{:S(2)}, u32[]{:S(2)}) collective-permute-start(bf16[168,1152]{1,0:T(8,128)(2,1)S(1)} %collective-permute-done.15.refs_2_.refs_4_), channel_id=1, source_target_pairs={{0,4},{1,13},{2,6},{3,15},{4,8},{5,1},{6,10},{7,3},{8,12},{9,5},{1... | collective-permute-start | bytes 1161224 | tf_op jit(solution)/shard_map/ppermute | solution.py:34
  44.5 1.4 %copy-start = (bf16[512,1024]{1,0:T(8,128)(2,1)S(1)}, bf16[512,1024]{1,0:T(8,128)(2,1)}, u32[]{:S(2)}) copy-start(bf16[512,1024]{1,0:T(8,128)(2,1)} %param.8) | copy-start | bytes 3145732
  47.3 4.9 %collective-permute-start.21 = (bf16[168,1152]{1,0:T(8,128)(2,1)S(1)}, bf16[168,1152]{1,0:T(8,128)(2,1)S(1)}, u32[]{:S(2)}, u32[]{:S(2)}) collective-permute-start(bf16[168,1152]{1,0:T(8,128)(2,1)S(1)} %collective-permute-done.15.refs_2_.refs_4_), channel_id=1, source_target_pairs={{0,1},{1,0},{2,3},{3,2},{4,5},{5,4},{6,7},{7,6},{8,9},{9,8},{10,11... | collective-permute-start | bytes 1161224 | tf_op jit(solution)/shard_map/ppermute | solution.py:34
  47.6 4.6 %collective-permute-start.22 = (bf16[168,1152]{1,0:T(8,128)(2,1)S(1)}, bf16[168,1152]{1,0:T(8,128)(2,1)S(1)}, u32[]{:S(2)}, u32[]{:S(2)}) collective-permute-start(bf16[168,1152]{1,0:T(8,128)(2,1)S(1)} %collective-permute-done.19.refs_3_.refs_5_), channel_id=1, source_target_pairs={{0,1},{1,0},{2,3},{3,2},{4,5},{5,4},{6,7},{7,6},{8,9},{9,8},{10,11... | collective-permute-start | bytes 1161224 | tf_op jit(solution)/shard_map/ppermute | solution.py:34
  51.3 2.5 %collective-permute-start.20 = (bf16[168,1152]{1,0:T(8,128)(2,1)S(1)}, bf16[168,1152]{1,0:T(8,128)(2,1)S(1)}, u32[]{:S(2)}, u32[]{:S(2)}) collective-permute-start(bf16[168,1152]{1,0:T(8,128)(2,1)S(1)} %collective-permute-done.18.refs_0_.refs_6_), channel_id=1, source_target_pairs={{0,1},{1,0},{2,3},{3,2},{4,5},{5,4},{6,7},{7,6},{8,9},{9,8},{10,11... | collective-permute-start | bytes 1161224 | tf_op jit(solution)/shard_map/ppermute | solution.py:34

commit v10 on v9

--- a/solution.py
+++ b/solution.py
@@ -42,7 +42,7 @@
     both = jnp.concatenate([chunk, move(chunk, fc=1)], axis=0)
     two, one = move(both, dz=2), move(both, dz=1)
     three, four = move(two, dz=1), move(two[:16], dz=2)
-    return [chunk, one, two, three, four], from_yh
+    return [chunk, one, two, three, four]
 
 
 STEPS = (0, 0, 1, 1, 2, -1, -1, 2)
@@ -219,9 +219,8 @@
     )
     spot = lax.broadcasted_iota(jnp.int32, (logit_grad.shape[0], 1), 0)
     near, far = (((spot == token) & (away == side)).astype(jnp.bfloat16) for side in (0, 1))
-    parts, early = gather_column(own, other)
-    held, _ = lax.optimization_barrier((logit_grad, early))
-    partner = move(held, fd=1)
+    parts = gather_column(own, other)
+    partner = move(logit_grad, fd=1)
     column = pack(plane, parts, columns, TOKENS, 0, SLOTS)
     swapped = move(column, fc=1)
     direct = [move(column, dx=1), move(swapped, dx=1)]

time: 57.9 us -> 58.1 us (level)
  waiting for transfers between devices: 12.3 us -> 13 us
  starting transfers between devices: 31 us -> 30.4 us
    ppermute x16, waiting for transfers between devices: 12.3 us -> 13 us  [move(): return lax.ppermute(value, ('dp', 'vocab'), pairs)]
where the time goes in v10:
time: 58.1 us; the launch traced here: 57.9 us
  starting transfers between devices  30.4 us (52%)
  waiting for transfers between devices  13 us (22%)
  Pallas kernels  8.78 us (15%)
  matrix products  2.79 us (5%)
  other arithmetic  1.01 us (2%)
  local copies, waits for them, and re-layouts  0.88 us (2%)
  loops' own time  0.7 us (1%)
    ppermute x16, starting transfers between devices, move(): return lax.ppermute(value, ('dp', 'vocab'), pairs)  30.4 us
    ppermute x16, waiting for transfers between devices, move(): return lax.ppermute(value, ('dp', 'vocab'), pairs)  13 us
    pallas_call x3, Pallas kernels, contract(): pl.pallas_call(functools.partial(contract_kernel, tuple(spots), len(added...  6.77 us
    pallas_call x2, Pallas kernels, pack(): pl.pallas_call(functools.partial(pack_kernel, columns, start, first, slot...  2.01 us
    dot_general x1, matrix products, body(): lax.dot_general(local, near, dims, preferred_element_type=jnp.float32)  1.42 us
    dot_general x1, matrix products, body(): lax.dot_general(partner, far, dims, preferred_element_type=jnp.float32)  1.37 us
  transfers between devices with their start and end apart: 16, of which 6 were waited for; matrix products, arithmetic and copies ran while one was open for 5% of the time, Pallas kernels for 10%

profile of v10, /device:TPU:1, one launch (start us, length us, event | category | flops | bytes accessed | tf_op | source)
XLA Modules:
  0.0 57.9 jit_solution(4778112976948930083)
XLA Ops:
  0.0 0.7 %broadcast_shift-right-arithmetic_fusion = (s32[4]{0:T(128)S(1)}, s32[4]{0:T(128)S(1)}, s32[4]{0:T(128)S(1)}) fusion(s32[4]{0:T(128)} %param.6), kind=kLoop, calls=%fused_computation.105 | loop fusion | flops 16 | bytes 64 | tf_op jit(solution)/shard_map/shift_right_arithmetic | solution.py:206
  0.9 0.8 %constant_dynamic-slice_fusion = (bf16[4,1152]{1,0:T(4,128)(2,1)S(1)}, bf16[4,1152]{1,0:T(4,128)(2,1)S(1)}, bf16[4,1152]{1,0:T(4,128)(2,1)S(1)}, bf16[4,1152]{1,0:T(4,128)(2,1)S(1)}) fusion(bf16[4,2304]{1,0:T(4,128)(2,1)} %param.9, s32[]{:T(128)S(6)} %select_n.383, s32[]{:T(128)S(6)} %select_n.379, bf16[4,2304]{1,0:T(4,128)(2,1)} %param.7), kind=kLoop, calls=%fused_computation.95 | loop fusion | bytes 73736 | tf_op jit(solution)/shard_map/dynamic_slice | solution.py:210
  1.8 3.7 %collective-permute-start.9 = (bf16[4,2432]{1,0:T(4,128)(2,1)S(1)}, bf16[4,2432]{1,0:T(4,128)(2,1)S(1)}, u32[]{:S(2)}, u32[]{:S(2)}) collective-permute-start(bf16[4,2432]{1,0:T(4,128)(2,1)S(1)} %get-tuple-element.48), channel_id=1, source_target_pairs={{0,130},{1,131},{2,128},{3,129},{4,134},{5,135},{6,132},{7,133},{8... | collective-permute-start | bytes 58376 | tf_op jit(solution)/shard_map/ppermute | solution.py:34
  5.4 1.3 %collective-permute-start.8 = (bf16[4,2432]{1,0:T(4,128)(2,1)S(1)}, bf16[4,2432]{1,0:T(4,128)(2,1)S(1)}, u32[]{:S(2)}, u32[]{:S(2)}) collective-permute-start(bf16[4,2432]{1,0:T(4,128)(2,1)S(1)} %get-tuple-element.47), channel_id=1, source_target_pairs={{0,2},{1,3},{2,0},{3,1},{4,6},{5,7},{6,4},{7,5},{8,10},{9,11},{10,... | collective-permute-start | bytes 58376 | tf_op jit(solution)/shard_map/ppermute | solution.py:34
  6.7 0.2 collective-permute-start.17
  6.9 1.1 %collective-permute-done.7 = bf16[4,2432]{1,0:T(4,128)(2,1)S(1)} collective-permute-done((bf16[4,2432]{1,0:T(4,128)(2,1)S(1)}, bf16[4,2432]{1,0:T(4,128)(2,1)S(1)}, u32[]{:S(2)}, u32[]{:S(2)}) %collective-permute-start.7) | collective-permute-done | bytes 19488 | tf_op jit(solution)/shard_map/ppermute | solution.py:34
  8.0 1.5 %collective-permute-done.8 = bf16[4,2432]{1,0:T(4,128)(2,1)S(1)} collective-permute-done((bf16[4,2432]{1,0:T(4,128)(2,1)S(1)}, bf16[4,2432]{1,0:T(4,128)(2,1)S(1)}, u32[]{:S(2)}, u32[]{:S(2)}) %collective-permute-start.8) | collective-permute-done | bytes 19488 | tf_op jit(solution)/shard_map/ppermute | solution.py:34
  9.6 2.3 %collective-permute-start.10 = (bf16[16,2432]{1,0:T(8,128)(2,1)S(1)}, bf16[16,2432]{1,0:T(8,128)(2,1)S(1)}, u32[]{:S(2)}, u32[]{:S(2)}) collective-permute-start(bf16[16,2432]{1,0:T(8,128)(2,1)S(1)} %pad_maximum_fusion.refs_0_), channel_id=1, source_target_pairs={{0,1},{1,0},{2,3},{3,2},{4,5},{5,4},{6,7},{7,6},{8,9},{9,8},{10,11... | collective-permute-start | bytes 233480 | tf_op jit(solution)/shard_map/ppermute | solution.py:34
  11.9 0.9 %collective-permute-done.10 = bf16[16,2432]{1,0:T(8,128)(2,1)S(1)} collective-permute-done((bf16[16,2432]{1,0:T(8,128)(2,1)S(1)}, bf16[16,2432]{1,0:T(8,128)(2,1)S(1)}, u32[]{:S(2)}, u32[]{:S(2)}) %collective-permute-start.10) | collective-permute-done | bytes 77856 | tf_op jit(solution)/shard_map/ppermute | solution.py:34
  12.8 0.1 concatenate.16
  12.9 6.1 %collective-permute-start.12 = (bf16[32,2432]{1,0:T(8,128)(2,1)S(1)}, bf16[32,2432]{1,0:T(8,128)(2,1)S(1)}, u32[]{:S(2)}, u32[]{:S(2)}) collective-permute-start(bf16[32,2432]{1,0:T(8,128)(2,1)S(1)} %concatenate.16), channel_id=1, source_target_pairs={{0,32},{1,97},{2,34},{3,99},{4,36},{5,101},{6,38},{7,103},{8,40},{... | collective-permute-start | bytes 466952 | tf_op jit(solution)/shard_map/ppermute | solution.py:34
  19.0 0.7 %collective-permute-start.11 = (bf16[32,2432]{1,0:T(8,128)(2,1)S(1)}, bf16[32,2432]{1,0:T(8,128)(2,1)S(1)}, u32[]{:S(2)}, u32[]{:S(2)}) collective-permute-start(bf16[32,2432]{1,0:T(8,128)(2,1)S(1)} %concatenate.16), channel_id=1, source_target_pairs={{0,16},{1,113},{2,18},{3,115},{4,20},{5,117},{6,22},{7,119},{8,24}... | collective-permute-start | bytes 466952 | tf_op jit(solution)/shard_map/ppermute | solution.py:34
  19.8 3.1 %collective-permute-done.12.refs_2_ = bf16[32,2432]{1,0:T(8,128)(2,1)S(1)} collective-permute-done((bf16[32,2432]{1,0:T(8,128)(2,1)S(1)}, bf16[32,2432]{1,0:T(8,128)(2,1)S(1)}, u32[]{:S(2)}, u32[]{:S(2)}) %collective-permute-start.12) | collective-permute-done | bytes 155680 | tf_op jit(solution)/shard_map/ppermute | solution.py:34
  22.9 2.0 %collective-permute-start.13 = (bf16[32,2432]{1,0:T(8,128)(2,1)S(1)}, bf16[32,2432]{1,0:T(8,128)(2,1)S(1)}, u32[]{:S(2)}, u32[]{:S(2)}) collective-permute-start(bf16[32,2432]{1,0:T(8,128)(2,1)S(1)} %collective-permute-done.12.refs_2_), channel_id=1, source_target_pairs={{0,16},{1,113},{2,18},{3,115},{4,20},{5,117},{6,22},{7,119},{8,24}... | collective-permute-start | bytes 466952 | tf_op jit(solution)/shard_map/ppermute | solution.py:34
  24.9 2.2 %collective-permute-start.14 = (bf16[16,2432]{1,0:T(8,128)(2,1)S(1)}, bf16[16,2432]{1,0:T(8,128)(2,1)S(1)}, u32[]{:S(2)}, u32[]{:S(2)}) collective-permute-start(bf16[16,2432]{1,0:T(8,128)(2,1)S(1)} %slice.4), channel_id=1, source_target_pairs={{0,32},{1,97},{2,34},{3,99},{4,36},{5,101},{6,38},{7,103},{8,40},{... | collective-permute-start | bytes 233480 | tf_op jit(solution)/shard_map/ppermute | solution.py:34
  27.0 3.0 %collective-permute-done.14.refs_4_ = bf16[16,2432]{1,0:T(8,128)(2,1)S(1)} collective-permute-done((bf16[16,2432]{1,0:T(8,128)(2,1)S(1)}, bf16[16,2432]{1,0:T(8,128)(2,1)S(1)}, u32[]{:S(2)}, u32[]{:S(2)}) %collective-permute-start.14) | collective-permute-done | bytes 77856 | tf_op jit(solution)/shard_map/ppermute | solution.py:34
  30.0 1.0 %shard_map.46.refs_0_.refs_2_ = bf16[168,1152]{1,0:T(8,128)(2,1)S(1)} custom-call(s32[2]{0:T(128)S(1)} %pad_add_fusion.plane_ref, bf16[16,2432]{1,0:T(8,128)(2,1)S(1)} %pad_maximum_fusion.refs_0_, bf16[32,2432]{1,0:T(8,128)(2,1)S(1)} %collective-permute-done.11.refs_1_, bf16[32,2432]{1,0:T(8,128)(2,1)S(1)} %collective-permute-done.12.refs_2_, ...), custom_call_target="tpu_custom_call" | custom-call | flops 67108864 | bytes 2097152 | tf_op jit(solution)/shard_map/pallas_call | solution.py:103
  31.0 3.4 %collective-permute-start.16 = (bf16[168,1152]{1,0:T(8,128)(2,1)S(1)}, bf16[168,1152]{1,0:T(8,128)(2,1)S(1)}, u32[]{:S(2)}, u32[]{:S(2)}) collective-permute-start(bf16[168,1152]{1,0:T(8,128)(2,1)S(1)} %shard_map.46.refs_0_.refs_2_), channel_id=1, source_target_pairs={{0,1},{1,0},{2,3},{3,2},{4,5},{5,4},{6,7},{7,6},{8,9},{9,8},{10,11... | collective-permute-start | bytes 1161224 | tf_op jit(solution)/shard_map/ppermute | solution.py:34
  34.5 2.5 %collective-permute-start.15 = (bf16[168,1152]{1,0:T(8,128)(2,1)S(1)}, bf16[168,1152]{1,0:T(8,128)(2,1)S(1)}, u32[]{:S(2)}, u32[]{:S(2)}) collective-permute-start(bf16[168,1152]{1,0:T(8,128)(2,1)S(1)} %shard_map.46.refs_0_.refs_2_), channel_id=1, source_target_pairs={{0,4},{1,13},{2,6},{3,15},{4,8},{5,1},{6,10},{7,3},{8,12},{9,5},{1... | collective-permute-start | bytes 1161224 | tf_op jit(solution)/shard_map/ppermute | solution.py:34
  37.0 1.3 %collective-permute-start.19 = (bf16[168,1152]{1,0:T(8,128)(2,1)S(1)}, bf16[168,1152]{1,0:T(8,128)(2,1)S(1)}, u32[]{:S(2)}, u32[]{:S(2)}) collective-permute-start(bf16[168,1152]{1,0:T(8,128)(2,1)S(1)} %collective-permute-done.16.refs_1_.refs_3_), channel_id=1, source_target_pairs={{0,4},{1,13},{2,6},{3,15},{4,8},{5,1},{6,10},{7,3},{8,12},{9,5},{1... | collective-permute-start | bytes 1161224 | tf_op jit(solution)/shard_map/ppermute | solution.py:34
  38.3 3.3 %collective-permute-done.15.refs_2_.refs_4_ = bf16[168,1152]{1,0:T(8,128)(2,1)S(1)} collective-permute-done((bf16[168,1152]{1,0:T(8,128)(2,1)S(1)}, bf16[168,1152]{1,0:T(8,128)(2,1)S(1)}, u32[]{:S(2)}, u32[]{:S(2)}) %collective-permute-start.15) | collective-permute-done | bytes 387104 | tf_op jit(solution)/shard_map/ppermute | solution.py:34
  41.6 3.1 %collective-permute-start.18 = (bf16[168,1152]{1,0:T(8,128)(2,1)S(1)}, bf16[168,1152]{1,0:T(8,128)(2,1)S(1)}, u32[]{:S(2)}, u32[]{:S(2)}) collective-permute-start(bf16[168,1152]{1,0:T(8,128)(2,1)S(1)} %collective-permute-done.15.refs_2_.refs_4_), channel_id=1, source_target_pairs={{0,4},{1,13},{2,6},{3,15},{4,8},{5,1},{6,10},{7,3},{8,12},{9,5},{1... | collective-permute-start | bytes 1161224 | tf_op jit(solution)/shard_map/ppermute | solution.py:34
  44.7 1.4 %fusion.4 = f32[1024,1024]{0,1:T(8,128)S(1)} fusion(bf16[512,1024]{1,0:T(8,128)(2,1)S(1)} %collective-permute-done.17, s32[1024]{0:T(1024)S(1)} %bitcast.11, pred[1024]{0:T(1024)(128)(4,1)S(1)} %broadcast_compare_fusion.1), kind=kOutput, calls=%fused_computation.5 | convolution fusion | flops 1074790400 | bytes 5248000 | tf_op jit(solution)/shard_map/dot_general | solution.py:229
  46.1 1.4 %fusion.logit_ref = bf16[1024,1024]{1,0:T(8,128)(2,1)S(1)} fusion(f32[1024,1024]{0,1:T(8,128)S(1)} %fusion.4, bf16[512,1024]{1,0:T(8,128)(2,1)S(1)} %copy-done, s32[1024]{0:T(1024)S(1)} %bitcast.12, pred[1024]{0:T(1024)(128)(4,1)S(1)} %broadcast_compare_fusion), kind=kOutput, calls=%fused_computation.1 | convolution fusion | flops 1076887552 | bytes 7345152 | tf_op jit(solution)/shard_map/dot_general | solution.py:228
  47.5 0.3 collective-permute-start.21
  47.8 0.5 collective-permute-start.22
  48.3 2.2 %shard_map.47.refs_3_ = f32[1024,1152]{1,0:T(8,128)S(1)} custom-call(s32[1]{0:T(128)} %bitcast.offset_ref, bf16[1024,1024]{1,0:T(8,128)(2,1)S(1)} %fusion.logit_ref, bf16[168,1152]{1,0:T(8,128)(2,1)S(1)} %shard_map.46.refs_0_.refs_2_, bf16[168,1152]{1,0:T(8,128)(2,1)S(1)} %collective-permute-done.16.refs_1_.refs_3_, ...), custom_call_target="tpu_custom_call" | custom-call | flops 1811939328 | bytes 8388608 | tf_op jit(solution)/shard_map/pallas_call | solution.py:161
  50.5 1.0 %shard_map.48 = bf16[104,1152]{1,0:T(8,128)(2,1)S(1)} custom-call(s32[2]{0:T(128)S(1)} %pad_add_fusion.plane_ref, bf16[16,2432]{1,0:T(8,128)(2,1)S(1)} %pad_maximum_fusion.refs_0_, bf16[32,2432]{1,0:T(8,128)(2,1)S(1)} %collective-permute-done.11.refs_1_, bf16[32,2432]{1,0:T(8,128)(2,1)S(1)} %collective-permute-done.12.refs_2_, ...), custom_call_target="tpu_custom_call" | custom-call | flops 67108864 | bytes 2097152 | tf_op jit(solution)/shard_map/pallas_call | solution.py:103
  51.5 0.9 %collective-permute-start.20 = (bf16[168,1152]{1,0:T(8,128)(2,1)S(1)}, bf16[168,1152]{1,0:T(8,128)(2,1)S(1)}, u32[]{:S(2)}, u32[]{:S(2)}) collective-permute-start(bf16[168,1152]{1,0:T(8,128)(2,1)S(1)} %collective-permute-done.18.refs_0_.refs_6_), channel_id=1, source_target_pairs={{0,1},{1,0},{2,3},{3,2},{4,5},{5,4},{6,7},{7,6},{8,9},{9,8},{10,11... | collective-permute-start | bytes 1161224 | tf_op jit(solution)/shard_map/ppermute | solution.py:34
  52.4 1.6 %shard_map.49.refs_1_ = f32[1024,1152]{1,0:T(8,128)S(1)} custom-call(s32[1]{0:T(128)} %bitcast.offset_ref, bf16[1024,1024]{1,0:T(8,128)(2,1)S(1)} %fusion.logit_ref, bf16[168,1152]{1,0:T(8,128)(2,1)S(1)} %collective-permute-done.18.refs_0_.refs_6_, bf16[168,1152]{1,0:T(8,128)(2,1)S(1)} %collective-permute-done.21.refs_1_.refs_7_, ...), custom_call_target="tpu_custom_call" | custom-call | flops 1358954496 | bytes 8388608 | tf_op jit(solution)/shard_map/pallas_call | solution.py:161
  54.0 3.0 %shard_map.50 = (f32[1024,1152]{1,0:T(8,128)}, s32[1]{0:T(128)}) custom-call(s32[1]{0:T(128)} %bitcast.offset_ref, bf16[1024,1024]{1,0:T(8,128)(2,1)S(1)} %fusion.logit_ref, bf16[168,1152]{1,0:T(8,128)(2,1)S(1)} %collective-permute-done.20.refs_0_, f32[1024,1152]{1,0:T(8,128)S(1)} %shard_map.49.refs_1_, bf16[168,1152]{1,0:T(8,128)(2,1)S(1)} %shard_map.46.refs_0_.refs_2_, ...), custom_call_target="tpu_custom_call" | custom-call | flops 452984832 | bytes 8388608 | tf_op jit(solution)/shard_map/pallas_call | solution.py:161
  57.0 0.7 %while.9 = (f32[1024,1152]{1,0:T(8,128)}, s32[]{:T(128)}, bf16[104,1152]{1,0:T(8,128)(2,1)S(1)}, s32[1]{0:T(128)}) while((f32[1024,1152]{1,0:T(8,128)}, s32[]{:T(128)}, bf16[104,1152]{1,0:T(8,128)(2,1)S(1)}, s32[1]{0:T(128)}) %tuple.31), condition=%region_1.2_spmd, body=%region_0.1_spmd | while | flops 1 | bytes 6709577 | solution.py:248
  (23 shorter events, 0.4 us)
Async XLA Ops:
  1.8 5.1 %collective-permute-start.9 = (bf16[4,2432]{1,0:T(4,128)(2,1)S(1)}, bf16[4,2432]{1,0:T(4,128)(2,1)S(1)}, u32[]{:S(2)}, u32[]{:S(2)}) collective-permute-start(bf16[4,2432]{1,0:T(4,128)(2,1)S(1)} %get-tuple-element.48), channel_id=1, source_target_pairs={{0,130},{1,131},{2,128},{3,129},{4,134},{5,135},{6,132},{7,133},{8... | collective-permute-start | bytes 58376 | tf_op jit(solution)/shard_map/ppermute | solution.py:34
  5.4 2.6 %collective-permute-start.7 = (bf16[4,2432]{1,0:T(4,128)(2,1)S(1)}, bf16[4,2432]{1,0:T(4,128)(2,1)S(1)}, u32[]{:S(2)}, u32[]{:S(2)}) collective-permute-start(bf16[4,2432]{1,0:T(4,128)(2,1)S(1)} %get-tuple-element.48), channel_id=1, source_target_pairs={{0,128},{1,129},{2,130},{3,131},{4,132},{5,133},{6,134},{7,135},{8... | collective-permute-start | bytes 58376 | tf_op jit(solution)/shard_map/ppermute | solution.py:34
  5.4 4.1 %collective-permute-start.8 = (bf16[4,2432]{1,0:T(4,128)(2,1)S(1)}, bf16[4,2432]{1,0:T(4,128)(2,1)S(1)}, u32[]{:S(2)}, u32[]{:S(2)}) collective-permute-start(bf16[4,2432]{1,0:T(4,128)(2,1)S(1)} %get-tuple-element.47), channel_id=1, source_target_pairs={{0,2},{1,3},{2,0},{3,1},{4,6},{5,7},{6,4},{7,5},{8,10},{9,11},{10,... | collective-permute-start | bytes 58376 | tf_op jit(solution)/shard_map/ppermute | solution.py:34
  6.7 38.0 %collective-permute-start.17 = (bf16[512,1024]{1,0:T(8,128)(2,1)}, bf16[512,1024]{1,0:T(8,128)(2,1)S(1)}, u32[]{:S(2)}, u32[]{:S(2)}) collective-permute-start(bf16[512,1024]{1,0:T(8,128)(2,1)} %param.8), channel_id=1, source_target_pairs={{0,128},{1,129},{2,130},{3,131},{4,132},{5,133},{6,134},{7,135},{8... | collective-permute-start | bytes 3145736 | tf_op jit(solution)/shard_map/ppermute | solution.py:34
  9.6 3.2 %collective-permute-start.10 = (bf16[16,2432]{1,0:T(8,128)(2,1)S(1)}, bf16[16,2432]{1,0:T(8,128)(2,1)S(1)}, u32[]{:S(2)}, u32[]{:S(2)}) collective-permute-start(bf16[16,2432]{1,0:T(8,128)(2,1)S(1)} %pad_maximum_fusion.refs_0_), channel_id=1, source_target_pairs={{0,1},{1,0},{2,3},{3,2},{4,5},{5,4},{6,7},{7,6},{8,9},{9,8},{10,11... | collective-permute-start | bytes 233480 | tf_op jit(solution)/shard_map/ppermute | solution.py:34
  12.9 9.9 %collective-permute-start.12 = (bf16[32,2432]{1,0:T(8,128)(2,1)S(1)}, bf16[32,2432]{1,0:T(8,128)(2,1)S(1)}, u32[]{:S(2)}, u32[]{:S(2)}) collective-permute-start(bf16[32,2432]{1,0:T(8,128)(2,1)S(1)} %concatenate.16), channel_id=1, source_target_pairs={{0,32},{1,97},{2,34},{3,99},{4,36},{5,101},{6,38},{7,103},{8,40},{... | collective-permute-start | bytes 466952 | tf_op jit(solution)/shard_map/ppermute | solution.py:34
  19.0 8.0 %collective-permute-start.11 = (bf16[32,2432]{1,0:T(8,128)(2,1)S(1)}, bf16[32,2432]{1,0:T(8,128)(2,1)S(1)}, u32[]{:S(2)}, u32[]{:S(2)}) collective-permute-start(bf16[32,2432]{1,0:T(8,128)(2,1)S(1)} %concatenate.16), channel_id=1, source_target_pairs={{0,16},{1,113},{2,18},{3,115},{4,20},{5,117},{6,22},{7,119},{8,24}... | collective-permute-start | bytes 466952 | tf_op jit(solution)/shard_map/ppermute | solution.py:34
  22.9 7.1 %collective-permute-start.13 = (bf16[32,2432]{1,0:T(8,128)(2,1)S(1)}, bf16[32,2432]{1,0:T(8,128)(2,1)S(1)}, u32[]{:S(2)}, u32[]{:S(2)}) collective-permute-start(bf16[32,2432]{1,0:T(8,128)(2,1)S(1)} %collective-permute-done.12.refs_2_), channel_id=1, source_target_pairs={{0,16},{1,113},{2,18},{3,115},{4,20},{5,117},{6,22},{7,119},{8,24}... | collective-permute-start | bytes 466952 | tf_op jit(solution)/shard_map/ppermute | solution.py:34
  24.9 21.2 %copy-start = (bf16[512,1024]{1,0:T(8,128)(2,1)S(1)}, bf16[512,1024]{1,0:T(8,128)(2,1)}, u32[]{:S(2)}) copy-start(bf16[512,1024]{1,0:T(8,128)(2,1)} %param.8) | copy-start | bytes 3145732
  24.9 5.1 %collective-permute-start.14 = (bf16[16,2432]{1,0:T(8,128)(2,1)S(1)}, bf16[16,2432]{1,0:T(8,128)(2,1)S(1)}, u32[]{:S(2)}, u32[]{:S(2)}) collective-permute-start(bf16[16,2432]{1,0:T(8,128)(2,1)S(1)} %slice.4), channel_id=1, source_target_pairs={{0,32},{1,97},{2,34},{3,99},{4,36},{5,101},{6,38},{7,103},{8,40},{... | collective-permute-start | bytes 233480 | tf_op jit(solution)/shard_map/ppermute | solution.py:34
  31.0 5.9 %collective-permute-start.16 = (bf16[168,1152]{1,0:T(8,128)(2,1)S(1)}, bf16[168,1152]{1,0:T(8,128)(2,1)S(1)}, u32[]{:S(2)}, u32[]{:S(2)}) collective-permute-start(bf16[168,1152]{1,0:T(8,128)(2,1)S(1)} %shard_map.46.refs_0_.refs_2_), channel_id=1, source_target_pairs={{0,1},{1,0},{2,3},{3,2},{4,5},{5,4},{6,7},{7,6},{8,9},{9,8},{10,11... | collective-permute-start | bytes 1161224 | tf_op jit(solution)/shard_map/ppermute | solution.py:34
  34.5 7.1 %collective-permute-start.15 = (bf16[168,1152]{1,0:T(8,128)(2,1)S(1)}, bf16[168,1152]{1,0:T(8,128)(2,1)S(1)}, u32[]{:S(2)}, u32[]{:S(2)}) collective-permute-start(bf16[168,1152]{1,0:T(8,128)(2,1)S(1)} %shard_map.46.refs_0_.refs_2_), channel_id=1, source_target_pairs={{0,4},{1,13},{2,6},{3,15},{4,8},{5,1},{6,10},{7,3},{8,12},{9,5},{1... | collective-permute-start | bytes 1161224 | tf_op jit(solution)/shard_map/ppermute | solution.py:34
  37.0 10.8 %collective-permute-start.19 = (bf16[168,1152]{1,0:T(8,128)(2,1)S(1)}, bf16[168,1152]{1,0:T(8,128)(2,1)S(1)}, u32[]{:S(2)}, u32[]{:S(2)}) collective-permute-start(bf16[168,1152]{1,0:T(8,128)(2,1)S(1)} %collective-permute-done.16.refs_1_.refs_3_), channel_id=1, source_target_pairs={{0,4},{1,13},{2,6},{3,15},{4,8},{5,1},{6,10},{7,3},{8,12},{9,5},{1... | collective-permute-start | bytes 1161224 | tf_op jit(solution)/shard_map/ppermute | solution.py:34
  41.6 9.9 %collective-permute-start.18 = (bf16[168,1152]{1,0:T(8,128)(2,1)S(1)}, bf16[168,1152]{1,0:T(8,128)(2,1)S(1)}, u32[]{:S(2)}, u32[]{:S(2)}) collective-permute-start(bf16[168,1152]{1,0:T(8,128)(2,1)S(1)} %collective-permute-done.15.refs_2_.refs_4_), channel_id=1, source_target_pairs={{0,4},{1,13},{2,6},{3,15},{4,8},{5,1},{6,10},{7,3},{8,12},{9,5},{1... | collective-permute-start | bytes 1161224 | tf_op jit(solution)/shard_map/ppermute | solution.py:34
  47.5 4.9 %collective-permute-start.21 = (bf16[168,1152]{1,0:T(8,128)(2,1)S(1)}, bf16[168,1152]{1,0:T(8,128)(2,1)S(1)}, u32[]{:S(2)}, u32[]{:S(2)}) collective-permute-start(bf16[168,1152]{1,0:T(8,128)(2,1)S(1)} %collective-permute-done.15.refs_2_.refs_4_), channel_id=1, source_target_pairs={{0,1},{1,0},{2,3},{3,2},{4,5},{5,4},{6,7},{7,6},{8,9},{9,8},{10,11... | collective-permute-start | bytes 1161224 | tf_op jit(solution)/shard_map/ppermute | solution.py:34
  47.8 4.6 %collective-permute-start.22 = (bf16[168,1152]{1,0:T(8,128)(2,1)S(1)}, bf16[168,1152]{1,0:T(8,128)(2,1)S(1)}, u32[]{:S(2)}, u32[]{:S(2)}) collective-permute-start(bf16[168,1152]{1,0:T(8,128)(2,1)S(1)} %collective-permute-done.19.refs_3_.refs_5_), channel_id=1, source_target_pairs={{0,1},{1,0},{2,3},{3,2},{4,5},{5,4},{6,7},{7,6},{8,9},{9,8},{10,11... | collective-permute-start | bytes 1161224 | tf_op jit(solution)/shard_map/ppermute | solution.py:34
  51.5 2.5 %collective-permute-start.20 = (bf16[168,1152]{1,0:T(8,128)(2,1)S(1)}, bf16[168,1152]{1,0:T(8,128)(2,1)S(1)}, u32[]{:S(2)}, u32[]{:S(2)}) collective-permute-start(bf16[168,1152]{1,0:T(8,128)(2,1)S(1)} %collective-permute-done.18.refs_0_.refs_6_), channel_id=1, source_target_pairs={{0,1},{1,0},{2,3},{3,2},{4,5},{5,4},{6,7},{7,6},{8,9},{9,8},{10,11... | collective-permute-start | bytes 1161224 | tf_op jit(solution)/shard_map/ppermute | solution.py:34
